TPU v7x, 32 devices: a whole 2x2x4 slice. The times are simulated.
32 devices in a mesh: dp: 8 (over z, x), mp: 4 (over y, core).
Axes of the slice: x: 2, y: 2, z: 4, core: 2. Of those that a mesh axis runs over, the one named last changes fastest.
Arguments:
- tokens_in: bfloat16 [8, 1024, 2048], P('dp'), may hold values from -6 to 6
- cotangent: bfloat16 [8, 1024, 2048], P('dp'), may hold values from -6 to 6
- select_mask: int32 [8, 1024], P('dp'), may hold values 0 or 1
- doc_ids: int32 [8, 1024], P('dp'), may hold values from 0 to 3, never falling along the last dimension, each value on 1 to 512 neighbouring positions
- norm_gains: float32 [2, 2048], replicated, may hold values from 0.5 to 1.5
- weight_blocks: float32 [2688, 128, 128], P(('dp', 'mp'))
- ema_blocks: float32 [2688, 128, 128], P(('dp', 'mp')), may hold values from -1.5 to 1.5
- left_stats: float32 [2688, 128, 128], P(('dp', 'mp')), as said below
- right_stats: float32 [2688, 128, 128], P(('dp', 'mp')), as said below
- left_roots: float32 [2688, 128, 128], P(('dp', 'mp')), as said below
- right_roots: float32 [2688, 128, 128], P(('dp', 'mp')), as said below
Outputs:
- block_out: bfloat16 [8, 1024, 2048], P('dp')
- input_grad: float32 [8, 1024, 2048], P('dp')
- block_grads: float32 [2688, 128, 128], P(('dp', 'mp'))
- new_weights: float32 [2688, 128, 128], P(('dp', 'mp'))
- new_ema: float32 [2688, 128, 128], P(('dp', 'mp'))
- new_left: float32 [2688, 128, 128], P(('dp', 'mp'))
- new_right: float32 [2688, 128, 128], P(('dp', 'mp'))
- gain_grads: float32 [2, 2048], P(None, 'dp')
- new_gains: float32 [2, 2048], P(None, 'dp')
Inputs may be any that keep to these rules, and one draw needn't show every extreme that they name: `doc_ids`: within each sequence the ids never fall; every one of the 4 documents has 1 to 512 positions. `left_stats`: each block is symmetric. `right_stats`: each block is symmetric. `left_roots`: each block is symmetric. `right_roots`: each block is symmetric.
All inputs are finite; a program needn't handle non-finite values. No bound on the sum of `select_mask` on one device may be relied on, other than what follows from the above.
Results may differ from a plain program's by a relative error of at most 0.015.
The roundings to bfloat16 on the way count: a program that leaves them out, or rounds other values in their place, can miss the bound.
Values may be sent and summed in bfloat16 or wider, within the bound.
No kernel may reach another device: no remote copies, remote signals or barrier semaphores. Data moves between devices by JAX's collectives and lax.ppermute only.
A program may use at most 320 MiB of HBM per device.

v0:
```python
import jax
import jax.numpy as jnp
from jax import lax
from jax.sharding import PartitionSpec as P

HEADS = 32
KV_HEADS = 4
HD = 64
FF = 5632


highest = lax.Precision.HIGHEST
weight_rate = 1.0
gain_rate = 0.2
average_decay = 0.9


def doc_positions(doc_ids):
    length = doc_ids.shape[-1]
    offsets = jnp.arange(length, dtype=jnp.int32)
    starts = jnp.concatenate(
        [jnp.ones(doc_ids.shape[:-1] + (1,), jnp.bool_), doc_ids[..., 1:] != doc_ids[..., :-1]],
        axis=-1,
    )
    first_index = lax.cummax(jnp.where(starts, offsets, 0), axis=doc_ids.ndim - 1)
    return offsets - first_index


def rope_tables(positions, head_size):
    half_size = head_size // 2
    exponent = jnp.arange(half_size, dtype=jnp.float32) * (2.0 / head_size)
    inverse = jnp.power(jnp.float32(10000.0), -exponent)
    angles = positions.astype(jnp.float32)[..., None] * inverse
    return (jnp.cos(angles), jnp.sin(angles))


def rotate(values, cosine_table, sine_table):
    half_size = values.shape[-1] // 2
    first_half = values[..., :half_size]
    second_half = values[..., half_size:]
    return jnp.concatenate(
        [
            first_half * cosine_table - second_half * sine_table,
            second_half * cosine_table + first_half * sine_table,
        ],
        axis=-1,
    )


def rotate_back(grads, cosine_table, sine_table):
    half_size = grads.shape[-1] // 2
    first_half = grads[..., :half_size]
    second_half = grads[..., half_size:]
    return jnp.concatenate(
        [
            first_half * cosine_table + second_half * sine_table,
            second_half * cosine_table - first_half * sine_table,
        ],
        axis=-1,
    )


def normalize(values, gain):
    inverse_rms = lax.rsqrt(jnp.mean(values * values, axis=-1, keepdims=True) + 1e-05)
    unit = values * inverse_rms
    return (unit * gain, unit, inverse_rms)


def normalize_back(grad_out, unit, inverse_rms, gain):
    scaled = grad_out * gain
    return inverse_rms * (scaled - unit * jnp.mean(scaled * unit, axis=-1, keepdims=True))


def project(inputs, weights):
    row_count = inputs.shape[0]
    shaped = inputs.reshape(row_count, weights.shape[0], weights.shape[-1])
    return jnp.einsum("tri,rcij->tcj", shaped, weights, preferred_element_type=jnp.float32).reshape(
        row_count, -1
    )


def project_back(grads, weights):
    row_count = grads.shape[0]
    shaped = grads.reshape(row_count, weights.shape[1], weights.shape[-1])
    return jnp.einsum("tcj,rcij->tri", shaped, weights, preferred_element_type=jnp.float32).reshape(
        row_count, -1
    )


def weight_grad(inputs, grads, block_size):
    row_count = inputs.shape[0]
    left_shaped = inputs.reshape(row_count, -1, block_size)
    right_shaped = grads.reshape(row_count, -1, block_size)
    return jnp.einsum(
        "tri,tcj->rcij", left_shaped, right_shaped, preferred_element_type=jnp.float32
    )


def split_weights(gathered, row_blocks, attn_blocks, in_blocks, out_attn_blocks):
    block_size = gathered.shape[-1]
    in_count = row_blocks * in_blocks
    w_input = gathered[:in_count].reshape(row_blocks, in_blocks, block_size, block_size)
    w_output = gathered[in_count:].reshape(-1, row_blocks, block_size, block_size)
    return (
        w_input[:, :attn_blocks],
        w_input[:, attn_blocks:],
        w_output[:out_attn_blocks],
        w_output[out_attn_blocks:],
    )


def block_scores(query_part, keys, doc_ids, offset, scale):
    row_count = query_part.shape[0]
    query_index = offset + jnp.arange(row_count)
    key_index = jnp.arange(keys.shape[0])
    allowed = (key_index[None, :] <= query_index[:, None]) & (
        doc_ids[None, :] == doc_ids[offset : offset + row_count][:, None]
    )
    scores = (
        jnp.einsum("qgjd,kgd->gjqk", query_part, keys, preferred_element_type=jnp.float32) * scale
    )
    return jnp.where(allowed, scores, -1e30)


def attend_forward(queries, keys, values, doc_ids, query_block):
    length = queries.shape[0]
    scale = float(queries.shape[-1]) ** (-0.5)
    outputs = []
    totals = []
    for offset in range(0, length, query_block):
        scores = block_scores(queries[offset : offset + query_block], keys, doc_ids, offset, scale)
        maximum = jnp.max(scores, axis=-1, keepdims=True)
        expo_values = jnp.exp(scores - maximum)
        denominator = jnp.sum(expo_values, axis=-1, keepdims=True)
        probs = (expo_values / denominator).astype(jnp.bfloat16)
        outputs.append(
            jnp.einsum("gjqk,kgd->qgjd", probs, values, preferred_element_type=jnp.float32)
        )
        totals.append(maximum + jnp.log(denominator))
    return (jnp.concatenate(outputs, axis=0), jnp.concatenate(totals, axis=2))


def attend_backward(queries, keys, values, doc_ids, log_totals, out_grads, query_block):
    length = queries.shape[0]
    scale = float(queries.shape[-1]) ** (-0.5)
    key_grads = jnp.zeros(keys.shape, jnp.float32)
    value_grads = jnp.zeros(values.shape, jnp.float32)
    query_grads = []
    for offset in range(0, length, query_block):
        query_part = queries[offset : offset + query_block]
        scores = block_scores(query_part, keys, doc_ids, offset, scale)
        probs = jnp.exp(scores - log_totals[:, :, offset : offset + query_block])
        grad_part = out_grads[offset : offset + query_block]
        value_grads = value_grads + jnp.einsum(
            "gjqk,qgjd->kgd",
            probs.astype(jnp.bfloat16),
            grad_part,
            preferred_element_type=jnp.float32,
        )
        prob_grads = jnp.einsum(
            "qgjd,kgd->gjqk", grad_part, values, preferred_element_type=jnp.float32
        )
        inner = jnp.sum(probs * prob_grads, axis=-1, keepdims=True)
        score_grads = (probs * (prob_grads - inner)).astype(jnp.bfloat16)
        query_grads.append(
            jnp.einsum("gjqk,kgd->qgjd", score_grads, keys, preferred_element_type=jnp.float32)
            * scale
        )
        key_grads = (
            key_grads
            + jnp.einsum(
                "gjqk,qgjd->kgd", score_grads, query_part, preferred_element_type=jnp.float32
            )
            * scale
        )
    return (jnp.concatenate(query_grads, axis=0), key_grads, value_grads)


def on_device(
    tokens_in,
    cotangent,
    select_mask,
    doc_ids,
    norm_gains,
    weight_blocks,
    ema_blocks,
    left_stats,
    right_stats,
    left_roots,
    right_roots,
):
    mp_count = lax.axis_size("mp")
    dp_count = lax.axis_size("dp")
    sequences, length, model_width = tokens_in.shape
    row_count = sequences * length
    block_size = weight_blocks.shape[-1]
    query_cols = HEADS * HD // mp_count
    key_cols = KV_HEADS * HD // mp_count
    hidden_cols = FF // mp_count
    kv_local = KV_HEADS // mp_count
    group_size = HEADS // KV_HEADS
    row_blocks = model_width // block_size
    attn_blocks = (query_cols + 2 * key_cols) // block_size
    in_blocks = attn_blocks + 2 * hidden_cols // block_size
    out_attn_blocks = query_cols // block_size
    query_block = min(512, length)
    share_rows = row_count // mp_count
    share_start = lax.axis_index("mp") * share_rows

    def row_share(values):
        return lax.dynamic_slice_in_dim(values, share_start, share_rows, 0)

    weights_low = weight_blocks.astype(jnp.bfloat16)
    gathered = lax.all_gather(weights_low, "dp", axis=0, tiled=True)
    w_qkv, w_gateup, w_attn_out, w_down = split_weights(
        gathered, row_blocks, attn_blocks, in_blocks, out_attn_blocks
    )
    positions = doc_positions(doc_ids)
    cosine_table, sine_table = rope_tables(positions, HD)
    query_cos = cosine_table[:, :, None, None, :]
    query_sin = sine_table[:, :, None, None, :]
    key_cos = cosine_table[:, :, None, :]
    key_sin = sine_table[:, :, None, :]
    tokens = tokens_in.astype(jnp.float32).reshape(row_count, model_width)
    first_norm, first_unit, first_scale = normalize(tokens, norm_gains[0])
    first_in = first_norm.astype(jnp.bfloat16)
    qkv = project(first_in, w_qkv)
    queries_raw = qkv[:, :query_cols].reshape(sequences, length, kv_local, group_size, HD)
    keys_raw = qkv[:, query_cols : query_cols + key_cols].reshape(sequences, length, kv_local, HD)
    values_raw = qkv[:, query_cols + key_cols :].reshape(sequences, length, kv_local, HD)
    query_use = rotate(queries_raw, query_cos, query_sin).astype(jnp.bfloat16)
    key_use = rotate(keys_raw, key_cos, key_sin).astype(jnp.bfloat16)
    value_use = values_raw.astype(jnp.bfloat16)

    def forward_one(items):
        return attend_forward(items[0], items[1], items[2], items[3], query_block)

    mixed, log_totals = lax.map(forward_one, (query_use, key_use, value_use, doc_ids))
    mixed_use = mixed.reshape(row_count, query_cols).astype(jnp.bfloat16)
    attended_part = lax.psum_scatter(
        project(mixed_use, w_attn_out), "mp", scatter_dimension=0, tiled=True
    )
    middle = row_share(tokens) + attended_part
    second_norm, second_unit, second_scale = normalize(middle, norm_gains[1])
    second_in = lax.all_gather(second_norm.astype(jnp.bfloat16), "mp", axis=0, tiled=True)
    gateup = project(second_in, w_gateup)
    gate = gateup[:, :hidden_cols]
    up_part = gateup[:, hidden_cols:]
    sigmoid_gate = jax.nn.sigmoid(gate)
    hidden = (gate * sigmoid_gate * up_part).astype(jnp.bfloat16)
    feed_part = lax.psum_scatter(project(hidden, w_down), "mp", scatter_dimension=0, tiled=True)
    out_whole = lax.all_gather((middle + feed_part).astype(jnp.bfloat16), "mp", axis=0, tiled=True)
    block_out = out_whole.reshape(sequences, length, model_width)
    out_grad = cotangent.astype(jnp.float32).reshape(row_count, model_width) * select_mask.astype(
        jnp.float32
    ).reshape(row_count, 1)
    mlp_grad = out_grad.astype(jnp.bfloat16)
    grad_down = weight_grad(hidden, mlp_grad, block_size)
    hidden_grad = project_back(mlp_grad, w_down)
    gate_grad = hidden_grad * up_part * sigmoid_gate * (1.0 + gate * (1.0 - sigmoid_gate))
    up_grad = hidden_grad * gate * sigmoid_gate
    gateup_grad = jnp.concatenate([gate_grad, up_grad], axis=1).astype(jnp.bfloat16)
    grad_gateup = weight_grad(second_in, gateup_grad, block_size)
    second_grad = lax.psum_scatter(
        project_back(gateup_grad, w_gateup), "mp", scatter_dimension=0, tiled=True
    )
    middle_grad = row_share(out_grad) + normalize_back(
        second_grad, second_unit, second_scale, norm_gains[1]
    )
    second_gain = jnp.sum(second_grad * second_unit, axis=0)
    attn_grad = lax.all_gather(middle_grad.astype(jnp.bfloat16), "mp", axis=0, tiled=True)
    grad_attn_out = weight_grad(mixed_use, attn_grad, block_size)
    mixed_grad = (
        project_back(attn_grad, w_attn_out)
        .astype(jnp.bfloat16)
        .reshape(sequences, length, kv_local, group_size, HD)
    )

    def backward_one(items):
        return attend_backward(
            items[0], items[1], items[2], items[3], items[4], items[5], query_block
        )

    query_grad, key_grad, value_grad = lax.map(
        backward_one, (query_use, key_use, value_use, doc_ids, log_totals, mixed_grad)
    )
    query_grad = rotate_back(query_grad, query_cos, query_sin).reshape(row_count, query_cols)
    key_grad = rotate_back(key_grad, key_cos, key_sin).reshape(row_count, key_cols)
    qkv_grad = jnp.concatenate(
        [query_grad, key_grad, value_grad.reshape(row_count, key_cols)], axis=1
    ).astype(jnp.bfloat16)
    grad_qkv = weight_grad(first_in, qkv_grad, block_size)
    first_grad = lax.psum_scatter(
        project_back(qkv_grad, w_qkv), "mp", scatter_dimension=0, tiled=True
    )
    unit_share = row_share(first_unit)
    input_part = middle_grad + normalize_back(
        first_grad, unit_share, row_share(first_scale), norm_gains[0]
    )
    first_gain = jnp.sum(first_grad * unit_share, axis=0)
    gain_part = jnp.stack([first_gain, second_gain], axis=0)
    input_grad, gain_rows = (
        lax.all_gather(input_part, "mp", axis=0, tiled=True),
        lax.all_gather(gain_part, "mp", axis=0, tiled=True),
    )
    gain_terms = jnp.sum(gain_rows.reshape(mp_count, 2, model_width), axis=0)
    in_grads = jnp.concatenate([grad_qkv, grad_gateup], axis=1).reshape(-1, block_size, block_size)
    out_grads = jnp.concatenate([grad_attn_out, grad_down], axis=0).reshape(
        -1, block_size, block_size
    )
    all_grads = jnp.concatenate([in_grads, out_grads], axis=0)
    reduced, gain_sums = (
        lax.psum_scatter(all_grads, "dp", scatter_dimension=0, tiled=True),
        lax.psum_scatter(gain_terms, "dp", scatter_dimension=1, tiled=True),
    )
    factor = float(row_count * dp_count) ** (-0.5)
    grads = reduced * factor
    gain_grads = gain_sums * factor
    new_left = 0.5 * left_stats + 0.5 * jnp.einsum("bij,bkj->bik", grads, grads, precision=highest)
    new_right = 0.5 * right_stats + 0.5 * jnp.einsum(
        "bji,bjk->bik", grads, grads, precision=highest
    )
    right_part = jnp.einsum("bij,bjk->bik", grads, right_roots, precision=highest)
    direction = jnp.einsum("bij,bjk->bik", left_roots, right_part, precision=highest)
    new_weights = weight_blocks - weight_rate * direction
    new_ema = average_decay * ema_blocks + (1.0 - average_decay) * new_weights
    share = model_width // dp_count
    gain_share = lax.dynamic_slice_in_dim(norm_gains, lax.axis_index("dp") * share, share, 1)
    new_gains = gain_share - gain_rate * gain_grads
    input_out = input_grad.reshape(sequences, length, model_width)
    return (
        block_out,
        input_out,
        grads,
        new_weights,
        new_ema,
        new_left,
        new_right,
        gain_grads,
        new_gains,
    )


def solution(mesh):
    in_specs = (
        P("dp", None, None),
        P("dp", None, None),
        P("dp", None),
        P("dp", None),
        P(),
        P(("dp", "mp"), None, None),
        P(("dp", "mp"), None, None),
        P(("dp", "mp"), None, None),
        P(("dp", "mp"), None, None),
        P(("dp", "mp"), None, None),
        P(("dp", "mp"), None, None),
    )
    out_specs = (
        P("dp", None, None),
        P("dp", None, None),
        P(("dp", "mp"), None, None),
        P(("dp", "mp"), None, None),
        P(("dp", "mp"), None, None),
        P(("dp", "mp"), None, None),
        P(("dp", "mp"), None, None),
        P(None, "dp"),
        P(None, "dp"),
    )
    return jax.shard_map(
        on_device, mesh=mesh, in_specs=in_specs, out_specs=out_specs, check_vma=False
    )
```

profile of v0, /device:TPU:0, one launch (start us, length us, event | category | flops | bytes accessed | tf_op | source)
XLA Modules:
  0.0 2003.4 jit_solution(1288071016080694105)
XLA Ops:
  7.2 4.7 convert_element_type.128
  12.0 14.3 convert_bitcast_fusion.1
  26.3 8.7 copy.178
  41.2 395.0 %all-gather.7.cloned.1.call-done = bf16[672,128,128]{2,1,0:T(8,128)(2,1)} async-done(((bf16[84,128,128]{2,1,0:T(8,128)(2,1)}), bf16[672,128,128]{2,1,0:T(8,128)(2,1)}) %all-gather.7.cloned.1.call-update) | async-done | bytes 22020112 | tf_op jit(solution)/shard_map/all_gather | solution.py:214
  436.2 8.0 slice.158
  444.2 4.9 copy-done.1
  454.5 9.0 fusion.66
  465.0 7.2 fusion.137
  472.2 8.0 fusion.7
  480.3 7.4 fusion.76
  487.7 7.5 fusion.138
  495.3 8.0 fusion.6
  503.4 7.4 fusion.73
  515.5 7.3 convolution_bitcast_fusion.5
  522.9 71.8 %reduce-scatter.9.cloned.1.call-done = f32[256,2048]{1,0:T(8,128)} async-done(((f32[1024,2048]{1,0:T(8,128)}), f32[256,2048]{1,0:T(8,128)}) %reduce-scatter.9.cloned.1.call-update) | async-done | bytes 2097168 | tf_op jit(solution)/shard_map/reduce_scatter | solution.py:240
  601.7 3.4 copy.179
  605.1 12.5 slice_bitcast_fusion.3
  617.6 5.3 copy.118
  622.9 15.2 copy.173
  638.1 3.9 slice.173
  644.4 3.8 copy.112
  648.1 18.9 convolution_bitcast_fusion.1
  667.0 15.0 fusion.30
  682.0 4.5 copy.115
  686.6 4.5 copy.117
  691.1 4.5 copy.114
  695.6 4.5 copy.116
  700.2 19.0 convolution_bitcast_fusion.3
  719.3 8.3 copy.110
  727.6 5.0 copy.109
  732.5 12.2 convolution_bitcast_fusion.4
  744.9 6.6 convert_bitcast_fusion
  751.5 39.7 %reduce-scatter.13.cloned.1.call-done = f32[256,2048]{1,0:T(8,128)} async-done(((f32[1024,2048]{1,0:T(8,128)}), f32[256,2048]{1,0:T(8,128)}) %reduce-scatter.13.cloned.1.call-update) | async-done | bytes 2097168 | tf_op jit(solution)/shard_map/reduce_scatter | solution.py:264
  793.3 72.0 %reduce-scatter.11.cloned.1.call-done = f32[256,2048]{1,0:T(8,128)} async-done(((f32[1024,2048]{1,0:T(8,128)}), f32[256,2048]{1,0:T(8,128)}) %reduce-scatter.11.cloned.1.call-update) | async-done | bytes 2097168 | tf_op jit(solution)/shard_map/reduce_scatter | solution.py:251
  865.3 5.7 fusion.132
  876.4 29.4 %all-gather.13.cloned.1.call-done = bf16[1024,2048]{1,0:T(8,128)(2,1)} async-done(((bf16[256,2048]{1,0:T(8,128)(2,1)}), bf16[1024,2048]{1,0:T(8,128)(2,1)}) %all-gather.13.cloned.1.call-update) | async-done | bytes 4194320 | tf_op jit(solution)/shard_map/all_gather | solution.py:271
  905.7 5.2 bitcast_convert_fusion
  911.0 7.4 fusion.82
  918.4 13.0 fusion.3
  932.2 8.3 fusion
  940.4 7.9 fusion.18
  955.4 12.0 fusion.17
  974.2 5.7 convolution_bitcast_fusion.2
  980.8 71.0 %reduce-scatter.15.cloned.1.call-done = f32[256,2048]{1,0:T(8,128)} async-done(((f32[1024,2048]{1,0:T(8,128)}), f32[256,2048]{1,0:T(8,128)}) %reduce-scatter.15.cloned.1.call-update) | async-done | bytes 2097168 | tf_op jit(solution)/shard_map/reduce_scatter | solution.py:293
  1054.6 5.2 all-gather
  1061.3 4.7 multiply_add_fusion.1
  1073.5 9.9 fusion.52
  1083.3 20.1 %convolution_bitcast_fusion = f32[16,22,128,128]{2,3,0,1:T(8,128)} fusion(bf16[1024,11,128]{2,0,1:T(8,128)(2,1)} %copy.117, bf16[1024,11,128]{2,0,1:T(8,128)(2,1)} %copy.116, bf16[1024,2048]{1,0:T(8,128)(2,1)} %all-gather.9.cloned.1.call-done), kind=kOutput, calls=%fused_computation.27 | convolution fusion | flops 11822694400 | bytes 33030144 | tf_op jit(solution)/shard_map/tri,tcj->rcij/dot_general | solution.py:94
  1103.4 3.6 copy.181
  1109.5 6.0 pad_maximum_fusion.2
  1115.5 15.8 copy.138
  1131.4 4.8 fusion.57
  1136.2 18.6 pad_maximum_fusion.1
  1154.8 28.3 %copy.132 = f32[16,27,128,128]{3,2,1,0:T(8,128)} copy(f32[16,27,128,128]{2,3,0,1:T(8,128)} %pad_maximum_fusion.1) | data formatting | bytes 56623104 | tf_op jit(solution)/shard_map/concatenate | solution.py:307
  1183.1 30.2 %pad_maximum_fusion = f32[672,128,128]{2,1,0:T(8,128)} fusion(f32[240,128,128]{2,1,0:T(8,128)} %bitcast.360, f32[432,128,128]{2,1,0:T(8,128)} %bitcast.359), kind=kLoop, calls=%fused_computation | loop fusion | flops 11010048 | bytes 88080384 | tf_op jit(solution)/shard_map/concatenate | solution.py:311
  1213.4 6.1 copy.140
  1219.4 6.1 copy.141
  1227.8 686.6 %reduce-scatter.17.cloned.1.call-done = f32[84,128,128]{2,1,0:T(8,128)} async-done(((f32[672,128,128]{2,1,0:T(8,128)}), f32[84,128,128]{2,1,0:T(8,128)}) %reduce-scatter.17.cloned.1.call-update) | async-done | bytes 5505040 | tf_op jit(solution)/shard_map/reduce_scatter | solution.py:313
  1920.5 11.7 fusion.143
  1932.3 16.3 multiply_add_fusion
  1948.6 6.1 copy.143
  1954.7 6.2 copy.144
  1960.8 17.8 add_multiply_fusion.1
  1978.7 12.6 add_multiply_fusion
  (216 shorter events, 78.0 us)
Async XLA Ops:
  7.2 429.0 %all-gather.7.cloned.1.call-start = ((), (), s32[]{:S(2)}) async-start(), calls=%async_computation.6 | async-start | bytes 24772608 | tf_op jit(solution)/shard_map/all_gather | solution.py:214
  11.9 582.8 %reduce-scatter.9.cloned.1.call-start = ((), (), s32[]{:S(2)}) async-start(), calls=%async_computation.7 | async-start | bytes 10485760 | tf_op jit(solution)/shard_map/reduce_scatter | solution.py:240
  26.3 8.7 copy-start.37
  35.0 6.2 copy-start.44
  35.8 427.9 %copy-start.45 = (f32[32]{0:T(128)}, f32[32]{0:T(128)S(1)}, u32[]{:S(2)}) copy-start(f32[32]{0:T(128)S(1)} %negate_power_fusion) | copy-start | bytes 388
  39.0 415.5 %copy-start.42 = (f32[1024]{0:T(1024)}, f32[1024]{0:T(1024)S(1)}, u32[]{:S(2)}) copy-start(f32[1024]{0:T(1024)S(1)} %add_rsqrt_fusion) | copy-start | bytes 12292
  39.1 424.7 %copy-start.35 = (f32[1024]{0:T(1024)}, f32[1024]{0:T(1024)S(1)}, u32[]{:S(2)}) copy-start(f32[1024]{0:T(1024)S(1)} %fusion.124) | copy-start | bytes 12292
  39.6 424.7 %copy-start.25 = (f32[1024,32]{0,1:T(8,128)}, f32[1024,32]{0,1:T(8,128)S(1)}, u32[]{:S(2)}) copy-start(f32[1024,32]{0,1:T(8,128)S(1)} %get-tuple-element.118) | copy-start | bytes 393220
  39.6 424.7 %copy-start.27 = (f32[1024,32]{0,1:T(8,128)}, f32[1024,32]{0,1:T(8,128)S(1)}, u32[]{:S(2)}) copy-start(f32[1024,32]{0,1:T(8,128)S(1)} %get-tuple-element.119) | copy-start | bytes 393220
  41.2 413.4 %copy-start.33 = (f32[1,2048]{1,0:T(1,128)}, f32[1,2048]{1,0:T(1,128)S(1)}, u32[]{:S(2)}) copy-start(f32[1,2048]{1,0:T(1,128)S(1)} %get-tuple-element.117) | copy-start | bytes 24580
  444.2 5.0 copy-start.1
  463.6 39.7 %copy-start.12 = (f32[1024,640]{0,1:T(8,128)}, f32[1024,640]{0,1:T(8,128)S(1)}, u32[]{:S(2)}) copy-start(f32[1024,640]{0,1:T(8,128)S(1)} %fusion.66) | copy-start | bytes 7864324
  464.4 23.4 %copy-start.19 = (bf16[1024,32]{0,1:T(8,128)(2,1)}, bf16[1024,32]{0,1:T(8,128)(2,1)S(1)}, u32[]{:S(2)}) copy-start(bf16[1024,32]{0,1:T(8,128)(2,1)S(1)} %get-tuple-element.114) | copy-start | bytes 196612
  464.4 23.4 %copy-start.21 = (bf16[1024,32]{0,1:T(8,128)(2,1)}, bf16[1024,32]{0,1:T(8,128)(2,1)S(1)}, u32[]{:S(2)}) copy-start(bf16[1024,32]{0,1:T(8,128)(2,1)S(1)} %get-tuple-element.115) | copy-start | bytes 196612
  464.7 23.0 %copy-start.4 = (bf16[1,1024,1,8,32]{1,4,3,2,0:T(8,128)(2,1)}, bf16[1,1024,1,8,32]{1,4,3,2,0:T(8,128)(2,1)S(1)}, u32[]{:S(2)}) copy-start(bf16[1,1024,1,8,32]{1,4,3,2,0:T(8,128)(2,1)S(1)} %get-tuple-element.107) | copy-start | bytes 1572868
  464.7 23.0 %copy-start.6 = (bf16[1,1024,1,8,32]{1,4,3,2,0:T(8,128)(2,1)}, bf16[1,1024,1,8,32]{1,4,3,2,0:T(8,128)(2,1)S(1)}, u32[]{:S(2)}) copy-start(bf16[1,1024,1,8,32]{1,4,3,2,0:T(8,128)(2,1)S(1)} %get-tuple-element.108) | copy-start | bytes 1572868
  472.2 8.0 copy-start.29
  480.2 7.4 copy-start.38
  487.7 27.7 %copy-start.14 = (bf16[64,8,512]{2,0,1:T(8,128)(2,1)}, bf16[64,8,512]{2,0,1:T(8,128)(2,1)S(1)}, u32[]{:S(2)}) copy-start(bf16[64,8,512]{2,0,1:T(8,128)(2,1)S(1)} %fusion.76) | copy-start | bytes 1572868
  495.3 8.1 copy-start.31
  503.3 7.4 copy-start.40
  510.8 12.0 copy-start.16
  512.7 10.1 copy-start.3
  522.8 75.7 %copy-start.47 = (s32[1,1024]{1,0:T(1,128)S(1)}, s32[1,1024]{1,0:T(1,128)}, u32[]{:S(2)}) copy-start(s32[1,1024]{1,0:T(1,128)} %param.13) | copy-start | bytes 12292
  522.8 125.3 %all-gather.9.cloned.1.call-start = ((), (), s32[]{:S(2)}) async-start(), calls=%async_computation.8 | async-start | bytes 5242880 | tf_op jit(solution)/shard_map/all_gather | solution.py:245
  598.5 192.6 %reduce-scatter.13.cloned.1.call-start = ((), (), s32[]{:S(2)}) async-start(), calls=%async_computation.11 | async-start | bytes 10485760 | tf_op jit(solution)/shard_map/reduce_scatter | solution.py:264
  648.1 18.9 copy-start.10
  719.2 146.1 %reduce-scatter.11.cloned.1.call-start = ((), (), s32[]{:S(2)}) async-start(), calls=%async_computation.9 | async-start | bytes 10485760 | tf_op jit(solution)/shard_map/reduce_scatter | solution.py:251
  744.8 160.9 %all-gather.13.cloned.1.call-start = ((), (), s32[]{:S(2)}) async-start(), calls=%async_computation.12 | async-start | bytes 5242880 | tf_op jit(solution)/shard_map/all_gather | solution.py:271
  871.0 3.6 copy-start.8
  871.0 5.3 copy-start.32
  871.0 5.3 copy-start.41
  871.0 5.3 copy-start.30
  871.0 5.3 copy-start.39
  871.1 180.7 %reduce-scatter.15.cloned.1.call-start = ((), (), s32[]{:S(2)}) async-start(), calls=%async_computation.13 | async-start | bytes 10485760 | tf_op jit(solution)/shard_map/reduce_scatter | solution.py:293
  911.0 20.4 %slice-start = ((s8[16777216]{0:T(1024)(128)(4,1)}), s8[4194304]{0:T(1024)(128)(4,1)S(1)}, s32[]{:S(2)}) async-start(s8[16777216]{0:T(1024)(128)(4,1)} %bitcast.355), calls=%async_computation.17 | async-start | bytes 8388608
  911.0 20.4 %slice-start.1 = ((s8[16777216]{0:T(1024)(128)(4,1)}), s8[4194304]{0:T(1024)(128)(4,1)S(1)}, s32[]{:S(2)}) async-start(s8[16777216]{0:T(1024)(128)(4,1)} %bitcast.355), calls=%async_computation.18 | async-start | bytes 8388608
  918.4 13.0 slice-start.2
  918.4 13.7 slice-start.3
  940.4 7.9 copy-start.5
  940.4 7.9 copy-start.7
  969.0 2.7 copy-start.36
  969.0 2.7 copy-start.46
  969.1 3.4 copy-start.26
  969.1 3.4 copy-start.28
  979.9 71.9 %copy-start.34 = (f32[1,2048]{1,0:T(1,128)S(1)}, f32[1,2048]{1,0:T(1,128)}, u32[]{:S(2)}) copy-start(f32[1,2048]{1,0:T(1,128)} %copy-done.33) | copy-start | bytes 24580
  979.9 81.4 %copy-start.9 = (f32[256,2048]{1,0:T(8,128)S(1)}, f32[256,2048]{1,0:T(8,128)}, u32[]{:S(2)}) copy-start(f32[256,2048]{1,0:T(8,128)} %get-tuple-element.92) | copy-start | bytes 6291460
  979.9 245.6 %all-gather.11.cloned.1.call-start = ((), (), s32[]{:S(2)}) async-start(), calls=%async_computation.10 | async-start | bytes 5242880 | tf_op jit(solution)/shard_map/all_gather | solution.py:252
  980.7 244.9 %reduce-scatter.19.cloned.1.call-start = ((), (), s32[]{:S(2)}) async-start(), calls=%async_computation.16 | async-start | bytes 1179648
  1061.2 166.6 %all-gather.15.cloned.1.call-start = ((), (), s32[]{:S(2)}) async-start(), calls=%async_computation.14 | async-start | bytes 10485760 | tf_op jit(solution)/shard_map/all_gather | solution.py:303
  1066.0 848.4 %reduce-scatter.17.cloned.1.call-start = ((), (), s32[]{:S(2)}) async-start(), calls=%async_computation.15 | async-start | bytes 49545216 | tf_op jit(solution)/shard_map/reduce_scatter | solution.py:313
  1069.5 3.5 copy-start.15
  1069.5 3.7 copy-start.17
  1115.5 15.8 copy-start.24
  1914.4 17.8 slice-start.6
  1914.4 17.8 slice-start.8
  1917.8 2.7 copy-start
  1920.5 11.7 slice-start.7
  1920.5 11.8 slice-start.9
  1954.7 24.0 %slice-start.4 = ((s8[5505024]{0:T(1024)(128)(4,1)}), s8[1310720]{0:T(1024)(128)(4,1)S(1)}, s32[]{:S(2)}) async-start(s8[5505024]{0:T(1024)(128)(4,1)} %bitcast.357), calls=%async_computation.21 | async-start | bytes 2621440
  1960.8 17.8 slice-start.5
  1960.8 32.4 %slice-start.10 = ((s8[8388608]{0:T(1024)(128)(4,1)}), s8[4194304]{0:T(1024)(128)(4,1)S(1)}, s32[]{:S(2)}) async-start(s8[8388608]{0:T(1024)(128)(4,1)} %bitcast.376), calls=%async_computation.27 | async-start | bytes 8388608
  1978.6 12.6 copy-start.11
  1978.7 14.6 slice-start.11
  (7 other events, 13.0 us)
Sparse Core Ops, SparseCore 0:
  12.0 424.1 all-gather.6
  522.9 71.6 reduce-scatter.8
  598.6 34.4 all-gather.8
  719.4 71.7 reduce-scatter.12
  793.6 71.7 reduce-scatter.10
  871.2 34.4 all-gather.12
  980.0 71.6 reduce-scatter.14
  1053.3 34.4 all-gather.10
  1091.2 63.4 reduce-scatter.18
  1156.8 57.2 all-gather.14
  1218.5 695.8 reduce-scatter.16
where the time goes:
time: 2010 us; the launch traced here: 2000 us
  waiting for transfers between devices  1370 us (68%)
  matrix products  257 us (13%)
  local copies, waits for them, and re-layouts  204 us (10%)
  other arithmetic  155 us (8%)
    reduce_scatter x1, waiting for transfers between devices, on_device(): lax.psum_scatter(all_grads, 'dp', scatter_dimension=0, tiled=True)  687 us
    all_gather x1, waiting for transfers between devices, on_device(): gathered = lax.all_gather(weights_low, 'dp', axis=0, tiled=True)  395 us
    unnamed x134, local copies, waits for them, and re-layouts  81.5 us
    reduce_scatter x1, waiting for transfers between devices, on_device(): lax.psum_scatter(project(hidden, w_down), 'mp', scatter_dimension=0, tile...  72 us
    reduce_scatter x1, waiting for transfers between devices, on_device(): lax.psum_scatter(project(mixed_use, w_attn_out), 'mp', scatter_dimension=...  71.8 us
    reduce_scatter x1, waiting for transfers between devices, on_device(): lax.psum_scatter(project_back(qkv_grad, w_qkv), 'mp', scatter_dimension=0...  71 us
    dot_general x4, matrix products, project(): jnp.einsum('tri,rcij->tcj', shaped, weights, preferred_element_type=jnp.f...  47.5 us
    dot_general x4, matrix products, project_back(): jnp.einsum('tcj,rcij->tri', shaped, weights, preferred_element_type=jnp.f...  45 us
  transfers between devices with their start and end apart: 11, of which 7 were waited for; matrix products, arithmetic and copies ran while one was open for 14% of the time, Pallas kernels for 0%

commit v1 on v0

--- a/solution.py
+++ b/solution.py
@@ -174,6 +174,16 @@
             * scale
         )
     return (jnp.concatenate(query_grads, axis=0), key_grads, value_grads)
+
+
+def ring_order(count):
+    return list(range(0, count, 2)) + list(range(1, count, 2))[::-1]
+
+
+def sum_rows(values):
+    return lax.psum_scatter(
+        values.astype(jnp.bfloat16), "mp", scatter_dimension=0, tiled=True
+    ).astype(jnp.float32)
 
 
 def on_device(
@@ -210,8 +220,14 @@
     def row_share(values):
         return lax.dynamic_slice_in_dim(values, share_start, share_rows, 0)
 
+    ring = ring_order(dp_count)
+    places = [ring.index(rank) for rank in range(dp_count)]
+    own = weight_blocks.shape[0]
     weights_low = weight_blocks.astype(jnp.bfloat16)
-    gathered = lax.all_gather(weights_low, "dp", axis=0, tiled=True)
+    in_ring = lax.all_gather(weights_low, "dp", axis=0, tiled=True, axis_index_groups=[ring])
+    gathered = jnp.concatenate(
+        [in_ring[place * own : (place + 1) * own] for place in places], axis=0
+    )
     w_qkv, w_gateup, w_attn_out, w_down = split_weights(
         gathered, row_blocks, attn_blocks, in_blocks, out_attn_blocks
     )
@@ -237,9 +253,7 @@
 
     mixed, log_totals = lax.map(forward_one, (query_use, key_use, value_use, doc_ids))
     mixed_use = mixed.reshape(row_count, query_cols).astype(jnp.bfloat16)
-    attended_part = lax.psum_scatter(
-        project(mixed_use, w_attn_out), "mp", scatter_dimension=0, tiled=True
-    )
+    attended_part = sum_rows(project(mixed_use, w_attn_out))
     middle = row_share(tokens) + attended_part
     second_norm, second_unit, second_scale = normalize(middle, norm_gains[1])
     second_in = lax.all_gather(second_norm.astype(jnp.bfloat16), "mp", axis=0, tiled=True)
@@ -248,7 +262,7 @@
     up_part = gateup[:, hidden_cols:]
     sigmoid_gate = jax.nn.sigmoid(gate)
     hidden = (gate * sigmoid_gate * up_part).astype(jnp.bfloat16)
-    feed_part = lax.psum_scatter(project(hidden, w_down), "mp", scatter_dimension=0, tiled=True)
+    feed_part = sum_rows(project(hidden, w_down))
     out_whole = lax.all_gather((middle + feed_part).astype(jnp.bfloat16), "mp", axis=0, tiled=True)
     block_out = out_whole.reshape(sequences, length, model_width)
     out_grad = cotangent.astype(jnp.float32).reshape(row_count, model_width) * select_mask.astype(
@@ -261,9 +275,7 @@
     up_grad = hidden_grad * gate * sigmoid_gate
     gateup_grad = jnp.concatenate([gate_grad, up_grad], axis=1).astype(jnp.bfloat16)
     grad_gateup = weight_grad(second_in, gateup_grad, block_size)
-    second_grad = lax.psum_scatter(
-        project_back(gateup_grad, w_gateup), "mp", scatter_dimension=0, tiled=True
-    )
+    second_grad = sum_rows(project_back(gateup_grad, w_gateup))
     middle_grad = row_share(out_grad) + normalize_back(
         second_grad, second_unit, second_scale, norm_gains[1]
     )
@@ -290,9 +302,7 @@
         [query_grad, key_grad, value_grad.reshape(row_count, key_cols)], axis=1
     ).astype(jnp.bfloat16)
     grad_qkv = weight_grad(first_in, qkv_grad, block_size)
-    first_grad = lax.psum_scatter(
-        project_back(qkv_grad, w_qkv), "mp", scatter_dimension=0, tiled=True
-    )
+    first_grad = sum_rows(project_back(qkv_grad, w_qkv))
     unit_share = row_share(first_unit)
     input_part = middle_grad + normalize_back(
         first_grad, unit_share, row_share(first_scale), norm_gains[0]
@@ -300,7 +310,7 @@
     first_gain = jnp.sum(first_grad * unit_share, axis=0)
     gain_part = jnp.stack([first_gain, second_gain], axis=0)
     input_grad, gain_rows = (
-        lax.all_gather(input_part, "mp", axis=0, tiled=True),
+        lax.all_gather(input_part.astype(jnp.bfloat16), "mp", axis=0, tiled=True).astype(jnp.float32),
         lax.all_gather(gain_part, "mp", axis=0, tiled=True),
     )
     gain_terms = jnp.sum(gain_rows.reshape(mp_count, 2, model_width), axis=0)
@@ -308,9 +318,15 @@
     out_grads = jnp.concatenate([grad_attn_out, grad_down], axis=0).reshape(
         -1, block_size, block_size
     )
-    all_grads = jnp.concatenate([in_grads, out_grads], axis=0)
+    all_grads = jnp.concatenate([in_grads, out_grads], axis=0).astype(jnp.bfloat16)
     reduced, gain_sums = (
-        lax.psum_scatter(all_grads, "dp", scatter_dimension=0, tiled=True),
+        lax.psum_scatter(
+            jnp.concatenate([all_grads[rank * own : (rank + 1) * own] for rank in ring], axis=0),
+            "dp",
+            scatter_dimension=0,
+            tiled=True,
+            axis_index_groups=[ring],
+        ).astype(jnp.float32),
         lax.psum_scatter(gain_terms, "dp", scatter_dimension=1, tiled=True),
     )
     factor = float(row_count * dp_count) ** (-0.5)

time: 2010 us -> 1210 us (0.60)
  waiting for transfers between devices: 1370 us -> 573 us
  other arithmetic: 155 us -> 122 us
  local copies, waits for them, and re-layouts: 204 us -> 235 us
    reduce_scatter x5, waiting for transfers between devices: 941 us -> 351 us  [the longest x1 212 us: on_device(): lax.psum_scatter(jnp.concatenate([all_grads[rank * own:(rank + 1) * own]...]
    all_gather x2, waiting for transfers between devices: 395 us -> 192 us  [the longest x1 189 us: on_device(): lax.all_gather(weights_low, 'dp', axis=0, tiled=True, axis_index_groups=[...]
    unnamed x134 -> x165, local copies, waits for them, and re-layouts: 81.5 us -> 119 us
    concatenate x1, other arithmetic: 30.2 us -> 0.5 us  [on_device(): jnp.concatenate([in_ring[place * own:(place + 1) * own] for place in plac...]
  transfers between devices with their start and end apart: 11 -> 11, of which waited for: 7 -> 8; matrix products, arithmetic and copies ran while one was open for 14% -> 21% of each run, Pallas kernels for 0% -> 0%
where the time goes in v1:
time: 1210 us; the launch traced here: 1200 us
  waiting for transfers between devices  573 us (47%)
  matrix products  250 us (21%)
  local copies, waits for them, and re-layouts  235 us (19%)
  other arithmetic  122 us (10%)
  between operations  15.4 us (1%)
    reduce_scatter x1, waiting for transfers between devices, on_device(): lax.psum_scatter(jnp.concatenate([all_grads[rank * own:(rank + 1) * own]...  212 us
    all_gather x1, waiting for transfers between devices, on_device(): lax.all_gather(weights_low, 'dp', axis=0, tiled=True, axis_index_groups=[...  189 us
    reduce_scatter x4, waiting for transfers between devices, sum_rows(): lax.psum_scatter(values.astype(jnp.bfloat16), 'mp', scatter_dimension=0,...  139 us
    unnamed x165, local copies, waits for them, and re-layouts  119 us
    dot_general x4, matrix products, project_back(): jnp.einsum('tcj,rcij->tri', shaped, weights, preferred_element_type=jnp.f...  43.6 us
    dot_general x4, matrix products, project(): jnp.einsum('tri,rcij->tcj', shaped, weights, preferred_element_type=jnp.f...  43.3 us
    dot_general x4, matrix products, weight_grad(): jnp.einsum('tri,tcj->rcij', left_shaped, right_shaped, preferred_element_...  33.9 us
    all_gather x1, waiting for transfers between devices, on_device(): lax.all_gather(middle_grad.astype(jnp.bfloat16), 'mp', axis=0, tiled=True)  29.4 us
  transfers between devices with their start and end apart: 11, of which 8 were waited for; matrix products, arithmetic and copies ran while one was open for 21% of the time, Pallas kernels for 0%

profile of v1, /device:TPU:0, one launch (start us, length us, event | category | flops | bytes accessed | tf_op | source)
XLA Modules:
  0.0 1200.8 jit_solution(14629774651332840294)
XLA Ops:
  7.2 4.7 convert_element_type.160
  12.0 14.3 %convert_bitcast_fusion.2 = (f32[1024,2048]{1,0:T(8,128)}, f32[128,8,16,128]{3,1,2,0:T(8,128)}, f32[1,1024,2048]{2,1,0:T(8,128)}) fusion(bf16[1,1024,2048]{2,1,0:T(8,128)(2,1)} %param.11), kind=kLoop, calls=%fused_computation.50 | loop fusion | flops 2097152 | bytes 29360128 | tf_op jit(solution)/shard_map/reshape | solution.py:240
  26.3 8.7 copy.178
  41.2 188.6 %all-gather.7.cloned.1.call-done = bf16[672,128,128]{2,1,0:T(8,128)(2,1)} async-done(((bf16[84,128,128]{2,1,0:T(8,128)(2,1)}), bf16[672,128,128]{2,1,0:T(8,128)(2,1)}) %all-gather.7.cloned.1.call-update) | async-done | bytes 22020112 | tf_op jit(solution)/shard_map/all_gather | solution.py:227
  229.8 3.9 slice_dynamic-update-slice_fusion.10
  233.6 4.4 slice_dynamic-update-slice_fusion.9
  238.0 4.4 slice_dynamic-update-slice_fusion.8
  249.8 3.8 fusion.144
  253.6 8.0 slice.234
  261.6 5.0 copy-done.1
  271.9 9.0 fusion.76
  282.4 7.2 fusion.148
  289.5 8.0 fusion.7
  297.6 7.4 fusion.86
  305.1 7.5 fusion.149
  312.7 8.2 fusion.6
  320.9 9.0 fusion.83
  336.3 4.4 bitcast_convert_fusion.3
  340.8 44.6 %reduce-scatter.9.cloned.1.call-done = bf16[256,2048]{1,0:T(8,128)(2,1)} async-done(((bf16[1024,2048]{1,0:T(8,128)(2,1)}), bf16[256,2048]{1,0:T(8,128)(2,1)}) %reduce-scatter.9.cloned.1.call-update) | async-done | bytes 1048592 | tf_op jit(solution)/shard_map/reduce_scatter | solution.py:184
  395.5 12.5 %slice_bitcast_fusion.3 = (bf16[16,128,22,128]{3,1,2,0:T(8,128)(2,1)S(1)}, bf16[16,22,128,128]{3,2,1,0:T(8,128)(2,1)}) fusion(bf16[16,27,128,128]{3,2,1,0:T(8,128)(2,1)} %bitcast.372), kind=kLoop, calls=%fused_computation.222 | loop fusion | bytes 34603008 | tf_op jit(solution)/shard_map/tcj,rcij->tri/dot_general | solution.py:85
  408.0 5.4 copy.118
  413.4 15.1 %copy.173 = bf16[16,22,128,128]{2,3,1,0:T(8,128)(2,1)} copy(bf16[16,22,128,128]{3,2,1,0:T(8,128)(2,1)} %get-tuple-element.102) | data formatting | bytes 23068672
  438.5 18.9 %convolution_bitcast_fusion = f32[1024,2816]{1,0:T(8,128)} fusion(bf16[2816,128,16]{1,0,2:T(8,128)(2,1)} %bitcast.384, bf16[1024,2048]{1,0:T(8,128)(2,1)} %all-gather.9.cloned.1.call-done), kind=kOutput, calls=%fused_computation.49 | convolution fusion | flops 11811160064 | bytes 27262976 | tf_op jit(solution)/shard_map/tri,rcij->tcj/dot_general | solution.py:77
  457.5 15.0 %fusion.30 = (bf16[1024,1408]{1,0:T(8,128)(2,1)}, bf16[1024,1408]{1,0:T(8,128)(2,1)}, bf16[1024,1408]{1,0:T(8,128)(2,1)}) fusion(f32[1024,2816]{1,0:T(8,128)} %convolution_bitcast_fusion, bf16[1408,16,128]{2,0,1:T(8,128)(2,1)S(1)} %bitcast.389, bf16[1024,16,128]{2,1,0:T(8,128)(2,1)} %bitcast.395), kind=kOutput, calls=%fused_computation.59 | convolution fusion | flops 5928648704 | bytes 30146560 | tf_op jit(solution)/shard_map/tcj,rcij->tri/dot_general | solution.py:85
  472.5 4.5 copy.115
  477.0 4.5 copy.117
  481.5 4.5 copy.114
  486.1 4.5 copy.116
  490.6 18.4 %bitcast_convert_fusion.1 = bf16[1024,2048]{1,0:T(8,128)(2,1)} fusion(bf16[2048,22,128]{2,0,1:T(8,128)(2,1)} %bitcast.383, bf16[1024,11,128]{2,0,1:T(8,128)(2,1)} %copy.117, bf16[1024,11,128]{2,0,1:T(8,128)(2,1)} %copy.116), kind=kOutput, calls=%fused_computation.34 | convolution fusion | flops 11816140800 | bytes 21495808 | tf_op jit(solution)/shard_map/tcj,rcij->tri/dot_general | solution.py:85
  509.0 8.4 copy.110
  517.4 4.9 copy.109
  522.3 11.0 bitcast_convert_fusion.2
  533.4 6.6 convert_bitcast_fusion.1
  540.0 13.6 %reduce-scatter.13.cloned.1.call-done = bf16[256,2048]{1,0:T(8,128)(2,1)} async-done(((bf16[1024,2048]{1,0:T(8,128)(2,1)}), bf16[256,2048]{1,0:T(8,128)(2,1)}) %reduce-scatter.13.cloned.1.call-update) | async-done | bytes 1048592 | tf_op jit(solution)/shard_map/reduce_scatter | solution.py:184
  555.7 45.5 %reduce-scatter.11.cloned.1.call-done = bf16[256,2048]{1,0:T(8,128)(2,1)} async-done(((bf16[1024,2048]{1,0:T(8,128)(2,1)}), bf16[256,2048]{1,0:T(8,128)(2,1)}) %reduce-scatter.11.cloned.1.call-update) | async-done | bytes 1048592 | tf_op jit(solution)/shard_map/reduce_scatter | solution.py:184
  601.1 5.1 fusion.142
  611.5 29.4 %all-gather.13.cloned.1.call-done = bf16[1024,2048]{1,0:T(8,128)(2,1)} async-done(((bf16[256,2048]{1,0:T(8,128)(2,1)}), bf16[1024,2048]{1,0:T(8,128)(2,1)}) %all-gather.13.cloned.1.call-update) | async-done | bytes 4194320 | tf_op jit(solution)/shard_map/all_gather | solution.py:283
  640.9 5.2 bitcast_convert_fusion.5
  646.3 7.4 fusion.92
  653.6 13.0 %fusion.3 = (f32[8,512]{1,0:T(8,128)S(1)}, f32[1024,512,8]{1,0,2:T(8,128)}) fusion(f32[1,8,512,1024]{2,3,1,0:T(8,128)} %get-tuple-element.131, f32[8,512]{1,0:T(8,128)S(1)} %log_add_fusion.1, bf16[512,8,64]{0,2,1:T(8,128)(2,1)S(1)} %bitcast.394, f32[1024,640]{0,1:T(8,128)} %copy-done.15), kind=kOutput, calls=%fused_computation.9 | convolution fusion | flops 549449728 | bytes 34242560 | tf_op jit(solution)/shard_map/while/body/eval_jaxpr/qgjd,kgd->gjqk/dot_general | solution.py:160
  667.4 8.3 fusion
  675.6 7.9 fusion.18
  690.6 12.0 %fusion.17 = bf16[8,512,1024]{1,2,0:T(8,128)(2,1)S(1)} fusion(f32[1024,512,8]{1,0,2:T(8,128)} %get-tuple-element.135, f32[1,8,512,1024]{2,3,1,0:T(8,128)} %get-tuple-element.131, f32[8,512]{1,0:T(8,128)S(1)} %get-tuple-element.134, f32[8,512]{1,0:T(8,128)S(1)} %log_add_fusion.1), kind=kLoop, calls=%fused_computation.31 | loop fusion | flops 16777216 | bytes 41975808 | tf_op jit(solution)/shard_map/reshape.88
  709.4 5.0 bitcast_convert_fusion
  724.1 35.0 %reduce-scatter.15.cloned.1.call-done = bf16[256,2048]{1,0:T(8,128)(2,1)} async-done(((bf16[1024,2048]{1,0:T(8,128)(2,1)}), bf16[256,2048]{1,0:T(8,128)(2,1)}) %reduce-scatter.15.cloned.1.call-update) | async-done | bytes 1048592 | tf_op jit(solution)/shard_map/reduce_scatter | solution.py:184
  761.9 5.2 all-gather
  772.3 16.2 %convert_bitcast_fusion = bf16[16,22,128,128]{2,3,0,1:T(8,128)(2,1)S(1)} fusion(bf16[1024,11,128]{2,0,1:T(8,128)(2,1)} %copy.117, bf16[1024,11,128]{2,0,1:T(8,128)(2,1)} %copy.116, bf16[1024,2048]{1,0:T(8,128)(2,1)} %all-gather.9.cloned.1.call-done), kind=kOutput, calls=%fused_computation.23 | convolution fusion | flops 11828461568 | bytes 21495808 | tf_op jit(solution)/shard_map/tri,tcj->rcij/dot_general | solution.py:94
  788.6 11.2 convert_bitcast_fusion.4
  803.5 8.1 pad_maximum_fusion
  811.6 18.8 %copy.132 = bf16[16,27,128,128]{3,2,1,0:T(8,128)(2,1)} copy(bf16[16,27,128,128]{2,3,0,1:T(8,128)(2,1)} %pad_maximum_fusion) | data formatting | bytes 28311552 | tf_op jit(solution)/shard_map/concatenate | solution.py:317
  836.9 6.6 pad_maximum_fusion.1
  843.5 10.7 copy.138
  857.9 3.9 slice_dynamic-update-slice_fusion.4
  872.0 3.8 slice_dynamic-update-slice_fusion.2
  879.5 6.1 copy.140
  885.7 6.1 copy.141
  897.7 6.7 bitcast_convert_fusion.4
  904.3 212.1 %reduce-scatter.17.cloned.1.call-done = bf16[84,128,128]{2,1,0:T(8,128)(2,1)} async-done(((bf16[672,128,128]{2,1,0:T(8,128)(2,1)}), bf16[84,128,128]{2,1,0:T(8,128)(2,1)}) %reduce-scatter.17.cloned.1.call-update) | async-done | bytes 2752528 | tf_op jit(solution)/shard_map/reduce_scatter | solution.py:323
  1121.6 11.7 fusion.154
  1133.4 16.3 %multiply_add_fusion = (f32[84,128,128]{1,2,0:T(8,128)}, f32[84,128,128]{1,2,0:T(8,128)}) fusion(f32[84,128,128]{1,2,0:T(8,128)S(1)} %bitcast.380, f32[84,128,128]{1,2,0:T(8,128)S(1)} %bitcast.378, f32[84,128,128]{1,2,0:T(8,128)S(1)} %fusion.154, f32[84,128,128]{2,1,0:T(8,128)} %param.20), kind=kOutput, calls=%fused_computation.69 | convolution fusion | flops 2119434240 | bytes 33030144 | tf_op jit(solution)/shard_map/bij,bjk->bik/dot_general | solution.py:340
  1149.7 6.1 copy.143
  1155.8 6.2 copy.144
  1162.0 17.2 %add_multiply_fusion.1 = f32[84,128,128]{2,1,0:T(8,128)} fusion(f32[84,128,128]{2,1,0:T(8,128)} %param.18, f32[84,128,128]{2,1,0:T(8,128)} %copy-done), kind=kOutput, calls=%fused_computation.68 | convolution fusion | flops 2116681728 | bytes 16515072 | tf_op jit(solution)/shard_map/bij,bkj->bik/dot_general | solution.py:335
  1179.2 12.6 %add_multiply_fusion = f32[84,128,128]{2,1,0:T(8,128)} fusion(f32[84,128,128]{2,1,0:T(8,128)} %param.19, f32[84,128,128]{2,1,0:T(8,128)S(1)} %bitcast.360), kind=kOutput, calls=%fused_computation.67 | convolution fusion | flops 2116681728 | bytes 16515072 | tf_op jit(solution)/shard_map/bji,bjk->bik/dot_general | solution.py:336
  (253 shorter events, 127.1 us)
Async XLA Ops:
  7.2 222.6 %all-gather.7.cloned.1.call-start = ((), (), s32[]{:S(2)}) async-start(), calls=%async_computation.6 | async-start | bytes 24772608 | tf_op jit(solution)/shard_map/all_gather | solution.py:227
  11.9 373.5 %reduce-scatter.9.cloned.1.call-start = ((), (), s32[]{:S(2)}) async-start(), calls=%async_computation.7 | async-start | bytes 5242880 | tf_op jit(solution)/shard_map/reduce_scatter | solution.py:184
  26.3 8.7 copy-start.42
  35.0 6.1 copy-start.49
  35.8 245.3 %copy-start.50 = (f32[32]{0:T(128)}, f32[32]{0:T(128)S(1)}, u32[]{:S(2)}) copy-start(f32[32]{0:T(128)S(1)} %negate_power_fusion) | copy-start | bytes 388
  39.0 232.9 %copy-start.47 = (f32[1024]{0:T(1024)}, f32[1024]{0:T(1024)S(1)}, u32[]{:S(2)}) copy-start(f32[1024]{0:T(1024)S(1)} %add_rsqrt_fusion) | copy-start | bytes 12292
  39.1 242.1 %copy-start.40 = (f32[1024]{0:T(1024)}, f32[1024]{0:T(1024)S(1)}, u32[]{:S(2)}) copy-start(f32[1024]{0:T(1024)S(1)} %fusion.134) | copy-start | bytes 12292
  39.6 242.1 %copy-start.28 = (f32[1024,32]{0,1:T(8,128)}, f32[1024,32]{0,1:T(8,128)S(1)}, u32[]{:S(2)}) copy-start(f32[1024,32]{0,1:T(8,128)S(1)} %get-tuple-element.120) | copy-start | bytes 393220
  39.6 242.1 %copy-start.30 = (f32[1024,32]{0,1:T(8,128)}, f32[1024,32]{0,1:T(8,128)S(1)}, u32[]{:S(2)}) copy-start(f32[1024,32]{0,1:T(8,128)S(1)} %get-tuple-element.121) | copy-start | bytes 393220
  41.1 230.8 %copy-start.38 = (f32[1,2048]{1,0:T(1,128)}, f32[1,2048]{1,0:T(1,128)S(1)}, u32[]{:S(2)}) copy-start(f32[1,2048]{1,0:T(1,128)S(1)} %get-tuple-element.119) | copy-start | bytes 24580
  229.8 20.0 %copy-start.3 = (bf16[672,128,128]{2,1,0:T(8,128)(2,1)S(1)}, bf16[672,128,128]{2,1,0:T(8,128)(2,1)}, u32[]{:S(2)}) copy-start(bf16[672,128,128]{2,1,0:T(8,128)(2,1)} %all-gather.7.cloned.1.call-done) | copy-start | bytes 66060292
  280.9 16.6 %copy-start.15 = (f32[1024,640]{0,1:T(8,128)}, f32[1024,640]{0,1:T(8,128)S(1)}, u32[]{:S(2)}) copy-start(f32[1024,640]{0,1:T(8,128)S(1)} %fusion.76) | copy-start | bytes 7864324
  281.7 23.3 %copy-start.22 = (bf16[1024,32]{0,1:T(8,128)(2,1)}, bf16[1024,32]{0,1:T(8,128)(2,1)S(1)}, u32[]{:S(2)}) copy-start(bf16[1024,32]{0,1:T(8,128)(2,1)S(1)} %get-tuple-element.116) | copy-start | bytes 196612
  281.7 23.3 %copy-start.24 = (bf16[1024,32]{0,1:T(8,128)(2,1)}, bf16[1024,32]{0,1:T(8,128)(2,1)S(1)}, u32[]{:S(2)}) copy-start(bf16[1024,32]{0,1:T(8,128)(2,1)S(1)} %get-tuple-element.117) | copy-start | bytes 196612
  282.1 23.0 %copy-start.4 = (bf16[1,1024,1,8,32]{1,4,3,2,0:T(8,128)(2,1)}, bf16[1,1024,1,8,32]{1,4,3,2,0:T(8,128)(2,1)S(1)}, u32[]{:S(2)}) copy-start(bf16[1,1024,1,8,32]{1,4,3,2,0:T(8,128)(2,1)S(1)} %get-tuple-element.109) | copy-start | bytes 1572868
  282.1 23.0 %copy-start.6 = (bf16[1,1024,1,8,32]{1,4,3,2,0:T(8,128)(2,1)}, bf16[1,1024,1,8,32]{1,4,3,2,0:T(8,128)(2,1)S(1)}, u32[]{:S(2)}) copy-start(bf16[1,1024,1,8,32]{1,4,3,2,0:T(8,128)(2,1)S(1)} %get-tuple-element.110) | copy-start | bytes 1572868
  289.5 8.1 copy-start.34
  297.6 7.4 copy-start.43
  305.1 31.1 %copy-start.17 = (bf16[64,8,512]{2,0,1:T(8,128)(2,1)}, bf16[64,8,512]{2,0,1:T(8,128)(2,1)S(1)}, u32[]{:S(2)}) copy-start(bf16[64,8,512]{2,0,1:T(8,128)(2,1)S(1)} %fusion.86) | copy-start | bytes 1572868
  312.6 8.3 copy-start.36
  312.6 17.3 %slice-start.8 = ((s8[22020096]{0:T(1024)(128)(4,1)}), s8[1048576]{0:T(1024)(128)(4,1)S(1)}, s32[]{:S(2)}) async-start(s8[22020096]{0:T(1024)(128)(4,1)} %bitcast.375), calls=%async_computation.25 | async-start | bytes 2097152
  312.6 17.3 %slice-start.9 = ((s8[22020096]{0:T(1024)(128)(4,1)}), s8[4194304]{0:T(1024)(128)(4,1)S(1)}, s32[]{:S(2)}) async-start(s8[22020096]{0:T(1024)(128)(4,1)} %bitcast.375), calls=%async_computation.26 | async-start | bytes 8388608
  320.9 9.0 copy-start.45
  320.9 9.0 slice-start.10
  320.9 9.0 slice-start.11
  320.9 9.5 slice-start.12
  320.9 10.7 slice-start.13
  331.6 9.1 copy-start.19
  340.7 48.2 %copy-start.52 = (s32[1,1024]{1,0:T(1,128)S(1)}, s32[1,1024]{1,0:T(1,128)}, u32[]{:S(2)}) copy-start(s32[1,1024]{1,0:T(1,128)} %param.13) | copy-start | bytes 12292
  340.7 97.8 %all-gather.9.cloned.1.call-start = ((), (), s32[]{:S(2)}) async-start(), calls=%async_computation.8 | async-start | bytes 5242880 | tf_op jit(solution)/shard_map/all_gather | solution.py:259
  388.9 164.7 %reduce-scatter.13.cloned.1.call-start = ((), (), s32[]{:S(2)}) async-start(), calls=%async_computation.11 | async-start | bytes 5242880 | tf_op jit(solution)/shard_map/reduce_scatter | solution.py:184
  438.5 18.9 %copy-start.11 = (bf16[11,16,128,128]{3,2,0,1:T(8,128)(2,1)S(1)}, bf16[11,16,128,128]{3,2,0,1:T(8,128)(2,1)}, u32[]{:S(2)}) copy-start(bf16[11,16,128,128]{3,2,0,1:T(8,128)(2,1)} %copy.112) | copy-start | bytes 17301508
  509.0 92.2 %reduce-scatter.11.cloned.1.call-start = ((), (), s32[]{:S(2)}) async-start(), calls=%async_computation.9 | async-start | bytes 5242880 | tf_op jit(solution)/shard_map/reduce_scatter | solution.py:184
  533.3 107.6 %all-gather.13.cloned.1.call-start = ((), (), s32[]{:S(2)}) async-start(), calls=%async_computation.12 | async-start | bytes 5242880 | tf_op jit(solution)/shard_map/all_gather | solution.py:283
  606.2 5.2 copy-start.37
  606.2 5.2 copy-start.46
  606.2 5.2 copy-start.35
  606.2 5.2 copy-start.44
  606.3 152.8 %reduce-scatter.15.cloned.1.call-start = ((), (), s32[]{:S(2)}) async-start(), calls=%async_computation.13 | async-start | bytes 5242880 | tf_op jit(solution)/shard_map/reduce_scatter | solution.py:184
  646.2 20.4 %slice-start = ((s8[16777216]{0:T(1024)(128)(4,1)}), s8[4194304]{0:T(1024)(128)(4,1)S(1)}, s32[]{:S(2)}) async-start(s8[16777216]{0:T(1024)(128)(4,1)} %bitcast.357), calls=%async_computation.17 | async-start | bytes 8388608
  646.3 20.4 %slice-start.1 = ((s8[16777216]{0:T(1024)(128)(4,1)}), s8[4194304]{0:T(1024)(128)(4,1)S(1)}, s32[]{:S(2)}) async-start(s8[16777216]{0:T(1024)(128)(4,1)} %bitcast.357), calls=%async_computation.18 | async-start | bytes 8388608
  653.6 13.0 %slice-start.2 = ((s8[16777216]{0:T(1024)(128)(4,1)}), s8[4194304]{0:T(1024)(128)(4,1)S(1)}, s32[]{:S(2)}) async-start(s8[16777216]{0:T(1024)(128)(4,1)} %bitcast.357), calls=%async_computation.19 | async-start | bytes 8388608
  653.6 13.7 %slice-start.3 = ((s8[16777216]{0:T(1024)(128)(4,1)}), s8[4194304]{0:T(1024)(128)(4,1)S(1)}, s32[]{:S(2)}) async-start(s8[16777216]{0:T(1024)(128)(4,1)} %bitcast.357), calls=%async_computation.20 | async-start | bytes 8388608
  675.6 7.9 copy-start.5
  675.6 7.9 copy-start.7
  709.4 5.9 copy-start.48
  709.4 5.9 copy-start.39
  714.4 177.3 %all-gather.11.cloned.1.call-start = ((), (), s32[]{:S(2)}) async-start(), calls=%async_computation.10 | async-start | bytes 5242880 | tf_op jit(solution)/shard_map/all_gather | solution.py:266
  715.2 176.6 %reduce-scatter.19.cloned.1.call-start = ((), (), s32[]{:S(2)}) async-start(), calls=%async_computation.16 | async-start | bytes 1179648
  722.1 46.5 %copy-start.10 = (f32[256,2048]{1,0:T(8,128)S(1)}, f32[256,2048]{1,0:T(8,128)}, u32[]{:S(2)}) copy-start(f32[256,2048]{1,0:T(8,128)} %get-tuple-element.92) | copy-start | bytes 6291460
  759.1 9.5 copy-start.14
  768.6 129.1 %all-gather.15.cloned.1.call-start = ((), (), s32[]{:S(2)}) async-start(), calls=%async_computation.14 | async-start | bytes 5242880 | tf_op jit(solution)/shard_map/all_gather | solution.py:313
  772.2 344.2 %reduce-scatter.17.cloned.1.call-start = ((), (), s32[]{:S(2)}) async-start(), calls=%async_computation.15 | async-start | bytes 24772608 | tf_op jit(solution)/shard_map/reduce_scatter | solution.py:323
  788.5 11.2 copy-start.13
  788.6 11.2 copy-start.27
  854.1 11.4 slice-start.6
  857.9 7.6 slice-start.7
  1116.4 16.9 %slice-start.15 = ((s8[5505024]{0:T(1024)(128)(4,1)}), s8[4194304]{0:T(1024)(128)(4,1)S(1)}, s32[]{:S(2)}) async-start(s8[5505024]{0:T(1024)(128)(4,1)} %bitcast.377), calls=%async_computation.32 | async-start | bytes 8388608
  1116.4 17.0 %slice-start.17 = ((s8[5505024]{0:T(1024)(128)(4,1)}), s8[4194304]{0:T(1024)(128)(4,1)S(1)}, s32[]{:S(2)}) async-start(s8[5505024]{0:T(1024)(128)(4,1)} %bitcast.379), calls=%async_computation.34 | async-start | bytes 8388608
  1121.6 11.7 slice-start.16
  1121.6 11.8 slice-start.18
  1155.8 23.4 %slice-start.4 = ((s8[5505024]{0:T(1024)(128)(4,1)}), s8[1310720]{0:T(1024)(128)(4,1)S(1)}, s32[]{:S(2)}) async-start(s8[5505024]{0:T(1024)(128)(4,1)} %bitcast.359), calls=%async_computation.21 | async-start | bytes 2621440
  1162.0 17.2 %slice-start.5 = ((s8[5505024]{0:T(1024)(128)(4,1)}), s8[4194304]{0:T(1024)(128)(4,1)S(1)}, s32[]{:S(2)}) async-start(s8[5505024]{0:T(1024)(128)(4,1)} %bitcast.359), calls=%async_computation.22 | async-start | bytes 8388608
  1179.2 12.6 %copy-start.12 = (bf16[1024,2048]{1,0:T(8,128)(2,1)S(1)}, bf16[1024,2048]{1,0:T(8,128)(2,1)}, u32[]{:S(2)}) copy-start(bf16[1024,2048]{1,0:T(8,128)(2,1)} %all-gather.11.cloned.1.call-done) | copy-start | bytes 12582916
  (19 other events, 56.7 us)
Sparse Core Ops, SparseCore 0:
  12.0 217.6 all-gather.6
  340.8 44.4 reduce-scatter.8
  389.0 34.4 all-gather.8
  509.1 44.5 reduce-scatter.12
  556.6 44.4 reduce-scatter.10
  606.4 34.4 all-gather.12
  714.6 44.5 reduce-scatter.14
  760.7 34.4 all-gather.10
  798.6 63.4 reduce-scatter.18
  864.1 33.4 all-gather.14
  900.1 216.2 reduce-scatter.16

commit v2 on v0

v2 whole, which is shorter than its diff:
```python
import functools

import jax
import jax.numpy as jnp
import numpy as np
from jax import lax
from jax.experimental import pallas as pl
from jax.experimental.pallas import tpu as pltpu
from jax.sharding import PartitionSpec as P

HEADS = 32
KV_HEADS = 4
HD = 64
FF = 5632
LOW = jnp.bfloat16
F32 = jnp.float32

weight_rate = 1.0
gain_rate = 0.2
average_decay = 0.9
VMEM_LIMIT = 60 * 1024 * 1024


def ring_order(count):
    return list(range(0, count, 2)) + list(range(1, count, 2))[::-1]


class Layout:
    def __init__(self, dp, own, rows, attn_cols, in_cols, out_attn_rows):
        self.dp, self.own = dp, own
        self.ring = ring_order(dp)
        n_in = rows * in_cols
        kinds, spots = [], []
        for k in range(dp * own):
            if k < n_in:
                r, c = divmod(k, in_cols)
                if c < attn_cols:
                    kinds.append(0), spots.append((0, r, c))
                else:
                    kinds.append(2), spots.append((2, r, c - attn_cols))
            else:
                r, c = divmod(k - n_in, rows)
                if r < out_attn_rows:
                    kinds.append(1), spots.append((1, r, c))
                else:
                    kinds.append(2), spots.append((3, r - out_attn_rows, c))
        self.order = np.zeros((dp, own), np.int32)
        for d in range(dp):
            mine = kinds[d * own : (d + 1) * own]
            self.order[d] = sorted(range(own), key=lambda l: (mine[l], l))
        count = np.array(kinds).reshape(dp, own)
        first = int((count == 0).sum(1).max())
        second = int((count <= 1).sum(1).max())
        bounds = [0, first, max(first, second), own]
        self.chunks = [(a, b - a) for a, b in zip(bounds[:-1], bounds[1:]) if b > a]
        self.table = []
        for p, d in enumerate(self.ring):
            for j, l in enumerate(self.order[d]):
                (x,) = [i for i, (a, n) in enumerate(self.chunks) if a <= j < a + n]
                a, n = self.chunks[x]
                self.table.append(spots[d * own + int(l)] + (x, p * n + j - a))

    def of_chunk(self, x, matrix):
        rows = [(s, r, c) for m, r, c, y, s in self.table if y == x and m == matrix]
        return np.array(sorted(rows), np.int32).reshape(-1, 3)

    def of_matrix(self, matrix, rows, cols):
        out = np.zeros((cols, rows, 2), np.int32)
        for m, r, c, x, s in self.table:
            if m == matrix:
                out[c, r] = (x, s)
        return out


ANY = pl.BlockSpec(memory_space=pl.ANY)
SMEM = pl.BlockSpec(memory_space=pltpu.SMEM)
VMEM = pl.BlockSpec(memory_space=pltpu.VMEM)


def sort_blocks(weights, order, chunks):
    block = weights.shape[1:]

    def body(order_ref, w_ref, *outs):
        for (start, count), out in zip(chunks, outs):

            def one(j, carry, start=start, out=out):
                out[j] = w_ref[order_ref[start + j]].astype(LOW)
                return carry

            lax.fori_loop(0, count, one, 0)

    return pl.pallas_call(
        body,
        out_shape=[jax.ShapeDtypeStruct((n,) + block, LOW) for _, n in chunks],
        in_specs=[SMEM, VMEM],
        out_specs=[VMEM] * len(chunks),
        compiler_params=pltpu.CompilerParams(vmem_limit_bytes=VMEM_LIMIT),
        name="sort_blocks",
    )(order, weights)


def place_blocks(gathered, tables, shapes, partial):
    block = gathered.shape[-1]
    used = [i for i, t in enumerate(tables) if len(t)]
    count = sum(len(tables[i]) for i in used)
    known = [i for i in used if partial[i] is not None]

    def body(*refs):
        table_refs = refs[: len(used)]
        src = refs[len(used)]
        outs = refs[len(used) + 1 + len(known) : -3]
        stage, sem_in, sem_out = refs[-3:]
        load = pltpu.make_async_copy(src, stage, sem_in)
        load.start()
        load.wait()
        for i, table_ref, out in zip(used, table_refs, outs):

            def one(j, carry, table_ref=table_ref, out=out):
                row = pl.multiple_of(table_ref[3 * j + 1] * block, block)
                col = pl.multiple_of(table_ref[3 * j + 2] * block, block)
                pltpu.make_async_copy(
                    stage.at[table_ref[3 * j]],
                    out.at[pl.ds(row, block), pl.ds(col, block)],
                    sem_out,
                ).start()
                return carry

            lax.fori_loop(0, len(tables[i]), one, 0)
        pltpu.make_async_copy(stage, stage, sem_out).wait()

    assert count == gathered.shape[0]
    results = pl.pallas_call(
        body,
        out_shape=[jax.ShapeDtypeStruct(shapes[i], LOW) for i in used],
        in_specs=[SMEM] * len(used) + [ANY] * (1 + len(known)),
        out_specs=[ANY] * len(used),
        input_output_aliases={len(used) + 1 + j: used.index(i) for j, i in enumerate(known)},
        scratch_shapes=[
            pltpu.VMEM(gathered.shape, LOW),
            pltpu.SemaphoreType.DMA,
            pltpu.SemaphoreType.DMA,
        ],
        compiler_params=pltpu.CompilerParams(vmem_limit_bytes=VMEM_LIMIT),
        name="place_blocks",
    )(
        *[jnp.asarray(tables[i].reshape(-1)) for i in used],
        gathered,
        *[partial[i] for i in known],
    )
    merged = list(partial)
    for i, value in zip(used, results):
        merged[i] = value
    return merged


def grad_blocks(left, right, table, wide, buffers, sizes, block):
    tokens, height = left.shape
    width = right.shape[1]
    rows, cols = height // block, width // block
    steps = cols // wide
    per_step = rows * wide
    used = sorted(set(table[:, :, 0].reshape(-1).tolist()))
    known = [x for x in used if buffers[x] is not None]

    def body(*refs):
        table_ref, left_ref, right_ref = refs[:3]
        outs = refs[3 + len(known) : 3 + len(known) + len(used)]
        turned, stage, sems = refs[-3:]
        turned[...] = left_ref[...].T

        def finish(slot):
            pltpu.make_async_copy(stage.at[slot], stage.at[slot], sems.at[slot]).wait()

        def step(t, carry):
            slot = lax.rem(t, 2)

            @pl.when(t >= 2)
            def _():
                finish(slot)

            col = pl.multiple_of(t * (wide * block), wide * block)
            part = jnp.dot(
                turned[...], right_ref[:, pl.ds(col, wide * block)], preferred_element_type=F32
            ).astype(LOW)
            for r in range(rows):
                for c in range(wide):
                    stage[slot, c * rows + r] = part[
                        r * block : (r + 1) * block, c * block : (c + 1) * block
                    ]

            def send(j, carry):
                at = 2 * (t * per_step + j)
                for x, out in zip(used, outs):

                    @pl.when(table_ref[at] == x)
                    def _(out=out):
                        pltpu.make_async_copy(
                            stage.at[slot, j], out.at[table_ref[at + 1]], sems.at[slot]
                        ).start()

                return carry

            lax.fori_loop(0, per_step, send, 0)
            return carry

        lax.fori_loop(0, steps, step, 0)
        for t in range(max(0, steps - 2), steps):
            finish(t % 2)

    results = pl.pallas_call(
        body,
        out_shape=[jax.ShapeDtypeStruct((sizes[x], block, block), LOW) for x in used],
        in_specs=[SMEM, VMEM, VMEM] + [ANY] * len(known),
        out_specs=[ANY] * len(used),
        input_output_aliases={3 + j: used.index(x) for j, x in enumerate(known)},
        scratch_shapes=[
            pltpu.VMEM((height, tokens), LOW),
            pltpu.VMEM((2, per_step, block, block), LOW),
            pltpu.SemaphoreType.DMA((2,)),
        ],
        compiler_params=pltpu.CompilerParams(vmem_limit_bytes=VMEM_LIMIT),
        cost_estimate=pl.CostEstimate(
            flops=2 * tokens * height * width,
            bytes_accessed=2 * (tokens * (height + width) + height * width),
            transcendentals=0,
        ),
        name="grad_blocks",
    )(jnp.asarray(table.reshape(-1)), left, right, *[buffers[x] for x in known])
    merged = list(buffers)
    for x, value in zip(used, results):
        merged[x] = value
    return merged


def shampoo(sums, places, factor, weights, ema, left, right, left_roots, right_roots, before):
    count, block, _ = sums.shape

    def mm(a, b, dims):
        return lax.dot_general(
            a.astype(LOW), b.astype(LOW), (dims, ((), ())), preferred_element_type=F32
        )

    def body(places_ref, g_ref, w_ref, e_ref, l_ref, r_ref, lr_ref, rr_ref, *rest):
        og, ow, oe, ol, orr = rest[-5:]
        low = g_ref[0]
        og[0] = low.astype(F32) * factor
        both = 0.5 * factor * factor
        ol[0] = 0.5 * l_ref[0] + both * mm(low, low, ((1,), (1,)))
        orr[0] = 0.5 * r_ref[0] + both * mm(low, low, ((0,), (0,)))
        part = mm(low, rr_ref[0], ((1,), (0,))) * factor
        fresh = w_ref[0] - weight_rate * mm(lr_ref[0], part, ((1,), (0,)))
        ow[0] = fresh
        oe[0] = average_decay * e_ref[0] + (1.0 - average_decay) * fresh

    own = pl.BlockSpec((1, block, block), lambda i, places_ref: (places_ref[i], 0, 0))
    here = pl.BlockSpec((1, block, block), lambda i, places_ref: (i, 0, 0))
    extra = [] if before is None else list(before)
    shape = jax.ShapeDtypeStruct(weights.shape, F32)
    return pl.pallas_call(
        body,
        out_shape=[shape] * 5,
        grid_spec=pltpu.PrefetchScalarGridSpec(
            num_scalar_prefetch=1,
            grid=(count,),
            in_specs=[here] + [own] * 6 + [ANY] * len(extra),
            out_specs=[own] * 5,
        ),
        input_output_aliases={8 + i: i for i in range(len(extra))},
        compiler_params=pltpu.CompilerParams(dimension_semantics=("arbitrary",)),
        cost_estimate=pl.CostEstimate(
            flops=8 * count * block**3,
            bytes_accessed=46 * count * block * block,
            transcendentals=0,
        ),
        name="shampoo",
    )(places, sums, weights, ema, left, right, left_roots, right_roots, *extra)


def doc_positions(doc_ids):
    length = doc_ids.shape[-1]
    offsets = jnp.arange(length, dtype=jnp.int32)
    starts = jnp.concatenate(
        [jnp.ones(doc_ids.shape[:-1] + (1,), jnp.bool_), doc_ids[..., 1:] != doc_ids[..., :-1]],
        axis=-1,
    )
    first_index = lax.cummax(jnp.where(starts, offsets, 0), axis=doc_ids.ndim - 1)
    return offsets - first_index


def rope_tables(positions, head_size):
    half_size = head_size // 2
    exponent = jnp.arange(half_size, dtype=F32) * (2.0 / head_size)
    inverse = jnp.power(F32(10000.0), -exponent)
    angles = positions.astype(F32)[..., None] * inverse
    return (jnp.cos(angles), jnp.sin(angles))


def rotate(values, cosine_table, sine_table):
    half_size = values.shape[-1] // 2
    first_half = values[..., :half_size]
    second_half = values[..., half_size:]
    return jnp.concatenate(
        [
            first_half * cosine_table - second_half * sine_table,
            second_half * cosine_table + first_half * sine_table,
        ],
        axis=-1,
    )


def rotate_back(grads, cosine_table, sine_table):
    return rotate(grads, cosine_table, -sine_table)


def block_scores(query_part, keys, doc_ids, offset, scale):
    row_count = query_part.shape[0]
    query_index = offset + jnp.arange(row_count)
    key_index = jnp.arange(keys.shape[0])
    allowed = (key_index[None, :] <= query_index[:, None]) & (
        doc_ids[None, :] == doc_ids[offset : offset + row_count][:, None]
    )
    scores = jnp.einsum("qgjd,kgd->gjqk", query_part, keys, preferred_element_type=F32) * scale
    return jnp.where(allowed, scores, -1e30)


def attend_forward(queries, keys, values, doc_ids, query_block):
    length = queries.shape[0]
    scale = float(queries.shape[-1]) ** (-0.5)
    outputs = []
    totals = []
    for offset in range(0, length, query_block):
        scores = block_scores(queries[offset : offset + query_block], keys, doc_ids, offset, scale)
        maximum = jnp.max(scores, axis=-1, keepdims=True)
        expo_values = jnp.exp(scores - maximum)
        denominator = jnp.sum(expo_values, axis=-1, keepdims=True)
        probs = (expo_values / denominator).astype(LOW)
        outputs.append(jnp.einsum("gjqk,kgd->qgjd", probs, values, preferred_element_type=F32))
        totals.append(maximum + jnp.log(denominator))
    return (jnp.concatenate(outputs, axis=0), jnp.concatenate(totals, axis=2))


def attend_backward(queries, keys, values, doc_ids, log_totals, out_grads, query_block):
    length = queries.shape[0]
    scale = float(queries.shape[-1]) ** (-0.5)
    key_grads = jnp.zeros(keys.shape, F32)
    value_grads = jnp.zeros(values.shape, F32)
    query_grads = []
    for offset in range(0, length, query_block):
        query_part = queries[offset : offset + query_block]
        scores = block_scores(query_part, keys, doc_ids, offset, scale)
        probs = jnp.exp(scores - log_totals[:, :, offset : offset + query_block])
        grad_part = out_grads[offset : offset + query_block]
        value_grads = value_grads + jnp.einsum(
            "gjqk,qgjd->kgd", probs.astype(LOW), grad_part, preferred_element_type=F32
        )
        prob_grads = jnp.einsum("qgjd,kgd->gjqk", grad_part, values, preferred_element_type=F32)
        inner = jnp.sum(probs * prob_grads, axis=-1, keepdims=True)
        score_grads = (probs * (prob_grads - inner)).astype(LOW)
        query_grads.append(
            jnp.einsum("gjqk,kgd->qgjd", score_grads, keys, preferred_element_type=F32) * scale
        )
        key_grads = (
            key_grads
            + jnp.einsum("gjqk,qgjd->kgd", score_grads, query_part, preferred_element_type=F32)
            * scale
        )
    return (jnp.concatenate(query_grads, axis=0), key_grads, value_grads)


def dot(left, right):
    return jnp.dot(left, right, preferred_element_type=F32)


def dot_turned(left, right):
    return lax.dot_general(left, right, (((1,), (1,)), ((), ())), preferred_element_type=F32)


EXCHANGE = (0, 2, 1, 3)


def on_device(
    tokens_in,
    cotangent,
    select_mask,
    doc_ids,
    norm_gains,
    weight_blocks,
    ema_blocks,
    left_stats,
    right_stats,
    left_roots,
    right_roots,
):
    mp_count = lax.axis_size("mp")
    dp_count = lax.axis_size("dp")
    sequences, length, model_width = tokens_in.shape
    assert sequences == 1 and mp_count == 4 and dp_count & (dp_count - 1) == 0
    rows = sequences * length
    own, block, _ = weight_blocks.shape
    query_cols = HEADS * HD // mp_count
    key_cols = KV_HEADS * HD // mp_count
    hidden_cols = FF // mp_count
    kv_local = KV_HEADS // mp_count
    group_size = HEADS // KV_HEADS
    row_blocks = model_width // block
    attn_blocks = (query_cols + 2 * key_cols) // block
    hidden_blocks = hidden_cols // block
    in_blocks = attn_blocks + 2 * hidden_blocks
    out_attn_blocks = query_cols // block
    query_block = min(512, length)
    share = rows // mp_count
    m_index = lax.axis_index("mp")
    d_index = lax.axis_index("dp")

    plan = Layout(dp_count, own, row_blocks, attn_blocks, in_blocks, out_attn_blocks)
    order = lax.dynamic_slice_in_dim(jnp.asarray(plan.order), d_index, 1, 0).reshape(-1)
    shapes = [
        (model_width, attn_blocks * block),
        (query_cols, model_width),
        (model_width, 2 * hidden_cols),
        (hidden_cols, model_width),
    ]

    def partner(values, bit):
        return lax.ppermute(values, "mp", [(i, i ^ bit) for i in range(mp_count)])

    def true_share(values, group):
        return lax.dynamic_slice_in_dim(values, (m_index ^ group) * share, share, 0)

    def to_exchange(values):
        return jnp.concatenate([true_share(values, g) for g in EXCHANGE], axis=0)

    def to_true(parts):
        by_group = [parts[EXCHANGE.index(g)] for g in range(4)]
        low, high = m_index & 1, m_index & 2
        pairs = []
        for a, b in ((0, 1), (2, 3)):
            pairs.append(
                (
                    jnp.where(low == 0, by_group[a], by_group[b]),
                    jnp.where(low == 0, by_group[b], by_group[a]),
                )
            )
        flat = []
        for first, second in ((0, 1), (1, 0)):
            for i in range(2):
                flat.append(jnp.where(high == 0, pairs[first][i], pairs[second][i]))
        return jnp.concatenate(flat, axis=0)

    def sum_shares(sent, kept):
        got = partner(sent, 1).astype(F32)
        kept = kept.astype(F32) + got
        return kept[:share] + partner(kept[share:].astype(LOW), 2).astype(F32)

    def spread_share(mine):
        near = partner(mine, 1)
        far = partner(mine, 2)
        return [mine, far, near, partner(far, 1)]

    sorted_low = sort_blocks(weight_blocks, order, plan.chunks)
    matrices = [None] * 4
    for x, chunk in enumerate(sorted_low):
        gathered = lax.all_gather(chunk, "dp", axis=0, tiled=True, axis_index_groups=[plan.ring])
        matrices = place_blocks(
            gathered, [plan.of_chunk(x, i) for i in range(4)], shapes, matrices
        )
        if x == 0:
            w_qkv = matrices[0]
    w_attn_out, w_gateup, w_down = matrices[1:]

    positions = doc_positions(doc_ids)
    cosine_table, sine_table = rope_tables(positions, HD)
    query_cos = cosine_table[:, :, None, None, :]
    query_sin = sine_table[:, :, None, None, :]
    key_cos = cosine_table[:, :, None, :]
    key_sin = sine_table[:, :, None, :]

    tokens_low = tokens_in.reshape(rows, model_width)
    tokens = tokens_low.astype(F32)
    first_scale = lax.rsqrt(jnp.mean(tokens * tokens, axis=-1, keepdims=True) + 1e-05)
    first_in = (tokens * first_scale * norm_gains[0]).astype(LOW)
    out_grad = cotangent.reshape(rows, model_width).astype(F32) * select_mask.astype(F32).reshape(
        rows, 1
    )
    mlp_grad = to_exchange(out_grad.astype(LOW))
    own_tokens = true_share(tokens_low, 0).astype(F32)
    own_scale = lax.rsqrt(jnp.mean(own_tokens * own_tokens, axis=-1, keepdims=True) + 1e-05)
    own_unit = own_tokens * own_scale

    qkv = dot(first_in, w_qkv)
    queries_raw = qkv[:, :query_cols].reshape(sequences, length, kv_local, group_size, HD)
    keys_raw = qkv[:, query_cols : query_cols + key_cols].reshape(sequences, length, kv_local, HD)
    values_raw = qkv[:, query_cols + key_cols :].reshape(sequences, length, kv_local, HD)
    query_use = rotate(queries_raw, query_cos, query_sin).astype(LOW)
    key_use = rotate(keys_raw, key_cos, key_sin).astype(LOW)
    value_use = values_raw.astype(LOW)
    mixed, log_totals = attend_forward(
        query_use[0], key_use[0], value_use[0], doc_ids[0], query_block
    )
    mixed_use = to_exchange(mixed.reshape(rows, query_cols).astype(LOW))
    half = rows // 2
    attended_part = sum_shares(
        dot(mixed_use[half:], w_attn_out).astype(LOW), dot(mixed_use[:half], w_attn_out).astype(LOW)
    )
    middle = own_tokens + attended_part
    second_scale = lax.rsqrt(jnp.mean(middle * middle, axis=-1, keepdims=True) + 1e-05)
    second_unit = middle * second_scale
    second_in = jnp.concatenate(
        spread_share((second_unit * norm_gains[1]).astype(LOW)), axis=0
    )
    hidden_grad = dot_turned(mlp_grad, w_down)
    gateup = dot(second_in, w_gateup)
    gate = gateup[:, :hidden_cols]
    up_part = gateup[:, hidden_cols:]
    sigmoid_gate = jax.nn.sigmoid(gate)
    hidden = (gate * sigmoid_gate * up_part).astype(LOW)
    gate_grad = hidden_grad * up_part * sigmoid_gate * (1.0 + gate * (1.0 - sigmoid_gate))
    up_grad = hidden_grad * gate * sigmoid_gate
    gateup_grad = jnp.concatenate([gate_grad.astype(LOW), up_grad.astype(LOW)], axis=1)

    second_grad = sum_shares(
        dot_turned(gateup_grad[half:], w_gateup).astype(LOW),
        dot_turned(gateup_grad[:half], w_gateup).astype(LOW),
    )
    scaled = second_grad * norm_gains[1]
    middle_grad = true_share(out_grad, 0) + second_scale * (
        scaled - second_unit * jnp.mean(scaled * second_unit, axis=-1, keepdims=True)
    )
    second_gain = jnp.sum(second_grad * second_unit, axis=0)

    sizes = [dp_count * n for _, n in plan.chunks]
    sums = [None] * len(sizes)
    sums = grad_blocks(
        hidden, mlp_grad, plan.of_matrix(3, hidden_blocks, row_blocks), 2, sums, sizes, block
    )
    sums = grad_blocks(
        second_in, gateup_grad, plan.of_matrix(2, row_blocks, 2 * hidden_blocks), 2, sums, sizes, block
    )
    reduced = [None] * len(sizes)

    def scatter(x):
        reduced[x] = lax.psum_scatter(
            sums[x], "dp", scatter_dimension=0, tiled=True, axis_index_groups=[plan.ring]
        )

    if len(sizes) > 2:
        scatter(2)

    feed_part = sum_shares(
        dot(hidden[half:], w_down).astype(LOW), dot(hidden[:half], w_down).astype(LOW)
    )
    out_parts = spread_share((middle + feed_part).astype(LOW))
    block_out = to_true(out_parts).reshape(sequences, length, model_width)

    attn_grad = jnp.concatenate(spread_share(middle_grad.astype(LOW)), axis=0)
    sums = grad_blocks(
        mixed_use, attn_grad, plan.of_matrix(1, out_attn_blocks, row_blocks), 4, sums, sizes, block
    )
    scatter(1)
    mixed_grad_parts = dot_turned(attn_grad, w_attn_out).astype(LOW)
    mixed_grad = to_true([mixed_grad_parts[i * share : (i + 1) * share] for i in range(4)]).reshape(
        sequences, length, kv_local, group_size, HD
    )
    query_grad, key_grad, value_grad = attend_backward(
        query_use[0], key_use[0], value_use[0], doc_ids[0], log_totals, mixed_grad[0], query_block
    )
    query_grad = rotate_back(query_grad[None], query_cos, query_sin).reshape(rows, query_cols)
    key_grad = rotate_back(key_grad[None], key_cos, key_sin).reshape(rows, key_cols)
    qkv_grad = jnp.concatenate(
        [query_grad, key_grad, value_grad.reshape(rows, key_cols)], axis=1
    ).astype(LOW)
    sums = grad_blocks(
        first_in,
        qkv_grad,
        plan.of_matrix(0, row_blocks, attn_blocks),
        attn_blocks,
        sums,
        sizes,
        block,
    )
    scatter(0)
    qkv_local = to_exchange(qkv_grad)
    first_grad = sum_shares(
        dot_turned(qkv_local[half:], w_qkv).astype(LOW),
        dot_turned(qkv_local[:half], w_qkv).astype(LOW),
    )
    scaled = first_grad * norm_gains[0]
    input_part = middle_grad + own_scale * (
        scaled - own_unit * jnp.mean(scaled * own_unit, axis=-1, keepdims=True)
    )
    input_parts = spread_share(input_part.astype(LOW))
    input_grad = to_true(input_parts).astype(F32).reshape(sequences, length, model_width)

    factor = float(rows * dp_count) ** (-0.5)
    gain_sums = jnp.stack([jnp.sum(first_grad * own_unit, axis=0), second_gain], axis=0)
    for bit in (1, 2):
        gain_sums = gain_sums + partner(gain_sums, bit)
    bit = 1
    while bit < dp_count:
        gain_sums = gain_sums + lax.ppermute(
            gain_sums, "dp", [(i, i ^ bit) for i in range(dp_count)]
        )
        bit *= 2
    gain_share = model_width // dp_count
    gain_grads = factor * lax.dynamic_slice_in_dim(gain_sums, d_index * gain_share, gain_share, 1)
    old_gains = lax.dynamic_slice_in_dim(norm_gains, d_index * gain_share, gain_share, 1)
    new_gains = old_gains - gain_rate * gain_grads

    state = None
    for x in reversed(range(len(sizes))):
        start, count = plan.chunks[x]
        state = shampoo(
            reduced[x],
            lax.slice_in_dim(order, start, start + count),
            factor,
            weight_blocks,
            ema_blocks,
            left_stats,
            right_stats,
            left_roots,
            right_roots,
            state,
        )
    grads, new_weights, new_ema, new_left, new_right = state
    return (
        block_out,
        input_grad,
        grads,
        new_weights,
        new_ema,
        new_left,
        new_right,
        gain_grads,
        new_gains,
    )


def solution(mesh):
    in_specs = (
        P("dp", None, None),
        P("dp", None, None),
        P("dp", None),
        P("dp", None),
        P(),
        P(("dp", "mp"), None, None),
        P(("dp", "mp"), None, None),
        P(("dp", "mp"), None, None),
        P(("dp", "mp"), None, None),
        P(("dp", "mp"), None, None),
        P(("dp", "mp"), None, None),
    )
    out_specs = (
        P("dp", None, None),
        P("dp", None, None),
        P(("dp", "mp"), None, None),
        P(("dp", "mp"), None, None),
        P(("dp", "mp"), None, None),
        P(("dp", "mp"), None, None),
        P(("dp", "mp"), None, None),
        P(None, "dp"),
        P(None, "dp"),
    )
    return jax.shard_map(
        on_device, mesh=mesh, in_specs=in_specs, out_specs=out_specs, check_vma=False
    )
```

time: 2010 us -> 777 us (0.39)
  waiting for transfers between devices: 1370 us -> 282 us
  local copies, waits for them, and re-layouts: 204 us -> 25.2 us
  Pallas kernels: 0 us -> 147 us
  matrix products: 257 us -> 180 us
  other arithmetic: 155 us -> 98.9 us
    reduce_scatter x5 -> x3, waiting for transfers between devices: 941 us -> 0.02 us  [scatter(): lax.psum_scatter(sums[x], 'dp', scatter_dimension=0, tiled=True, axis_ind...]
    all_gather x5 -> x3, waiting for transfers between devices: 424 us -> 98.9 us  [on_device(): lax.all_gather(chunk, 'dp', axis=0, tiled=True, axis_index_groups=[plan.r...]
    ppermute x0 -> x25, waiting for transfers between devices: none -> 181 us  [the longest x22 180 us: partner(): return lax.ppermute(values, 'mp', [(i, i ^ bit) for i in range(mp_count)])]
    pallas_call x0 -> x11, Pallas kernels: none -> 147 us  [the longest x3 66.9 us: shampoo(): pl.pallas_call(body, out_shape=[shape] * 5, grid_spec=pltpu.PrefetchScala...]
    dot_general x26 -> x22, matrix products: 252 us -> 168 us  [the longest x6 48.4 us: dot(): return jnp.dot(left, right, preferred_element_type=F32)]
    unnamed x134 -> x145, local copies, waits for them, and re-layouts: 81.5 us -> 16.8 us
    concatenate x6 -> x2, local copies, waits for them, and re-layouts: 53.7 us -> 0.43 us  [to_true(): return jnp.concatenate(flat, axis=0)]
    concatenate x5 -> x8, other arithmetic: 55.1 us -> 18.6 us  [the longest x1 5.52 us: on_device(): jnp.concatenate([gate_grad.astype(LOW), up_grad.astype(LOW)], axis=1)]
  transfers between devices with their start and end apart: 11 -> 31, of which waited for: 7 -> 15; matrix products, arithmetic and copies ran while one was open for 14% -> 31% of each run, Pallas kernels for 0% -> 11%
where the time goes in v2:
time: 777 us; the launch traced here: 768 us
  waiting for transfers between devices  282 us (36%)
  matrix products  180 us (23%)
  Pallas kernels  147 us (19%)
  other arithmetic  98.9 us (13%)
  local copies, waits for them, and re-layouts  25.2 us (3%)
  starting transfers between devices  19.5 us (3%)
  between operations  15.7 us (2%)
    ppermute x22, waiting for transfers between devices, partner(): return lax.ppermute(values, 'mp', [(i, i ^ bit) for i in range(mp_count)])  180 us
    all_gather x3, waiting for transfers between devices, on_device(): lax.all_gather(chunk, 'dp', axis=0, tiled=True, axis_index_groups=[plan.r...  98.9 us
    pallas_call x3, Pallas kernels, shampoo(): pl.pallas_call(body, out_shape=[shape] * 5, grid_spec=pltpu.PrefetchScala...  66.9 us
    pallas_call x4, Pallas kernels, grad_blocks(): pl.pallas_call(body, out_shape=[jax.ShapeDtypeStruct((sizes[x], block, bl...  54.9 us
    dot_general x6, matrix products, dot(): return jnp.dot(left, right, preferred_element_type=F32)  48.4 us
    dot_general x6, matrix products, dot_turned(): lax.dot_general(left, right, (((1,), (1,)), ((), ())), preferred_element_...  47.2 us
    another operation x7, other arithmetic  25.1 us
    pallas_call x3, Pallas kernels, place_blocks(): pl.pallas_call(body, out_shape=[jax.ShapeDtypeStruct(shapes[i], LOW) for...  20.7 us
  transfers between devices with their start and end apart: 31, of which 15 were waited for; matrix products, arithmetic and copies ran while one was open for 31% of the time, Pallas kernels for 11%

profile of v2, /device:TPU:0, one launch (start us, length us, event | category | flops | bytes accessed | tf_op | source)
XLA Modules:
  0.0 768.2 jit_solution(16009926328466884350)
XLA Ops:
  8.5 4.9 sort_blocks.1
  15.1 3.1 fusion.10
  19.1 5.2 fusion.12.refs_1_
  27.0 42.1 %all-gather.4.cloned.1.call-done.refs_4_ = bf16[144,128,128]{2,1,0:T(8,128)(2,1)} async-done(((bf16[18,128,128]{2,1,0:T(8,128)(2,1)}), bf16[144,128,128]{2,1,0:T(8,128)(2,1)}) %all-gather.4.cloned.1.call-update) | async-done | bytes 4718608 | tf_op jit(solution)/shard_map/all_gather | solution.py:463
  69.0 5.4 place_blocks.3
  74.5 5.5 fusion.139
  81.9 2.4 fusion.106
  85.8 7.3 fusion.134
  93.2 8.2 %fusion.6 = f32[8,512]{1,0:T(8,128)S(1)} fusion(f32[1,8,512,1024]{2,3,1,0:T(8,128)} %get-tuple-element.142, f32[8,512]{1,0:T(8,128)S(1)} %get-tuple-element.141), kind=kLoop, calls=%fused_computation.18 | loop fusion | flops 8384512 | bytes 16809984 | tf_op jit(solution)/shard_map/reduce_sum | solution.py:335
  101.4 9.0 %fusion.60 = bf16[512,1,8,64]{0,3,2,1:T(8,128)(2,1)S(1)} fusion(f32[8,512]{1,0:T(8,128)S(1)} %fusion.6, f32[1,8,512,1024]{2,3,1,0:T(8,128)} %get-tuple-element.142, f32[8,512]{1,0:T(8,128)S(1)} %get-tuple-element.141, f32[1024,640]{0,1:T(8,128)} %copy-done.20), kind=kOutput, calls=%fused_computation.112 | convolution fusion | flops 549715968 | bytes 17465344 | tf_op jit(solution)/shard_map/gjqk,kgd->qgjd/dot_general | solution.py:337
  110.4 7.8 %fusion.133 = (f32[8,512]{1,0:T(8,128)S(1)}, f32[1,8,512,1024]{2,3,1,0:T(8,128)}) fusion(bf16[1024,64,1]{1,0,2:T(8,128)(2,1)S(1)} %maximum_bitcast_fusion.2, bf16[1,1024,1,8,32]{1,4,3,2,0:T(8,128)(2,1)S(1)} %get-tuple-element.108, bf16[1,1024,1,8,32]{1,4,3,2,0:T(8,128)(2,1)S(1)} %get-tuple-element.107, pred[512,1024]{0,1:T(8,128)(4,1)S(1)} %get-tuple-element.136), kind=kOutput, calls=%fused_computation.256 | convolution fusion | flops 550498304 | bytes 18497536 | tf_op jit(solution)/shard_map/qgjd,kgd->gjqk/dot_general | solution.py:322
  118.2 8.2 %fusion.7 = f32[8,512]{1,0:T(8,128)S(1)} fusion(f32[1,8,512,1024]{2,3,1,0:T(8,128)} %get-tuple-element.140, f32[8,512]{1,0:T(8,128)S(1)} %get-tuple-element.139), kind=kLoop, calls=%fused_computation.19 | loop fusion | flops 8384512 | bytes 16809984 | tf_op jit(solution)/shard_map/reduce_sum | solution.py:335
  126.4 9.0 %fusion.57 = bf16[512,1,8,64]{0,3,2,1:T(8,128)(2,1)S(1)} fusion(f32[8,512]{1,0:T(8,128)S(1)} %fusion.7, f32[1,8,512,1024]{2,3,1,0:T(8,128)} %get-tuple-element.140, f32[8,512]{1,0:T(8,128)S(1)} %get-tuple-element.139, f32[1024,640]{0,1:T(8,128)} %copy-done.20), kind=kOutput, calls=%fused_computation.111 | convolution fusion | flops 549715968 | bytes 17465344 | tf_op jit(solution)/shard_map/gjqk,kgd->qgjd/dot_general | solution.py:337
  136.0 56.9 %all-gather.6.cloned.1.call-done.refs_3_ = bf16[368,128,128]{2,1,0:T(8,128)(2,1)} async-done(((bf16[46,128,128]{2,1,0:T(8,128)(2,1)}), bf16[368,128,128]{2,1,0:T(8,128)(2,1)}) %all-gather.6.cloned.1.call-update) | async-done | bytes 12058640 | tf_op jit(solution)/shard_map/all_gather | solution.py:463
  192.8 9.6 %place_blocks.4 = (bf16[512,2048]{1,0:T(8,128)(2,1)}, bf16[2048,2816]{1,0:T(8,128)(2,1)}, bf16[1408,2048]{1,0:T(8,128)(2,1)}) custom-call(s32[138]{0:T(256)} %constant.100.clone.refs_0_, s32[690]{0:T(1024)} %constant.101.clone.refs_1_, s32[276]{0:T(512)} %constant.102.clone.refs_2_, ...), custom_call_target="tpu_custom_call", output_to_operand_aliasing={{0}: (4, {}), {1}: (5, {}), {2}: (6, {})} | custom-call | tf_op jit(solution)/shard_map/place_blocks/pallas_call | solution.py:132
  202.5 4.3 convolution_convert_fusion.2
  207.1 4.2 collective-permute-done
  211.3 2.9 convert_add_fusion.3
  215.9 23.7 %collective-permute-done.1 = bf16[256,2048]{1,0:T(8,128)(2,1)S(1)} collective-permute-done((bf16[256,2048]{1,0:T(8,128)(2,1)S(1)}, bf16[256,2048]{1,0:T(8,128)(2,1)S(1)}, u32[]{:S(2)}, u32[]{:S(2)}) %collective-permute-start.1) | collective-permute-done | bytes 1048608 | tf_op jit(solution)/shard_map/ppermute | solution.py:425
  239.6 2.4 multiply_reduce_fusion.2
  246.2 23.3 %collective-permute-done.2 = bf16[256,2048]{1,0:T(8,128)(2,1)} collective-permute-done((bf16[256,2048]{1,0:T(8,128)(2,1)}, bf16[256,2048]{1,0:T(8,128)(2,1)}, u32[]{:S(2)}, u32[]{:S(2)}) %collective-permute-start.2) | collective-permute-done | bytes 1048608 | tf_op jit(solution)/shard_map/ppermute | solution.py:425
  269.5 4.3 convert_multiply_fusion.2
  275.3 2.3 pad_maximum_fusion.2.refs_2_
  277.6 5.6 place_blocks.5
  283.2 21.5 %fusion.129 = f32[1024,2816]{1,0:T(8,128)} fusion(bf16[2048,2816]{1,0:T(8,128)(2,1)} %get-tuple-element.54, bf16[256,2048]{1,0:T(8,128)(2,1)} %collective-permute-done.4, bf16[256,2048]{1,0:T(8,128)(2,1)} %collective-permute-done.3, bf16[256,2048]{1,0:T(8,128)(2,1)} %collective-permute-done.2, bf16[256,2048]{1,0:T(8,128)(2,1)} %multiply_convert_fusion.3), kind=kOutput, calls=%fused_computation.252 | convolution fusion | flops 11827937280 | bytes 27262976 | tf_op jit(solution)/shard_map/dot_general | solution.py:371
  304.7 17.4 %multiply_convert_fusion = (bf16[1024,1408]{1,0:T(8,128)(2,1)}, bf16[1024,1408]{1,0:T(8,128)(2,1)}, bf16[1024,1408]{1,0:T(8,128)(2,1)}) fusion(f32[1024,2816]{1,0:T(8,128)} %fusion.129, bf16[1408,2048]{1,0:T(8,128)(2,1)} %get-tuple-element.55, bf16[256,2048]{1,0:T(8,128)(2,1)S(1)} %get-tuple-element.98, bf16[256,2048]{1,0:T(8,128)(2,1)S(1)} %get-tuple-element.99, ...), kind=kOutput, calls=%fused_computation.45 | convolution fusion | flops 5945425920 | bytes 30146560 | tf_op jit(solution)/shard_map/dot_general | solution.py:375
  322.1 5.5 pad_maximum_fusion.refs_2_
  327.6 14.8 %grad_blocks.4 = (bf16[144,128,128]{2,1,0:T(8,128)(2,1)}, bf16[368,128,128]{2,1,0:T(8,128)(2,1)}, bf16[160,128,128]{2,1,0:T(8,128)(2,1)}) custom-call(s32[352]{0:T(512)} %constant.105.clone.refs_0_, bf16[1024,1408]{1,0:T(8,128)(2,1)} %get-tuple-element.89.refs_1_, bf16[1024,2048]{1,0:T(8,128)(2,1)} %pad_maximum_fusion.2.refs_2_), custom_call_target="tpu_custom_call" | custom-call | flops 5905580032 | bytes 12845056 | tf_op jit(solution)/shard_map/grad_blocks/pallas_call | solution.py:210
  342.4 3.7 pad_maximum_fusion.1.refs_1_
  346.1 25.0 %grad_blocks.5 = (bf16[144,128,128]{2,1,0:T(8,128)(2,1)}, bf16[368,128,128]{2,1,0:T(8,128)(2,1)}, bf16[160,128,128]{2,1,0:T(8,128)(2,1)}) custom-call(s32[704]{0:T(1024)} %constant.106.clone.refs_0_, bf16[1024,2048]{1,0:T(8,128)(2,1)} %pad_maximum_fusion.1.refs_1_, ...), custom_call_target="tpu_custom_call", output_to_operand_aliasing={{0}: (3, {}), {1}: (4, {}), {2}: (5, {})} | custom-call | flops 11811160064 | bytes 21495808 | tf_op jit(solution)/shard_map/grad_blocks/pallas_call | solution.py:210
  372.9 10.7 %convolution_convert_fusion = bf16[512,2048]{1,0:T(8,128)(2,1)S(1)} fusion(bf16[2048,2816]{1,0:T(8,128)(2,1)} %get-tuple-element.54, bf16[1024,1408]{1,0:T(8,128)(2,1)} %get-tuple-element.88, bf16[1024,1408]{1,0:T(8,128)(2,1)S(1)} %copy-done.21), kind=kOutput, calls=%fused_computation.61 | convolution fusion | flops 5912395776 | bytes 19398656 | tf_op jit(solution)/shard_map/dot_general | solution.py:375
  384.2 8.2 %convolution_convert_fusion.6 = bf16[512,2048]{1,0:T(8,128)(2,1)} fusion(bf16[1408,2048]{1,0:T(8,128)(2,1)} %get-tuple-element.55, bf16[1024,1408]{1,0:T(8,128)(2,1)} %get-tuple-element.89.refs_1_), kind=kOutput, calls=%fused_computation.67 | convolution fusion | flops 2953838592 | bytes 9306112 | tf_op jit(solution)/shard_map/dot_general | solution.py:371
  392.5 9.2 %convert_add_fusion.1 = f32[512,2048]{1,0:T(8,128)} fusion(bf16[512,2048]{1,0:T(8,128)(2,1)S(1)} %collective-permute-done.10, bf16[2048,2816]{1,0:T(8,128)(2,1)S(1)} %bitcast.225, bf16[1024,1408]{1,0:T(8,128)(2,1)} %get-tuple-element.88, bf16[1024,1408]{1,0:T(8,128)(2,1)} %get-tuple-element.87), kind=kOutput, calls=%fused_computation.55 | convolution fusion | flops 5915541504 | bytes 23592960 | tf_op jit(solution)/shard_map/dot_general | solution.py:375
  405.1 5.9 convert_add_fusion.2
  411.9 17.7 %collective-permute-done.11 = bf16[256,2048]{1,0:T(8,128)(2,1)S(1)} collective-permute-done((bf16[256,2048]{1,0:T(8,128)(2,1)S(1)}, bf16[256,2048]{1,0:T(8,128)(2,1)S(1)}, u32[]{:S(2)}, u32[]{:S(2)}) %collective-permute-start.11) | collective-permute-done | bytes 1048608 | tf_op jit(solution)/shard_map/ppermute | solution.py:425
  430.4 21.2 %collective-permute-done.6 = bf16[256,2048]{1,0:T(8,128)(2,1)S(1)} collective-permute-done((bf16[256,2048]{1,0:T(8,128)(2,1)S(1)}, bf16[256,2048]{1,0:T(8,128)(2,1)S(1)}, u32[]{:S(2)}, u32[]{:S(2)}) %collective-permute-start.6) | collective-permute-done | bytes 1048608 | tf_op jit(solution)/shard_map/ppermute | solution.py:425
  451.5 4.8 fusion.130
  457.8 23.1 %collective-permute-done.12 = bf16[256,2048]{1,0:T(8,128)(2,1)S(1)} collective-permute-done((bf16[256,2048]{1,0:T(8,128)(2,1)S(1)}, bf16[256,2048]{1,0:T(8,128)(2,1)S(1)}, u32[]{:S(2)}, u32[]{:S(2)}) %collective-permute-start.12) | collective-permute-done | bytes 1048608 | tf_op jit(solution)/shard_map/ppermute | solution.py:425
  483.6 2.4 pad_maximum_fusion.3.refs_2_
  485.9 7.4 grad_blocks.6
  495.0 4.2 convolution_convert_fusion.8
  499.9 11.0 %fusion.3 = (f32[8,512]{1,0:T(8,128)S(1)}, f32[1024,512,8]{1,0,2:T(8,128)}) fusion(f32[1,8,512,1024]{2,3,1,0:T(8,128)} %get-tuple-element.142, f32[8,512]{1,0:T(8,128)S(1)} %log_add_fusion.1, bf16[512,8,64]{0,2,1:T(8,128)(2,1)S(1)} %bitcast.231, f32[1024,640]{0,1:T(8,128)} %copy-done.20), kind=kOutput, calls=%fused_computation.9 | convolution fusion | flops 549449728 | bytes 34242560 | tf_op jit(solution)/shard_map/qgjd,kgd->gjqk/dot_general | solution.py:356
  510.9 12.6 %fusion.19 = bf16[8,512,1024]{1,2,0:T(8,128)(2,1)S(1)} fusion(f32[1024,512,8]{1,0,2:T(8,128)} %get-tuple-element.146, f32[1,8,512,1024]{2,3,1,0:T(8,128)} %get-tuple-element.142, f32[8,512]{1,0:T(8,128)S(1)} %get-tuple-element.145, f32[8,512]{1,0:T(8,128)S(1)} %log_add_fusion.1), kind=kLoop, calls=%fused_computation.31 | loop fusion | flops 16777216 | bytes 41975808 | tf_op jit(solution)/shard_map/reshape.62
  525.2 2.6 copy-done
  530.1 8.5 %fusion = (f32[8,512]{1,0:T(8,128)S(1)}, f32[1024,512,8]{1,0,2:T(8,128)}) fusion(f32[1,8,512,1024]{2,3,1,0:T(8,128)S(1)} %bitcast.223, f32[8,512]{1,0:T(8,128)S(1)} %log_add_fusion, bf16[512,8,64]{0,2,1:T(8,128)(2,1)S(1)} %bitcast.229, f32[1024,640]{0,1:T(8,128)} %copy-done.20), kind=kOutput, calls=%fused_computation.4 | convolution fusion | flops 549449728 | bytes 34242560 | tf_op jit(solution)/shard_map/qgjd,kgd->gjqk/dot_general | solution.py:356
  538.6 7.9 %fusion.20 = bf16[8,512,1024]{1,2,0:T(8,128)(2,1)S(1)} fusion(f32[1024,512,8]{1,0,2:T(8,128)} %get-tuple-element.144, f32[1,8,512,1024]{2,3,1,0:T(8,128)S(1)} %bitcast.223, f32[8,512]{1,0:T(8,128)S(1)} %get-tuple-element.143, f32[8,512]{1,0:T(8,128)S(1)} %log_add_fusion), kind=kLoop, calls=%fused_computation.32 | loop fusion | flops 16777216 | bytes 41975808 | tf_op jit(solution)/shard_map/reshape.71
  552.6 6.0 convolution_bitcast_fusion
  558.7 6.2 fusion.63
  565.0 7.6 fusion.64
  572.6 8.7 %fusion.70 = bf16[64,1024]{1,0:T(8,128)(2,1)S(1)} fusion(f32[64,1024]{1,0:T(8,128)S(1)} %fusion.64, bf16[512,8,64]{0,2,1:T(8,128)(2,1)S(1)} %bitcast.230, f32[1,8,512,1024]{2,3,1,0:T(8,128)} %get-tuple-element.140, f32[8,512]{1,0:T(8,128)S(1)} %log_add_fusion), kind=kOutput, calls=%fused_computation.118 | convolution fusion | flops 545390592 | bytes 17711104 | tf_op jit(solution)/shard_map/gjqk,qgjd->kgd/dot_general | solution.py:353
  581.5 2.4 fusion.89
  585.4 7.7 grad_blocks.7
  594.5 3.8 convolution_convert_fusion.4
  600.2 2.4 collective-permute-done.15
  607.0 17.5 %collective-permute-done.8 = bf16[256,2048]{1,0:T(8,128)(2,1)S(1)} collective-permute-done((bf16[256,2048]{1,0:T(8,128)(2,1)S(1)}, bf16[256,2048]{1,0:T(8,128)(2,1)S(1)}, u32[]{:S(2)}, u32[]{:S(2)}) %collective-permute-start.8) | collective-permute-done | bytes 1048608 | tf_op jit(solution)/shard_map/ppermute | solution.py:425
  624.5 22.0 %collective-permute-done.16 = bf16[256,2048]{1,0:T(8,128)(2,1)S(1)} collective-permute-done((bf16[256,2048]{1,0:T(8,128)(2,1)S(1)}, bf16[256,2048]{1,0:T(8,128)(2,1)S(1)}, u32[]{:S(2)}, u32[]{:S(2)}) %collective-permute-start.16) | collective-permute-done | bytes 1048608 | tf_op jit(solution)/shard_map/ppermute | solution.py:425
  651.0 23.1 %collective-permute-done.21 = f32[2,2048]{1,0:T(2,128)S(1)} collective-permute-done((f32[2,2048]{1,0:T(2,128)S(1)}, f32[2,2048]{1,0:T(2,128)S(1)}, u32[]{:S(2)}, u32[]{:S(2)}) %collective-permute-start.21) | collective-permute-done | bytes 16416 | tf_op jit(solution)/shard_map/ppermute | solution.py:425
  681.8 2.7 collective-permute-start.24
  684.4 2.3 maximum_bitcast_fusion
  688.0 16.4 %shampoo.3 = (f32[84,128,128]{2,1,0:T(8,128)}, f32[84,128,128]{2,1,0:T(8,128)}, f32[84,128,128]{2,1,0:T(8,128)}, f32[84,128,128]{2,1,0:T(8,128)}, f32[84,128,128]{2,1,0:T(8,128)}) custom-call(s32[20]{0:T(128)} %slice_bitcast_fusion.places_ref, bf16[20,128,128]{2,1,0:T(8,128)(2,1)} %reduce-scatter.8.cloned.1.call-done.g_ref, f32[84,128,128]{2,1,0:T(8,128)} %w_ref.7, ...), custom_call_target="tpu_custom_call" | custom-call | flops 335544320 | bytes 15073280 | tf_op jit(solution)/shard_map/shampoo/pallas_call | solution.py:259
  704.4 2.2 select_bitcast_fusion.3
  706.6 3.9 maximum_convert_fusion
  710.5 35.5 %shampoo.4 = (f32[84,128,128]{2,1,0:T(8,128)}, f32[84,128,128]{2,1,0:T(8,128)}, f32[84,128,128]{2,1,0:T(8,128)}, f32[84,128,128]{2,1,0:T(8,128)}, f32[84,128,128]{2,1,0:T(8,128)}) custom-call(s32[46]{0:T(128)} %slice_bitcast_fusion.1.places_ref, ...), custom_call_target="tpu_custom_call", output_to_operand_aliasing={{0}: (8, {}), {1}: (9, {}), {2}: (10, {}), {3}: (11, {}), {... | custom-call | flops 771751936 | bytes 34668544 | tf_op jit(solution)/shard_map/shampoo/pallas_call | solution.py:259
  746.1 15.0 %shampoo.5 = (f32[84,128,128]{2,1,0:T(8,128)}, f32[84,128,128]{2,1,0:T(8,128)}, f32[84,128,128]{2,1,0:T(8,128)}, f32[84,128,128]{2,1,0:T(8,128)}, f32[84,128,128]{2,1,0:T(8,128)}) custom-call(s32[18]{0:T(128)} %slice_bitcast_fusion.2.places_ref, ...), custom_call_target="tpu_custom_call", output_to_operand_aliasing={{0}: (8, {}), {1}: (9, {}), {2}: (10, {}), {3}: (11, {}), {... | custom-call | flops 301989888 | bytes 13565952 | tf_op jit(solution)/shard_map/shampoo/pallas_call | solution.py:259
  (269 shorter events, 64.2 us)
Async XLA Ops:
  7.2 61.9 %all-gather.4.cloned.1.call-start = ((), (), s32[]{:S(2)}) async-start(), calls=%async_computation.3 | async-start | bytes 5308416 | tf_op jit(solution)/shard_map/all_gather | solution.py:463
  13.4 179.5 %all-gather.6.cloned.1.call-start = ((), (), s32[]{:S(2)}) async-start(), calls=%async_computation.4 | async-start | bytes 13565952 | tf_op jit(solution)/shard_map/all_gather | solution.py:463
  14.1 263.4 %all-gather.8.cloned.1.call-start = ((), (), s32[]{:S(2)}) async-start(), calls=%async_computation.5 | async-start | bytes 5898240 | tf_op jit(solution)/shard_map/all_gather | solution.py:463
  14.9 673.1 %reduce-scatter.8.cloned.1.call-start = ((), (), s32[]{:S(2)}) async-start(), calls=%async_computation.8 | async-start | bytes 5898240 | tf_op jit(solution)/shard_map/reduce_scatter | solution.py:542
  14.9 66.9 %copy-start.55 = (f32[32]{0:T(128)}, f32[32]{0:T(128)S(1)}, u32[]{:S(2)}) copy-start(f32[32]{0:T(128)S(1)} %negate_power_fusion) | copy-start | bytes 388
  15.1 9.2 %copy-start.39 = (f32[1,2048]{1,0:T(1,128)}, f32[1,2048]{1,0:T(1,128)S(1)}, u32[]{:S(2)}) copy-start(f32[1,2048]{1,0:T(1,128)S(1)} %get-tuple-element.129) | copy-start | bytes 24580
  15.1 227.0 %copy-start.41 = (f32[1,2048]{1,0:T(1,128)}, f32[1,2048]{1,0:T(1,128)S(1)}, u32[]{:S(2)}) copy-start(f32[1,2048]{1,0:T(1,128)S(1)} %get-tuple-element.128) | copy-start | bytes 24580
  19.1 62.8 %copy-start.43 = (f32[1024]{0:T(1024)}, f32[1024]{0:T(1024)S(1)}, u32[]{:S(2)}) copy-start(f32[1024]{0:T(1024)S(1)} %fusion.112) | copy-start | bytes 12292
  25.5 59.0 %copy-start.26 = (f32[1024,32]{0,1:T(8,128)}, f32[1024,32]{0,1:T(8,128)S(1)}, u32[]{:S(2)}) copy-start(f32[1024,32]{0,1:T(8,128)S(1)} %get-tuple-element.132) | copy-start | bytes 393220
  84.4 25.9 %copy-start.14 = (bf16[1024,64,1]{1,0,2:T(8,128)(2,1)}, bf16[1024,64,1]{1,0,2:T(8,128)(2,1)S(1)}, u32[]{:S(2)}) copy-start(bf16[1024,64,1]{1,0,2:T(8,128)(2,1)S(1)} %maximum_bitcast_fusion.2) | copy-start | bytes 393220
  85.8 24.6 %copy-start.6 = (bf16[1,1024,1,8,32]{1,4,3,2,0:T(8,128)(2,1)}, bf16[1,1024,1,8,32]{1,4,3,2,0:T(8,128)(2,1)S(1)}, u32[]{:S(2)}) copy-start(bf16[1,1024,1,8,32]{1,4,3,2,0:T(8,128)(2,1)S(1)} %get-tuple-element.107) | copy-start | bytes 1572868
  85.8 24.6 %copy-start.8 = (bf16[1,1024,1,8,32]{1,4,3,2,0:T(8,128)(2,1)}, bf16[1,1024,1,8,32]{1,4,3,2,0:T(8,128)(2,1)S(1)}, u32[]{:S(2)}) copy-start(bf16[1,1024,1,8,32]{1,4,3,2,0:T(8,128)(2,1)S(1)} %get-tuple-element.108) | copy-start | bytes 1572868
  135.8 66.7 %copy-start.28 = (bf16[256,512]{1,0:T(8,128)(2,1)}, bf16[256,512]{1,0:T(8,128)(2,1)S(1)}, u32[]{:S(2)}) copy-start(bf16[256,512]{1,0:T(8,128)(2,1)S(1)} %copy.168) | copy-start | bytes 786436
  136.0 66.5 %copy-start.30 = (bf16[256,512]{1,0:T(8,128)(2,1)}, bf16[256,512]{1,0:T(8,128)(2,1)S(1)}, u32[]{:S(2)}) copy-start(bf16[256,512]{1,0:T(8,128)(2,1)S(1)} %copy.169) | copy-start | bytes 786436
  206.8 4.5 collective-permute-start
  214.3 31.8 %copy-start.58 = (s32[1,1024]{1,0:T(1,128)S(1)}, s32[1,1024]{1,0:T(1,128)}, u32[]{:S(2)}) copy-start(s32[1,1024]{1,0:T(1,128)} %param.27) | copy-start | bytes 12292
  214.4 55.1 %copy-start.16 = (bf16[1,1024,2048]{2,1,0:T(8,128)(2,1)S(1)}, bf16[1,1024,2048]{2,1,0:T(8,128)(2,1)}, u32[]{:S(2)}) copy-start(bf16[1,1024,2048]{2,1,0:T(8,128)(2,1)} %param.26) | copy-start | bytes 12582916
  214.4 25.3 %collective-permute-start.1 = (bf16[256,2048]{1,0:T(8,128)(2,1)S(1)}, bf16[256,2048]{1,0:T(8,128)(2,1)S(1)}, u32[]{:S(2)}, u32[]{:S(2)}) collective-permute-start(bf16[256,2048]{1,0:T(8,128)(2,1)S(1)} %slice.386), channel_id=1, source_target_pairs={{0,2},{1,3},{2,0},{3,1},{4,6},{5,7},{6,4},{7,5},{8,10},{9,11},{10,... | collective-permute-start | bytes 3145736 | tf_op jit(solution)/shard_map/ppermute | solution.py:425
  242.1 27.4 %copy-start.53 = (f32[256]{0:T(256)}, f32[256]{0:T(256)S(1)}, u32[]{:S(2)}) copy-start(f32[256]{0:T(256)S(1)} %add_rsqrt_fusion.2) | copy-start | bytes 3076
  244.7 24.8 %collective-permute-start.2 = (bf16[256,2048]{1,0:T(8,128)(2,1)}, bf16[256,2048]{1,0:T(8,128)(2,1)}, u32[]{:S(2)}, u32[]{:S(2)}) collective-permute-start(bf16[256,2048]{1,0:T(8,128)(2,1)} %multiply_convert_fusion.3), channel_id=1, source_target_pairs={{0,2},{1,3},{2,0},{3,1},{4,6},{5,7},{6,4},{7,5},{8,10},{9,11},{10,... | collective-permute-start | bytes 3145736 | tf_op jit(solution)/shard_map/ppermute | solution.py:425
  246.1 37.0 %collective-permute-start.3 = (bf16[256,2048]{1,0:T(8,128)(2,1)}, bf16[256,2048]{1,0:T(8,128)(2,1)}, u32[]{:S(2)}, u32[]{:S(2)}) collective-permute-start(bf16[256,2048]{1,0:T(8,128)(2,1)} %multiply_convert_fusion.3), channel_id=1, source_target_pairs={{0,1},{1,0},{2,3},{3,2},{4,5},{5,4},{6,7},{7,6},{8,9},{9,8},{10,11... | collective-permute-start | bytes 3145736 | tf_op jit(solution)/shard_map/ppermute | solution.py:425
  269.5 13.7 %collective-permute-start.4 = (bf16[256,2048]{1,0:T(8,128)(2,1)}, bf16[256,2048]{1,0:T(8,128)(2,1)}, u32[]{:S(2)}, u32[]{:S(2)}) collective-permute-start(bf16[256,2048]{1,0:T(8,128)(2,1)} %collective-permute-done.2), channel_id=1, source_target_pairs={{0,1},{1,0},{2,3},{3,2},{4,5},{5,4},{6,7},{7,6},{8,9},{9,8},{10,11... | collective-permute-start | bytes 3145736 | tf_op jit(solution)/shard_map/ppermute | solution.py:425
  371.1 339.4 %reduce-scatter.6.cloned.1.call-start = ((), (), s32[]{:S(2)}) async-start(), calls=%async_computation.7 | async-start | bytes 13565952 | tf_op jit(solution)/shard_map/reduce_scatter | solution.py:542
  372.9 19.6 %slice-start.4 = ((s8[11534336]{0:T(1024)(128)(4,1)}), s8[4194304]{0:T(1024)(128)(4,1)S(1)}, s32[]{:S(2)}) async-start(s8[11534336]{0:T(1024)(128)(4,1)} %bitcast.224), calls=%async_computation.13 | async-start | bytes 8388608
  372.9 19.6 %slice-start.5 = ((s8[11534336]{0:T(1024)(128)(4,1)}), s8[4194304]{0:T(1024)(128)(4,1)S(1)}, s32[]{:S(2)}) async-start(s8[11534336]{0:T(1024)(128)(4,1)} %bitcast.224), calls=%async_computation.14 | async-start | bytes 8388608
  383.7 8.8 %collective-permute-start.10 = (bf16[512,2048]{1,0:T(8,128)(2,1)S(1)}, bf16[512,2048]{1,0:T(8,128)(2,1)S(1)}, u32[]{:S(2)}, u32[]{:S(2)}) collective-permute-start(bf16[512,2048]{1,0:T(8,128)(2,1)S(1)} %convolution_convert_fusion), channel_id=1, source_target_pairs={{0,1},{1,0},{2,3},{3,2},{4,5},{5,4},{6,7},{7,6},{8,9},{9,8},{10,11... | collective-permute-start | bytes 6291464 | tf_op jit(solution)/shard_map/ppermute | solution.py:425
  384.2 20.9 %slice-start.7 = ((s8[5767168]{0:T(1024)(128)(4,1)}), s8[4194304]{0:T(1024)(128)(4,1)S(1)}, s32[]{:S(2)}) async-start(s8[5767168]{0:T(1024)(128)(4,1)} %bitcast.226), calls=%async_computation.16 | async-start | bytes 8388608
  392.5 12.6 %slice-start.8 = ((s8[5767168]{0:T(1024)(128)(4,1)}), s8[1572864]{0:T(1024)(128)(4,1)S(1)}, s32[]{:S(2)}) async-start(s8[5767168]{0:T(1024)(128)(4,1)} %bitcast.226), calls=%async_computation.17 | async-start | bytes 3145728
  392.5 12.6 %collective-permute-start.5 = (bf16[512,2048]{1,0:T(8,128)(2,1)}, bf16[512,2048]{1,0:T(8,128)(2,1)}, u32[]{:S(2)}, u32[]{:S(2)}) collective-permute-start(bf16[512,2048]{1,0:T(8,128)(2,1)} %convolution_convert_fusion.6), channel_id=1, source_target_pairs={{0,1},{1,0},{2,3},{3,2},{4,5},{5,4},{6,7},{7,6},{8,9},{9,8},{10,11... | collective-permute-start | bytes 6291464 | tf_op jit(solution)/shard_map/ppermute | solution.py:425
  403.5 26.1 %copy-start.3 = (f32[256,2048]{1,0:T(8,128)S(1)}, f32[256,2048]{1,0:T(8,128)}, u32[]{:S(2)}) copy-start(f32[256,2048]{1,0:T(8,128)} %copy-done.2) | copy-start | bytes 6291460
  403.5 26.1 %copy-start.13 = (f32[512,2048]{1,0:T(8,128)S(1)}, f32[512,2048]{1,0:T(8,128)}, u32[]{:S(2)}) copy-start(f32[512,2048]{1,0:T(8,128)} %convert_add_fusion.1) | copy-start | bytes 12582916
  403.5 26.1 %copy-start.42 = (f32[1,2048]{1,0:T(1,128)S(1)}, f32[1,2048]{1,0:T(1,128)}, u32[]{:S(2)}) copy-start(f32[1,2048]{1,0:T(1,128)} %copy-done.41) | copy-start | bytes 24580
  403.6 26.1 %copy-start.54 = (f32[256]{0:T(256)S(1)}, f32[256]{0:T(256)}, u32[]{:S(2)}) copy-start(f32[256]{0:T(256)} %copy-done.53) | copy-start | bytes 3076
  403.6 26.0 %collective-permute-start.11 = (bf16[256,2048]{1,0:T(8,128)(2,1)S(1)}, bf16[256,2048]{1,0:T(8,128)(2,1)S(1)}, u32[]{:S(2)}, u32[]{:S(2)}) collective-permute-start(bf16[256,2048]{1,0:T(8,128)(2,1)S(1)} %slice.384), channel_id=1, source_target_pairs={{0,2},{1,3},{2,0},{3,1},{4,6},{5,7},{6,4},{7,5},{8,10},{9,11},{10,... | collective-permute-start | bytes 3145736 | tf_op jit(solution)/shard_map/ppermute | solution.py:425
  411.2 40.3 %collective-permute-start.6 = (bf16[256,2048]{1,0:T(8,128)(2,1)S(1)}, bf16[256,2048]{1,0:T(8,128)(2,1)S(1)}, u32[]{:S(2)}, u32[]{:S(2)}) collective-permute-start(bf16[256,2048]{1,0:T(8,128)(2,1)S(1)} %slice.385), channel_id=1, source_target_pairs={{0,2},{1,3},{2,0},{3,1},{4,6},{5,7},{6,4},{7,5},{8,10},{9,11},{10,... | collective-permute-start | bytes 3145736 | tf_op jit(solution)/shard_map/ppermute | solution.py:425
  451.5 29.4 %copy-start.23 = (bf16[256,512]{1,0:T(8,128)(2,1)S(1)}, bf16[256,512]{1,0:T(8,128)(2,1)}, u32[]{:S(2)}) copy-start(bf16[256,512]{1,0:T(8,128)(2,1)} %copy-done.22) | copy-start | bytes 786436
  451.5 29.4 %copy-start.25 = (bf16[256,512]{1,0:T(8,128)(2,1)S(1)}, bf16[256,512]{1,0:T(8,128)(2,1)}, u32[]{:S(2)}) copy-start(bf16[256,512]{1,0:T(8,128)(2,1)} %copy-done.24) | copy-start | bytes 786436
  451.5 29.4 %copy-start.29 = (bf16[256,512]{1,0:T(8,128)(2,1)S(1)}, bf16[256,512]{1,0:T(8,128)(2,1)}, u32[]{:S(2)}) copy-start(bf16[256,512]{1,0:T(8,128)(2,1)} %copy-done.28) | copy-start | bytes 786436
  451.5 29.4 %copy-start.31 = (bf16[256,512]{1,0:T(8,128)(2,1)S(1)}, bf16[256,512]{1,0:T(8,128)(2,1)}, u32[]{:S(2)}) copy-start(bf16[256,512]{1,0:T(8,128)(2,1)} %copy-done.30) | copy-start | bytes 786436
  456.3 24.6 %collective-permute-start.12 = (bf16[256,2048]{1,0:T(8,128)(2,1)S(1)}, bf16[256,2048]{1,0:T(8,128)(2,1)S(1)}, u32[]{:S(2)}, u32[]{:S(2)}) collective-permute-start(bf16[256,2048]{1,0:T(8,128)(2,1)S(1)} %get-tuple-element.83), channel_id=1, source_target_pairs={{0,2},{1,3},{2,0},{3,1},{4,6},{5,7},{6,4},{7,5},{8,10},{9,11},{10,... | collective-permute-start | bytes 3145736 | tf_op jit(solution)/shard_map/ppermute | solution.py:425
  457.8 24.3 %collective-permute-start.13 = (bf16[256,2048]{1,0:T(8,128)(2,1)S(1)}, bf16[256,2048]{1,0:T(8,128)(2,1)S(1)}, u32[]{:S(2)}, u32[]{:S(2)}) collective-permute-start(bf16[256,2048]{1,0:T(8,128)(2,1)S(1)} %get-tuple-element.83), channel_id=1, source_target_pairs={{0,1},{1,0},{2,3},{3,2},{4,5},{5,4},{6,7},{7,6},{8,9},{9,8},{10,11... | collective-permute-start | bytes 3145736 | tf_op jit(solution)/shard_map/ppermute | solution.py:425
  480.9 2.7 collective-permute-start.14
  493.4 252.6 %reduce-scatter.4.cloned.1.call-start = ((), (), s32[]{:S(2)}) async-start(), calls=%async_computation.6 | async-start | bytes 5308416 | tf_op jit(solution)/shard_map/reduce_scatter | solution.py:542
  510.9 16.9 %slice-start = ((s8[16777216]{0:T(1024)(128)(4,1)}), s8[4194304]{0:T(1024)(128)(4,1)S(1)}, s32[]{:S(2)}) async-start(s8[16777216]{0:T(1024)(128)(4,1)} %bitcast.222), calls=%async_computation.9 | async-start | bytes 8388608
  510.9 12.7 %copy-start.15 = (bf16[1024,64,1]{1,0,2:T(8,128)(2,1)S(1)}, bf16[1024,64,1]{1,0,2:T(8,128)(2,1)}, u32[]{:S(2)}) copy-start(bf16[1024,64,1]{1,0,2:T(8,128)(2,1)} %copy-done.14) | copy-start | bytes 393220
  510.9 16.9 %slice-start.1 = ((s8[16777216]{0:T(1024)(128)(4,1)}), s8[4194304]{0:T(1024)(128)(4,1)S(1)}, s32[]{:S(2)}) async-start(s8[16777216]{0:T(1024)(128)(4,1)} %bitcast.222), calls=%async_computation.10 | async-start | bytes 8388608
  510.9 17.8 %slice-start.2 = ((s8[16777216]{0:T(1024)(128)(4,1)}), s8[4194304]{0:T(1024)(128)(4,1)S(1)}, s32[]{:S(2)}) async-start(s8[16777216]{0:T(1024)(128)(4,1)} %bitcast.222), calls=%async_computation.11 | async-start | bytes 8388608
  510.9 19.2 %slice-start.3 = ((s8[16777216]{0:T(1024)(128)(4,1)}), s8[4194304]{0:T(1024)(128)(4,1)S(1)}, s32[]{:S(2)}) async-start(s8[16777216]{0:T(1024)(128)(4,1)} %bitcast.222), calls=%async_computation.12 | async-start | bytes 8388608
  598.3 4.2 collective-permute-start.15
  598.5 26.0 %collective-permute-start.8 = (bf16[256,2048]{1,0:T(8,128)(2,1)S(1)}, bf16[256,2048]{1,0:T(8,128)(2,1)S(1)}, u32[]{:S(2)}, u32[]{:S(2)}) collective-permute-start(bf16[256,2048]{1,0:T(8,128)(2,1)S(1)} %copy-done.18), channel_id=1, source_target_pairs={{0,2},{1,3},{2,0},{3,1},{4,6},{5,7},{6,4},{7,5},{8,10},{9,11},{10,... | collective-permute-start | bytes 3145736 | tf_op jit(solution)/shard_map/ppermute | solution.py:425
  602.6 43.9 %copy-start.4 = (bf16[1,1024,2048]{2,1,0:T(8,128)(2,1)S(1)}, bf16[1,1024,2048]{2,1,0:T(8,128)(2,1)}, u32[]{:S(2)}) copy-start(bf16[1,1024,2048]{2,1,0:T(8,128)(2,1)} %param.25) | copy-start | bytes 12582916
  602.6 43.9 %copy-start.40 = (f32[1,2048]{1,0:T(1,128)S(1)}, f32[1,2048]{1,0:T(1,128)}, u32[]{:S(2)}) copy-start(f32[1,2048]{1,0:T(1,128)} %copy-done.39) | copy-start | bytes 24580
  604.5 43.0 %copy-start.12 = (f32[256,2048]{1,0:T(8,128)S(1)}, f32[256,2048]{1,0:T(8,128)}, u32[]{:S(2)}) copy-start(f32[256,2048]{1,0:T(8,128)} %get-tuple-element.84) | copy-start | bytes 6291460
  604.6 41.8 %collective-permute-start.16 = (bf16[256,2048]{1,0:T(8,128)(2,1)S(1)}, bf16[256,2048]{1,0:T(8,128)(2,1)S(1)}, u32[]{:S(2)}, u32[]{:S(2)}) collective-permute-start(bf16[256,2048]{1,0:T(8,128)(2,1)S(1)} %slice.383), channel_id=1, source_target_pairs={{0,2},{1,3},{2,0},{3,1},{4,6},{5,7},{6,4},{7,5},{8,10},{9,11},{10,... | collective-permute-start | bytes 3145736 | tf_op jit(solution)/shard_map/ppermute | solution.py:425
  607.0 72.7 %collective-permute-start.7 = (bf16[256,2048]{1,0:T(8,128)(2,1)S(1)}, bf16[256,2048]{1,0:T(8,128)(2,1)}, u32[]{:S(2)}, u32[]{:S(2)}) collective-permute-start(bf16[256,2048]{1,0:T(8,128)(2,1)S(1)} %copy-done.18), channel_id=1, source_target_pairs={{0,1},{1,0},{2,3},{3,2},{4,5},{5,4},{6,7},{7,6},{8,9},{9,8},{10,11... | collective-permute-start | bytes 3145736 | tf_op jit(solution)/shard_map/ppermute | solution.py:425
  624.5 55.2 %collective-permute-start.9 = (bf16[256,2048]{1,0:T(8,128)(2,1)S(1)}, bf16[256,2048]{1,0:T(8,128)(2,1)}, u32[]{:S(2)}, u32[]{:S(2)}) collective-permute-start(bf16[256,2048]{1,0:T(8,128)(2,1)S(1)} %collective-permute-done.8), channel_id=1, source_target_pairs={{0,1},{1,0},{2,3},{3,2},{4,5},{5,4},{6,7},{7,6},{8,9},{9,8},{10,11... | collective-permute-start | bytes 3145736 | tf_op jit(solution)/shard_map/ppermute | solution.py:425
  647.3 2.6 collective-permute-start.20
  648.1 31.5 %collective-permute-start.18 = (bf16[256,2048]{1,0:T(8,128)(2,1)S(1)}, bf16[256,2048]{1,0:T(8,128)(2,1)}, u32[]{:S(2)}, u32[]{:S(2)}) collective-permute-start(bf16[256,2048]{1,0:T(8,128)(2,1)S(1)} %fusion.40), channel_id=1, source_target_pairs={{0,2},{1,3},{2,0},{3,1},{4,6},{5,7},{6,4},{7,5},{8,10},{9,11},{10,... | collective-permute-start | bytes 3145736 | tf_op jit(solution)/shard_map/ppermute | solution.py:425
  649.9 24.2 %collective-permute-start.21 = (f32[2,2048]{1,0:T(2,128)S(1)}, f32[2,2048]{1,0:T(2,128)S(1)}, u32[]{:S(2)}, u32[]{:S(2)}) collective-permute-start(f32[2,2048]{1,0:T(2,128)S(1)} %fusion.124), channel_id=1, source_target_pairs={{0,2},{1,3},{2,0},{3,1},{4,6},{5,7},{6,4},{7,5},{8,10},{9,11},{10,... | collective-permute-start | bytes 49160 | tf_op jit(solution)/shard_map/ppermute | solution.py:425
  674.1 3.8 collective-permute-start.22
  676.4 28.0 %collective-permute-start.17 = (bf16[256,2048]{1,0:T(8,128)(2,1)S(1)}, bf16[256,2048]{1,0:T(8,128)(2,1)}, u32[]{:S(2)}, u32[]{:S(2)}) collective-permute-start(bf16[256,2048]{1,0:T(8,128)(2,1)S(1)} %fusion.40), channel_id=1, source_target_pairs={{0,1},{1,0},{2,3},{3,2},{4,5},{5,4},{6,7},{7,6},{8,9},{9,8},{10,11... | collective-permute-start | bytes 3145736 | tf_op jit(solution)/shard_map/ppermute | solution.py:425
  677.9 3.8 collective-permute-start.23
  679.7 24.7 %collective-permute-start.19 = (bf16[256,2048]{1,0:T(8,128)(2,1)}, bf16[256,2048]{1,0:T(8,128)(2,1)}, u32[]{:S(2)}, u32[]{:S(2)}) collective-permute-start(bf16[256,2048]{1,0:T(8,128)(2,1)} %collective-permute-done.18), channel_id=1, source_target_pairs={{0,1},{1,0},{2,3},{3,2},{4,5},{5,4},{6,7},{7,6},{8,9},{9,8},{10,11... | collective-permute-start | bytes 3145736 | tf_op jit(solution)/shard_map/ppermute | solution.py:425
  681.8 4.9 collective-permute-start.24
  (37 other events, 164.2 us)
Sparse Core Ops, SparseCore 0:
  13.5 55.5 all-gather.3
  71.2 121.6 all-gather.5
  194.9 57.7 all-gather.7
  371.3 58.5 reduce-scatter.7
  493.6 122.9 reduce-scatter.5
  618.7 53.4 reduce-scatter.3

commit v3 on v2

v3 whole, which is shorter than its diff:
```python
import functools

import jax
import jax.numpy as jnp
import numpy as np
from jax import lax
from jax.experimental import pallas as pl
from jax.experimental.pallas import tpu as pltpu
from jax.sharding import PartitionSpec as P

HEADS = 32
KV_HEADS = 4
HD = 64
FF = 5632
LOW = jnp.bfloat16
F32 = jnp.float32

weight_rate = 1.0
gain_rate = 0.2
average_decay = 0.9
VMEM_LIMIT = 60 * 1024 * 1024


def ring_order(count):
    return list(range(0, count, 2)) + list(range(1, count, 2))[::-1]


class Layout:
    def __init__(self, dp, own, rows, attn_cols, in_cols, out_attn_rows):
        self.dp, self.own = dp, own
        self.ring = ring_order(dp)
        n_in = rows * in_cols
        kinds, spots = [], []
        for k in range(dp * own):
            if k < n_in:
                r, c = divmod(k, in_cols)
                if c < attn_cols:
                    kinds.append(0), spots.append((0, r, c))
                else:
                    kinds.append(2), spots.append((2, r, c - attn_cols))
            else:
                r, c = divmod(k - n_in, rows)
                if r < out_attn_rows:
                    kinds.append(1), spots.append((1, r, c))
                else:
                    kinds.append(2), spots.append((3, r - out_attn_rows, c))
        self.order = np.zeros((dp, own), np.int32)
        for d in range(dp):
            mine = kinds[d * own : (d + 1) * own]
            self.order[d] = sorted(range(own), key=lambda l: (mine[l], l))
        count = np.array(kinds).reshape(dp, own)
        first = int((count == 0).sum(1).max())
        second = int((count <= 1).sum(1).max())
        bounds = [0, first, max(first, second), own]
        self.chunks = [(a, b - a) for a, b in zip(bounds[:-1], bounds[1:]) if b > a]
        self.table = []
        for p, d in enumerate(self.ring):
            for j, l in enumerate(self.order[d]):
                (x,) = [i for i, (a, n) in enumerate(self.chunks) if a <= j < a + n]
                a, n = self.chunks[x]
                self.table.append(spots[d * own + int(l)] + (x, p * n + j - a))

    def of_chunk(self, x, matrix):
        rows = [(s, r, c) for m, r, c, y, s in self.table if y == x and m == matrix]
        return np.array(sorted(rows), np.int32).reshape(-1, 3)

    def of_matrix(self, matrix, rows, cols):
        out = np.zeros((cols, rows, 2), np.int32)
        for m, r, c, x, s in self.table:
            if m == matrix:
                out[c, r] = (x, s)
        return out


ANY = pl.BlockSpec(memory_space=pl.ANY)
SMEM = pl.BlockSpec(memory_space=pltpu.SMEM)
VMEM = pl.BlockSpec(memory_space=pltpu.VMEM)


def sort_blocks(weights, order, chunks):
    block = weights.shape[1:]

    def body(order_ref, w_ref, *outs):
        for (start, count), out in zip(chunks, outs):

            def one(j, carry, start=start, out=out):
                out[j] = w_ref[order_ref[start + j]].astype(LOW)
                return carry

            lax.fori_loop(0, count, one, 0)

    return pl.pallas_call(
        body,
        out_shape=[jax.ShapeDtypeStruct((n,) + block, LOW) for _, n in chunks],
        in_specs=[SMEM, VMEM],
        out_specs=[VMEM] * len(chunks),
        compiler_params=pltpu.CompilerParams(vmem_limit_bytes=VMEM_LIMIT),
        name="sort_blocks",
    )(order, weights)


def place_blocks(gathered, tables, shapes, partial):
    block = gathered.shape[-1]
    used = [i for i, t in enumerate(tables) if len(t)]
    if not used:
        return partial
    count = sum(len(tables[i]) for i in used)
    known = [i for i in used if partial[i] is not None]

    def body(*refs):
        table_refs = refs[: len(used)]
        src = refs[len(used)]
        outs = refs[len(used) + 1 + len(known) : -3]
        stage, sem_in, sem_out = refs[-3:]
        at = 0
        for i, table_ref in zip(used, table_refs):

            def load(j, carry, table_ref=table_ref, at=at):
                pltpu.make_async_copy(src.at[table_ref[3 * j]], stage.at[at + j], sem_in).start()
                return carry

            lax.fori_loop(0, len(tables[i]), load, 0)
            at += len(tables[i])
        pltpu.make_async_copy(stage, stage, sem_in).wait()
        at = 0
        for i, table_ref, out in zip(used, table_refs, outs):

            def put(j, carry, table_ref=table_ref, out=out, at=at):
                row = pl.multiple_of(table_ref[3 * j + 1] * block, block)
                col = pl.multiple_of(table_ref[3 * j + 2] * block, block)
                pltpu.make_async_copy(
                    stage.at[at + j], out.at[pl.ds(row, block), pl.ds(col, block)], sem_out
                ).start()
                return carry

            lax.fori_loop(0, len(tables[i]), put, 0)
            at += len(tables[i])
        pltpu.make_async_copy(stage, stage, sem_out).wait()

    results = pl.pallas_call(
        body,
        out_shape=[jax.ShapeDtypeStruct(shapes[i], LOW) for i in used],
        in_specs=[SMEM] * len(used) + [ANY] * (1 + len(known)),
        out_specs=[ANY] * len(used),
        input_output_aliases={len(used) + 1 + j: used.index(i) for j, i in enumerate(known)},
        scratch_shapes=[
            pltpu.VMEM((count, block, block), LOW),
            pltpu.SemaphoreType.DMA,
            pltpu.SemaphoreType.DMA,
        ],
        compiler_params=pltpu.CompilerParams(vmem_limit_bytes=VMEM_LIMIT),
        cost_estimate=pl.CostEstimate(
            flops=0, bytes_accessed=4 * count * block * block, transcendentals=0
        ),
        name="place_blocks",
    )(
        *[jnp.asarray(tables[i].reshape(-1)) for i in used],
        gathered,
        *[partial[i] for i in known],
    )
    merged = list(partial)
    for i, value in zip(used, results):
        merged[i] = value
    return merged


def fill(scratch, pieces, order_ref):
    count = pieces[0].shape[0]
    for i, piece in enumerate(pieces):
        if order_ref is None:
            scratch[i * count : (i + 1) * count] = piece[...]
        else:
            scratch[pl.ds(pl.multiple_of(order_ref[i] * count, count), count)] = piece[...]


def grad_blocks(left, rights, order, pairs, table, wide, buffers, sizes, block):
    tokens, height = left.shape
    by_column = len(rights) > 1 and rights[0].shape[0] == tokens
    width = rights[0].shape[-1] * (2 if pairs else len(rights) if by_column else 1)
    rows, cols = height // block, width // block
    if pairs:
        table = np.stack([table[: cols // 2], table[cols // 2 :]], 1).reshape(table.shape)
        wide = 2
    steps = cols // wide
    assert not by_column or steps == 1
    per_step = rows * wide
    targets = table.reshape(steps, per_step, 2).tolist()
    used = sorted(set(table[:, :, 0].reshape(-1).tolist()))
    known = [x for x in used if buffers[x] is not None]
    n_order = 0 if order is None else 1
    joined = len(rights) > 1
    first_known = n_order + 1 + len(rights)
    first_out = first_known + len(known)

    def body(*refs):
        left_ref = refs[n_order]
        right_refs = refs[n_order + 1 : first_known]
        outs = refs[first_out : first_out + len(used)]
        stage, sems = refs[first_out + len(used) : first_out + len(used) + 2]
        t = pl.program_id(0)
        slot = lax.rem(t, 2)
        if joined:
            right_ref = refs[-1]
            if by_column:
                for i, piece in enumerate(right_refs):
                    right_ref[:, i * block : (i + 1) * block] = piece[...]
            else:
                fill(right_ref, right_refs, refs[0] if n_order else None)
            taken = right_ref[...]
        elif pairs:
            taken = jnp.concatenate([right_refs[0][0], right_refs[0][1]], axis=1)
        else:
            taken = right_refs[0][...]

        def finish(slot):
            pltpu.make_async_copy(stage.at[slot], stage.at[slot], sems.at[slot]).wait()

        @pl.when(t >= 2)
        def _():
            finish(slot)

        part = lax.dot_general(
            left_ref[...], taken, (((0,), (0,)), ((), ())), preferred_element_type=F32
        ).astype(LOW)
        for r in range(rows):
            for c in range(wide):
                stage[slot, c * rows + r] = part[
                    r * block : (r + 1) * block, c * block : (c + 1) * block
                ]
        for step in range(steps):

            @pl.when(t == step)
            def _(step=step):
                for j, (x, spot) in enumerate(targets[step]):
                    pltpu.make_async_copy(
                        stage.at[step % 2, j], outs[used.index(x)].at[spot], sems.at[step % 2]
                    ).start()

        @pl.when(t == steps - 1)
        def _():
            for step in range(max(0, steps - 2), steps):
                finish(step % 2)

    span = wide * block
    if pairs:
        right_specs = [pl.BlockSpec((2, tokens, block), lambda j: (0, 0, j))]
    elif by_column:
        right_specs = [pl.BlockSpec((tokens, block), lambda j: (0, 0))] * len(rights)
    else:
        right_specs = [pl.BlockSpec((x.shape[0], span), lambda j: (0, j)) for x in rights]
    results = pl.pallas_call(
        body,
        grid=(steps,),
        out_shape=[jax.ShapeDtypeStruct((sizes[x], block, block), LOW) for x in used],
        in_specs=[SMEM] * n_order
        + [pl.BlockSpec((tokens, height), lambda j: (0, 0))]
        + right_specs
        + [ANY] * len(known),
        out_specs=[ANY] * len(used),
        input_output_aliases={first_known + j: used.index(x) for j, x in enumerate(known)},
        scratch_shapes=[
            pltpu.VMEM((2, per_step, block, block), LOW),
            pltpu.SemaphoreType.DMA((2,)),
        ]
        + ([pltpu.VMEM((tokens, span), LOW)] if joined else []),
        compiler_params=pltpu.CompilerParams(vmem_limit_bytes=VMEM_LIMIT),
        cost_estimate=pl.CostEstimate(
            flops=4 * tokens * height * width,
            bytes_accessed=2 * (tokens * (height + width) + height * width),
            transcendentals=0,
        ),
        name="grad_blocks",
    )(*([] if order is None else [order]), left, *rights, *[buffers[x] for x in known])
    merged = list(buffers)
    for x, value in zip(used, results):
        merged[x] = value
    return merged


def feed_forward(pieces, weights, hidden_grad, block):
    share, width = pieces[0].shape
    rows = share * len(pieces)
    hidden = weights.shape[1] // 2
    steps = hidden // block

    def body(*refs):
        gate_w, up_w, grad_ref, hid_ref, out_ref, joined = refs[len(pieces) :]

        @pl.when(pl.program_id(0) == 0)
        def _():
            fill(joined, refs[: len(pieces)], None)

        both = jnp.dot(
            joined[...],
            jnp.concatenate([gate_w[...], up_w[...]], axis=1),
            preferred_element_type=F32,
        )
        gate, up = both[:, :block], both[:, block:]
        grad = grad_ref[...]
        sig = jax.nn.sigmoid(gate)
        act = gate * sig
        hid_ref[...] = (act * up).astype(LOW)
        out_ref[0] = (grad * up * sig * (1.0 + gate * (1.0 - sig))).astype(LOW)
        out_ref[1] = (grad * act).astype(LOW)

    return pl.pallas_call(
        body,
        grid=(steps,),
        in_specs=[pl.BlockSpec((share, width), lambda j: (0, 0))] * len(pieces)
        + [
            pl.BlockSpec((width, block), lambda j: (0, j)),
            pl.BlockSpec((width, block), lambda j: (0, steps + j)),
            pl.BlockSpec((rows, block), lambda j: (0, j)),
        ],
        out_specs=[
            pl.BlockSpec((rows, block), lambda j: (0, j)),
            pl.BlockSpec((2, rows, block), lambda j: (0, 0, j)),
            pl.BlockSpec((rows, width), lambda j: (0, 0)),
        ],
        out_shape=[
            jax.ShapeDtypeStruct((rows, hidden), LOW),
            jax.ShapeDtypeStruct((2, rows, hidden), LOW),
            jax.ShapeDtypeStruct((rows, width), LOW),
        ],
        compiler_params=pltpu.CompilerParams(vmem_limit_bytes=VMEM_LIMIT),
        cost_estimate=pl.CostEstimate(
            flops=4 * rows * width * hidden,
            bytes_accessed=2 * rows * width + 4 * width * hidden + 10 * rows * hidden,
            transcendentals=rows * hidden,
        ),
        name="feed_forward",
    )(*pieces, weights, weights, hidden_grad)


def project_rows(parts, weights, order, turned, tile):
    stacked = parts[0].ndim == 3
    rows = parts[0].shape[-2]
    half = rows // 2
    widths = [parts[0].shape[2]] * parts[0].shape[0] if stacked else [x.shape[1] for x in parts]
    starts = [sum(widths[:i]) for i in range(len(widths))]
    width = weights.shape[0] if turned else weights.shape[1]
    depth = sum(widths)
    share = rows // 4
    n_order = 0 if order is None else 1

    def body(*refs):
        part_refs = refs[n_order : n_order + len(parts)]
        w_ref, kept_ref, sent_ref = refs[n_order + len(parts) : n_order + len(parts) + 3]
        if n_order:
            joined = refs[-1]

            @pl.when(pl.program_id(0) == 0)
            def _():
                for i in range(4):
                    take = pl.ds(pl.multiple_of(refs[0][i] * share, share), share)
                    for part, at, size in zip(part_refs, starts, widths):
                        joined[i * share : (i + 1) * share, at : at + size] = part[take]

            pieces = [(joined[...], 0, depth)]
        elif stacked:
            pieces = [(part_refs[0][i], at, widths[i]) for i, at in enumerate(starts)]
        else:
            pieces = [(p[...], at, size) for p, at, size in zip(part_refs, starts, widths)]
        total = None
        for value, at, size in pieces:
            if turned:
                one = dot_turned(value, w_ref[:, at : at + size])
            else:
                one = dot(value, w_ref[at : at + size])
            total = one if total is None else total + one
        total = total.astype(LOW)
        kept_ref[...] = total[:half]
        sent_ref[...] = total[half:]

    whole = [pl.BlockSpec(x.shape, lambda j, n=x.ndim: (0,) * n) for x in parts]
    if turned:
        weight_spec = pl.BlockSpec((tile, depth), lambda j: (j, 0))
    else:
        weight_spec = pl.BlockSpec((depth, tile), lambda j: (0, j))
    kept, sent = pl.pallas_call(
        body,
        grid=(width // tile,),
        in_specs=[SMEM] * n_order + whole + [weight_spec],
        out_specs=[pl.BlockSpec((half, tile), lambda j: (0, j))] * 2,
        out_shape=[jax.ShapeDtypeStruct((half, width), LOW)] * 2,
        scratch_shapes=[pltpu.VMEM((rows, depth), LOW)] * n_order,
        compiler_params=pltpu.CompilerParams(vmem_limit_bytes=VMEM_LIMIT),
        cost_estimate=pl.CostEstimate(
            flops=2 * rows * depth * width,
            bytes_accessed=2 * (rows * depth + depth * width + rows * width),
            transcendentals=0,
        ),
        name="project_rows",
    )(*([order] if n_order else []), *parts, weights)
    return sent, kept


def to_heads(pieces, weights, order):
    share = pieces[0].shape[0]
    width = weights.shape[0]

    def body(order_ref, *refs):
        w_ref, out_ref = refs[-2:]
        for i, piece in enumerate(refs[:-2]):
            put = pl.ds(pl.multiple_of(order_ref[i] * share, share), share)
            out_ref[put] = dot_turned(piece[...], w_ref[...]).astype(LOW)

    rows = share * len(pieces)
    return pl.pallas_call(
        body,
        in_specs=[SMEM] + [VMEM] * (len(pieces) + 1),
        out_specs=VMEM,
        out_shape=jax.ShapeDtypeStruct((rows, width), LOW),
        compiler_params=pltpu.CompilerParams(vmem_limit_bytes=VMEM_LIMIT),
        cost_estimate=pl.CostEstimate(
            flops=2 * rows * width * weights.shape[1],
            bytes_accessed=2 * (rows + width) * weights.shape[1],
            transcendentals=0,
        ),
        name="to_heads",
    )(order, *pieces, weights)


LANES = 128
QUERIES = 256
LONGEST = 512


def turn(values, cos, sin):
    lane = lax.broadcasted_iota(jnp.int32, values.shape, 1)
    other = jnp.where(
        lane % HD < HD // 2,
        pltpu.roll(values, LANES - HD // 2, 1),
        pltpu.roll(values, HD // 2, 1),
    )
    return values * cos + other * sin


def key_tables(cos, sin):
    lane = lax.broadcasted_iota(jnp.int32, cos.shape, 1)
    return jnp.where(lane < HD, cos, 1.0), jnp.where(lane < HD, sin, 0.0)


def project_heads(inputs, weights, cos, sin):
    rows, depth = inputs.shape
    width = weights.shape[1]
    assert width % LANES == 0 and HD == 64

    def body(x_ref, w_ref, cos_ref, sin_ref, q_ref, kv_ref):
        for at in range(0, width, LANES):
            raw = dot(x_ref[...], w_ref[:, at : at + LANES])
            if at < width - LANES:
                q_ref[:, at : at + LANES] = (
                    turn(raw, cos_ref[...], sin_ref[...]).astype(LOW) * LOW(HD**-0.5)
                )
            else:
                kv_ref[...] = turn(raw, *key_tables(cos_ref[...], sin_ref[...])).astype(LOW)

    return pl.pallas_call(
        body,
        in_specs=[VMEM] * 4,
        out_specs=[VMEM] * 2,
        out_shape=[
            jax.ShapeDtypeStruct((rows, width - LANES), LOW),
            jax.ShapeDtypeStruct((rows, LANES), LOW),
        ],
        compiler_params=pltpu.CompilerParams(vmem_limit_bytes=VMEM_LIMIT),
        cost_estimate=pl.CostEstimate(
            flops=2 * rows * depth * width,
            bytes_accessed=2 * (rows * depth + depth * width + rows * width),
            transcendentals=0,
        ),
        name="project_heads",
    )(inputs, weights, cos, sin)


def key_range(at):
    low = max(0, (at - LONGEST + 1) // QUERIES * QUERIES)
    return low, at + QUERIES


def visible(start_ref, at, low, high):
    shape = (high - low, QUERIES)
    key = low + lax.broadcasted_iota(jnp.int32, shape, 0)
    query = at + lax.broadcasted_iota(jnp.int32, shape, 1)
    return (key >= start_ref[:, at : at + QUERIES]) & (key <= query)


def attend(queries, kv, starts):
    rows, width = queries.shape
    groups = width // LANES

    def body(start_ref, q_ref, kv_ref, o_ref, log_ref):
        for at in range(0, rows, QUERIES):
            low, high = key_range(at)
            seen = visible(start_ref, at, low, high)
            keys = kv_ref[low:high, :HD]
            values = kv_ref[low:high, HD:]
            for h in range(LANES // HD):
                query = q_ref[at : at + QUERIES, h * HD : (h + 1) * HD]
                scores = jnp.where(seen, dot_turned(keys, query), -1e30)
                top = jnp.max(scores, axis=0, keepdims=True)
                expo = jnp.exp(scores - top)
                total = jnp.sum(expo, axis=0, keepdims=True)
                probs = (expo * (1.0 / total)).astype(LOW)
                o_ref[at : at + QUERIES, h * HD : (h + 1) * HD] = lax.dot_general(
                    probs, values, (((0,), (0,)), ((), ())), preferred_element_type=F32
                ).astype(LOW)
                log_ref[0, h : h + 1, at : at + QUERIES] = top + jnp.log(total)

    column = pl.BlockSpec((rows, LANES), lambda j: (0, j))
    return pl.pallas_call(
        body,
        grid=(groups,),
        in_specs=[
            pl.BlockSpec((1, rows), lambda j: (0, 0)),
            column,
            pl.BlockSpec((rows, LANES), lambda j: (0, 0)),
        ],
        out_specs=[column, pl.BlockSpec((1, LANES // HD, rows), lambda j: (j, 0, 0))],
        out_shape=[
            jax.ShapeDtypeStruct((rows, width), LOW),
            jax.ShapeDtypeStruct((groups, LANES // HD, rows), F32),
        ],
        compiler_params=pltpu.CompilerParams(vmem_limit_bytes=VMEM_LIMIT),
        cost_estimate=pl.CostEstimate(
            flops=30 * rows * rows * width,
            bytes_accessed=4 * rows * width,
            transcendentals=rows * rows * width // HD,
        ),
        name="attend",
    )(starts, queries, kv)


def attend_back(group, queries, kv, starts, logs, grads, cos, sin, before, last):
    rows, _ = queries.shape
    first = before is None

    def body(start_ref, q_ref, kv_ref, log_ref, g_ref, cos_ref, sin_ref, *rest):
        before_ref = None if first else rest[0]
        dq_ref, sum_ref, acc = rest[-3:]
        acc[...] = jnp.zeros_like(acc) if first else before_ref[...]
        for at in range(0, rows, QUERIES):
            low, high = key_range(at)
            seen = visible(start_ref, at, low, high)
            keys = kv_ref[low:high, :HD]
            values = kv_ref[low:high, HD:]
            parts = []
            key_part, value_part = 0.0, 0.0
            for h in range(LANES // HD):
                query = q_ref[at : at + QUERIES, h * HD : (h + 1) * HD]
                grad = g_ref[at : at + QUERIES, h * HD : (h + 1) * HD]
                scores = jnp.where(seen, dot_turned(keys, query), -1e30)
                probs = jnp.exp(scores - log_ref[0, h : h + 1, at : at + QUERIES])
                value_part += dot(probs.astype(LOW), grad)
                prob_grads = dot_turned(values, grad)
                inner = jnp.sum(probs * prob_grads, axis=0, keepdims=True)
                score_grads = (probs * (prob_grads - inner)).astype(LOW)
                key_part += dot(score_grads, query)
                parts.append(
                    lax.dot_general(
                        score_grads, keys, (((0,), (0,)), ((), ())), preferred_element_type=F32
                    )
                )
            acc[low:high] += jnp.concatenate([key_part, value_part], axis=1)
            span = slice(at, at + QUERIES)
            dq_ref[span] = turn(
                jnp.concatenate(parts, axis=1) * HD**-0.5, cos_ref[span], -sin_ref[span]
            ).astype(LOW)
        if last:
            key_cos, key_sin = key_tables(cos_ref[...], sin_ref[...])
            sum_ref[...] = turn(acc[...], key_cos, -key_sin).astype(LOW)
        else:
            sum_ref[...] = acc[...]

    column = pl.BlockSpec((rows, LANES), lambda j: (0, group))
    whole = pl.BlockSpec((rows, LANES), lambda j: (0, 0))
    return pl.pallas_call(
        body,
        grid=(1,),
        in_specs=[
            pl.BlockSpec((1, rows), lambda j: (0, 0)),
            column,
            whole,
            pl.BlockSpec((1, LANES // HD, rows), lambda j: (group, 0, 0)),
            column,
            whole,
            whole,
        ]
        + ([] if first else [whole]),
        out_specs=[whole] * 2,
        out_shape=[
            jax.ShapeDtypeStruct((rows, LANES), LOW),
            jax.ShapeDtypeStruct((rows, LANES), LOW if last else F32),
        ],
        scratch_shapes=[pltpu.VMEM((rows, LANES), F32)],
        compiler_params=pltpu.CompilerParams(vmem_limit_bytes=VMEM_LIMIT),
        cost_estimate=pl.CostEstimate(
            flops=80 * rows * rows * LANES,
            bytes_accessed=16 * rows * LANES,
            transcendentals=rows * rows * LANES // HD,
        ),
        name="attend_back",
    )(starts, queries, kv, logs, grads, cos, sin, *([] if first else [before]))


def shampoo(sums, places, factor, weights, ema, left, right, left_roots, right_roots, before):
    count, block, _ = sums.shape
    group = 2 if count % 2 == 0 else 1
    steps = count // group
    depth = min(4, steps)
    extra = [] if before is None else list(before)

    def mm(a, b, dims):
        return lax.dot_general(
            a.astype(LOW), b.astype(LOW), (dims, ((), ())), preferred_element_type=F32
        )

    def body(places_ref, g_ref, *refs):
        ins, outs = refs[:6], refs[6 + len(extra) : 11 + len(extra)]
        given, made, sem_in, sem_out = refs[11 + len(extra) :]

        def load(t, slot):
            for u in range(group):
                place = places_ref[t * group + u]
                for i, ref in enumerate(ins):
                    pltpu.make_async_copy(
                        ref.at[place], given.at[slot, u, i], sem_in.at[slot]
                    ).start()

        def wait(buffer, slot, sems):
            pltpu.make_async_copy(buffer.at[slot], buffer.at[slot], sems.at[slot]).wait()

        for t in range(depth):
            load(t, t)

        def step(t, carry):
            slot = lax.rem(t, depth)
            wait(given, slot, sem_in)

            @pl.when(t >= depth)
            def _():
                wait(made, slot, sem_out)

            both = 0.5 * factor * factor
            for u in range(group):
                low = g_ref[t * group + u]
                made[slot, u, 0] = low.astype(F32) * factor
                made[slot, u, 3] = 0.5 * given[slot, u, 2] + both * mm(low, low, ((1,), (1,)))
                made[slot, u, 4] = 0.5 * given[slot, u, 3] + both * mm(low, low, ((0,), (0,)))
                part = mm(low, given[slot, u, 5], ((1,), (0,))) * factor
                fresh = given[slot, u, 0] - weight_rate * mm(given[slot, u, 4], part, ((1,), (0,)))
                made[slot, u, 1] = fresh
                made[slot, u, 2] = (
                    average_decay * given[slot, u, 1] + (1.0 - average_decay) * fresh
                )
            for u in range(group):
                place = places_ref[t * group + u]
                for i, ref in enumerate(outs):
                    pltpu.make_async_copy(
                        made.at[slot, u, i], ref.at[place], sem_out.at[slot]
                    ).start()

            @pl.when(t + depth < steps)
            def _():
                load(t + depth, slot)

            return carry

        lax.fori_loop(0, steps, step, 0)
        for t in range(steps - depth, steps):
            wait(made, t % depth, sem_out)

    return pl.pallas_call(
        body,
        out_shape=[jax.ShapeDtypeStruct(weights.shape, F32)] * 5,
        in_specs=[SMEM, VMEM] + [ANY] * (6 + len(extra)),
        out_specs=[ANY] * 5,
        input_output_aliases={8 + i: i for i in range(len(extra))},
        scratch_shapes=[
            pltpu.VMEM((depth, group, 6, block, block), F32),
            pltpu.VMEM((depth, group, 5, block, block), F32),
            pltpu.SemaphoreType.DMA((depth,)),
            pltpu.SemaphoreType.DMA((depth,)),
        ],
        compiler_params=pltpu.CompilerParams(vmem_limit_bytes=VMEM_LIMIT),
        cost_estimate=pl.CostEstimate(
            flops=8 * count * block**3,
            bytes_accessed=46 * count * block * block,
            transcendentals=0,
        ),
        name="shampoo",
    )(places, sums, weights, ema, left, right, left_roots, right_roots, *extra)


def rows_call(body, ins, outs, name, step=64):
    rows = max(x.shape[0] for x in ins)

    def spec(x):
        if x.shape[0] == rows:
            return pl.BlockSpec((step, x.shape[1]), lambda j: (j, 0))
        return pl.BlockSpec(x.shape, lambda j: (0, 0))

    return pl.pallas_call(
        body,
        grid=(rows // step,),
        in_specs=[spec(x) for x in ins],
        out_specs=[spec(x) for x in outs],
        out_shape=outs,
        compiler_params=pltpu.CompilerParams(vmem_limit_bytes=VMEM_LIMIT),
        cost_estimate=pl.CostEstimate(
            flops=10 * rows * ins[0].shape[1],
            bytes_accessed=sum(x.size * x.dtype.itemsize for x in list(ins) + list(outs)),
            transcendentals=0,
        ),
        name=name,
    )(*ins)


def add_near(kept, got):
    share = kept.shape[0] // 2
    width = kept.shape[1]
    step = 64

    def body(a_ref, c_ref, b_ref, d_ref, mine_ref, other_ref):
        mine_ref[...] = a_ref[...].astype(F32) + b_ref[...].astype(F32)
        other_ref[...] = (c_ref[...].astype(F32) + d_ref[...].astype(F32)).astype(LOW)

    first = pl.BlockSpec((step, width), lambda j: (j, 0))
    second = pl.BlockSpec((step, width), lambda j: (share // step + j, 0))
    return pl.pallas_call(
        body,
        grid=(share // step,),
        in_specs=[first, second, first, second],
        out_specs=[first] * 2,
        out_shape=[
            jax.ShapeDtypeStruct((share, width), F32),
            jax.ShapeDtypeStruct((share, width), LOW),
        ],
        compiler_params=pltpu.CompilerParams(vmem_limit_bytes=VMEM_LIMIT),
        cost_estimate=pl.CostEstimate(
            flops=2 * share * width, bytes_accessed=14 * share * width, transcendentals=0
        ),
        name="add_near",
    )(kept, kept, got, got)


def second_norm(tokens, mine, got, gain):
    def body(x_ref, a_ref, b_ref, gain_ref, middle_ref, low_ref):
        middle = x_ref[...].astype(F32) + (a_ref[...] + b_ref[...].astype(F32))
        middle_ref[...] = middle
        scale = lax.rsqrt(jnp.mean(middle * middle, axis=-1, keepdims=True) + 1e-05)
        low_ref[...] = (middle * scale * gain_ref[...]).astype(LOW)

    return rows_call(
        body,
        [tokens, mine, got, gain],
        [jax.ShapeDtypeStruct(tokens.shape, F32), jax.ShapeDtypeStruct(tokens.shape, LOW)],
        "second_norm",
    )


def norm_back(values, mine, got, gain, residual):
    def body(x_ref, a_ref, b_ref, gain_ref, r_ref, out_ref, low_ref, sum_ref):
        x = x_ref[...].astype(F32)
        grad = a_ref[...] + b_ref[...].astype(F32)
        scale = lax.rsqrt(jnp.mean(x * x, axis=-1, keepdims=True) + 1e-05)
        unit = x * scale
        scaled = grad * gain_ref[...]
        out = r_ref[...].astype(F32) + scale * (
            scaled - unit * jnp.mean(scaled * unit, axis=-1, keepdims=True)
        )
        out_ref[...] = out
        low_ref[...] = out.astype(LOW)

        @pl.when(pl.program_id(0) == 0)
        def _():
            sum_ref[...] = jnp.zeros_like(sum_ref)

        sum_ref[...] += jnp.sum(grad * unit, axis=0, keepdims=True)

    shape = values.shape
    return rows_call(
        body,
        [values, mine, got, gain, residual],
        [
            jax.ShapeDtypeStruct(shape, F32),
            jax.ShapeDtypeStruct(shape, LOW),
            jax.ShapeDtypeStruct((1, shape[1]), F32),
        ],
        "norm_back",
    )


def doc_positions(doc_ids):
    length = doc_ids.shape[-1]
    offsets = jnp.arange(length, dtype=jnp.int32)
    starts = jnp.concatenate(
        [jnp.ones(doc_ids.shape[:-1] + (1,), jnp.bool_), doc_ids[..., 1:] != doc_ids[..., :-1]],
        axis=-1,
    )
    first_index = lax.cummax(jnp.where(starts, offsets, 0), axis=doc_ids.ndim - 1)
    return offsets - first_index


def rope_tables(positions, head_size):
    half_size = head_size // 2
    exponent = jnp.arange(half_size, dtype=F32) * (2.0 / head_size)
    inverse = jnp.power(F32(10000.0), -exponent)
    angles = positions.astype(F32)[..., None] * inverse
    cos, sin = jnp.cos(angles), jnp.sin(angles)
    repeats = LANES // head_size
    return (
        jnp.concatenate([cos, cos] * repeats, axis=-1),
        jnp.concatenate([-sin, sin] * repeats, axis=-1),
    )


def after(value, *others):
    return lax.optimization_barrier((value,) + others)[0]


def dot(left, right):
    return jnp.dot(left, right, preferred_element_type=F32)


def dot_turned(left, right):
    return lax.dot_general(left, right, (((1,), (1,)), ((), ())), preferred_element_type=F32)


EXCHANGE = (0, 2, 1, 3)


def on_device(
    tokens_in,
    cotangent,
    select_mask,
    doc_ids,
    norm_gains,
    weight_blocks,
    ema_blocks,
    left_stats,
    right_stats,
    left_roots,
    right_roots,
):
    mp_count = lax.axis_size("mp")
    dp_count = lax.axis_size("dp")
    sequences, length, model_width = tokens_in.shape
    assert sequences == 1 and mp_count == 4 and dp_count & (dp_count - 1) == 0
    rows = sequences * length
    own, block, _ = weight_blocks.shape
    query_cols = HEADS * HD // mp_count
    key_cols = KV_HEADS * HD // mp_count
    hidden_cols = FF // mp_count
    assert KV_HEADS == mp_count and length % QUERIES == 0
    row_blocks = model_width // block
    attn_blocks = (query_cols + 2 * key_cols) // block
    hidden_blocks = hidden_cols // block
    in_blocks = attn_blocks + 2 * hidden_blocks
    out_attn_blocks = query_cols // block
    share = rows // mp_count
    m_index = lax.axis_index("mp")
    d_index = lax.axis_index("dp")

    plan = Layout(dp_count, own, row_blocks, attn_blocks, in_blocks, out_attn_blocks)
    order = lax.dynamic_slice_in_dim(jnp.asarray(plan.order), d_index, 1, 0).reshape(-1)
    shapes = [
        (model_width, attn_blocks * block),
        (query_cols, model_width),
        (model_width, 2 * hidden_cols),
        (hidden_cols, model_width),
    ]

    def partner(values, bit):
        return lax.ppermute(values, "mp", [(i, i ^ bit) for i in range(mp_count)])

    def true_share(values, group):
        return lax.dynamic_slice_in_dim(values, (m_index ^ group) * share, share, 0)

    def to_exchange(values):
        return jnp.concatenate([true_share(values, g) for g in EXCHANGE], axis=0)

    def to_true(parts):
        by_group = [parts[EXCHANGE.index(g)] for g in range(4)]
        low, high = m_index & 1, m_index & 2
        pairs = []
        for a, b in ((0, 1), (2, 3)):
            pairs.append(
                (
                    jnp.where(low == 0, by_group[a], by_group[b]),
                    jnp.where(low == 0, by_group[b], by_group[a]),
                )
            )
        flat = []
        for first, second in ((0, 1), (1, 0)):
            for i in range(2):
                flat.append(jnp.where(high == 0, pairs[first][i], pairs[second][i]))
        return jnp.concatenate(flat, axis=0)

    def near_sum(sent, kept):
        return add_near(kept, partner(sent, 1))

    def spread_share(mine, *cover):
        far = partner(mine, 2)
        near = partner(mine, 1)
        if cover:
            far = after(far, *cover)
        return [mine, far, near, partner(far, 1)]

    sorted_low = sort_blocks(weight_blocks, order, plan.chunks)
    gathered = [
        lax.all_gather(chunk, "dp", axis=0, tiled=True, axis_index_groups=[plan.ring])
        for chunk in sorted_low
    ]
    none = np.zeros((0, 3), np.int32)
    last = len(gathered) - 1

    def place(x, source, which, matrices):
        tables = [plan.of_chunk(x, i) if i in which else none for i in range(4)]
        return place_blocks(source, tables, shapes, matrices)

    matrices = place(0, gathered[0], (0, 1, 2, 3), [None] * 4)
    w_qkv = matrices[0]
    if last >= 1:
        matrices = place(1, gathered[1], (1,), matrices)
    w_attn_out = matrices[1]

    positions = doc_positions(doc_ids)
    starts = jnp.arange(length, dtype=jnp.int32)[None] - positions
    cos, sin = rope_tables(positions[0], HD)

    tokens_low = tokens_in.reshape(rows, model_width)
    tokens = tokens_low.astype(F32)
    first_scale = lax.rsqrt(jnp.mean(tokens * tokens, axis=-1, keepdims=True) + 1e-05)
    first_in = (tokens * first_scale * norm_gains[0]).astype(LOW)
    out_grad = cotangent.reshape(rows, model_width) * select_mask.astype(LOW).reshape(rows, 1)
    own_tokens = true_share(tokens_low, 0)
    own_grad = true_share(out_grad, 0)
    mlp_grad = to_exchange(out_grad)

    shares = (m_index ^ jnp.array(EXCHANGE, jnp.int32)).astype(jnp.int32)
    queries, kv = project_heads(first_in, w_qkv, cos, sin)
    kv, mlp_grad, own_tokens, own_grad = lax.optimization_barrier(
        (kv, mlp_grad, own_tokens, own_grad)
    )
    mixed, logs = attend(queries, kv, starts)
    attended_sent, attended_kept = project_rows([mixed], w_attn_out, shares, False, 512)
    mine, other = near_sum(attended_sent, attended_kept)
    if last >= 1:
        matrices = place(1, after(gathered[1], other), (2, 3), matrices)
        mine, *matrices[2:] = lax.optimization_barrier((mine, *matrices[2:]))
    middle, second_low = second_norm(own_tokens, mine, partner(other, 2), norm_gains[1:])
    if last >= 2:
        matrices = place(2, after(gathered[2], second_low), (2, 3), matrices)
    w_gateup, w_down = matrices[2:]
    hidden_grad = dot_turned(mlp_grad, w_down)
    second_pieces = spread_share(second_low, hidden_grad)
    hidden, gateup_grad, second_in = feed_forward(second_pieces, w_gateup, hidden_grad, block)

    second_sent, second_kept = project_rows([gateup_grad], w_gateup, None, True, 256)
    sizes = [dp_count * n for _, n in plan.chunks]
    sums = [None] * len(sizes)
    sums = grad_blocks(
        after(hidden, second_sent),
        [mlp_grad],
        None,
        False,
        plan.of_matrix(3, hidden_blocks, row_blocks),
        2,
        sums,
        sizes,
        block,
    )
    mine, other = near_sum(second_sent, after(second_kept, *[x for x in sums if x is not None]))
    second_in = after(second_in, other)
    got = partner(other, 2)
    sums = grad_blocks(
        second_in,
        [gateup_grad],
        None,
        True,
        plan.of_matrix(2, row_blocks, 2 * hidden_blocks),
        2,
        sums,
        sizes,
        block,
    )
    reduced = [None] * len(sizes)

    def scatter(x):
        reduced[x] = lax.psum_scatter(
            sums[x], "dp", scatter_dimension=0, tiled=True, axis_index_groups=[plan.ring]
        )

    if last >= 2:
        scatter(2)

    mine = after(mine, *[x for x in sums if x is not None])
    middle_grad, attn_low, second_gain = norm_back(
        middle, mine, got, norm_gains[1:], own_grad
    )
    feed_sent, feed_kept = project_rows([after(hidden, attn_low)], w_down, None, False, 512)
    attn_grad = spread_share(attn_low, feed_kept)
    sums = grad_blocks(
        mixed,
        attn_grad,
        shares,
        False,
        plan.of_matrix(1, out_attn_blocks, row_blocks),
        4,
        sums,
        sizes,
        block,
    )
    if last >= 1:
        scatter(1)

    mixed_grad = to_heads(attn_grad, after(w_attn_out, *[x for x in sums if x is not None]), shares)

    feed_mine, feed_other = near_sum(feed_sent, after(feed_kept, mixed_grad))
    groups = query_cols // LANES
    query_grads, kv_grad = [], None
    feed_step = feed_other
    for group in range(groups):
        pair_grad, kv_grad = attend_back(
            group,
            queries,
            kv,
            starts,
            logs,
            after(mixed_grad, feed_step),
            cos,
            sin,
            kv_grad,
            group == groups - 1,
        )
        query_grads.append(pair_grad)
        if group == groups - 3:
            feed_part = after(feed_mine, pair_grad) + partner(feed_other, 2).astype(F32)
            feed_step = out_low = (middle + feed_part).astype(LOW)
    out_parts = spread_share(out_low)
    qkv_grads = query_grads + [kv_grad]
    sums = grad_blocks(
        first_in,
        qkv_grads,
        None,
        False,
        plan.of_matrix(0, row_blocks, attn_blocks),
        attn_blocks,
        sums,
        sizes,
        block,
    )
    scatter(0)
    first_sent, first_kept = project_rows(
        [after(qkv_grads[0], sums[0])] + qkv_grads[1:], w_qkv, shares, True, 512
    )
    mine, other = near_sum(first_sent, first_kept)
    factor = float(rows * dp_count) ** (-0.5)

    def update(x, state, *others):
        start, count = plan.chunks[x]
        return shampoo(
            reduced[x],
            after(lax.slice_in_dim(order, start, start + count), *others),
            factor,
            weight_blocks,
            ema_blocks,
            left_stats,
            right_stats,
            left_roots,
            right_roots,
            state,
        )

    state = None
    if last >= 2:
        state = update(2, state, other)
        mine = after(mine, *state)
    _, input_low, first_gain = norm_back(
        own_tokens, mine, partner(other, 2), norm_gains[:1], middle_grad
    )
    gain_sums = jnp.concatenate([first_gain, second_gain], axis=0)
    gain_sums = gain_sums + partner(gain_sums, 2)
    input_low = after(input_low, gain_sums)
    if last >= 1:
        state = update(1, state, other)
        input_low = after(input_low, *state)
    input_parts = spread_share(input_low)
    gain_sums = gain_sums + partner(gain_sums, 1)
    bit = 1
    while bit < dp_count:
        gain_sums = gain_sums + lax.ppermute(
            gain_sums, "dp", [(i, i ^ bit) for i in range(dp_count)]
        )
        bit *= 2
    gain_share = model_width // dp_count
    gain_grads = factor * lax.dynamic_slice_in_dim(gain_sums, d_index * gain_share, gain_share, 1)
    old_gains = lax.dynamic_slice_in_dim(norm_gains, d_index * gain_share, gain_share, 1)
    new_gains = old_gains - gain_rate * gain_grads
    block_out = to_true(out_parts).reshape(sequences, length, model_width)
    input_grad = to_true(input_parts).astype(F32).reshape(sequences, length, model_width)
    grads, new_weights, new_ema, new_left, new_right = update(
        0, state, block_out, input_grad, new_gains
    )
    return (
        block_out,
        input_grad,
        grads,
        new_weights,
        new_ema,
        new_left,
        new_right,
        gain_grads,
        new_gains,
    )


def solution(mesh):
    in_specs = (
        P("dp", None, None),
        P("dp", None, None),
        P("dp", None),
        P("dp", None),
        P(),
        P(("dp", "mp"), None, None),
        P(("dp", "mp"), None, None),
        P(("dp", "mp"), None, None),
        P(("dp", "mp"), None, None),
        P(("dp", "mp"), None, None),
        P(("dp", "mp"), None, None),
    )
    out_specs = (
        P("dp", None, None),
        P("dp", None, None),
        P(("dp", "mp"), None, None),
        P(("dp", "mp"), None, None),
        P(("dp", "mp"), None, None),
        P(("dp", "mp"), None, None),
        P(("dp", "mp"), None, None),
        P(None, "dp"),
        P(None, "dp"),
    )
    return jax.shard_map(
        on_device, mesh=mesh, in_specs=in_specs, out_specs=out_specs, check_vma=False
    )
```

time: 777 us -> 626 us (0.81)
  matrix products: 180 us -> 12 us
  Pallas kernels: 147 us -> 264 us
  other arithmetic: 98.9 us -> 27.7 us
  waiting for transfers between devices: 282 us -> 265 us
  local copies, waits for them, and re-layouts: 25.2 us -> 17.2 us
    dot_general x18 -> x0, matrix products: 133 us -> none  [the longest x6 48.4 us: dot(): return jnp.dot(left, right, preferred_element_type=F32)]
    pallas_call x7 -> x26, Pallas kernels: 122 us -> 236 us  [the longest x4 47.4 us: grad_blocks(): pl.pallas_call(body, grid=(steps,), out_shape=[jax.ShapeDtypeStruct((size...]
    ppermute x22, waiting for transfers between devices: 180 us -> 120 us  [partner(): return lax.ppermute(values, 'mp', [(i, i ^ bit) for i in range(mp_count)])]
    all_gather x3, waiting for transfers between devices: 98.9 us -> 142 us  [on_device(): lax.all_gather(chunk, 'dp', axis=0, tiled=True, axis_index_groups=[plan.r...]
    dot_general x6 -> x1, matrix products: 47.2 us -> 12 us  [dot_turned(): lax.dot_general(left, right, (((1,), (1,)), ((), ())), preferred_element_...]
    another operation x8 -> x3, other arithmetic: 25.1 us -> 1.06 us  [the longest x1 0.6 us: doc_positions(): lax.cummax(jnp.where(starts, offsets, 0), axis=doc_ids.ndim - 1)]
    reduce_sum x5 -> x0, other arithmetic: 20.4 us -> none  [the longest x2 16.4 us: attend_forward(): denominator = jnp.sum(expo_values, axis=-1, keepdims=True)]
    concatenate x8 -> x2, other arithmetic: 15.6 us -> 2.65 us  [the longest x1 1.93 us: rope_tables(): jnp.concatenate([cos, cos] * repeats, axis=-1)]
  transfers between devices with their start and end apart: 31 -> 31, of which waited for: 15 -> 17; matrix products, arithmetic and copies ran while one was open for 31% -> 7% of each run, Pallas kernels for 11% -> 30%
where the time goes in v3:
time: 626 us; the launch traced here: 619 us
  waiting for transfers between devices  265 us (42%)
  Pallas kernels  264 us (42%)
  other arithmetic  27.7 us (4%)
  starting transfers between devices  18.8 us (3%)
  local copies, waits for them, and re-layouts  17.2 us (3%)
  between operations  15 us (2%)
  matrix products  12 us (2%)
    all_gather x3, waiting for transfers between devices, on_device(): lax.all_gather(chunk, 'dp', axis=0, tiled=True, axis_index_groups=[plan.r...  142 us
    ppermute x22, waiting for transfers between devices, partner(): return lax.ppermute(values, 'mp', [(i, i ^ bit) for i in range(mp_count)])  120 us
    pallas_call x4, Pallas kernels, grad_blocks(): pl.pallas_call(body, grid=(steps,), out_shape=[jax.ShapeDtypeStruct((size...  47.4 us
    pallas_call x4, Pallas kernels, project_rows(): pl.pallas_call(body, grid=(width // tile,), in_specs=[SMEM] * n_order + w...  41.6 us
    pallas_call x3, Pallas kernels, shampoo(): pl.pallas_call(body, out_shape=[jax.ShapeDtypeStruct(weights.shape, F32)]...  32.2 us
    pallas_call x4, Pallas kernels, attend_back(): pl.pallas_call(body, grid=(1,), in_specs=[pl.BlockSpec((1, rows), lambda...  31.7 us
    pallas_call x4, Pallas kernels, place_blocks(): pl.pallas_call(body, out_shape=[jax.ShapeDtypeStruct(shapes[i], LOW) for...  22.6 us
    pallas_call x1, Pallas kernels, feed_forward(): pl.pallas_call(body, grid=(steps,), in_specs=[pl.BlockSpec((share, width)...  20.4 us
  transfers between devices with their start and end apart: 31, of which 17 were waited for; matrix products, arithmetic and copies ran while one was open for 7% of the time, Pallas kernels for 30%

profile of v3, /device:TPU:0, one launch (start us, length us, event | category | flops | bytes accessed | tf_op | source)
XLA Modules:
  0.0 619.4 jit_solution(7024831751090479055)
XLA Ops:
  8.5 4.9 sort_blocks.1
  16.6 1.9 fusion.3
  18.5 1.9 pad_maximum_fusion.1
  23.6 2.8 pad_maximum_fusion.refs_1_
  27.6 3.0 fusion.2.x_ref.refs_0_
  30.7 38.4 %all-gather.4.cloned.1.call-done.refs_4_ = bf16[144,128,128]{2,1,0:T(8,128)(2,1)} async-done(((bf16[18,128,128]{2,1,0:T(8,128)(2,1)}), bf16[144,128,128]{2,1,0:T(8,128)(2,1)}) %all-gather.4.cloned.1.call-update) | async-done | bytes 4718608 | tf_op jit(solution)/shard_map/all_gather | solution.py:913
  69.1 5.2 place_blocks.4
  74.3 10.3 %project_heads.1 = (bf16[1024,512]{1,0:T(8,128)(2,1)}, bf16[1024,128]{1,0:T(8,128)(2,1)}) custom-call(bf16[1024,2048]{1,0:T(8,128)(2,1)} %fusion.2.x_ref.refs_0_, bf16[2048,640]{1,0:T(8,128)(2,1)} %get-tuple-element.110.w_ref.refs_6_, f32[1024,128]{1,0:T(8,128)} %get-tuple-element.230.cos_ref, f32[1024,128]{1,0:T(8,128)} %get-tuple-element.231.sin_ref), custom_call_target="tpu_custom_call" | custom-call | flops 2684354560 | bytes 8126464 | tf_op jit(solution)/shard_map/project_heads/pallas_call | solution.py:459
  84.5 13.0 %attend.1 = (bf16[1024,512]{1,0:T(8,128)(2,1)}, f32[4,2,1024]{2,1,0:T(2,128)}) custom-call(s32[1,1024]{1,0:T(1,128)} %reduce_window_max.29.start_ref, bf16[1024,512]{1,0:T(8,128)(2,1)} %get-tuple-element.113.q_ref, bf16[1024,128]{1,0:T(8,128)(2,1)} %get-tuple-element.114.kv_ref), custom_call_target="tpu_custom_call" | custom-call | flops 16106127360 | bytes 2097152 | tf_op jit(solution)/shard_map/attend/pallas_call | solution.py:512
  97.5 95.3 %all-gather.6.cloned.1.call-done.refs_1_.refs_2_ = bf16[368,128,128]{2,1,0:T(8,128)(2,1)} async-done(((bf16[46,128,128]{2,1,0:T(8,128)(2,1)}), bf16[368,128,128]{2,1,0:T(8,128)(2,1)}) %all-gather.6.cloned.1.call-update) | async-done | bytes 12058640 | tf_op jit(solution)/shard_map/all_gather | solution.py:913
  192.8 3.2 place_blocks.5.refs_2_.refs_4_
  196.0 5.8 project_rows.4
  201.8 4.4 collective-permute-done.b_ref.d_ref
  207.5 4.3 add_near.4
  213.3 8.7 %place_blocks.6 = (bf16[2048,2816]{1,0:T(8,128)(2,1)}, bf16[1408,2048]{1,0:T(8,128)(2,1)}) custom-call(s32[690]{0:T(1024)} %constant.78.clone.refs_0_, s32[276]{0:T(512)} %constant.79.clone.refs_1_, bf16[368,128,128]{2,1,0:T(8,128)(2,1)} %all-gather.6.cloned.1.call-done.refs_1_.refs_2_, ...), custom_call_target="tpu_custom_call", output_to_operand_aliasing={{0}: (3, {}), {1}: (4, {})} | custom-call | bytes 21102592 | tf_op jit(solution)/shard_map/place_blocks/pallas_call | solution.py:140
  222.0 15.3 %collective-permute-done.1.b_ref = bf16[256,2048]{1,0:T(8,128)(2,1)S(1)} collective-permute-done((bf16[256,2048]{1,0:T(8,128)(2,1)}, bf16[256,2048]{1,0:T(8,128)(2,1)S(1)}, u32[]{:S(2)}, u32[]{:S(2)}) %collective-permute-start.1) | collective-permute-done | bytes 1048608 | tf_op jit(solution)/shard_map/ppermute | solution.py:876
  238.2 4.6 second_norm.1
  244.3 7.9 %all-gather.8.cloned.1.call-done.refs_2_ = bf16[160,128,128]{2,1,0:T(8,128)(2,1)} async-done(((bf16[20,128,128]{2,1,0:T(8,128)(2,1)}), bf16[160,128,128]{2,1,0:T(8,128)(2,1)}) %all-gather.8.cloned.1.call-update) | async-done | bytes 5242896 | tf_op jit(solution)/shard_map/all_gather | solution.py:913
  252.1 5.5 place_blocks.7
  257.7 12.0 %fusion.11.refs_6_ = f32[1024,1408]{1,0:T(8,128)} fusion(bf16[1024,2048]{1,0:T(8,128)(2,1)} %pad_maximum_fusion.refs_1_, bf16[1408,2048]{1,0:T(8,128)(2,1)} %get-tuple-element.135.refs_1_), kind=kOutput, calls=%fused_computation.62 | convolution fusion | flops 5905580032 | bytes 15728640 | tf_op jit(solution)/shard_map/dot_general | solution.py:828
  269.7 2.6 collective-permute-done.4.refs_3_
  273.3 20.4 %feed_forward.1 = (bf16[1024,1408]{1,0:T(8,128)(2,1)}, bf16[2,1024,1408]{2,1,0:T(8,128)(2,1)}, bf16[1024,2048]{1,0:T(8,128)(2,1)}) custom-call(bf16[256,2048]{1,0:T(8,128)(2,1)} %get-tuple-element.129.refs_0_, bf16[256,2048]{1,0:T(8,128)(2,1)} %copy-done.22, bf16[256,2048]{1,0:T(8,128)(2,1)} %copy-done.23, bf16[256,2048]{1,0:T(8,128)(2,1)} %copy-done.25, ...), custom_call_target="tpu_custom_call" | custom-call | flops 11811160064 | bytes 30146560 | tf_op jit(solution)/shard_map/feed_forward/pallas_call | solution.py:306
  293.7 18.4 %project_rows.5 = (bf16[512,2048]{1,0:T(8,128)(2,1)}, bf16[512,2048]{1,0:T(8,128)(2,1)}) custom-call(bf16[2,1024,1408]{2,1,0:T(8,128)(2,1)} %get-tuple-element.139.refs_0_.refs_1_, bf16[2048,2816]{1,0:T(8,128)(2,1)} %get-tuple-element.137.refs_4_.refs_5_.refs_1_), custom_call_target="tpu_custom_call" | custom-call | flops 11811160064 | bytes 21495808 | tf_op jit(solution)/shard_map/project_rows/pallas_call | solution.py:380
  312.3 12.3 %grad_blocks.4 = (bf16[144,128,128]{2,1,0:T(8,128)(2,1)}, bf16[368,128,128]{2,1,0:T(8,128)(2,1)}, bf16[160,128,128]{2,1,0:T(8,128)(2,1)}) custom-call(bf16[1024,1408]{1,0:T(8,128)(2,1)} %get-tuple-element.157.refs_0_, bf16[1024,2048]{1,0:T(8,128)(2,1)} %pad_maximum_fusion.refs_1_), custom_call_target="tpu_custom_call" | custom-call | flops 11811160064 | bytes 12845056 | tf_op jit(solution)/shard_map/grad_blocks/pallas_call | solution.py:251
  326.0 4.3 add_near.5
  330.3 20.5 %grad_blocks.5 = (bf16[144,128,128]{2,1,0:T(8,128)(2,1)}, bf16[368,128,128]{2,1,0:T(8,128)(2,1)}, bf16[160,128,128]{2,1,0:T(8,128)(2,1)}) custom-call(bf16[1024,2048]{1,0:T(8,128)(2,1)} %get-tuple-element.150.refs_0_, bf16[2,1024,1408]{2,1,0:T(8,128)(2,1)} %get-tuple-element.139.refs_0_.refs_1_, ...), custom_call_target="tpu_custom_call", output_to_operand_aliasing={{0}: (2, {}), {1}: (3, {}), {2}: (4, {})} | custom-call | flops 23622320128 | bytes 21495808 | tf_op jit(solution)/shard_map/grad_blocks/pallas_call | solution.py:251
  352.0 1.5 collective-permute-start.6
  353.5 24.0 %collective-permute-done.6.b_ref = bf16[256,2048]{1,0:T(8,128)(2,1)S(1)} collective-permute-done((bf16[256,2048]{1,0:T(8,128)(2,1)S(1)}, bf16[256,2048]{1,0:T(8,128)(2,1)S(1)}, u32[]{:S(2)}, u32[]{:S(2)}) %collective-permute-start.6) | collective-permute-done | bytes 1048608 | tf_op jit(solution)/shard_map/ppermute | solution.py:876
  378.5 5.6 norm_back.2
  384.0 1.5 collective-permute-start.7
  385.5 10.3 %project_rows.6 = (bf16[512,2048]{1,0:T(8,128)(2,1)}, bf16[512,2048]{1,0:T(8,128)(2,1)}) custom-call(bf16[1024,1408]{1,0:T(8,128)(2,1)} %get-tuple-element.157.refs_0_, bf16[1408,2048]{1,0:T(8,128)(2,1)} %get-tuple-element.135.refs_1_), custom_call_target="tpu_custom_call" | custom-call | flops 5905580032 | bytes 12845056 | tf_op jit(solution)/shard_map/project_rows/pallas_call | solution.py:380
  395.9 13.1 %collective-permute-done.7.refs_3_.refs_1_ = bf16[256,2048]{1,0:T(8,128)(2,1)S(1)} collective-permute-done((bf16[256,2048]{1,0:T(8,128)(2,1)}, bf16[256,2048]{1,0:T(8,128)(2,1)S(1)}, u32[]{:S(2)}, u32[]{:S(2)}) %collective-permute-start.7) | collective-permute-done | bytes 1048608 | tf_op jit(solution)/shard_map/ppermute | solution.py:876
  409.0 2.6 collective-permute-done.9.refs_5_.refs_3_
  412.7 6.8 %grad_blocks.6 = (bf16[144,128,128]{2,1,0:T(8,128)(2,1)}, bf16[368,128,128]{2,1,0:T(8,128)(2,1)}) custom-call(s32[4]{0:T(128)} %broadcast_xor_fusion.refs_0_.order_ref, bf16[1024,512]{1,0:T(8,128)(2,1)} %get-tuple-element.115.refs_1_, bf16[256,2048]{1,0:T(8,128)(2,1)} %get-tuple-element.156.refs_2_.refs_0_, ...), custom_call_target="tpu_custom_call", output_to_operand_aliasing={{0}: (6, {}), {1}: (7, {})} | custom-call | flops 4294967296 | bytes 7340032 | tf_op jit(solution)/shard_map/grad_blocks/pallas_call | solution.py:251
  419.8 6.2 %to_heads.1.g_ref = bf16[1024,512]{1,0:T(8,128)(2,1)} custom-call(s32[4]{0:T(128)} %broadcast_xor_fusion.refs_0_.order_ref, bf16[256,2048]{1,0:T(8,128)(2,1)} %get-tuple-element.156.refs_2_.refs_0_, bf16[256,2048]{1,0:T(8,128)(2,1)} %copy-done.9, bf16[256,2048]{1,0:T(8,128)(2,1)} %copy-done.10, bf16[256,2048]{1,0:T(8,128)(2,1)} %copy-done.11, ...), custom_call_target="tpu_custom_call" | custom-call | flops 2147483648 | bytes 6291456 | tf_op jit(solution)/shard_map/to_heads/pallas_call | solution.py:409
  427.3 4.7 add_near.6
  432.0 1.5 collective-permute-start.11
  433.6 7.8 %attend_back.4 = (bf16[1024,128]{1,0:T(8,128)(2,1)}, f32[1024,128]{1,0:T(8,128)}) custom-call(s32[1,1024]{1,0:T(1,128)} %reduce_window_max.29.start_ref, bf16[1024,512]{1,0:T(8,128)(2,1)} %get-tuple-element.113.q_ref, bf16[1024,128]{1,0:T(8,128)(2,1)} %get-tuple-element.114.kv_ref, f32[4,2,1024]{2,1,0:T(2,128)} %get-tuple-element.166.log_ref, ...), custom_call_target="tpu_custom_call" | custom-call | flops 10737418240 | bytes 2097152 | tf_op jit(solution)/shard_map/attend_back/pallas_call | solution.py:578
  441.3 8.1 %attend_back.5 = (bf16[1024,128]{1,0:T(8,128)(2,1)}, f32[1024,128]{1,0:T(8,128)}) custom-call(s32[1,1024]{1,0:T(1,128)} %reduce_window_max.29.start_ref, bf16[1024,512]{1,0:T(8,128)(2,1)} %get-tuple-element.113.q_ref, bf16[1024,128]{1,0:T(8,128)(2,1)} %get-tuple-element.114.kv_ref, f32[4,2,1024]{2,1,0:T(2,128)} %get-tuple-element.166.log_ref, ...), custom_call_target="tpu_custom_call" | custom-call | flops 10737418240 | bytes 2097152 | tf_op jit(solution)/shard_map/attend_back/pallas_call | solution.py:578
  449.5 8.4 %collective-permute-done.11 = bf16[256,2048]{1,0:T(8,128)(2,1)} collective-permute-done((bf16[256,2048]{1,0:T(8,128)(2,1)}, bf16[256,2048]{1,0:T(8,128)(2,1)}, u32[]{:S(2)}, u32[]{:S(2)}) %collective-permute-start.11) | collective-permute-done | bytes 1048608 | tf_op jit(solution)/shard_map/ppermute | solution.py:876
  457.8 2.5 add_convert_fusion
  460.3 8.1 %attend_back.6 = (bf16[1024,128]{1,0:T(8,128)(2,1)}, f32[1024,128]{1,0:T(8,128)}) custom-call(s32[1,1024]{1,0:T(1,128)} %reduce_window_max.29.start_ref, bf16[1024,512]{1,0:T(8,128)(2,1)} %get-tuple-element.113.q_ref, bf16[1024,128]{1,0:T(8,128)(2,1)} %get-tuple-element.114.kv_ref, f32[4,2,1024]{2,1,0:T(2,128)} %get-tuple-element.166.log_ref, ...), custom_call_target="tpu_custom_call" | custom-call | flops 10737418240 | bytes 2097152 | tf_op jit(solution)/shard_map/attend_back/pallas_call | solution.py:578
  468.4 7.8 %attend_back.7 = (bf16[1024,128]{1,0:T(8,128)(2,1)}, bf16[1024,128]{1,0:T(8,128)(2,1)}) custom-call(s32[1,1024]{1,0:T(1,128)} %reduce_window_max.29.start_ref, bf16[1024,512]{1,0:T(8,128)(2,1)} %get-tuple-element.113.q_ref, bf16[1024,128]{1,0:T(8,128)(2,1)} %get-tuple-element.114.kv_ref, f32[4,2,1024]{2,1,0:T(2,128)} %get-tuple-element.166.log_ref, ...), custom_call_target="tpu_custom_call" | custom-call | flops 10737418240 | bytes 2097152 | tf_op jit(solution)/shard_map/attend_back/pallas_call | solution.py:578
  476.1 7.8 %grad_blocks.7 = bf16[144,128,128]{2,1,0:T(8,128)(2,1)} custom-call(bf16[1024,2048]{1,0:T(8,128)(2,1)} %fusion.2.x_ref.refs_0_, bf16[1024,128]{1,0:T(8,128)(2,1)} %get-tuple-element.179.refs_1_, bf16[1024,128]{1,0:T(8,128)(2,1)} %get-tuple-element.170.refs_2_, bf16[1024,128]{1,0:T(8,128)(2,1)} %get-tuple-element.175.refs_3_, ...), custom_call_target="tpu_custom_call", output_to_operand_aliasing={{}: (6, {})} | custom-call | flops 5368709120 | bytes 8126464 | tf_op jit(solution)/shard_map/grad_blocks/pallas_call | solution.py:251
  484.2 7.0 %project_rows.7 = (bf16[512,2048]{1,0:T(8,128)(2,1)}, bf16[512,2048]{1,0:T(8,128)(2,1)}) custom-call(s32[4]{0:T(128)} %broadcast_xor_fusion.refs_0_.order_ref, bf16[1024,128]{1,0:T(8,128)(2,1)} %get-tuple-element.179.refs_1_, bf16[1024,128]{1,0:T(8,128)(2,1)} %get-tuple-element.170.refs_2_, bf16[1024,128]{1,0:T(8,128)(2,1)} %get-tuple-element.175.refs_3_, ...), custom_call_target="tpu_custom_call" | custom-call | flops 2684354560 | bytes 8126464 | tf_op jit(solution)/shard_map/project_rows/pallas_call | solution.py:380
  491.2 4.4 collective-permute-done.15.b_ref.d_ref
  496.9 4.4 add_near.7
  503.9 8.4 %shampoo.3 = (f32[84,128,128]{2,1,0:T(8,128)}, f32[84,128,128]{2,1,0:T(8,128)}, f32[84,128,128]{2,1,0:T(8,128)}, f32[84,128,128]{2,1,0:T(8,128)}, f32[84,128,128]{2,1,0:T(8,128)}) custom-call(s32[20]{0:T(128)} %slice_bitcast_fusion.2.places_ref, bf16[20,128,128]{2,1,0:T(8,128)(2,1)} %reduce-scatter.4.cloned.1.call-done.g_ref, f32[84,128,128]{2,1,0:T(8,128)} %refs_0_.9, ...), custom_call_target="tpu_custom_call" | custom-call | flops 335544320 | bytes 15073280 | tf_op jit(solution)/shard_map/shampoo/pallas_call | solution.py:674
  512.3 15.2 %collective-permute-done.16.b_ref = bf16[256,2048]{1,0:T(8,128)(2,1)S(1)} collective-permute-done((bf16[256,2048]{1,0:T(8,128)(2,1)}, bf16[256,2048]{1,0:T(8,128)(2,1)S(1)}, u32[]{:S(2)}, u32[]{:S(2)}) %collective-permute-start.16) | collective-permute-done | bytes 1048608 | tf_op jit(solution)/shard_map/ppermute | solution.py:876
  528.5 5.5 norm_back.3
  534.7 1.5 collective-permute-start.17
  536.8 12.8 %collective-permute-done.17 = f32[2,2048]{1,0:T(2,128)S(1)} collective-permute-done((f32[2,2048]{1,0:T(2,128)S(1)}, f32[2,2048]{1,0:T(2,128)S(1)}, u32[]{:S(2)}, u32[]{:S(2)}) %collective-permute-start.17) | collective-permute-done | bytes 16416 | tf_op jit(solution)/shard_map/ppermute | solution.py:876
  550.3 15.9 %shampoo.4 = (f32[84,128,128]{2,1,0:T(8,128)}, f32[84,128,128]{2,1,0:T(8,128)}, f32[84,128,128]{2,1,0:T(8,128)}, f32[84,128,128]{2,1,0:T(8,128)}, f32[84,128,128]{2,1,0:T(8,128)}) custom-call(s32[46]{0:T(128)} %slice_bitcast_fusion.1.places_ref, ...), custom_call_target="tpu_custom_call", output_to_operand_aliasing={{0}: (8, {}), {1}: (9, {}), {2}: (10, {}), {3}: (11, {}), {... | custom-call | flops 771751936 | bytes 34668544 | tf_op jit(solution)/shard_map/shampoo/pallas_call | solution.py:674
  566.2 1.6 collective-permute-start.19
  568.4 2.2 collective-permute-done.21
  570.6 1.6 collective-permute-start.22
  572.7 2.2 collective-permute-done.22
  576.0 14.6 %collective-permute-done.19 = bf16[256,2048]{1,0:T(8,128)(2,1)} collective-permute-done((bf16[256,2048]{1,0:T(8,128)(2,1)S(1)}, bf16[256,2048]{1,0:T(8,128)(2,1)}, u32[]{:S(2)}, u32[]{:S(2)}) %collective-permute-start.19) | collective-permute-done | bytes 1048608 | tf_op jit(solution)/shard_map/ppermute | solution.py:876
  590.6 1.9 broadcast_select_fusion.11
  592.5 2.5 collective-permute-start.24
  595.0 2.3 maximum_bitcast_fusion
  598.9 1.6 select_bitcast_fusion.3
  600.5 3.9 maximum_convert_fusion
  604.4 7.9 %shampoo.5 = (f32[84,128,128]{2,1,0:T(8,128)}, f32[84,128,128]{2,1,0:T(8,128)}, f32[84,128,128]{2,1,0:T(8,128)}, f32[84,128,128]{2,1,0:T(8,128)}, f32[84,128,128]{2,1,0:T(8,128)}) custom-call(s32[18]{0:T(128)} %slice_bitcast_fusion.places_ref, ...), custom_call_target="tpu_custom_call", output_to_operand_aliasing={{0}: (8, {}), {1}: (9, {}), {2}: (10, {}), {3}: (11, {}), {... | custom-call | flops 301989888 | bytes 13565952 | tf_op jit(solution)/shard_map/shampoo/pallas_call | solution.py:674
  (128 shorter events, 32.0 us)
Async XLA Ops:
  7.2 7.7 %copy-start.19 = (s32[1,1024]{1,0:T(1,128)S(1)}, s32[1,1024]{1,0:T(1,128)}, u32[]{:S(2)}) copy-start(s32[1,1024]{1,0:T(1,128)} %param.25) | copy-start | bytes 12292
  7.2 9.4 %copy-start.20 = (s32[1,1024]{1,0:T(1,128)S(1)}, s32[1,1024]{1,0:T(1,128)}, u32[]{:S(2)}) copy-start(s32[1,1024]{1,0:T(1,128)} %param.24) | copy-start | bytes 12292
  7.2 61.9 %all-gather.4.cloned.1.call-start = ((), (), s32[]{:S(2)}) async-start(), calls=%async_computation.3 | async-start | bytes 5308416 | tf_op jit(solution)/shard_map/all_gather | solution.py:913
  8.5 12.0 %copy-start.26 = (s32[4]{0:T(128)S(1)}, s32[4]{0:T(128)}, u32[]{:S(2)}) copy-start(s32[4]{0:T(128)} %constant.77.clone) | copy-start | bytes 52
  13.4 179.4 %all-gather.6.cloned.1.call-start = ((), (), s32[]{:S(2)}) async-start(), calls=%async_computation.4 | async-start | bytes 13565952 | tf_op jit(solution)/shard_map/all_gather | solution.py:913
  14.1 238.0 %all-gather.8.cloned.1.call-start = ((), (), s32[]{:S(2)}) async-start(), calls=%async_computation.5 | async-start | bytes 5898240 | tf_op jit(solution)/shard_map/all_gather | solution.py:913
  14.9 489.0 %reduce-scatter.4.cloned.1.call-start = ((), (), s32[]{:S(2)}) async-start(), calls=%async_computation.6 | async-start | bytes 5898240 | tf_op jit(solution)/shard_map/reduce_scatter | solution.py:992
  15.9 5.1 copy-start
  16.6 6.3 %copy-start.7 = (bf16[1,1024,2048]{2,1,0:T(8,128)(2,1)S(1)}, bf16[1,1024,2048]{2,1,0:T(8,128)(2,1)}, u32[]{:S(2)}) copy-start(bf16[1,1024,2048]{2,1,0:T(8,128)(2,1)} %param.23) | copy-start | bytes 12582916
  23.6 7.1 %copy-start.1 = (bf16[256,2048]{1,0:T(8,128)(2,1)}, bf16[256,2048]{1,0:T(8,128)(2,1)S(1)}, u32[]{:S(2)}) copy-start(bf16[256,2048]{1,0:T(8,128)(2,1)S(1)} %get-tuple-element.155.r_ref) | copy-start | bytes 3145732
  23.6 2.8 copy-start.18
  27.0 0.6 copy-start.15
  201.8 4.4 collective-permute-start
  206.2 1.3 copy-start.5
  211.8 25.4 %collective-permute-start.1 = (bf16[256,2048]{1,0:T(8,128)(2,1)}, bf16[256,2048]{1,0:T(8,128)(2,1)S(1)}, u32[]{:S(2)}, u32[]{:S(2)}) collective-permute-start(bf16[256,2048]{1,0:T(8,128)(2,1)} %get-tuple-element.121), channel_id=1, source_target_pairs={{0,2},{1,3},{2,0},{3,1},{4,6},{5,7},{6,4},{7,5},{8,10},{9,11},{10,... | collective-permute-start | bytes 3145736 | tf_op jit(solution)/shard_map/ppermute | solution.py:876
  237.3 1.0 copy-start.13
  242.8 26.8 %collective-permute-start.2 = (bf16[256,2048]{1,0:T(8,128)(2,1)}, bf16[256,2048]{1,0:T(8,128)(2,1)S(1)}, u32[]{:S(2)}, u32[]{:S(2)}) collective-permute-start(bf16[256,2048]{1,0:T(8,128)(2,1)} %get-tuple-element.129.refs_0_), channel_id=1, source_target_pairs={{0,2},{1,3},{2,0},{3,1},{4,6},{5,7},{6,4},{7,5},{8,10},{9,11},{10,... | collective-permute-start | bytes 3145736 | tf_op jit(solution)/shard_map/ppermute | solution.py:876
  244.3 25.4 %collective-permute-start.3 = (bf16[256,2048]{1,0:T(8,128)(2,1)}, bf16[256,2048]{1,0:T(8,128)(2,1)S(1)}, u32[]{:S(2)}, u32[]{:S(2)}) collective-permute-start(bf16[256,2048]{1,0:T(8,128)(2,1)} %get-tuple-element.129.refs_0_), channel_id=1, source_target_pairs={{0,1},{1,0},{2,3},{3,2},{4,5},{5,4},{6,7},{7,6},{8,9},{9,8},{10,11... | collective-permute-start | bytes 3145736 | tf_op jit(solution)/shard_map/ppermute | solution.py:876
  269.6 2.7 copy-start.22
  269.6 2.7 collective-permute-start.4
  269.7 2.6 copy-start.23
  272.3 1.0 copy-start.25
  312.2 12.5 %collective-permute-start.5 = (bf16[512,2048]{1,0:T(8,128)(2,1)}, bf16[512,2048]{1,0:T(8,128)(2,1)S(1)}, u32[]{:S(2)}, u32[]{:S(2)}) collective-permute-start(bf16[512,2048]{1,0:T(8,128)(2,1)} %get-tuple-element.141), channel_id=1, source_target_pairs={{0,1},{1,0},{2,3},{3,2},{4,5},{5,4},{6,7},{7,6},{8,9},{9,8},{10,11... | collective-permute-start | bytes 6291464 | tf_op jit(solution)/shard_map/ppermute | solution.py:876
  324.7 1.3 copy-start.3
  350.8 1.2 copy-start.24
  350.8 199.4 %reduce-scatter.6.cloned.1.call-start = ((), (), s32[]{:S(2)}) async-start(), calls=%async_computation.7 | async-start | bytes 13565952 | tf_op jit(solution)/shard_map/reduce_scatter | solution.py:992
  352.0 25.5 %collective-permute-start.6 = (bf16[256,2048]{1,0:T(8,128)(2,1)S(1)}, bf16[256,2048]{1,0:T(8,128)(2,1)S(1)}, u32[]{:S(2)}, u32[]{:S(2)}) collective-permute-start(bf16[256,2048]{1,0:T(8,128)(2,1)S(1)} %copy-done.24), channel_id=1, source_target_pairs={{0,2},{1,3},{2,0},{3,1},{4,6},{5,7},{6,4},{7,5},{8,10},{9,11},{10,... | collective-permute-start | bytes 3145736 | tf_op jit(solution)/shard_map/ppermute | solution.py:876
  377.5 1.0 copy-start.14
  384.0 25.0 %collective-permute-start.7 = (bf16[256,2048]{1,0:T(8,128)(2,1)}, bf16[256,2048]{1,0:T(8,128)(2,1)S(1)}, u32[]{:S(2)}, u32[]{:S(2)}) collective-permute-start(bf16[256,2048]{1,0:T(8,128)(2,1)} %get-tuple-element.156.refs_2_.refs_0_), channel_id=1, source_target_pairs={{0,2},{1,3},{2,0},{3,1},{4,6},{5,7},{6,4},{7,5},{8,10},{9,11},{10,... | collective-permute-start | bytes 3145736 | tf_op jit(solution)/shard_map/ppermute | solution.py:876
  385.5 23.5 %collective-permute-start.8 = (bf16[256,2048]{1,0:T(8,128)(2,1)}, bf16[256,2048]{1,0:T(8,128)(2,1)S(1)}, u32[]{:S(2)}, u32[]{:S(2)}) collective-permute-start(bf16[256,2048]{1,0:T(8,128)(2,1)} %get-tuple-element.156.refs_2_.refs_0_), channel_id=1, source_target_pairs={{0,1},{1,0},{2,3},{3,2},{4,5},{5,4},{6,7},{7,6},{8,9},{9,8},{10,11... | collective-permute-start | bytes 3145736 | tf_op jit(solution)/shard_map/ppermute | solution.py:876
  409.0 2.7 copy-start.9
  409.0 2.7 collective-permute-start.9
  409.0 2.7 copy-start.10
  411.7 1.0 copy-start.11
  419.5 184.9 %reduce-scatter.8.cloned.1.call-start = ((), (), s32[]{:S(2)}) async-start(), calls=%async_computation.8 | async-start | bytes 5308416 | tf_op jit(solution)/shard_map/reduce_scatter | solution.py:992
  419.6 6.4 %collective-permute-start.10 = (bf16[512,2048]{1,0:T(8,128)(2,1)}, bf16[512,2048]{1,0:T(8,128)(2,1)S(1)}, u32[]{:S(2)}, u32[]{:S(2)}) collective-permute-start(bf16[512,2048]{1,0:T(8,128)(2,1)} %get-tuple-element.164), channel_id=1, source_target_pairs={{0,1},{1,0},{2,3},{3,2},{4,5},{5,4},{6,7},{7,6},{8,9},{9,8},{10,11... | collective-permute-start | bytes 6291464 | tf_op jit(solution)/shard_map/ppermute | solution.py:876
  426.0 1.3 copy-start.4
  432.0 25.8 %collective-permute-start.11 = (bf16[256,2048]{1,0:T(8,128)(2,1)}, bf16[256,2048]{1,0:T(8,128)(2,1)}, u32[]{:S(2)}, u32[]{:S(2)}) collective-permute-start(bf16[256,2048]{1,0:T(8,128)(2,1)} %get-tuple-element.167), channel_id=1, source_target_pairs={{0,2},{1,3},{2,0},{3,1},{4,6},{5,7},{6,4},{7,5},{8,10},{9,11},{10,... | collective-permute-start | bytes 3145736 | tf_op jit(solution)/shard_map/ppermute | solution.py:876
  441.3 16.5 %copy-start.2 = (f32[256,2048]{1,0:T(8,128)S(1)}, f32[256,2048]{1,0:T(8,128)}, u32[]{:S(2)}) copy-start(f32[256,2048]{1,0:T(8,128)} %get-tuple-element.128.x_ref) | copy-start | bytes 6291460
  491.2 12.1 %copy-start.21 = (s32[1,84]{1,0:T(1,128)S(1)}, s32[1,84]{1,0:T(1,128)}, u32[]{:S(2)}) copy-start(s32[1,84]{1,0:T(1,128)} %get-tuple-element.228) | copy-start | bytes 1012
  491.2 4.4 collective-permute-start.15
  495.6 1.3 copy-start.6
  501.3 26.2 %collective-permute-start.16 = (bf16[256,2048]{1,0:T(8,128)(2,1)}, bf16[256,2048]{1,0:T(8,128)(2,1)S(1)}, u32[]{:S(2)}, u32[]{:S(2)}) collective-permute-start(bf16[256,2048]{1,0:T(8,128)(2,1)} %get-tuple-element.183), channel_id=1, source_target_pairs={{0,2},{1,3},{2,0},{3,1},{4,6},{5,7},{6,4},{7,5},{8,10},{9,11},{10,... | collective-permute-start | bytes 3145736 | tf_op jit(solution)/shard_map/ppermute | solution.py:876
  502.7 65.1 %collective-permute-start.13 = (bf16[256,2048]{1,0:T(8,128)(2,1)S(1)}, bf16[256,2048]{1,0:T(8,128)(2,1)S(1)}, u32[]{:S(2)}, u32[]{:S(2)}) collective-permute-start(bf16[256,2048]{1,0:T(8,128)(2,1)S(1)} %add_convert_fusion), channel_id=1, source_target_pairs={{0,2},{1,3},{2,0},{3,1},{4,6},{5,7},{6,4},{7,5},{8,10},{9,11},{10,... | collective-permute-start | bytes 3145736 | tf_op jit(solution)/shard_map/ppermute | solution.py:876
  512.3 21.6 %copy-start.16 = (f32[1,2048]{1,0:T(1,128)S(1)}, f32[1,2048]{1,0:T(1,128)}, u32[]{:S(2)}) copy-start(f32[1,2048]{1,0:T(1,128)} %get-tuple-element.194) | copy-start | bytes 24580
  527.5 1.0 copy-start.12
  534.7 14.8 %collective-permute-start.17 = (f32[2,2048]{1,0:T(2,128)S(1)}, f32[2,2048]{1,0:T(2,128)S(1)}, u32[]{:S(2)}, u32[]{:S(2)}) collective-permute-start(f32[2,2048]{1,0:T(2,128)S(1)} %pad_maximum_fusion.3), channel_id=1, source_target_pairs={{0,2},{1,3},{2,0},{3,1},{4,6},{5,7},{6,4},{7,5},{8,10},{9,11},{10,... | collective-permute-start | bytes 49160 | tf_op jit(solution)/shard_map/ppermute | solution.py:876
  550.2 16.0 %copy-start.8 = (bf16[256,2048]{1,0:T(8,128)(2,1)S(1)}, bf16[256,2048]{1,0:T(8,128)(2,1)}, u32[]{:S(2)}) copy-start(bf16[256,2048]{1,0:T(8,128)(2,1)} %get-tuple-element.202) | copy-start | bytes 3145732
  550.2 20.3 %copy-start.17 = (f32[1,2048]{1,0:T(1,128)S(1)}, f32[1,2048]{1,0:T(1,128)}, u32[]{:S(2)}) copy-start(f32[1,2048]{1,0:T(1,128)} %get-tuple-element.193) | copy-start | bytes 24580
  566.2 24.4 %collective-permute-start.19 = (bf16[256,2048]{1,0:T(8,128)(2,1)S(1)}, bf16[256,2048]{1,0:T(8,128)(2,1)}, u32[]{:S(2)}, u32[]{:S(2)}) collective-permute-start(bf16[256,2048]{1,0:T(8,128)(2,1)S(1)} %copy-done.8), channel_id=1, source_target_pairs={{0,2},{1,3},{2,0},{3,1},{4,6},{5,7},{6,4},{7,5},{8,10},{9,11},{10,... | collective-permute-start | bytes 3145736 | tf_op jit(solution)/shard_map/ppermute | solution.py:876
  567.8 22.8 %collective-permute-start.12 = (bf16[256,2048]{1,0:T(8,128)(2,1)S(1)}, bf16[256,2048]{1,0:T(8,128)(2,1)}, u32[]{:S(2)}, u32[]{:S(2)}) collective-permute-start(bf16[256,2048]{1,0:T(8,128)(2,1)S(1)} %add_convert_fusion), channel_id=1, source_target_pairs={{0,1},{1,0},{2,3},{3,2},{4,5},{5,4},{6,7},{7,6},{8,9},{9,8},{10,11... | collective-permute-start | bytes 3145736 | tf_op jit(solution)/shard_map/ppermute | solution.py:876
  567.8 22.8 %collective-permute-start.14 = (bf16[256,2048]{1,0:T(8,128)(2,1)S(1)}, bf16[256,2048]{1,0:T(8,128)(2,1)}, u32[]{:S(2)}, u32[]{:S(2)}) collective-permute-start(bf16[256,2048]{1,0:T(8,128)(2,1)S(1)} %collective-permute-done.13), channel_id=1, source_target_pairs={{0,1},{1,0},{2,3},{3,2},{4,5},{5,4},{6,7},{7,6},{8,9},{9,8},{10,11... | collective-permute-start | bytes 3145736 | tf_op jit(solution)/shard_map/ppermute | solution.py:876
  568.4 2.2 collective-permute-start.21
  570.6 4.3 collective-permute-start.22
  574.9 17.6 %collective-permute-start.23 = (f32[2,2048]{1,0:T(2,128)S(1)}, f32[2,2048]{1,0:T(2,128)S(1)}, u32[]{:S(2)}, u32[]{:S(2)}) collective-permute-start(f32[2,2048]{1,0:T(2,128)S(1)} %add.78), channel_id=1, source_target_pairs={{0,8},{4,12},{8,0},{12,4},{16,24},{20,28},{24,16},{28,20},{1,9},{5... | collective-permute-start | bytes 49160 | tf_op jit(solution)/shard_map/ppermute | solution.py:1094
  576.0 23.0 %collective-permute-start.18 = (bf16[256,2048]{1,0:T(8,128)(2,1)S(1)}, bf16[256,2048]{1,0:T(8,128)(2,1)S(1)}, u32[]{:S(2)}, u32[]{:S(2)}) collective-permute-start(bf16[256,2048]{1,0:T(8,128)(2,1)S(1)} %copy-done.8), channel_id=1, source_target_pairs={{0,1},{1,0},{2,3},{3,2},{4,5},{5,4},{6,7},{7,6},{8,9},{9,8},{10,11... | collective-permute-start | bytes 3145736 | tf_op jit(solution)/shard_map/ppermute | solution.py:876
  590.6 8.4 %collective-permute-start.20 = (bf16[256,2048]{1,0:T(8,128)(2,1)}, bf16[256,2048]{1,0:T(8,128)(2,1)S(1)}, u32[]{:S(2)}, u32[]{:S(2)}) collective-permute-start(bf16[256,2048]{1,0:T(8,128)(2,1)} %collective-permute-done.19), channel_id=1, source_target_pairs={{0,1},{1,0},{2,3},{3,2},{4,5},{5,4},{6,7},{7,6},{8,9},{9,8},{10,11... | collective-permute-start | bytes 3145736 | tf_op jit(solution)/shard_map/ppermute | solution.py:876
  592.5 5.1 collective-permute-start.24
Sparse Core Ops, SparseCore 0:
  13.5 55.5 all-gather.3
  71.2 121.6 all-gather.5
  194.4 57.7 all-gather.7
  351.0 58.4 reduce-scatter.3
  419.6 122.9 reduce-scatter.5
  544.8 54.0 reduce-scatter.7

commit v4 on v3

--- a/solution.py
+++ b/solution.py
@@ -30,24 +30,26 @@
         self.dp, self.own = dp, own
         self.ring = ring_order(dp)
         n_in = rows * in_cols
-        kinds, spots = [], []
+        units = (in_cols - attn_cols) // 2
+        kinds, spots, keys = [], [], []
         for k in range(dp * own):
             if k < n_in:
                 r, c = divmod(k, in_cols)
                 if c < attn_cols:
-                    kinds.append(0), spots.append((0, r, c))
+                    kinds.append(0), spots.append((0, r, c)), keys.append((0, k))
                 else:
-                    kinds.append(2), spots.append((2, r, c - attn_cols))
+                    c -= attn_cols
+                    kinds.append(2), spots.append((2, r, c)), keys.append((2, c % units / units, k))
             else:
                 r, c = divmod(k - n_in, rows)
                 if r < out_attn_rows:
-                    kinds.append(1), spots.append((1, r, c))
+                    kinds.append(1), spots.append((1, r, c)), keys.append((1, k))
                 else:
                     kinds.append(2), spots.append((3, r - out_attn_rows, c))
+                    keys.append((2, c / rows, k))
         self.order = np.zeros((dp, own), np.int32)
         for d in range(dp):
-            mine = kinds[d * own : (d + 1) * own]
-            self.order[d] = sorted(range(own), key=lambda l: (mine[l], l))
+            self.order[d] = sorted(range(own), key=lambda l: keys[d * own + l])
         count = np.array(kinds).reshape(dp, own)
         first = int((count == 0).sum(1).max())
         second = int((count <= 1).sum(1).max())
@@ -59,6 +61,18 @@
                 (x,) = [i for i, (a, n) in enumerate(self.chunks) if a <= j < a + n]
                 a, n = self.chunks[x]
                 self.table.append(spots[d * own + int(l)] + (x, p * n + j - a))
+        mixed = [p for p, d in enumerate(self.ring) if (count[d] == 1).any()]
+        last, size = len(self.chunks) - 1, self.chunks[-1][1]
+        late = [t for t in self.table if t[3] == last]
+        self.first_late = {}
+        for m, cols in ((2, units), (3, rows)):
+            own_late = [c % cols for i, r, c, x, s in late if i == m and s // size not in mixed]
+            self.first_late[m] = min(own_late, default=cols)
+        self.strips = sorted(
+            (m, r, c, s)
+            for m, r, c, x, s in late
+            if m >= 2 and s // size in mixed and c % (units if m == 2 else rows) < self.first_late[m]
+        )
 
     def of_chunk(self, x, matrix):
         rows = [(s, r, c) for m, r, c, y, s in self.table if y == x and m == matrix]
@@ -173,19 +187,30 @@
             scratch[pl.ds(pl.multiple_of(order_ref[i] * count, count), count)] = piece[...]
 
 
-def grad_blocks(left, rights, order, pairs, table, wide, buffers, sizes, block):
+def grad_blocks(
+    left, rights, order, pairs, table, wide, buffers, sizes, block, span=None, done=()
+):
     tokens, height = left.shape
     by_column = len(rights) > 1 and rights[0].shape[0] == tokens
-    width = rights[0].shape[-1] * (2 if pairs else len(rights) if by_column else 1)
+    width = sum(x.shape[-1] for x in rights) if by_column else rights[0].shape[-1]
+    if pairs:
+        width *= 2
     rows, cols = height // block, width // block
     if pairs:
         table = np.stack([table[: cols // 2], table[cols // 2 :]], 1).reshape(table.shape)
         wide = 2
-    steps = cols // wide
-    assert not by_column or steps == 1
+    first, end = (0, cols // wide) if span is None else span
+    steps = end - first
+    if steps <= 0:
+        return buffers
+    assert not by_column or wide == 1
     per_step = rows * wide
-    targets = table.reshape(steps, per_step, 2).tolist()
-    used = sorted(set(table[:, :, 0].reshape(-1).tolist()))
+    targets = [
+        [(j, x, spot) for j, (x, spot) in enumerate(step) if (x, spot) not in done]
+        for step in table.reshape(cols // wide, per_step, 2).tolist()[first:end]
+    ]
+    assert all(targets)
+    used = sorted({x for step in targets for _, x, _ in step})
     known = [x for x in used if buffers[x] is not None]
     n_order = 0 if order is None else 1
     joined = len(rights) > 1
@@ -202,8 +227,15 @@
         if joined:
             right_ref = refs[-1]
             if by_column:
-                for i, piece in enumerate(right_refs):
-                    right_ref[:, i * block : (i + 1) * block] = piece[...]
+                step = 0
+                for piece in right_refs:
+                    for at in range(0, piece.shape[1], block):
+
+                        @pl.when(t + first == step)
+                        def _(piece=piece, at=at):
+                            right_ref[...] = piece[:, at : at + block]
+
+                        step += 1
             else:
                 fill(right_ref, right_refs, refs[0] if n_order else None)
             taken = right_ref[...]
@@ -212,26 +244,38 @@
         else:
             taken = right_refs[0][...]
 
-        def finish(slot):
-            pltpu.make_async_copy(stage.at[slot], stage.at[slot], sems.at[slot]).wait()
-
-        @pl.when(t >= 2)
-        def _():
-            finish(slot)
-
-        part = lax.dot_general(
-            left_ref[...], taken, (((0,), (0,)), ((), ())), preferred_element_type=F32
-        ).astype(LOW)
-        for r in range(rows):
-            for c in range(wide):
-                stage[slot, c * rows + r] = part[
-                    r * block : (r + 1) * block, c * block : (c + 1) * block
-                ]
-        for step in range(steps):
+        def finish(step):
+            sent = stage.at[step % 2, : len(targets[step])]
+            pltpu.make_async_copy(sent, sent, sems.at[step % 2]).wait()
+
+        for step in range(2, steps):
 
             @pl.when(t == step)
             def _(step=step):
-                for j, (x, spot) in enumerate(targets[step]):
+                finish(step - 2)
+
+        def some(i, carry):
+            at = pl.multiple_of(i * (few * block), block)
+            part = lax.dot_general(
+                left_ref[:, pl.ds(at, few * block)],
+                taken,
+                (((0,), (0,)), ((), ())),
+                preferred_element_type=F32,
+            ).astype(LOW)
+            for r in range(few):
+                for c in range(wide):
+                    stage[slot, c * rows + i * few + r] = part[
+                        r * block : (r + 1) * block, c * block : (c + 1) * block
+                    ]
+            return carry
+
+        few = rows // 2 if rows % 2 == 0 else rows
+        lax.fori_loop(0, rows // few, some, 0)
+        for step in range(steps):
+
+            @pl.when(t == step)
+            def _(step=step):
+                for j, x, spot in targets[step]:
                     pltpu.make_async_copy(
                         stage.at[step % 2, j], outs[used.index(x)].at[spot], sems.at[step % 2]
                     ).start()
@@ -239,15 +283,17 @@
         @pl.when(t == steps - 1)
         def _():
             for step in range(max(0, steps - 2), steps):
-                finish(step % 2)
-
-    span = wide * block
+                finish(step)
+
+    taken_width = wide * block
     if pairs:
-        right_specs = [pl.BlockSpec((2, tokens, block), lambda j: (0, 0, j))]
+        right_specs = [pl.BlockSpec((2, tokens, block), lambda j: (0, 0, first + j))]
     elif by_column:
-        right_specs = [pl.BlockSpec((tokens, block), lambda j: (0, 0))] * len(rights)
+        right_specs = [pl.BlockSpec(x.shape, lambda j: (0, 0)) for x in rights]
     else:
-        right_specs = [pl.BlockSpec((x.shape[0], span), lambda j: (0, j)) for x in rights]
+        right_specs = [
+            pl.BlockSpec((x.shape[0], taken_width), lambda j: (0, first + j)) for x in rights
+        ]
     results = pl.pallas_call(
         body,
         grid=(steps,),
@@ -262,10 +308,10 @@
             pltpu.VMEM((2, per_step, block, block), LOW),
             pltpu.SemaphoreType.DMA((2,)),
         ]
-        + ([pltpu.VMEM((tokens, span), LOW)] if joined else []),
+        + ([pltpu.VMEM((tokens, taken_width), LOW)] if joined else []),
         compiler_params=pltpu.CompilerParams(vmem_limit_bytes=VMEM_LIMIT),
         cost_estimate=pl.CostEstimate(
-            flops=4 * tokens * height * width,
+            flops=4 * tokens * height * wide * block * steps,
             bytes_accessed=2 * (tokens * (height + width) + height * width),
             transcendentals=0,
         ),
@@ -275,6 +321,52 @@
     for x, value in zip(used, results):
         merged[x] = value
     return merged
+
+
+def grad_strips(strips, buffer_size, block):
+    def body(*refs):
+        out, stage, sem = refs[-3:]
+        at = 0
+        for i, (_, _, _, half, blocks) in enumerate(strips):
+            right = refs[2 * i + 1]
+            part = lax.dot_general(
+                refs[2 * i][...],
+                right[...] if half is None else right[0],
+                (((0,), (0,)), ((), ())),
+                preferred_element_type=F32,
+            ).astype(LOW)
+            for c, spot in blocks:
+                stage[at] = part[:, c * block : (c + 1) * block]
+                pltpu.make_async_copy(stage.at[at], out.at[spot], sem).start()
+                at += 1
+        pltpu.make_async_copy(stage, stage, sem).wait()
+
+    specs, values = [], []
+    for left, row, right, half, blocks in strips:
+        tokens = left.shape[0]
+        wide = (max(c for c, _ in blocks) + 1) * block
+        specs.append(pl.BlockSpec((tokens, block), lambda j, row=row: (0, row)))
+        if half is None:
+            specs.append(pl.BlockSpec((tokens, wide), lambda j: (0, 0)))
+        else:
+            specs.append(pl.BlockSpec((1, tokens, wide), lambda j, half=half: (half, 0, 0)))
+        values += [left, right]
+    count = sum(len(blocks) for *_, blocks in strips)
+    return pl.pallas_call(
+        body,
+        grid=(1,),
+        in_specs=specs,
+        out_specs=ANY,
+        out_shape=jax.ShapeDtypeStruct((buffer_size, block, block), LOW),
+        scratch_shapes=[pltpu.VMEM((count, block, block), LOW), pltpu.SemaphoreType.DMA],
+        compiler_params=pltpu.CompilerParams(vmem_limit_bytes=VMEM_LIMIT),
+        cost_estimate=pl.CostEstimate(
+            flops=4 * count * values[0].shape[0] * block**2,
+            bytes_accessed=4 * count * block * values[0].shape[0],
+            transcendentals=0,
+        ),
+        name="grad_strips",
+    )(*values)
 
 
 def feed_forward(pieces, weights, hidden_grad, block):
@@ -395,9 +487,50 @@
     return sent, kept
 
 
+def down_back(grads, weights):
+    rows, depth = grads.shape
+    hidden = weights.shape[0]
+    tile = 2 * LANES
+    full, rest = divmod(hidden, tile)
+
+    def body(g_ref, w_ref, o_ref):
+        t = pl.program_id(0)
+
+        @pl.when(t < full)
+        def _():
+            here = pl.ds(pl.multiple_of(t * tile, tile), tile)
+            o_ref[...] = dot_turned(g_ref[...], w_ref[here])
+
+        if rest:
+
+            @pl.when(t == full)
+            def _():
+                o_ref[:, :rest] = dot_turned(g_ref[...], w_ref[full * tile :])
+
+    return pl.pallas_call(
+        body,
+        grid=(full + (rest > 0),),
+        in_specs=[
+            pl.BlockSpec((rows, depth), lambda j: (0, 0)),
+            pl.BlockSpec((hidden, depth), lambda j: (0, 0)),
+        ],
+        out_specs=pl.BlockSpec((rows, tile), lambda j: (0, j)),
+        out_shape=jax.ShapeDtypeStruct((rows, hidden), F32),
+        compiler_params=pltpu.CompilerParams(vmem_limit_bytes=VMEM_LIMIT),
+        cost_estimate=pl.CostEstimate(
+            flops=2 * rows * depth * hidden,
+            bytes_accessed=2 * depth * (rows + hidden) + 4 * rows * hidden,
+            transcendentals=0,
+        ),
+        name="down_back",
+    )(grads, weights)
+
+
 def to_heads(pieces, weights, order):
     share = pieces[0].shape[0]
     width = weights.shape[0]
+
+    rows = share * len(pieces)
 
     def body(order_ref, *refs):
         w_ref, out_ref = refs[-2:]
@@ -405,7 +538,6 @@
             put = pl.ds(pl.multiple_of(order_ref[i] * share, share), share)
             out_ref[put] = dot_turned(piece[...], w_ref[...]).astype(LOW)
 
-    rows = share * len(pieces)
     return pl.pallas_call(
         body,
         in_specs=[SMEM] + [VMEM] * (len(pieces) + 1),
@@ -447,19 +579,29 @@
     assert width % LANES == 0 and HD == 64
 
     def body(x_ref, w_ref, cos_ref, sin_ref, q_ref, kv_ref):
-        for at in range(0, width, LANES):
-            raw = dot(x_ref[...], w_ref[:, at : at + LANES])
-            if at < width - LANES:
-                q_ref[:, at : at + LANES] = (
-                    turn(raw, cos_ref[...], sin_ref[...]).astype(LOW) * LOW(HD**-0.5)
-                )
-            else:
-                kv_ref[...] = turn(raw, *key_tables(cos_ref[...], sin_ref[...])).astype(LOW)
-
+        t = pl.program_id(0)
+        raw = dot(x_ref[...], w_ref[...])
+
+        @pl.when(t < steps - 1)
+        def _():
+            q_ref[...] = turn(raw, cos_ref[...], sin_ref[...]).astype(LOW) * LOW(HD**-0.5)
+
+        @pl.when(t == steps - 1)
+        def _():
+            kv_ref[...] = turn(raw, *key_tables(cos_ref[...], sin_ref[...])).astype(LOW)
+
+    steps = width // LANES
+    whole = pl.BlockSpec((rows, LANES), lambda j: (0, 0))
     return pl.pallas_call(
         body,
-        in_specs=[VMEM] * 4,
-        out_specs=[VMEM] * 2,
+        grid=(steps,),
+        in_specs=[
+            pl.BlockSpec((rows, depth), lambda j: (0, 0)),
+            pl.BlockSpec((depth, LANES), lambda j: (0, j)),
+            whole,
+            whole,
+        ],
+        out_specs=[pl.BlockSpec((rows, LANES), lambda j: (0, jnp.minimum(j, steps - 2))), whole],
         out_shape=[
             jax.ShapeDtypeStruct((rows, width - LANES), LOW),
             jax.ShapeDtypeStruct((rows, LANES), LOW),
@@ -474,39 +616,47 @@
     )(inputs, weights, cos, sin)
 
 
-def key_range(at):
-    low = max(0, (at - LONGEST + 1) // QUERIES * QUERIES)
-    return low, at + QUERIES
-
-
-def visible(start_ref, at, low, high):
-    shape = (high - low, QUERIES)
-    key = low + lax.broadcasted_iota(jnp.int32, shape, 0)
+def keep_keys(padded, kv_ref):
+    padded[:LONGEST] = jnp.zeros((LONGEST, LANES), LOW)
+    padded[LONGEST:] = kv_ref[...]
+
+
+def visible(start_ref, at):
+    shape = (LONGEST + QUERIES, QUERIES)
+    key = at - LONGEST + lax.broadcasted_iota(jnp.int32, shape, 0)
     query = at + lax.broadcasted_iota(jnp.int32, shape, 1)
-    return (key >= start_ref[:, at : at + QUERIES]) & (key <= query)
+    return (key >= start_ref[:, pl.ds(at, QUERIES)]) & (key <= query)
 
 
 def attend(queries, kv, starts):
     rows, width = queries.shape
     groups = width // LANES
 
-    def body(start_ref, q_ref, kv_ref, o_ref, log_ref):
-        for at in range(0, rows, QUERIES):
-            low, high = key_range(at)
-            seen = visible(start_ref, at, low, high)
-            keys = kv_ref[low:high, :HD]
-            values = kv_ref[low:high, HD:]
+    def body(start_ref, q_ref, kv_ref, o_ref, log_ref, padded):
+        @pl.when(pl.program_id(0) == 0)
+        def _():
+            keep_keys(padded, kv_ref)
+
+        def one(i, carry):
+            at = pl.multiple_of(i * QUERIES, QUERIES)
+            here = pl.ds(at, QUERIES)
+            seen = visible(start_ref, at)
+            window = padded[pl.ds(at, LONGEST + QUERIES)]
+            keys, values = window[:, :HD], window[:, HD:]
             for h in range(LANES // HD):
-                query = q_ref[at : at + QUERIES, h * HD : (h + 1) * HD]
+                query = q_ref[here, h * HD : (h + 1) * HD]
                 scores = jnp.where(seen, dot_turned(keys, query), -1e30)
                 top = jnp.max(scores, axis=0, keepdims=True)
                 expo = jnp.exp(scores - top)
                 total = jnp.sum(expo, axis=0, keepdims=True)
                 probs = (expo * (1.0 / total)).astype(LOW)
-                o_ref[at : at + QUERIES, h * HD : (h + 1) * HD] = lax.dot_general(
+                o_ref[here, h * HD : (h + 1) * HD] = lax.dot_general(
                     probs, values, (((0,), (0,)), ((), ())), preferred_element_type=F32
                 ).astype(LOW)
-                log_ref[0, h : h + 1, at : at + QUERIES] = top + jnp.log(total)
+                log_ref[0, h : h + 1, here] = top + jnp.log(total)
+            return carry
+
+        lax.fori_loop(0, rows // QUERIES, one, 0)
 
     column = pl.BlockSpec((rows, LANES), lambda j: (0, j))
     return pl.pallas_call(
@@ -522,6 +672,7 @@
             jax.ShapeDtypeStruct((rows, width), LOW),
             jax.ShapeDtypeStruct((groups, LANES // HD, rows), F32),
         ],
+        scratch_shapes=[pltpu.VMEM((LONGEST + rows, LANES), LOW)],
         compiler_params=pltpu.CompilerParams(vmem_limit_bytes=VMEM_LIMIT),
         cost_estimate=pl.CostEstimate(
             flops=30 * rows * rows * width,
@@ -532,26 +683,32 @@
     )(starts, queries, kv)
 
 
-def attend_back(group, queries, kv, starts, logs, grads, cos, sin, before, last):
-    rows, _ = queries.shape
-    first = before is None
-
-    def body(start_ref, q_ref, kv_ref, log_ref, g_ref, cos_ref, sin_ref, *rest):
-        before_ref = None if first else rest[0]
-        dq_ref, sum_ref, acc = rest[-3:]
-        acc[...] = jnp.zeros_like(acc) if first else before_ref[...]
-        for at in range(0, rows, QUERIES):
-            low, high = key_range(at)
-            seen = visible(start_ref, at, low, high)
-            keys = kv_ref[low:high, :HD]
-            values = kv_ref[low:high, HD:]
+def attend_back(queries, kv, starts, logs, grads, cos, sin):
+    rows, width = queries.shape
+    groups = width // LANES
+
+    def body(
+        start_ref, q_ref, kv_ref, log_ref, g_ref, cos_ref, sin_ref, dq_ref, sum_ref, acc, padded
+    ):
+        @pl.when(pl.program_id(0) == 0)
+        def _():
+            keep_keys(padded, kv_ref)
+            acc[...] = jnp.zeros_like(acc)
+
+        def one(i, carry):
+            at = pl.multiple_of(i * QUERIES, QUERIES)
+            here = pl.ds(at, QUERIES)
+            there = pl.ds(at, LONGEST + QUERIES)
+            seen = visible(start_ref, at)
+            window = padded[there]
+            keys, values = window[:, :HD], window[:, HD:]
             parts = []
             key_part, value_part = 0.0, 0.0
             for h in range(LANES // HD):
-                query = q_ref[at : at + QUERIES, h * HD : (h + 1) * HD]
-                grad = g_ref[at : at + QUERIES, h * HD : (h + 1) * HD]
+                query = q_ref[here, h * HD : (h + 1) * HD]
+                grad = g_ref[here, h * HD : (h + 1) * HD]
                 scores = jnp.where(seen, dot_turned(keys, query), -1e30)
-                probs = jnp.exp(scores - log_ref[0, h : h + 1, at : at + QUERIES])
+                probs = jnp.exp(scores - log_ref[0, h : h + 1, here])
                 value_part += dot(probs.astype(LOW), grad)
                 prob_grads = dot_turned(values, grad)
                 inner = jnp.sum(probs * prob_grads, axis=0, keepdims=True)
@@ -562,46 +719,50 @@
                         score_grads, keys, (((0,), (0,)), ((), ())), preferred_element_type=F32
                     )
                 )
-            acc[low:high] += jnp.concatenate([key_part, value_part], axis=1)
-            span = slice(at, at + QUERIES)
-            dq_ref[span] = turn(
-                jnp.concatenate(parts, axis=1) * HD**-0.5, cos_ref[span], -sin_ref[span]
+            acc[there] += jnp.concatenate([key_part, value_part], axis=1)
+            dq_ref[here] = turn(
+                jnp.concatenate(parts, axis=1) * HD**-0.5, cos_ref[here], -sin_ref[here]
             ).astype(LOW)
-        if last:
+            return carry
+
+        lax.fori_loop(0, rows // QUERIES, one, 0)
+
+        @pl.when(pl.program_id(0) == groups - 1)
+        def _():
             key_cos, key_sin = key_tables(cos_ref[...], sin_ref[...])
-            sum_ref[...] = turn(acc[...], key_cos, -key_sin).astype(LOW)
-        else:
-            sum_ref[...] = acc[...]
-
-    column = pl.BlockSpec((rows, LANES), lambda j: (0, group))
+            sum_ref[...] = turn(acc[LONGEST:], key_cos, -key_sin).astype(LOW)
+
+    column = pl.BlockSpec((rows, LANES), lambda j: (0, j))
     whole = pl.BlockSpec((rows, LANES), lambda j: (0, 0))
     return pl.pallas_call(
         body,
-        grid=(1,),
+        grid=(groups,),
         in_specs=[
             pl.BlockSpec((1, rows), lambda j: (0, 0)),
             column,
             whole,
-            pl.BlockSpec((1, LANES // HD, rows), lambda j: (group, 0, 0)),
+            pl.BlockSpec((1, LANES // HD, rows), lambda j: (j, 0, 0)),
             column,
             whole,
             whole,
-        ]
-        + ([] if first else [whole]),
-        out_specs=[whole] * 2,
+        ],
+        out_specs=[column, whole],
         out_shape=[
+            jax.ShapeDtypeStruct((rows, width), LOW),
             jax.ShapeDtypeStruct((rows, LANES), LOW),
-            jax.ShapeDtypeStruct((rows, LANES), LOW if last else F32),
-        ],
-        scratch_shapes=[pltpu.VMEM((rows, LANES), F32)],
+        ],
+        scratch_shapes=[
+            pltpu.VMEM((LONGEST + rows, LANES), F32),
+            pltpu.VMEM((LONGEST + rows, LANES), LOW),
+        ],
         compiler_params=pltpu.CompilerParams(vmem_limit_bytes=VMEM_LIMIT),
         cost_estimate=pl.CostEstimate(
-            flops=80 * rows * rows * LANES,
-            bytes_accessed=16 * rows * LANES,
-            transcendentals=rows * rows * LANES // HD,
+            flops=400 * rows * rows * width,
+            bytes_accessed=16 * rows * width,
+            transcendentals=rows * rows * width // HD,
         ),
         name="attend_back",
-    )(starts, queries, kv, logs, grads, cos, sin, *([] if first else [before]))
+    )(starts, queries, kv, logs, grads, cos, sin)
 
 
 def shampoo(sums, places, factor, weights, ema, left, right, left_roots, right_roots, before):
@@ -758,6 +919,20 @@
         [jax.ShapeDtypeStruct(tokens.shape, F32), jax.ShapeDtypeStruct(tokens.shape, LOW)],
         "second_norm",
     )
+
+
+def first_norm(tokens, gain):
+    def body(x_ref, gain_ref, low_ref):
+        x = x_ref[...].astype(F32)
+        scale = lax.rsqrt(jnp.mean(x * x, axis=-1, keepdims=True) + 1e-05)
+        low_ref[...] = (x * scale * gain_ref[...]).astype(LOW)
+
+    return rows_call(
+        body,
+        [tokens, gain],
+        [jax.ShapeDtypeStruct(tokens.shape, LOW)],
+        "first_norm",
+    )[0]
 
 
 def norm_back(values, mine, got, gain, residual):
@@ -931,18 +1106,20 @@
     cos, sin = rope_tables(positions[0], HD)
 
     tokens_low = tokens_in.reshape(rows, model_width)
-    tokens = tokens_low.astype(F32)
-    first_scale = lax.rsqrt(jnp.mean(tokens * tokens, axis=-1, keepdims=True) + 1e-05)
-    first_in = (tokens * first_scale * norm_gains[0]).astype(LOW)
+    first_in = first_norm(tokens_low, norm_gains[:1])
     out_grad = cotangent.reshape(rows, model_width) * select_mask.astype(LOW).reshape(rows, 1)
     own_tokens = true_share(tokens_low, 0)
     own_grad = true_share(out_grad, 0)
     mlp_grad = to_exchange(out_grad)
+    tokens_local = to_exchange(tokens_low)
+    unit_scale = lax.rsqrt(
+        jnp.mean(jnp.square(tokens_local.astype(F32)), axis=-1, keepdims=True) + 1e-05
+    )
 
     shares = (m_index ^ jnp.array(EXCHANGE, jnp.int32)).astype(jnp.int32)
     queries, kv = project_heads(first_in, w_qkv, cos, sin)
-    kv, mlp_grad, own_tokens, own_grad = lax.optimization_barrier(
-        (kv, mlp_grad, own_tokens, own_grad)
+    kv, mlp_grad, own_tokens, own_grad, tokens_local, unit_scale = lax.optimization_barrier(
+        (kv, mlp_grad, own_tokens, own_grad, tokens_local, unit_scale)
     )
     mixed, logs = attend(queries, kv, starts)
     attended_sent, attended_kept = project_rows([mixed], w_attn_out, shares, False, 512)
@@ -954,38 +1131,13 @@
     if last >= 2:
         matrices = place(2, after(gathered[2], second_low), (2, 3), matrices)
     w_gateup, w_down = matrices[2:]
-    hidden_grad = dot_turned(mlp_grad, w_down)
+    hidden_grad = down_back(mlp_grad, w_down)
     second_pieces = spread_share(second_low, hidden_grad)
     hidden, gateup_grad, second_in = feed_forward(second_pieces, w_gateup, hidden_grad, block)
 
     second_sent, second_kept = project_rows([gateup_grad], w_gateup, None, True, 256)
     sizes = [dp_count * n for _, n in plan.chunks]
     sums = [None] * len(sizes)
-    sums = grad_blocks(
-        after(hidden, second_sent),
-        [mlp_grad],
-        None,
-        False,
-        plan.of_matrix(3, hidden_blocks, row_blocks),
-        2,
-        sums,
-        sizes,
-        block,
-    )
-    mine, other = near_sum(second_sent, after(second_kept, *[x for x in sums if x is not None]))
-    second_in = after(second_in, other)
-    got = partner(other, 2)
-    sums = grad_blocks(
-        second_in,
-        [gateup_grad],
-        None,
-        True,
-        plan.of_matrix(2, row_blocks, 2 * hidden_blocks),
-        2,
-        sums,
-        sizes,
-        block,
-    )
     reduced = [None] * len(sizes)
 
     def scatter(x):
@@ -993,14 +1145,62 @@
             sums[x], "dp", scatter_dimension=0, tiled=True, axis_index_groups=[plan.ring]
         )
 
+    def known(values):
+        return [x for x in values if x is not None]
+
+    cuts = {2: 0, 3: 0}
+    sent = set()
+    if last >= 2:
+        cuts = {2: plan.first_late[2], 3: plan.first_late[3] // 2}
+        sent = {(last, spot) for *_, spot in plan.strips}
+    if sent:
+        strips = {}
+        for matrix, r, c, spot in plan.strips:
+            half = c // hidden_blocks if matrix == 2 else None
+            at = c if half is None else c % hidden_blocks
+            strips.setdefault((matrix, r, half), []).append((at, spot))
+        sums[last] = grad_strips(
+            [
+                (
+                    after(second_in, second_sent) if matrix == 2 else after(hidden, second_sent),
+                    r,
+                    gateup_grad if matrix == 2 else mlp_grad,
+                    half,
+                    blocks,
+                )
+                for (matrix, r, half), blocks in strips.items()
+            ],
+            sizes[last],
+            block,
+        )
+
+    def down_grads(sums, hidden, span):
+        table = plan.of_matrix(3, hidden_blocks, row_blocks)
+        return grad_blocks(
+            hidden, [mlp_grad], None, False, table, 2, sums, sizes, block, span, sent
+        )
+
+    def gateup_grads(sums, second_in, span):
+        table = plan.of_matrix(2, row_blocks, 2 * hidden_blocks)
+        return grad_blocks(
+            second_in, [gateup_grad], None, True, table, 2, sums, sizes, block, span, sent
+        )
+
+    sums = down_grads(sums, after(hidden, second_sent), (cuts[3], row_blocks // 2))
+    mine, other = near_sum(second_sent, after(second_kept, *known(sums)))
+    sums = gateup_grads(sums, after(second_in, other), (cuts[2], hidden_blocks))
     if last >= 2:
         scatter(2)
-
-    mine = after(mine, *[x for x in sums if x is not None])
+    got = partner(other, 2)
+    sums = gateup_grads(sums, second_in, (0, cuts[2]))
+    mine = after(mine, *known(sums[:2]))
     middle_grad, attn_low, second_gain = norm_back(
         middle, mine, got, norm_gains[1:], own_grad
     )
-    feed_sent, feed_kept = project_rows([after(hidden, attn_low)], w_down, None, False, 512)
+    sums = down_grads(sums, after(hidden, attn_low), (0, cuts[3]))
+    feed_sent, feed_kept = project_rows(
+        [after(hidden, *known(sums[:2]))], w_down, None, False, 512
+    )
     attn_grad = spread_share(attn_low, feed_kept)
     sums = grad_blocks(
         mixed,
@@ -1016,47 +1216,40 @@
     if last >= 1:
         scatter(1)
 
-    mixed_grad = to_heads(attn_grad, after(w_attn_out, *[x for x in sums if x is not None]), shares)
-
-    feed_mine, feed_other = near_sum(feed_sent, after(feed_kept, mixed_grad))
-    groups = query_cols // LANES
-    query_grads, kv_grad = [], None
-    feed_step = feed_other
-    for group in range(groups):
-        pair_grad, kv_grad = attend_back(
-            group,
-            queries,
-            kv,
-            starts,
-            logs,
-            after(mixed_grad, feed_step),
-            cos,
-            sin,
-            kv_grad,
-            group == groups - 1,
+    feed_mine, feed_other = near_sum(feed_sent, after(feed_kept, *known(sums[:2])))
+    mixed_grad = to_heads(attn_grad, after(w_attn_out, feed_other), shares)
+    query_grad, kv_grad = attend_back(queries, kv, starts, logs, mixed_grad, cos, sin)
+    feed_part = after(feed_mine, query_grad) + partner(feed_other, 2).astype(F32)
+    out_low = (middle + feed_part).astype(LOW)
+    qkv_grads = [query_grad, kv_grad]
+    first_sent, first_kept = project_rows(
+        [after(query_grad, out_low), kv_grad], w_qkv, shares, True, 512
+    )
+    mine, other = near_sum(first_sent, first_kept)
+
+    half = rows // 2
+    first_gain = sum(
+        jnp.sum(part.astype(F32) * (x.astype(F32) * scale), axis=0, keepdims=True)
+        for part, x, scale in (
+            (first_kept, tokens_local[:half], unit_scale[:half]),
+            (first_sent, tokens_local[half:], unit_scale[half:]),
         )
-        query_grads.append(pair_grad)
-        if group == groups - 3:
-            feed_part = after(feed_mine, pair_grad) + partner(feed_other, 2).astype(F32)
-            feed_step = out_low = (middle + feed_part).astype(LOW)
-    out_parts = spread_share(out_low)
-    qkv_grads = query_grads + [kv_grad]
+    )
+    gain_sums = jnp.concatenate([first_gain, second_gain], axis=0)
+    gain_sums = gain_sums + partner(gain_sums, 2)
+    other = after(other, gain_sums)
     sums = grad_blocks(
-        first_in,
+        after(first_in, other),
         qkv_grads,
         None,
         False,
         plan.of_matrix(0, row_blocks, attn_blocks),
-        attn_blocks,
+        1,
         sums,
         sizes,
         block,
     )
     scatter(0)
-    first_sent, first_kept = project_rows(
-        [after(qkv_grads[0], sums[0])] + qkv_grads[1:], w_qkv, shares, True, 512
-    )
-    mine, other = near_sum(first_sent, first_kept)
     factor = float(rows * dp_count) ** (-0.5)
 
     def update(x, state, *others):
@@ -1074,20 +1267,19 @@
             state,
         )
 
+    _, input_low, _ = norm_back(
+        own_tokens,
+        after(mine, sums[0]),
+        partner(other, 2),
+        norm_gains[:1],
+        middle_grad,
+    )
     state = None
     if last >= 2:
-        state = update(2, state, other)
-        mine = after(mine, *state)
-    _, input_low, first_gain = norm_back(
-        own_tokens, mine, partner(other, 2), norm_gains[:1], middle_grad
-    )
-    gain_sums = jnp.concatenate([first_gain, second_gain], axis=0)
-    gain_sums = gain_sums + partner(gain_sums, 2)
-    input_low = after(input_low, gain_sums)
+        state = update(2, state, input_low)
     if last >= 1:
-        state = update(1, state, other)
-        input_low = after(input_low, *state)
-    input_parts = spread_share(input_low)
+        state = update(1, state, input_low)
+    gain_sums = after(gain_sums, input_low, *(state or ()))
     gain_sums = gain_sums + partner(gain_sums, 1)
     bit = 1
     while bit < dp_count:
@@ -1095,14 +1287,16 @@
             gain_sums, "dp", [(i, i ^ bit) for i in range(dp_count)]
         )
         bit *= 2
+    input_parts = spread_share(input_low, *(state or ()))
     gain_share = model_width // dp_count
     gain_grads = factor * lax.dynamic_slice_in_dim(gain_sums, d_index * gain_share, gain_share, 1)
     old_gains = lax.dynamic_slice_in_dim(norm_gains, d_index * gain_share, gain_share, 1)
     new_gains = old_gains - gain_rate * gain_grads
+    out_parts = spread_share(after(out_low, input_low), *(state or ()))
     block_out = to_true(out_parts).reshape(sequences, length, model_width)
     input_grad = to_true(input_parts).astype(F32).reshape(sequences, length, model_width)
     grads, new_weights, new_ema, new_left, new_right = update(
-        0, state, block_out, input_grad, new_gains
+        0, state, input_grad, block_out, new_gains
     )
     return (
         block_out,

time: 626 us -> 603 us (0.963)
  waiting for transfers between devices: 265 us -> 197 us
  Pallas kernels: 264 us -> 324 us
  matrix products: 12 us -> 0 us
    ppermute x22, waiting for transfers between devices: 120 us -> 68 us  [partner(): return lax.ppermute(values, 'mp', [(i, i ^ bit) for i in range(mp_count)])]
    all_gather x3, waiting for transfers between devices: 142 us -> 114 us  [on_device(): lax.all_gather(chunk, 'dp', axis=0, tiled=True, axis_index_groups=[plan.r...]
    pallas_call x5 -> x4, Pallas kernels: 42 us -> 61.6 us  [the longest x1 33.7 us: attend_back(): pl.pallas_call(body, grid=(groups,), in_specs=[pl.BlockSpec((1, rows), la...]
    pallas_call x1, Pallas kernels: 13 us -> 29.4 us  [attend(): pl.pallas_call(body, grid=(groups,), in_specs=[pl.BlockSpec((1, rows), la...]
    pallas_call x4 -> x6, Pallas kernels: 47.4 us -> 61.2 us  [grad_blocks(): pl.pallas_call(body, grid=(steps,), out_shape=[jax.ShapeDtypeStruct((size...]
    dot_general x1 -> x0, matrix products: 12 us -> none  [dot_turned(): lax.dot_general(left, right, (((1,), (1,)), ((), ())), preferred_element_...]
    pallas_call x3 -> x4, Pallas kernels: 15.6 us -> 26.8 us  [rows_call(): pl.pallas_call(body, grid=(rows // step,), in_specs=[spec(x) for x in ins...]
    reduce_scatter x3, waiting for transfers between devices: 0.02 us -> 7.48 us  [scatter(): lax.psum_scatter(sums[x], 'dp', scatter_dimension=0, tiled=True, axis_ind...]
  transfers between devices with their start and end apart: 31 -> 31, of which waited for: 17 -> 17; matrix products, arithmetic and copies ran while one was open for 7% -> 5% of each run, Pallas kernels for 30% -> 43%
where the time goes in v4:
time: 603 us; the launch traced here: 600 us
  Pallas kernels  324 us (54%)
  waiting for transfers between devices  197 us (33%)
  other arithmetic  28.3 us (5%)
  local copies, waits for them, and re-layouts  18.5 us (3%)
  starting transfers between devices  18.5 us (3%)
  between operations  14.6 us (2%)
    all_gather x3, waiting for transfers between devices, on_device(): lax.all_gather(chunk, 'dp', axis=0, tiled=True, axis_index_groups=[plan.r...  114 us
    ppermute x22, waiting for transfers between devices, partner(): return lax.ppermute(values, 'mp', [(i, i ^ bit) for i in range(mp_count)])  68 us
    pallas_call x6, Pallas kernels, grad_blocks(): pl.pallas_call(body, grid=(steps,), out_shape=[jax.ShapeDtypeStruct((size...  61.2 us
    pallas_call x4, Pallas kernels, project_rows(): pl.pallas_call(body, grid=(width // tile,), in_specs=[SMEM] * n_order + w...  41.5 us
    pallas_call x1, Pallas kernels, attend_back(): pl.pallas_call(body, grid=(groups,), in_specs=[pl.BlockSpec((1, rows), la...  33.7 us
    pallas_call x3, Pallas kernels, shampoo(): pl.pallas_call(body, out_shape=[jax.ShapeDtypeStruct(weights.shape, F32)]...  32 us
    pallas_call x1, Pallas kernels, attend(): pl.pallas_call(body, grid=(groups,), in_specs=[pl.BlockSpec((1, rows), la...  29.4 us
    pallas_call x4, Pallas kernels, rows_call(): pl.pallas_call(body, grid=(rows // step,), in_specs=[spec(x) for x in ins...  26.8 us
  transfers between devices with their start and end apart: 31, of which 17 were waited for; matrix products, arithmetic and copies ran while one was open for 5% of the time, Pallas kernels for 43%

profile of v4, /device:TPU:0, one launch (start us, length us, event | category | flops | bytes accessed | tf_op | source)
XLA Modules:
  0.0 600.5 jit_solution(16969838824524462248)
XLA Ops:
  8.5 4.9 sort_blocks.1
  17.1 11.1 %first_norm.1.x_ref.refs_0_ = bf16[1024,2048]{1,0:T(8,128)(2,1)} custom-call(bf16[1024,2048]{1,0:T(8,128)(2,1)} %bitcast.48, f32[1,2048]{1,0:T(1,128)} %get-tuple-element.234.gain_ref), custom_call_target="tpu_custom_call" | custom-call | flops 20971520 | bytes 8396800 | tf_op jit(solution)/shard_map/first_norm/pallas_call | solution.py:865
  28.3 1.9 fusion
  30.2 1.9 pad_maximum_fusion.2
  33.2 2.6 multiply_reduce_fusion
  38.2 2.3 pad_maximum_fusion.g_ref.refs_3_.refs_1_
  40.6 28.5 %all-gather.4.cloned.1.call-done.refs_4_ = bf16[144,128,128]{2,1,0:T(8,128)(2,1)} async-done(((bf16[18,128,128]{2,1,0:T(8,128)(2,1)}), bf16[144,128,128]{2,1,0:T(8,128)(2,1)}) %all-gather.4.cloned.1.call-update) | async-done | bytes 4718608 | tf_op jit(solution)/shard_map/all_gather | solution.py:1088
  69.1 5.2 place_blocks.4
  74.3 11.6 %project_heads.1 = (bf16[1024,512]{1,0:T(8,128)(2,1)}, bf16[1024,128]{1,0:T(8,128)(2,1)}) custom-call(bf16[1024,2048]{1,0:T(8,128)(2,1)} %first_norm.1.x_ref.refs_0_, bf16[2048,640]{1,0:T(8,128)(2,1)} %get-tuple-element.111.w_ref.refs_3_, f32[1024,128]{1,0:T(8,128)} %get-tuple-element.242.cos_ref, f32[1024,128]{1,0:T(8,128)} %get-tuple-element.243.sin_ref), custom_call_target="tpu_custom_call" | custom-call | flops 2684354560 | bytes 8126464 | tf_op jit(solution)/shard_map/project_heads/pallas_call | solution.py:595
  85.8 29.4 %attend.1 = (bf16[1024,512]{1,0:T(8,128)(2,1)}, f32[4,2,1024]{2,1,0:T(2,128)}) custom-call(s32[1,1024]{1,0:T(1,128)} %reduce_window_max.29.start_ref, bf16[1024,512]{1,0:T(8,128)(2,1)} %get-tuple-element.114.q_ref, bf16[1024,128]{1,0:T(8,128)(2,1)} %get-tuple-element.115.kv_ref), custom_call_target="tpu_custom_call" | custom-call | flops 16106127360 | bytes 2097152 | tf_op jit(solution)/shard_map/attend/pallas_call | solution.py:662
  115.2 77.6 %all-gather.6.cloned.1.call-done.refs_1_.refs_2_ = bf16[368,128,128]{2,1,0:T(8,128)(2,1)} async-done(((bf16[46,128,128]{2,1,0:T(8,128)(2,1)}), bf16[368,128,128]{2,1,0:T(8,128)(2,1)}) %all-gather.6.cloned.1.call-update) | async-done | bytes 12058640 | tf_op jit(solution)/shard_map/all_gather | solution.py:1088
  192.8 3.2 place_blocks.5.refs_2_.refs_4_
  196.1 5.8 project_rows.4
  201.9 4.4 collective-permute-done.b_ref.d_ref
  207.6 4.3 add_near.4
  213.4 8.7 %place_blocks.6 = (bf16[2048,2816]{1,0:T(8,128)(2,1)}, bf16[1408,2048]{1,0:T(8,128)(2,1)}) custom-call(s32[690]{0:T(1024)} %constant.81.clone.refs_0_, s32[276]{0:T(512)} %constant.82.clone.refs_1_, bf16[368,128,128]{2,1,0:T(8,128)(2,1)} %all-gather.6.cloned.1.call-done.refs_1_.refs_2_, ...), custom_call_target="tpu_custom_call", output_to_operand_aliasing={{0}: (3, {}), {1}: (4, {})} | custom-call | bytes 21102592 | tf_op jit(solution)/shard_map/place_blocks/pallas_call | solution.py:154
  222.1 15.3 %collective-permute-done.1.b_ref = bf16[256,2048]{1,0:T(8,128)(2,1)S(1)} collective-permute-done((bf16[256,2048]{1,0:T(8,128)(2,1)}, bf16[256,2048]{1,0:T(8,128)(2,1)S(1)}, u32[]{:S(2)}, u32[]{:S(2)}) %collective-permute-start.1) | collective-permute-done | bytes 1048608 | tf_op jit(solution)/shard_map/ppermute | solution.py:1051
  238.3 4.5 second_norm.1
  244.3 7.8 %all-gather.8.cloned.1.call-done.refs_2_ = bf16[160,128,128]{2,1,0:T(8,128)(2,1)} async-done(((bf16[20,128,128]{2,1,0:T(8,128)(2,1)}), bf16[160,128,128]{2,1,0:T(8,128)(2,1)}) %all-gather.8.cloned.1.call-update) | async-done | bytes 5242896 | tf_op jit(solution)/shard_map/all_gather | solution.py:1088
  252.1 5.5 place_blocks.7
  257.7 12.6 %down_back.1.refs_6_ = f32[1024,1408]{1,0:T(8,128)} custom-call(bf16[1024,2048]{1,0:T(8,128)(2,1)} %pad_maximum_fusion.g_ref.refs_3_.refs_1_, bf16[1408,2048]{1,0:T(8,128)(2,1)} %get-tuple-element.136.w_ref.refs_1_), custom_call_target="tpu_custom_call" | custom-call | flops 5905580032 | bytes 15728640 | tf_op jit(solution)/shard_map/down_back/pallas_call | solution.py:510
  270.3 2.6 collective-permute-done.4.refs_3_
  273.9 20.4 %feed_forward.1 = (bf16[1024,1408]{1,0:T(8,128)(2,1)}, bf16[2,1024,1408]{2,1,0:T(8,128)(2,1)}, bf16[1024,2048]{1,0:T(8,128)(2,1)}) custom-call(bf16[256,2048]{1,0:T(8,128)(2,1)} %get-tuple-element.130.refs_0_, bf16[256,2048]{1,0:T(8,128)(2,1)} %copy-done.21, bf16[256,2048]{1,0:T(8,128)(2,1)} %copy-done.22, bf16[256,2048]{1,0:T(8,128)(2,1)} %copy-done.25, ...), custom_call_target="tpu_custom_call" | custom-call | flops 11811160064 | bytes 30146560 | tf_op jit(solution)/shard_map/feed_forward/pallas_call | solution.py:398
  294.4 18.4 %project_rows.5 = (bf16[512,2048]{1,0:T(8,128)(2,1)}, bf16[512,2048]{1,0:T(8,128)(2,1)}) custom-call(bf16[2,1024,1408]{2,1,0:T(8,128)(2,1)} %get-tuple-element.140.refs_0_.refs_1_, bf16[2048,2816]{1,0:T(8,128)(2,1)} %get-tuple-element.138.refs_4_.refs_5_.refs_1_), custom_call_target="tpu_custom_call" | custom-call | flops 11811160064 | bytes 21495808 | tf_op jit(solution)/shard_map/project_rows/pallas_call | solution.py:472
  312.9 3.7 grad_strips.1.refs_2_
  316.6 4.9 grad_blocks.6
  322.8 4.4 add_near.5
  327.2 10.1 %grad_blocks.7 = (bf16[368,128,128]{2,1,0:T(8,128)(2,1)}, bf16[160,128,128]{2,1,0:T(8,128)(2,1)}) custom-call(bf16[1024,2048]{1,0:T(8,128)(2,1)} %get-tuple-element.151.refs_0_, bf16[2,1024,1408]{2,1,0:T(8,128)(2,1)} %get-tuple-element.140.refs_0_.refs_1_, ...), custom_call_target="tpu_custom_call", output_to_operand_aliasing={{0}: (2, {}), {1}: (3, {})} | custom-call | flops 8589934592 | bytes 21495808 | tf_op jit(solution)/shard_map/grad_blocks/pallas_call | solution.py:297
  340.0 16.6 %grad_blocks.8 = (bf16[144,128,128]{2,1,0:T(8,128)(2,1)}, bf16[368,128,128]{2,1,0:T(8,128)(2,1)}) custom-call(bf16[1024,2048]{1,0:T(8,128)(2,1)} %get-tuple-element.151.refs_0_, bf16[2,1024,1408]{2,1,0:T(8,128)(2,1)} %get-tuple-element.140.refs_0_.refs_1_, bf16[368,128,128]{2,1,0:T(8,128)(2,1)} %get-tuple-element.152.refs_2_), custom_call_target="tpu_custom_call", output_to_operand_aliasing={{1}: (2, {})} | custom-call | flops 15032385536 | bytes 21495808 | tf_op jit(solution)/shard_map/grad_blocks/pallas_call | solution.py:297
  356.6 7.4 %collective-permute-done.6.b_ref = bf16[256,2048]{1,0:T(8,128)(2,1)S(1)} collective-permute-done((bf16[256,2048]{1,0:T(8,128)(2,1)S(1)}, bf16[256,2048]{1,0:T(8,128)(2,1)S(1)}, u32[]{:S(2)}, u32[]{:S(2)}) %collective-permute-start.6) | collective-permute-done | bytes 1048608 | tf_op jit(solution)/shard_map/ppermute | solution.py:1051
  364.9 5.6 norm_back.2
  370.6 1.6 collective-permute-start.7
  372.1 9.8 %grad_blocks.9 = (bf16[144,128,128]{2,1,0:T(8,128)(2,1)}, bf16[368,128,128]{2,1,0:T(8,128)(2,1)}) custom-call(bf16[1024,1408]{1,0:T(8,128)(2,1)} %get-tuple-element.161.refs_2_.refs_0_, bf16[1024,2048]{1,0:T(8,128)(2,1)} %pad_maximum_fusion.g_ref.refs_3_.refs_1_, ...), custom_call_target="tpu_custom_call", output_to_operand_aliasing={{0}: (2, {}), {1}: (3, {})} | custom-call | flops 8858370048 | bytes 12845056 | tf_op jit(solution)/shard_map/grad_blocks/pallas_call | solution.py:297
  382.0 10.4 %project_rows.6 = (bf16[512,2048]{1,0:T(8,128)(2,1)}, bf16[512,2048]{1,0:T(8,128)(2,1)}) custom-call(bf16[1024,1408]{1,0:T(8,128)(2,1)} %get-tuple-element.161.refs_2_.refs_0_, bf16[1408,2048]{1,0:T(8,128)(2,1)} %get-tuple-element.136.w_ref.refs_1_), custom_call_target="tpu_custom_call" | custom-call | flops 5905580032 | bytes 12845056 | tf_op jit(solution)/shard_map/project_rows/pallas_call | solution.py:472
  392.9 2.7 collective-permute-done.7.refs_3_.refs_1_
  395.6 2.0 collective-permute-done.8.refs_4_.refs_2_
  399.9 7.4 %grad_blocks.10 = (bf16[144,128,128]{2,1,0:T(8,128)(2,1)}, bf16[368,128,128]{2,1,0:T(8,128)(2,1)}) custom-call(s32[4]{0:T(128)} %broadcast_xor_fusion.refs_0_.order_ref, bf16[1024,512]{1,0:T(8,128)(2,1)} %get-tuple-element.116.refs_1_, bf16[256,2048]{1,0:T(8,128)(2,1)} %get-tuple-element.157.refs_2_.refs_0_, ...), custom_call_target="tpu_custom_call", output_to_operand_aliasing={{0}: (6, {}), {1}: (7, {})} | custom-call | flops 4294967296 | bytes 7340032 | tf_op jit(solution)/shard_map/grad_blocks/pallas_call | solution.py:297
  408.7 4.3 add_near.6
  413.5 6.3 %to_heads.1.g_ref = bf16[1024,512]{1,0:T(8,128)(2,1)} custom-call(s32[4]{0:T(128)} %broadcast_xor_fusion.refs_0_.order_ref, bf16[256,2048]{1,0:T(8,128)(2,1)} %get-tuple-element.157.refs_2_.refs_0_, bf16[256,2048]{1,0:T(8,128)(2,1)} %collective-permute-done.7.refs_3_.refs_1_, bf16[256,2048]{1,0:T(8,128)(2,1)} %copy-done.11, ...), custom_call_target="tpu_custom_call" | custom-call | flops 2147483648 | bytes 6291456 | tf_op jit(solution)/shard_map/to_heads/pallas_call | solution.py:541
  419.8 33.7 %attend_back.1 = (bf16[1024,512]{1,0:T(8,128)(2,1)}, bf16[1024,128]{1,0:T(8,128)(2,1)}) custom-call(s32[1,1024]{1,0:T(1,128)} %reduce_window_max.29.start_ref, bf16[1024,512]{1,0:T(8,128)(2,1)} %get-tuple-element.114.q_ref, bf16[1024,128]{1,0:T(8,128)(2,1)} %get-tuple-element.115.kv_ref, f32[4,2,1024]{2,1,0:T(2,128)} %get-tuple-element.169.log_ref, ...), custom_call_target="tpu_custom_call" | custom-call | flops 214748364800 | bytes 8388608 | tf_op jit(solution)/shard_map/attend_back/pallas_call | solution.py:737
  453.5 2.4 add_convert_fusion
  455.9 6.9 %project_rows.7 = (bf16[512,2048]{1,0:T(8,128)(2,1)}, bf16[512,2048]{1,0:T(8,128)(2,1)}) custom-call(s32[4]{0:T(128)} %broadcast_xor_fusion.refs_0_.order_ref, bf16[1024,512]{1,0:T(8,128)(2,1)} %get-tuple-element.174.refs_1_, bf16[1024,128]{1,0:T(8,128)(2,1)} %get-tuple-element.175.refs_2_, bf16[2048,640]{1,0:T(8,128)(2,1)} %get-tuple-element.111.w_ref.refs_3_), custom_call_target="tpu_custom_call" | custom-call | flops 2684354560 | bytes 8126464 | tf_op jit(solution)/shard_map/project_rows/pallas_call | solution.py:472
  462.9 4.3 multiply_reduce_fusion.1
  467.2 1.7 collective-permute-start.13
  468.9 2.1 collective-permute-done.13
  472.4 4.3 add_near.7
  476.7 12.4 %grad_blocks.11 = bf16[144,128,128]{2,1,0:T(8,128)(2,1)} custom-call(bf16[1024,2048]{1,0:T(8,128)(2,1)} %first_norm.1.x_ref.refs_0_, bf16[1024,512]{1,0:T(8,128)(2,1)} %get-tuple-element.174.refs_1_, bf16[1024,128]{1,0:T(8,128)(2,1)} %get-tuple-element.175.refs_2_, bf16[144,128,128]{2,1,0:T(8,128)(2,1)} %get-tuple-element.164.refs_3_), custom_call_target="tpu_custom_call", output_to_operand_aliasing={{}: (3, {})} | custom-call | flops 5368709120 | bytes 8126464 | tf_op jit(solution)/shard_map/grad_blocks/pallas_call | solution.py:297
  490.3 1.6 collective-permute-start.14
  491.9 23.2 %collective-permute-done.14.b_ref = bf16[256,2048]{1,0:T(8,128)(2,1)S(1)} collective-permute-done((bf16[256,2048]{1,0:T(8,128)(2,1)S(1)}, bf16[256,2048]{1,0:T(8,128)(2,1)S(1)}, u32[]{:S(2)}, u32[]{:S(2)}) %collective-permute-start.14) | collective-permute-done | bytes 1048608 | tf_op jit(solution)/shard_map/ppermute | solution.py:1051
  516.1 5.5 norm_back.3
  521.6 1.8 collective-permute-start.16
  524.9 8.5 %shampoo.3 = (f32[84,128,128]{2,1,0:T(8,128)}, f32[84,128,128]{2,1,0:T(8,128)}, f32[84,128,128]{2,1,0:T(8,128)}, f32[84,128,128]{2,1,0:T(8,128)}, f32[84,128,128]{2,1,0:T(8,128)}) custom-call(s32[20]{0:T(128)} %slice_bitcast_fusion.1.places_ref, bf16[20,128,128]{2,1,0:T(8,128)(2,1)} %reduce-scatter.6.cloned.1.call-done.g_ref, f32[84,128,128]{2,1,0:T(8,128)} %refs_0_.9, ...), custom_call_target="tpu_custom_call" | custom-call | flops 335544320 | bytes 15073280 | tf_op jit(solution)/shard_map/shampoo/pallas_call | solution.py:835
  533.4 15.7 %shampoo.4 = (f32[84,128,128]{2,1,0:T(8,128)}, f32[84,128,128]{2,1,0:T(8,128)}, f32[84,128,128]{2,1,0:T(8,128)}, f32[84,128,128]{2,1,0:T(8,128)}, f32[84,128,128]{2,1,0:T(8,128)}) custom-call(s32[46]{0:T(128)} %slice_bitcast_fusion.2.places_ref, ...), custom_call_target="tpu_custom_call", output_to_operand_aliasing={{0}: (8, {}), {1}: (9, {}), {2}: (10, {}), {3}: (11, {}), {... | custom-call | flops 771751936 | bytes 34668544 | tf_op jit(solution)/shard_map/shampoo/pallas_call | solution.py:835
  549.7 2.1 collective-permute-done.21
  551.9 1.7 collective-permute-start.22
  553.6 2.6 collective-permute-done.22
  557.4 3.1 collective-permute-done.23
  560.5 2.1 collective-permute-start.24
  563.3 4.9 collective-permute-done.19
  569.4 2.3 broadcast_select_fusion.11
  571.7 2.3 maximum_bitcast_fusion
  574.3 3.9 maximum_convert_fusion
  578.3 7.5 %reduce-scatter.8.cloned.1.call-done.g_ref = bf16[18,128,128]{2,1,0:T(8,128)(2,1)} async-done(((bf16[144,128,128]{2,1,0:T(8,128)(2,1)}), bf16[18,128,128]{2,1,0:T(8,128)(2,1)}) %reduce-scatter.8.cloned.1.call-update) | async-done | bytes 589840 | tf_op jit(solution)/shard_map/reduce_scatter | solution.py:1144
  585.7 7.9 %shampoo.5 = (f32[84,128,128]{2,1,0:T(8,128)}, f32[84,128,128]{2,1,0:T(8,128)}, f32[84,128,128]{2,1,0:T(8,128)}, f32[84,128,128]{2,1,0:T(8,128)}, f32[84,128,128]{2,1,0:T(8,128)}) custom-call(s32[18]{0:T(128)} %slice_bitcast_fusion.places_ref, ...), custom_call_target="tpu_custom_call", output_to_operand_aliasing={{0}: (8, {}), {1}: (9, {}), {2}: (10, {}), {3}: (11, {}), {... | custom-call | flops 301989888 | bytes 13565952 | tf_op jit(solution)/shard_map/shampoo/pallas_call | solution.py:835
  (131 shorter events, 33.7 us)
Async XLA Ops:
  7.2 7.7 %copy-start.17 = (s32[1,1024]{1,0:T(1,128)S(1)}, s32[1,1024]{1,0:T(1,128)}, u32[]{:S(2)}) copy-start(s32[1,1024]{1,0:T(1,128)} %param.25) | copy-start | bytes 12292
  7.2 8.6 %copy-start.16 = (f32[2,2048]{1,0:T(2,128)S(1)}, f32[2,2048]{1,0:T(2,128)}, u32[]{:S(2)}) copy-start(f32[2,2048]{1,0:T(2,128)} %param.26) | copy-start | bytes 49156
  7.2 61.9 %all-gather.4.cloned.1.call-start = ((), (), s32[]{:S(2)}) async-start(), calls=%async_computation.3 | async-start | bytes 5308416 | tf_op jit(solution)/shard_map/all_gather | solution.py:1088
  13.4 179.5 %all-gather.6.cloned.1.call-start = ((), (), s32[]{:S(2)}) async-start(), calls=%async_computation.4 | async-start | bytes 13565952 | tf_op jit(solution)/shard_map/all_gather | solution.py:1088
  14.1 238.0 %all-gather.8.cloned.1.call-start = ((), (), s32[]{:S(2)}) async-start(), calls=%async_computation.5 | async-start | bytes 5898240 | tf_op jit(solution)/shard_map/all_gather | solution.py:1088
  14.9 510.0 %reduce-scatter.6.cloned.1.call-start = ((), (), s32[]{:S(2)}) async-start(), calls=%async_computation.7 | async-start | bytes 5898240 | tf_op jit(solution)/shard_map/reduce_scatter | solution.py:1144
  17.1 11.2 %copy-start.19 = (s32[1,1024]{1,0:T(1,128)S(1)}, s32[1,1024]{1,0:T(1,128)}, u32[]{:S(2)}) copy-start(s32[1,1024]{1,0:T(1,128)} %param.24) | copy-start | bytes 12292
  28.2 3.9 copy-start.26
  28.2 4.4 copy-start
  33.2 2.7 copy-start.1
  33.2 4.1 copy-start.8
  38.2 2.4 copy-start.2
  201.9 4.4 collective-permute-start
  206.3 1.3 copy-start.7
  211.9 25.4 %collective-permute-start.1 = (bf16[256,2048]{1,0:T(8,128)(2,1)}, bf16[256,2048]{1,0:T(8,128)(2,1)S(1)}, u32[]{:S(2)}, u32[]{:S(2)}) collective-permute-start(bf16[256,2048]{1,0:T(8,128)(2,1)} %get-tuple-element.122), channel_id=1, source_target_pairs={{0,2},{1,3},{2,0},{3,1},{4,6},{5,7},{6,4},{7,5},{8,10},{9,11},{10,... | collective-permute-start | bytes 3145736 | tf_op jit(solution)/shard_map/ppermute | solution.py:1051
  237.3 1.0 copy-start.13
  242.8 27.4 %collective-permute-start.2 = (bf16[256,2048]{1,0:T(8,128)(2,1)}, bf16[256,2048]{1,0:T(8,128)(2,1)S(1)}, u32[]{:S(2)}, u32[]{:S(2)}) collective-permute-start(bf16[256,2048]{1,0:T(8,128)(2,1)} %get-tuple-element.130.refs_0_), channel_id=1, source_target_pairs={{0,2},{1,3},{2,0},{3,1},{4,6},{5,7},{6,4},{7,5},{8,10},{9,11},{10,... | collective-permute-start | bytes 3145736 | tf_op jit(solution)/shard_map/ppermute | solution.py:1051
  244.3 26.0 %collective-permute-start.3 = (bf16[256,2048]{1,0:T(8,128)(2,1)}, bf16[256,2048]{1,0:T(8,128)(2,1)S(1)}, u32[]{:S(2)}, u32[]{:S(2)}) collective-permute-start(bf16[256,2048]{1,0:T(8,128)(2,1)} %get-tuple-element.130.refs_0_), channel_id=1, source_target_pairs={{0,1},{1,0},{2,3},{3,2},{4,5},{5,4},{6,7},{7,6},{8,9},{9,8},{10,11... | collective-permute-start | bytes 3145736 | tf_op jit(solution)/shard_map/ppermute | solution.py:1051
  270.3 2.7 copy-start.21
  270.3 2.7 collective-permute-start.4
  270.3 2.6 copy-start.22
  272.9 1.0 copy-start.25
  312.8 8.8 %collective-permute-start.5 = (bf16[512,2048]{1,0:T(8,128)(2,1)}, bf16[512,2048]{1,0:T(8,128)(2,1)S(1)}, u32[]{:S(2)}, u32[]{:S(2)}) collective-permute-start(bf16[512,2048]{1,0:T(8,128)(2,1)} %get-tuple-element.142), channel_id=1, source_target_pairs={{0,1},{1,0},{2,3},{3,2},{4,5},{5,4},{6,7},{7,6},{8,9},{9,8},{10,11... | collective-permute-start | bytes 6291464 | tf_op jit(solution)/shard_map/ppermute | solution.py:1051
  321.5 1.3 copy-start.6
  337.3 1.2 copy-start.23
  337.4 196.0 %reduce-scatter.4.cloned.1.call-start = ((), (), s32[]{:S(2)}) async-start(), calls=%async_computation.6 | async-start | bytes 13565952 | tf_op jit(solution)/shard_map/reduce_scatter | solution.py:1144
  338.5 25.4 %collective-permute-start.6 = (bf16[256,2048]{1,0:T(8,128)(2,1)S(1)}, bf16[256,2048]{1,0:T(8,128)(2,1)S(1)}, u32[]{:S(2)}, u32[]{:S(2)}) collective-permute-start(bf16[256,2048]{1,0:T(8,128)(2,1)S(1)} %copy-done.23), channel_id=1, source_target_pairs={{0,2},{1,3},{2,0},{3,1},{4,6},{5,7},{6,4},{7,5},{8,10},{9,11},{10,... | collective-permute-start | bytes 3145736 | tf_op jit(solution)/shard_map/ppermute | solution.py:1051
  364.0 1.0 copy-start.12
  370.6 25.1 %collective-permute-start.7 = (bf16[256,2048]{1,0:T(8,128)(2,1)}, bf16[256,2048]{1,0:T(8,128)(2,1)}, u32[]{:S(2)}, u32[]{:S(2)}) collective-permute-start(bf16[256,2048]{1,0:T(8,128)(2,1)} %get-tuple-element.157.refs_2_.refs_0_), channel_id=1, source_target_pairs={{0,2},{1,3},{2,0},{3,1},{4,6},{5,7},{6,4},{7,5},{8,10},{9,11},{10,... | collective-permute-start | bytes 3145736 | tf_op jit(solution)/shard_map/ppermute | solution.py:1051
  382.0 10.4 %copy-start.10 = (bf16[256,2048]{1,0:T(8,128)(2,1)S(1)}, bf16[256,2048]{1,0:T(8,128)(2,1)}, u32[]{:S(2)}) copy-start(bf16[256,2048]{1,0:T(8,128)(2,1)} %get-tuple-element.157.refs_2_.refs_0_) | copy-start | bytes 3145732
  392.4 15.0 %collective-permute-start.10 = (bf16[512,2048]{1,0:T(8,128)(2,1)}, bf16[512,2048]{1,0:T(8,128)(2,1)S(1)}, u32[]{:S(2)}, u32[]{:S(2)}) collective-permute-start(bf16[512,2048]{1,0:T(8,128)(2,1)} %get-tuple-element.167), channel_id=1, source_target_pairs={{0,1},{1,0},{2,3},{3,2},{4,5},{5,4},{6,7},{7,6},{8,9},{9,8},{10,11... | collective-permute-start | bytes 6291464 | tf_op jit(solution)/shard_map/ppermute | solution.py:1051
  392.4 5.3 collective-permute-start.8
  395.6 4.2 collective-permute-start.9
  397.7 1.0 copy-start.11
  407.3 178.4 %reduce-scatter.8.cloned.1.call-start = ((), (), s32[]{:S(2)}) async-start(), calls=%async_computation.8 | async-start | bytes 5308416 | tf_op jit(solution)/shard_map/reduce_scatter | solution.py:1144
  407.4 1.3 copy-start.4
  413.0 40.5 %collective-permute-start.11 = (bf16[256,2048]{1,0:T(8,128)(2,1)}, bf16[256,2048]{1,0:T(8,128)(2,1)}, u32[]{:S(2)}, u32[]{:S(2)}) collective-permute-start(bf16[256,2048]{1,0:T(8,128)(2,1)} %get-tuple-element.170), channel_id=1, source_target_pairs={{0,2},{1,3},{2,0},{3,1},{4,6},{5,7},{6,4},{7,5},{8,10},{9,11},{10,... | collective-permute-start | bytes 3145736 | tf_op jit(solution)/shard_map/ppermute | solution.py:1051
  419.8 33.7 %copy-start.3 = (f32[256,2048]{1,0:T(8,128)S(1)}, f32[256,2048]{1,0:T(8,128)}, u32[]{:S(2)}) copy-start(f32[256,2048]{1,0:T(8,128)} %get-tuple-element.129.x_ref) | copy-start | bytes 6291460
  455.9 7.0 %copy-start.18 = (f32[1024]{0:T(1024)S(1)}, f32[1024]{0:T(1024)}, u32[]{:S(2)}) copy-start(f32[1024]{0:T(1024)} %add_rsqrt_fusion) | copy-start | bytes 12292
  462.8 8.2 %collective-permute-start.12 = (bf16[512,2048]{1,0:T(8,128)(2,1)}, bf16[512,2048]{1,0:T(8,128)(2,1)S(1)}, u32[]{:S(2)}, u32[]{:S(2)}) collective-permute-start(bf16[512,2048]{1,0:T(8,128)(2,1)} %get-tuple-element.177), channel_id=1, source_target_pairs={{0,1},{1,0},{2,3},{3,2},{4,5},{5,4},{6,7},{7,6},{8,9},{9,8},{10,11... | collective-permute-start | bytes 6291464 | tf_op jit(solution)/shard_map/ppermute | solution.py:1051
  462.9 4.3 copy-start.15
  467.2 3.8 collective-permute-start.13
  471.0 1.3 copy-start.5
  489.1 1.3 copy-start.24
  490.3 33.1 %copy-start.20 = (s32[1,84]{1,0:T(1,128)S(1)}, s32[1,84]{1,0:T(1,128)}, u32[]{:S(2)}) copy-start(s32[1,84]{1,0:T(1,128)} %get-tuple-element.238) | copy-start | bytes 1012
  490.3 24.8 %collective-permute-start.14 = (bf16[256,2048]{1,0:T(8,128)(2,1)S(1)}, bf16[256,2048]{1,0:T(8,128)(2,1)S(1)}, u32[]{:S(2)}, u32[]{:S(2)}) collective-permute-start(bf16[256,2048]{1,0:T(8,128)(2,1)S(1)} %copy-done.24), channel_id=1, source_target_pairs={{0,2},{1,3},{2,0},{3,1},{4,6},{5,7},{6,4},{7,5},{8,10},{9,11},{10,... | collective-permute-start | bytes 3145736 | tf_op jit(solution)/shard_map/ppermute | solution.py:1051
  515.1 1.0 copy-start.14
  521.6 27.5 %collective-permute-start.16 = (bf16[256,2048]{1,0:T(8,128)(2,1)S(1)}, bf16[256,2048]{1,0:T(8,128)(2,1)}, u32[]{:S(2)}, u32[]{:S(2)}) collective-permute-start(bf16[256,2048]{1,0:T(8,128)(2,1)S(1)} %add_convert_fusion), channel_id=1, source_target_pairs={{0,2},{1,3},{2,0},{3,1},{4,6},{5,7},{6,4},{7,5},{8,10},{9,11},{10,... | collective-permute-start | bytes 3145736 | tf_op jit(solution)/shard_map/ppermute | solution.py:1051
  524.0 44.2 %collective-permute-start.19 = (bf16[256,2048]{1,0:T(8,128)(2,1)}, bf16[256,2048]{1,0:T(8,128)(2,1)S(1)}, u32[]{:S(2)}, u32[]{:S(2)}) collective-permute-start(bf16[256,2048]{1,0:T(8,128)(2,1)} %get-tuple-element.187), channel_id=1, source_target_pairs={{0,2},{1,3},{2,0},{3,1},{4,6},{5,7},{6,4},{7,5},{8,10},{9,11},{10,... | collective-permute-start | bytes 3145736 | tf_op jit(solution)/shard_map/ppermute | solution.py:1051
  524.9 44.6 %collective-permute-start.15 = (bf16[256,2048]{1,0:T(8,128)(2,1)S(1)}, bf16[256,2048]{1,0:T(8,128)(2,1)}, u32[]{:S(2)}, u32[]{:S(2)}) collective-permute-start(bf16[256,2048]{1,0:T(8,128)(2,1)S(1)} %add_convert_fusion), channel_id=1, source_target_pairs={{0,1},{1,0},{2,3},{3,2},{4,5},{5,4},{6,7},{7,6},{8,9},{9,8},{10,11... | collective-permute-start | bytes 3145736 | tf_op jit(solution)/shard_map/ppermute | solution.py:1051
  533.4 29.9 %copy-start.9 = (bf16[256,2048]{1,0:T(8,128)(2,1)S(1)}, bf16[256,2048]{1,0:T(8,128)(2,1)}, u32[]{:S(2)}) copy-start(bf16[256,2048]{1,0:T(8,128)(2,1)} %get-tuple-element.187) | copy-start | bytes 3145732
  549.1 20.3 %collective-permute-start.17 = (bf16[256,2048]{1,0:T(8,128)(2,1)}, bf16[256,2048]{1,0:T(8,128)(2,1)}, u32[]{:S(2)}, u32[]{:S(2)}) collective-permute-start(bf16[256,2048]{1,0:T(8,128)(2,1)} %collective-permute-done.16), channel_id=1, source_target_pairs={{0,1},{1,0},{2,3},{3,2},{4,5},{5,4},{6,7},{7,6},{8,9},{9,8},{10,11... | collective-permute-start | bytes 3145736 | tf_op jit(solution)/shard_map/ppermute | solution.py:1051
  549.6 2.2 collective-permute-start.21
  551.9 4.3 collective-permute-start.22
  556.2 4.3 collective-permute-start.23
  560.5 7.6 %collective-permute-start.24 = (f32[2,2048]{1,0:T(2,128)S(1)}, f32[2,2048]{1,0:T(2,128)S(1)}, u32[]{:S(2)}, u32[]{:S(2)}) collective-permute-start(f32[2,2048]{1,0:T(2,128)S(1)} %add.103), channel_id=1, source_target_pairs={{0,16},{4,20},{8,24},{12,28},{16,0},{20,4},{24,8},{28,12},{1,17},{... | collective-permute-start | bytes 49160 | tf_op jit(solution)/shard_map/ppermute | solution.py:1286
  563.3 10.7 %collective-permute-start.18 = (bf16[256,2048]{1,0:T(8,128)(2,1)S(1)}, bf16[256,2048]{1,0:T(8,128)(2,1)S(1)}, u32[]{:S(2)}, u32[]{:S(2)}) collective-permute-start(bf16[256,2048]{1,0:T(8,128)(2,1)S(1)} %copy-done.9), channel_id=1, source_target_pairs={{0,1},{1,0},{2,3},{3,2},{4,5},{5,4},{6,7},{7,6},{8,9},{9,8},{10,11... | collective-permute-start | bytes 3145736 | tf_op jit(solution)/shard_map/ppermute | solution.py:1051
  568.2 5.8 collective-permute-start.20
Sparse Core Ops, SparseCore 0:
  13.5 55.5 all-gather.3
  71.2 121.6 all-gather.5
  194.4 57.7 all-gather.7
  337.5 58.4 reduce-scatter.5
  407.4 122.0 reduce-scatter.3
  531.7 54.0 reduce-scatter.7

commit v5 on v4

--- a/solution.py
+++ b/solution.py
@@ -757,7 +757,7 @@
         ],
         compiler_params=pltpu.CompilerParams(vmem_limit_bytes=VMEM_LIMIT),
         cost_estimate=pl.CostEstimate(
-            flops=400 * rows * rows * width,
+            flops=80 * rows * rows * width,
             bytes_accessed=16 * rows * width,
             transcendentals=rows * rows * width // HD,
         ),
@@ -854,7 +854,7 @@
     )(places, sums, weights, ema, left, right, left_roots, right_roots, *extra)
 
 
-def rows_call(body, ins, outs, name, step=64):
+def rows_call(body, ins, outs, name, step=64, work=10):
     rows = max(x.shape[0] for x in ins)
 
     def spec(x):
@@ -870,7 +870,7 @@
         out_shape=outs,
         compiler_params=pltpu.CompilerParams(vmem_limit_bytes=VMEM_LIMIT),
         cost_estimate=pl.CostEstimate(
-            flops=10 * rows * ins[0].shape[1],
+            flops=work * rows * ins[0].shape[1],
             bytes_accessed=sum(x.size * x.dtype.itemsize for x in list(ins) + list(outs)),
             transcendentals=0,
         ),
@@ -964,6 +964,7 @@
             jax.ShapeDtypeStruct((1, shape[1]), F32),
         ],
         "norm_back",
+        work=1000000,
     )
 
 
@@ -1192,16 +1193,13 @@
     if last >= 2:
         scatter(2)
     got = partner(other, 2)
-    sums = gateup_grads(sums, second_in, (0, cuts[2]))
     mine = after(mine, *known(sums[:2]))
     middle_grad, attn_low, second_gain = norm_back(
         middle, mine, got, norm_gains[1:], own_grad
     )
+    sums = gateup_grads(sums, after(second_in, attn_low), (0, cuts[2]))
     sums = down_grads(sums, after(hidden, attn_low), (0, cuts[3]))
-    feed_sent, feed_kept = project_rows(
-        [after(hidden, *known(sums[:2]))], w_down, None, False, 512
-    )
-    attn_grad = spread_share(attn_low, feed_kept)
+    attn_grad = spread_share(attn_low, *known(sums[:2]))
     sums = grad_blocks(
         mixed,
         attn_grad,
@@ -1216,7 +1214,10 @@
     if last >= 1:
         scatter(1)
 
-    feed_mine, feed_other = near_sum(feed_sent, after(feed_kept, *known(sums[:2])))
+    feed_sent, feed_kept = project_rows(
+        [after(hidden, *known(sums[:2]))], w_down, None, False, 512
+    )
+    feed_mine, feed_other = near_sum(feed_sent, feed_kept)
     mixed_grad = to_heads(attn_grad, after(w_attn_out, feed_other), shares)
     query_grad, kv_grad = attend_back(queries, kv, starts, logs, mixed_grad, cos, sin)
     feed_part = after(feed_mine, query_grad) + partner(feed_other, 2).astype(F32)

time: 603 us -> 595 us (0.987)
  waiting for transfers between devices: 197 us -> 190 us
    unnamed x54 -> x56, local copies, waits for them, and re-layouts: 13.5 us -> 11.2 us
  transfers between devices with their start and end apart: 31 -> 31, of which waited for: 17 -> 16; matrix products, arithmetic and copies ran while one was open for 5% -> 6% of each run, Pallas kernels for 43% -> 45%
where the time goes in v5:
time: 595 us; the launch traced here: 593 us
  Pallas kernels  325 us (55%)
  waiting for transfers between devices  190 us (32%)
  other arithmetic  29.4 us (5%)
  starting transfers between devices  18.1 us (3%)
  local copies, waits for them, and re-layouts  16.1 us (3%)
  between operations  14.6 us (2%)
    all_gather x3, waiting for transfers between devices, on_device(): lax.all_gather(chunk, 'dp', axis=0, tiled=True, axis_index_groups=[plan.r...  114 us
    ppermute x22, waiting for transfers between devices, partner(): return lax.ppermute(values, 'mp', [(i, i ^ bit) for i in range(mp_count)])  63.2 us
    pallas_call x6, Pallas kernels, grad_blocks(): pl.pallas_call(body, grid=(steps,), out_shape=[jax.ShapeDtypeStruct((size...  61.1 us
    pallas_call x4, Pallas kernels, project_rows(): pl.pallas_call(body, grid=(width // tile,), in_specs=[SMEM] * n_order + w...  41.8 us
    pallas_call x1, Pallas kernels, attend_back(): pl.pallas_call(body, grid=(groups,), in_specs=[pl.BlockSpec((1, rows), la...  33.6 us
    pallas_call x3, Pallas kernels, shampoo(): pl.pallas_call(body, out_shape=[jax.ShapeDtypeStruct(weights.shape, F32)]...  32.2 us
    pallas_call x1, Pallas kernels, attend(): pl.pallas_call(body, grid=(groups,), in_specs=[pl.BlockSpec((1, rows), la...  29.4 us
    pallas_call x4, Pallas kernels, rows_call(): pl.pallas_call(body, grid=(rows // step,), in_specs=[spec(x) for x in ins...  26.9 us
  transfers between devices with their start and end apart: 31, of which 16 were waited for; matrix products, arithmetic and copies ran while one was open for 6% of the time, Pallas kernels for 45%

profile of v5, /device:TPU:0, one launch (start us, length us, event | category | flops | bytes accessed | tf_op | source)
XLA Modules:
  0.0 592.7 jit_solution(11622627850882467141)
XLA Ops:
  8.5 4.9 sort_blocks.1
  17.1 11.1 %first_norm.1.x_ref.refs_0_ = bf16[1024,2048]{1,0:T(8,128)(2,1)} custom-call(bf16[1024,2048]{1,0:T(8,128)(2,1)} %bitcast.48, f32[1,2048]{1,0:T(1,128)} %get-tuple-element.234.gain_ref), custom_call_target="tpu_custom_call" | custom-call | flops 20971520 | bytes 8396800 | tf_op jit(solution)/shard_map/first_norm/pallas_call | solution.py:865
  28.3 1.9 fusion
  30.2 1.9 pad_maximum_fusion.2
  33.2 2.6 multiply_reduce_fusion
  38.2 2.3 pad_maximum_fusion.g_ref.refs_3_.refs_1_
  40.6 28.5 %all-gather.4.cloned.1.call-done.refs_4_ = bf16[144,128,128]{2,1,0:T(8,128)(2,1)} async-done(((bf16[18,128,128]{2,1,0:T(8,128)(2,1)}), bf16[144,128,128]{2,1,0:T(8,128)(2,1)}) %all-gather.4.cloned.1.call-update) | async-done | bytes 4718608 | tf_op jit(solution)/shard_map/all_gather | solution.py:1089
  69.1 5.2 place_blocks.4
  74.3 11.6 %project_heads.1 = (bf16[1024,512]{1,0:T(8,128)(2,1)}, bf16[1024,128]{1,0:T(8,128)(2,1)}) custom-call(bf16[1024,2048]{1,0:T(8,128)(2,1)} %first_norm.1.x_ref.refs_0_, bf16[2048,640]{1,0:T(8,128)(2,1)} %get-tuple-element.111.w_ref.refs_3_, f32[1024,128]{1,0:T(8,128)} %get-tuple-element.242.cos_ref, f32[1024,128]{1,0:T(8,128)} %get-tuple-element.243.sin_ref), custom_call_target="tpu_custom_call" | custom-call | flops 2684354560 | bytes 8126464 | tf_op jit(solution)/shard_map/project_heads/pallas_call | solution.py:595
  85.8 29.4 %attend.1 = (bf16[1024,512]{1,0:T(8,128)(2,1)}, f32[4,2,1024]{2,1,0:T(2,128)}) custom-call(s32[1,1024]{1,0:T(1,128)} %reduce_window_max.29.start_ref, bf16[1024,512]{1,0:T(8,128)(2,1)} %get-tuple-element.114.q_ref, bf16[1024,128]{1,0:T(8,128)(2,1)} %get-tuple-element.115.kv_ref), custom_call_target="tpu_custom_call" | custom-call | flops 16106127360 | bytes 2097152 | tf_op jit(solution)/shard_map/attend/pallas_call | solution.py:662
  115.3 77.6 %all-gather.6.cloned.1.call-done.refs_1_.refs_2_ = bf16[368,128,128]{2,1,0:T(8,128)(2,1)} async-done(((bf16[46,128,128]{2,1,0:T(8,128)(2,1)}), bf16[368,128,128]{2,1,0:T(8,128)(2,1)}) %all-gather.6.cloned.1.call-update) | async-done | bytes 12058640 | tf_op jit(solution)/shard_map/all_gather | solution.py:1089
  192.8 3.2 place_blocks.5.refs_2_.refs_4_
  196.0 5.8 project_rows.4
  201.8 4.4 collective-permute-done.b_ref.d_ref
  207.5 4.3 add_near.4
  213.3 8.7 %place_blocks.6 = (bf16[2048,2816]{1,0:T(8,128)(2,1)}, bf16[1408,2048]{1,0:T(8,128)(2,1)}) custom-call(s32[690]{0:T(1024)} %constant.81.clone.refs_0_, s32[276]{0:T(512)} %constant.82.clone.refs_1_, bf16[368,128,128]{2,1,0:T(8,128)(2,1)} %all-gather.6.cloned.1.call-done.refs_1_.refs_2_, ...), custom_call_target="tpu_custom_call", output_to_operand_aliasing={{0}: (3, {}), {1}: (4, {})} | custom-call | bytes 21102592 | tf_op jit(solution)/shard_map/place_blocks/pallas_call | solution.py:154
  222.0 15.3 %collective-permute-done.1.b_ref = bf16[256,2048]{1,0:T(8,128)(2,1)S(1)} collective-permute-done((bf16[256,2048]{1,0:T(8,128)(2,1)}, bf16[256,2048]{1,0:T(8,128)(2,1)S(1)}, u32[]{:S(2)}, u32[]{:S(2)}) %collective-permute-start.1) | collective-permute-done | bytes 1048608 | tf_op jit(solution)/shard_map/ppermute | solution.py:1052
  238.3 4.6 second_norm.1
  242.8 1.5 collective-permute-start.2
  244.3 7.8 %all-gather.8.cloned.1.call-done.refs_2_ = bf16[160,128,128]{2,1,0:T(8,128)(2,1)} async-done(((bf16[20,128,128]{2,1,0:T(8,128)(2,1)}), bf16[160,128,128]{2,1,0:T(8,128)(2,1)}) %all-gather.8.cloned.1.call-update) | async-done | bytes 5242896 | tf_op jit(solution)/shard_map/all_gather | solution.py:1089
  252.1 5.5 place_blocks.7
  257.7 12.7 %down_back.1.refs_6_ = f32[1024,1408]{1,0:T(8,128)} custom-call(bf16[1024,2048]{1,0:T(8,128)(2,1)} %pad_maximum_fusion.g_ref.refs_3_.refs_1_, bf16[1408,2048]{1,0:T(8,128)(2,1)} %get-tuple-element.136.w_ref.refs_1_), custom_call_target="tpu_custom_call" | custom-call | flops 5905580032 | bytes 15728640 | tf_op jit(solution)/shard_map/down_back/pallas_call | solution.py:510
  270.3 2.6 collective-permute-done.4.refs_3_
  274.0 20.4 %feed_forward.1 = (bf16[1024,1408]{1,0:T(8,128)(2,1)}, bf16[2,1024,1408]{2,1,0:T(8,128)(2,1)}, bf16[1024,2048]{1,0:T(8,128)(2,1)}) custom-call(bf16[256,2048]{1,0:T(8,128)(2,1)} %get-tuple-element.130.refs_0_, bf16[256,2048]{1,0:T(8,128)(2,1)} %copy-done.22, bf16[256,2048]{1,0:T(8,128)(2,1)} %copy-done.23, bf16[256,2048]{1,0:T(8,128)(2,1)} %copy-done.26, ...), custom_call_target="tpu_custom_call" | custom-call | flops 11811160064 | bytes 30146560 | tf_op jit(solution)/shard_map/feed_forward/pallas_call | solution.py:398
  294.4 18.4 %project_rows.5 = (bf16[512,2048]{1,0:T(8,128)(2,1)}, bf16[512,2048]{1,0:T(8,128)(2,1)}) custom-call(bf16[2,1024,1408]{2,1,0:T(8,128)(2,1)} %get-tuple-element.140.refs_0_.refs_1_, bf16[2048,2816]{1,0:T(8,128)(2,1)} %get-tuple-element.138.refs_4_.refs_5_.refs_1_), custom_call_target="tpu_custom_call" | custom-call | flops 11811160064 | bytes 21495808 | tf_op jit(solution)/shard_map/project_rows/pallas_call | solution.py:472
  312.9 3.7 grad_strips.1.refs_2_
  316.7 4.9 grad_blocks.6
  322.9 4.4 add_near.5
  327.2 1.5 collective-permute-start.6
  328.7 10.1 %grad_blocks.7 = (bf16[368,128,128]{2,1,0:T(8,128)(2,1)}, bf16[160,128,128]{2,1,0:T(8,128)(2,1)}) custom-call(bf16[1024,2048]{1,0:T(8,128)(2,1)} %get-tuple-element.157.refs_0_, bf16[2,1024,1408]{2,1,0:T(8,128)(2,1)} %get-tuple-element.140.refs_0_.refs_1_, ...), custom_call_target="tpu_custom_call", output_to_operand_aliasing={{0}: (2, {}), {1}: (3, {})} | custom-call | flops 8589934592 | bytes 21495808 | tf_op jit(solution)/shard_map/grad_blocks/pallas_call | solution.py:297
  339.0 14.0 %collective-permute-done.6.b_ref = bf16[256,2048]{1,0:T(8,128)(2,1)S(1)} collective-permute-done((bf16[256,2048]{1,0:T(8,128)(2,1)}, bf16[256,2048]{1,0:T(8,128)(2,1)S(1)}, u32[]{:S(2)}, u32[]{:S(2)}) %collective-permute-start.6) | collective-permute-done | bytes 1048608 | tf_op jit(solution)/shard_map/ppermute | solution.py:1052
  353.9 5.6 norm_back.2
  359.5 1.5 collective-permute-start.7
  361.0 16.6 %grad_blocks.8 = (bf16[144,128,128]{2,1,0:T(8,128)(2,1)}, bf16[368,128,128]{2,1,0:T(8,128)(2,1)}) custom-call(bf16[1024,2048]{1,0:T(8,128)(2,1)} %get-tuple-element.157.refs_0_, bf16[2,1024,1408]{2,1,0:T(8,128)(2,1)} %get-tuple-element.140.refs_0_.refs_1_, bf16[368,128,128]{2,1,0:T(8,128)(2,1)} %get-tuple-element.152.refs_2_), custom_call_target="tpu_custom_call", output_to_operand_aliasing={{1}: (2, {})} | custom-call | flops 15032385536 | bytes 21495808 | tf_op jit(solution)/shard_map/grad_blocks/pallas_call | solution.py:297
  377.6 9.8 %grad_blocks.9 = (bf16[144,128,128]{2,1,0:T(8,128)(2,1)}, bf16[368,128,128]{2,1,0:T(8,128)(2,1)}) custom-call(bf16[1024,1408]{1,0:T(8,128)(2,1)} %get-tuple-element.165.refs_2_.refs_0_, bf16[1024,2048]{1,0:T(8,128)(2,1)} %pad_maximum_fusion.g_ref.refs_3_.refs_1_, ...), custom_call_target="tpu_custom_call", output_to_operand_aliasing={{0}: (2, {}), {1}: (3, {})} | custom-call | flops 8858370048 | bytes 12845056 | tf_op jit(solution)/shard_map/grad_blocks/pallas_call | solution.py:297
  388.1 2.3 collective-permute-done.9.refs_5_.refs_3_
  391.4 7.4 %grad_blocks.10 = (bf16[144,128,128]{2,1,0:T(8,128)(2,1)}, bf16[368,128,128]{2,1,0:T(8,128)(2,1)}) custom-call(s32[4]{0:T(128)} %broadcast_xor_fusion.refs_0_.order_ref, bf16[1024,512]{1,0:T(8,128)(2,1)} %get-tuple-element.116.refs_1_, bf16[256,2048]{1,0:T(8,128)(2,1)} %get-tuple-element.155.refs_2_.refs_0_, ...), custom_call_target="tpu_custom_call", output_to_operand_aliasing={{0}: (6, {}), {1}: (7, {})} | custom-call | flops 4294967296 | bytes 7340032 | tf_op jit(solution)/shard_map/grad_blocks/pallas_call | solution.py:297
  398.8 10.6 %project_rows.6 = (bf16[512,2048]{1,0:T(8,128)(2,1)}, bf16[512,2048]{1,0:T(8,128)(2,1)}) custom-call(bf16[1024,1408]{1,0:T(8,128)(2,1)} %get-tuple-element.165.refs_2_.refs_0_, bf16[1408,2048]{1,0:T(8,128)(2,1)} %get-tuple-element.136.w_ref.refs_1_), custom_call_target="tpu_custom_call" | custom-call | flops 5905580032 | bytes 12845056 | tf_op jit(solution)/shard_map/project_rows/pallas_call | solution.py:472
  409.8 4.0 collective-permute-done.10.b_ref.d_ref
  415.2 4.3 add_near.6
  420.2 6.3 %to_heads.1.g_ref = bf16[1024,512]{1,0:T(8,128)(2,1)} custom-call(s32[4]{0:T(128)} %broadcast_xor_fusion.refs_0_.order_ref, bf16[256,2048]{1,0:T(8,128)(2,1)} %get-tuple-element.155.refs_2_.refs_0_, bf16[256,2048]{1,0:T(8,128)(2,1)} %copy-done.11, bf16[256,2048]{1,0:T(8,128)(2,1)} %copy-done.12, bf16[256,2048]{1,0:T(8,128)(2,1)} %copy-done.13, ...), custom_call_target="tpu_custom_call" | custom-call | flops 2147483648 | bytes 6291456 | tf_op jit(solution)/shard_map/to_heads/pallas_call | solution.py:541
  426.5 33.6 %attend_back.1 = (bf16[1024,512]{1,0:T(8,128)(2,1)}, bf16[1024,128]{1,0:T(8,128)(2,1)}) custom-call(s32[1,1024]{1,0:T(1,128)} %reduce_window_max.29.start_ref, bf16[1024,512]{1,0:T(8,128)(2,1)} %get-tuple-element.114.q_ref, bf16[1024,128]{1,0:T(8,128)(2,1)} %get-tuple-element.115.kv_ref, f32[4,2,1024]{2,1,0:T(2,128)} %get-tuple-element.169.log_ref, ...), custom_call_target="tpu_custom_call" | custom-call | flops 42949672960 | bytes 8388608 | tf_op jit(solution)/shard_map/attend_back/pallas_call | solution.py:737
  460.2 3.1 add_convert_fusion
  463.2 6.9 %project_rows.7 = (bf16[512,2048]{1,0:T(8,128)(2,1)}, bf16[512,2048]{1,0:T(8,128)(2,1)}) custom-call(s32[4]{0:T(128)} %broadcast_xor_fusion.refs_0_.order_ref, bf16[1024,512]{1,0:T(8,128)(2,1)} %get-tuple-element.174.refs_1_, bf16[1024,128]{1,0:T(8,128)(2,1)} %get-tuple-element.175.refs_2_, bf16[2048,640]{1,0:T(8,128)(2,1)} %get-tuple-element.111.w_ref.refs_3_), custom_call_target="tpu_custom_call" | custom-call | flops 2684354560 | bytes 8126464 | tf_op jit(solution)/shard_map/project_rows/pallas_call | solution.py:472
  470.2 4.2 multiply_reduce_fusion.1
  474.4 1.5 collective-permute-start.13
  475.9 2.3 collective-permute-done.13
  480.2 4.3 add_near.7
  486.0 12.3 %grad_blocks.11 = bf16[144,128,128]{2,1,0:T(8,128)(2,1)} custom-call(bf16[1024,2048]{1,0:T(8,128)(2,1)} %first_norm.1.x_ref.refs_0_, bf16[1024,512]{1,0:T(8,128)(2,1)} %get-tuple-element.174.refs_1_, bf16[1024,128]{1,0:T(8,128)(2,1)} %get-tuple-element.175.refs_2_, bf16[144,128,128]{2,1,0:T(8,128)(2,1)} %get-tuple-element.163.refs_3_), custom_call_target="tpu_custom_call", output_to_operand_aliasing={{}: (3, {})} | custom-call | flops 5368709120 | bytes 8126464 | tf_op jit(solution)/shard_map/grad_blocks/pallas_call | solution.py:297
  498.3 11.3 %collective-permute-done.14.b_ref = bf16[256,2048]{1,0:T(8,128)(2,1)S(1)} collective-permute-done((bf16[256,2048]{1,0:T(8,128)(2,1)}, bf16[256,2048]{1,0:T(8,128)(2,1)S(1)}, u32[]{:S(2)}, u32[]{:S(2)}) %collective-permute-start.14) | collective-permute-done | bytes 1048608 | tf_op jit(solution)/shard_map/ppermute | solution.py:1052
  510.5 5.6 norm_back.3
  519.4 8.5 %shampoo.3 = (f32[84,128,128]{2,1,0:T(8,128)}, f32[84,128,128]{2,1,0:T(8,128)}, f32[84,128,128]{2,1,0:T(8,128)}, f32[84,128,128]{2,1,0:T(8,128)}, f32[84,128,128]{2,1,0:T(8,128)}) custom-call(s32[20]{0:T(128)} %slice_bitcast_fusion.1.places_ref, bf16[20,128,128]{2,1,0:T(8,128)(2,1)} %reduce-scatter.6.cloned.1.call-done.g_ref, f32[84,128,128]{2,1,0:T(8,128)} %refs_0_.9, ...), custom_call_target="tpu_custom_call" | custom-call | flops 335544320 | bytes 15073280 | tf_op jit(solution)/shard_map/shampoo/pallas_call | solution.py:835
  527.9 15.9 %shampoo.4 = (f32[84,128,128]{2,1,0:T(8,128)}, f32[84,128,128]{2,1,0:T(8,128)}, f32[84,128,128]{2,1,0:T(8,128)}, f32[84,128,128]{2,1,0:T(8,128)}, f32[84,128,128]{2,1,0:T(8,128)}) custom-call(s32[46]{0:T(128)} %slice_bitcast_fusion.2.places_ref, ...), custom_call_target="tpu_custom_call", output_to_operand_aliasing={{0}: (8, {}), {1}: (9, {}), {2}: (10, {}), {3}: (11, {}), {... | custom-call | flops 771751936 | bytes 34668544 | tf_op jit(solution)/shard_map/shampoo/pallas_call | solution.py:835
  544.4 2.1 collective-permute-done.21
  546.6 1.5 collective-permute-start.22
  548.1 2.8 collective-permute-done.22
  551.9 3.3 collective-permute-done.23
  555.2 1.9 collective-permute-start.24
  557.7 5.0 collective-permute-done.19
  564.0 2.2 broadcast_select_fusion.11
  566.2 2.3 maximum_bitcast_fusion
  568.9 3.9 maximum_convert_fusion
  572.8 5.2 reduce-scatter.8.cloned.1.call-done.g_ref
  577.9 7.9 %shampoo.5 = (f32[84,128,128]{2,1,0:T(8,128)}, f32[84,128,128]{2,1,0:T(8,128)}, f32[84,128,128]{2,1,0:T(8,128)}, f32[84,128,128]{2,1,0:T(8,128)}, f32[84,128,128]{2,1,0:T(8,128)}) custom-call(s32[18]{0:T(128)} %slice_bitcast_fusion.places_ref, ...), custom_call_target="tpu_custom_call", output_to_operand_aliasing={{0}: (8, {}), {1}: (9, {}), {2}: (10, {}), {3}: (11, {}), {... | custom-call | flops 301989888 | bytes 13565952 | tf_op jit(solution)/shard_map/shampoo/pallas_call | solution.py:835
  (133 shorter events, 31.4 us)
Async XLA Ops:
  7.2 7.7 %copy-start.18 = (s32[1,1024]{1,0:T(1,128)S(1)}, s32[1,1024]{1,0:T(1,128)}, u32[]{:S(2)}) copy-start(s32[1,1024]{1,0:T(1,128)} %param.25) | copy-start | bytes 12292
  7.2 8.6 %copy-start.17 = (f32[2,2048]{1,0:T(2,128)S(1)}, f32[2,2048]{1,0:T(2,128)}, u32[]{:S(2)}) copy-start(f32[2,2048]{1,0:T(2,128)} %param.26) | copy-start | bytes 49156
  7.2 61.9 %all-gather.4.cloned.1.call-start = ((), (), s32[]{:S(2)}) async-start(), calls=%async_computation.3 | async-start | bytes 5308416 | tf_op jit(solution)/shard_map/all_gather | solution.py:1089
  13.4 179.5 %all-gather.6.cloned.1.call-start = ((), (), s32[]{:S(2)}) async-start(), calls=%async_computation.4 | async-start | bytes 13565952 | tf_op jit(solution)/shard_map/all_gather | solution.py:1089
  14.1 238.0 %all-gather.8.cloned.1.call-start = ((), (), s32[]{:S(2)}) async-start(), calls=%async_computation.5 | async-start | bytes 5898240 | tf_op jit(solution)/shard_map/all_gather | solution.py:1089
  14.9 504.5 %reduce-scatter.6.cloned.1.call-start = ((), (), s32[]{:S(2)}) async-start(), calls=%async_computation.7 | async-start | bytes 5898240 | tf_op jit(solution)/shard_map/reduce_scatter | solution.py:1145
  17.1 11.2 %copy-start.20 = (s32[1,1024]{1,0:T(1,128)S(1)}, s32[1,1024]{1,0:T(1,128)}, u32[]{:S(2)}) copy-start(s32[1,1024]{1,0:T(1,128)} %param.24) | copy-start | bytes 12292
  28.2 3.9 copy-start.27
  28.2 4.4 copy-start
  33.2 2.7 copy-start.1
  33.2 4.1 copy-start.6
  38.2 2.4 copy-start.8
  201.8 4.4 collective-permute-start
  206.2 1.3 copy-start.4
  211.9 25.4 %collective-permute-start.1 = (bf16[256,2048]{1,0:T(8,128)(2,1)}, bf16[256,2048]{1,0:T(8,128)(2,1)S(1)}, u32[]{:S(2)}, u32[]{:S(2)}) collective-permute-start(bf16[256,2048]{1,0:T(8,128)(2,1)} %get-tuple-element.122), channel_id=1, source_target_pairs={{0,2},{1,3},{2,0},{3,1},{4,6},{5,7},{6,4},{7,5},{8,10},{9,11},{10,... | collective-permute-start | bytes 3145736 | tf_op jit(solution)/shard_map/ppermute | solution.py:1052
  237.3 1.0 copy-start.14
  242.8 27.5 %collective-permute-start.2 = (bf16[256,2048]{1,0:T(8,128)(2,1)}, bf16[256,2048]{1,0:T(8,128)(2,1)S(1)}, u32[]{:S(2)}, u32[]{:S(2)}) collective-permute-start(bf16[256,2048]{1,0:T(8,128)(2,1)} %get-tuple-element.130.refs_0_), channel_id=1, source_target_pairs={{0,2},{1,3},{2,0},{3,1},{4,6},{5,7},{6,4},{7,5},{8,10},{9,11},{10,... | collective-permute-start | bytes 3145736 | tf_op jit(solution)/shard_map/ppermute | solution.py:1052
  244.3 26.0 %collective-permute-start.3 = (bf16[256,2048]{1,0:T(8,128)(2,1)}, bf16[256,2048]{1,0:T(8,128)(2,1)S(1)}, u32[]{:S(2)}, u32[]{:S(2)}) collective-permute-start(bf16[256,2048]{1,0:T(8,128)(2,1)} %get-tuple-element.130.refs_0_), channel_id=1, source_target_pairs={{0,1},{1,0},{2,3},{3,2},{4,5},{5,4},{6,7},{7,6},{8,9},{9,8},{10,11... | collective-permute-start | bytes 3145736 | tf_op jit(solution)/shard_map/ppermute | solution.py:1052
  270.3 2.7 copy-start.22
  270.3 2.7 collective-permute-start.4
  270.3 2.6 copy-start.23
  273.0 1.0 copy-start.26
  312.8 8.7 %collective-permute-start.5 = (bf16[512,2048]{1,0:T(8,128)(2,1)}, bf16[512,2048]{1,0:T(8,128)(2,1)S(1)}, u32[]{:S(2)}, u32[]{:S(2)}) collective-permute-start(bf16[512,2048]{1,0:T(8,128)(2,1)} %get-tuple-element.142), channel_id=1, source_target_pairs={{0,1},{1,0},{2,3},{3,2},{4,5},{5,4},{6,7},{7,6},{8,9},{9,8},{10,11... | collective-permute-start | bytes 6291464 | tf_op jit(solution)/shard_map/ppermute | solution.py:1052
  321.6 1.3 copy-start.3
  327.2 25.7 %collective-permute-start.6 = (bf16[256,2048]{1,0:T(8,128)(2,1)}, bf16[256,2048]{1,0:T(8,128)(2,1)S(1)}, u32[]{:S(2)}, u32[]{:S(2)}) collective-permute-start(bf16[256,2048]{1,0:T(8,128)(2,1)} %get-tuple-element.150), channel_id=1, source_target_pairs={{0,2},{1,3},{2,0},{3,1},{4,6},{5,7},{6,4},{7,5},{8,10},{9,11},{10,... | collective-permute-start | bytes 3145736 | tf_op jit(solution)/shard_map/ppermute | solution.py:1052
  338.9 189.0 %reduce-scatter.4.cloned.1.call-start = ((), (), s32[]{:S(2)}) async-start(), calls=%async_computation.6 | async-start | bytes 13565952 | tf_op jit(solution)/shard_map/reduce_scatter | solution.py:1145
  352.9 1.0 copy-start.24
  359.5 27.9 %collective-permute-start.7 = (bf16[256,2048]{1,0:T(8,128)(2,1)}, bf16[256,2048]{1,0:T(8,128)(2,1)S(1)}, u32[]{:S(2)}, u32[]{:S(2)}) collective-permute-start(bf16[256,2048]{1,0:T(8,128)(2,1)} %get-tuple-element.155.refs_2_.refs_0_), channel_id=1, source_target_pairs={{0,2},{1,3},{2,0},{3,1},{4,6},{5,7},{6,4},{7,5},{8,10},{9,11},{10,... | collective-permute-start | bytes 3145736 | tf_op jit(solution)/shard_map/ppermute | solution.py:1052
  361.0 27.1 %collective-permute-start.8 = (bf16[256,2048]{1,0:T(8,128)(2,1)}, bf16[256,2048]{1,0:T(8,128)(2,1)S(1)}, u32[]{:S(2)}, u32[]{:S(2)}) collective-permute-start(bf16[256,2048]{1,0:T(8,128)(2,1)} %get-tuple-element.155.refs_2_.refs_0_), channel_id=1, source_target_pairs={{0,1},{1,0},{2,3},{3,2},{4,5},{5,4},{6,7},{7,6},{8,9},{9,8},{10,11... | collective-permute-start | bytes 3145736 | tf_op jit(solution)/shard_map/ppermute | solution.py:1052
  387.5 2.9 copy-start.11
  387.5 2.9 collective-permute-start.9
  388.1 2.3 copy-start.12
  390.4 1.0 copy-start.13
  398.8 179.2 %reduce-scatter.8.cloned.1.call-start = ((), (), s32[]{:S(2)}) async-start(), calls=%async_computation.8 | async-start | bytes 5308416 | tf_op jit(solution)/shard_map/reduce_scatter | solution.py:1145
  409.4 4.4 collective-permute-start.10
  413.8 1.3 copy-start.5
  419.5 40.7 %collective-permute-start.11 = (bf16[256,2048]{1,0:T(8,128)(2,1)}, bf16[256,2048]{1,0:T(8,128)(2,1)S(1)}, u32[]{:S(2)}, u32[]{:S(2)}) collective-permute-start(bf16[256,2048]{1,0:T(8,128)(2,1)} %get-tuple-element.170), channel_id=1, source_target_pairs={{0,2},{1,3},{2,0},{3,1},{4,6},{5,7},{6,4},{7,5},{8,10},{9,11},{10,... | collective-permute-start | bytes 3145736 | tf_op jit(solution)/shard_map/ppermute | solution.py:1052
  426.5 33.7 %copy-start.9 = (f32[256,2048]{1,0:T(8,128)S(1)}, f32[256,2048]{1,0:T(8,128)}, u32[]{:S(2)}) copy-start(f32[256,2048]{1,0:T(8,128)} %get-tuple-element.129.x_ref) | copy-start | bytes 6291460
  463.2 6.9 %copy-start.19 = (f32[1024]{0:T(1024)S(1)}, f32[1024]{0:T(1024)}, u32[]{:S(2)}) copy-start(f32[1024]{0:T(1024)} %add_rsqrt_fusion) | copy-start | bytes 12292
  470.1 8.7 %collective-permute-start.12 = (bf16[512,2048]{1,0:T(8,128)(2,1)}, bf16[512,2048]{1,0:T(8,128)(2,1)S(1)}, u32[]{:S(2)}, u32[]{:S(2)}) collective-permute-start(bf16[512,2048]{1,0:T(8,128)(2,1)} %get-tuple-element.177), channel_id=1, source_target_pairs={{0,1},{1,0},{2,3},{3,2},{4,5},{5,4},{6,7},{7,6},{8,9},{9,8},{10,11... | collective-permute-start | bytes 6291464 | tf_op jit(solution)/shard_map/ppermute | solution.py:1052
  470.1 4.2 copy-start.16
  474.4 3.8 collective-permute-start.13
  478.8 1.3 copy-start.2
  484.5 25.0 %collective-permute-start.14 = (bf16[256,2048]{1,0:T(8,128)(2,1)}, bf16[256,2048]{1,0:T(8,128)(2,1)S(1)}, u32[]{:S(2)}, u32[]{:S(2)}) collective-permute-start(bf16[256,2048]{1,0:T(8,128)(2,1)} %get-tuple-element.183), channel_id=1, source_target_pairs={{0,2},{1,3},{2,0},{3,1},{4,6},{5,7},{6,4},{7,5},{8,10},{9,11},{10,... | collective-permute-start | bytes 3145736 | tf_op jit(solution)/shard_map/ppermute | solution.py:1052
  509.5 1.0 copy-start.25
  510.5 5.6 copy-start.7
  510.5 7.1 %copy-start.21 = (s32[1,84]{1,0:T(1,128)S(1)}, s32[1,84]{1,0:T(1,128)}, u32[]{:S(2)}) copy-start(s32[1,84]{1,0:T(1,128)} %get-tuple-element.238) | copy-start | bytes 1012
  516.1 27.7 %collective-permute-start.16 = (bf16[256,2048]{1,0:T(8,128)(2,1)S(1)}, bf16[256,2048]{1,0:T(8,128)(2,1)}, u32[]{:S(2)}, u32[]{:S(2)}) collective-permute-start(bf16[256,2048]{1,0:T(8,128)(2,1)S(1)} %copy-done.7), channel_id=1, source_target_pairs={{0,2},{1,3},{2,0},{3,1},{4,6},{5,7},{6,4},{7,5},{8,10},{9,11},{10,... | collective-permute-start | bytes 3145736 | tf_op jit(solution)/shard_map/ppermute | solution.py:1052
  518.2 44.5 %collective-permute-start.19 = (bf16[256,2048]{1,0:T(8,128)(2,1)}, bf16[256,2048]{1,0:T(8,128)(2,1)S(1)}, u32[]{:S(2)}, u32[]{:S(2)}) collective-permute-start(bf16[256,2048]{1,0:T(8,128)(2,1)} %get-tuple-element.187), channel_id=1, source_target_pairs={{0,2},{1,3},{2,0},{3,1},{4,6},{5,7},{6,4},{7,5},{8,10},{9,11},{10,... | collective-permute-start | bytes 3145736 | tf_op jit(solution)/shard_map/ppermute | solution.py:1052
  519.4 44.6 %collective-permute-start.15 = (bf16[256,2048]{1,0:T(8,128)(2,1)S(1)}, bf16[256,2048]{1,0:T(8,128)(2,1)}, u32[]{:S(2)}, u32[]{:S(2)}) collective-permute-start(bf16[256,2048]{1,0:T(8,128)(2,1)S(1)} %copy-done.7), channel_id=1, source_target_pairs={{0,1},{1,0},{2,3},{3,2},{4,5},{5,4},{6,7},{7,6},{8,9},{9,8},{10,11... | collective-permute-start | bytes 3145736 | tf_op jit(solution)/shard_map/ppermute | solution.py:1052
  527.9 16.5 %copy-start.15 = (f32[2,2048]{1,0:T(2,128)S(1)}, f32[2,2048]{1,0:T(2,128)}, u32[]{:S(2)}) copy-start(f32[2,2048]{1,0:T(2,128)} %fusion.6) | copy-start | bytes 49156
  527.9 29.8 %copy-start.10 = (bf16[256,2048]{1,0:T(8,128)(2,1)S(1)}, bf16[256,2048]{1,0:T(8,128)(2,1)}, u32[]{:S(2)}) copy-start(bf16[256,2048]{1,0:T(8,128)(2,1)} %get-tuple-element.187) | copy-start | bytes 3145732
  543.8 20.2 %collective-permute-start.17 = (bf16[256,2048]{1,0:T(8,128)(2,1)}, bf16[256,2048]{1,0:T(8,128)(2,1)}, u32[]{:S(2)}, u32[]{:S(2)}) collective-permute-start(bf16[256,2048]{1,0:T(8,128)(2,1)} %collective-permute-done.16), channel_id=1, source_target_pairs={{0,1},{1,0},{2,3},{3,2},{4,5},{5,4},{6,7},{7,6},{8,9},{9,8},{10,11... | collective-permute-start | bytes 3145736 | tf_op jit(solution)/shard_map/ppermute | solution.py:1052
  544.3 2.2 collective-permute-start.21
  546.6 4.3 collective-permute-start.22
  550.9 4.3 collective-permute-start.23
  555.2 7.5 %collective-permute-start.24 = (f32[2,2048]{1,0:T(2,128)S(1)}, f32[2,2048]{1,0:T(2,128)S(1)}, u32[]{:S(2)}, u32[]{:S(2)}) collective-permute-start(f32[2,2048]{1,0:T(2,128)S(1)} %add.103), channel_id=1, source_target_pairs={{0,16},{4,20},{8,24},{12,28},{16,0},{20,4},{24,8},{28,12},{1,17},{... | collective-permute-start | bytes 49160 | tf_op jit(solution)/shard_map/ppermute | solution.py:1287
  557.7 10.8 %collective-permute-start.18 = (bf16[256,2048]{1,0:T(8,128)(2,1)S(1)}, bf16[256,2048]{1,0:T(8,128)(2,1)S(1)}, u32[]{:S(2)}, u32[]{:S(2)}) collective-permute-start(bf16[256,2048]{1,0:T(8,128)(2,1)S(1)} %copy-done.10), channel_id=1, source_target_pairs={{0,1},{1,0},{2,3},{3,2},{4,5},{5,4},{6,7},{7,6},{8,9},{9,8},{10,11... | collective-permute-start | bytes 3145736 | tf_op jit(solution)/shard_map/ppermute | solution.py:1052
  562.7 5.8 collective-permute-start.20
Sparse Core Ops, SparseCore 0:
  13.5 55.5 all-gather.3
  71.2 121.6 all-gather.5
  194.4 57.7 all-gather.7
  339.0 57.5 reduce-scatter.5
  398.9 122.7 reduce-scatter.3
  523.9 54.0 reduce-scatter.7

commit v6 on v5

--- a/solution.py
+++ b/solution.py
@@ -93,12 +93,22 @@
 
 def sort_blocks(weights, order, chunks):
     block = weights.shape[1:]
-
-    def body(order_ref, w_ref, *outs):
+    total = sum(n for _, n in chunks)
+    begin = chunks[0][0]
+
+    def body(order_ref, w_ref, *refs):
+        outs, (given, sem) = refs[: len(chunks)], refs[len(chunks) :]
+
+        def load(j, carry):
+            pltpu.make_async_copy(w_ref.at[order_ref[begin + j]], given.at[j], sem).start()
+            return carry
+
+        lax.fori_loop(0, total, load, 0)
+        pltpu.make_async_copy(given, given, sem).wait()
         for (start, count), out in zip(chunks, outs):
 
             def one(j, carry, start=start, out=out):
-                out[j] = w_ref[order_ref[start + j]].astype(LOW)
+                out[j] = given[start - begin + j].astype(LOW)
                 return carry
 
             lax.fori_loop(0, count, one, 0)
@@ -106,8 +116,9 @@
     return pl.pallas_call(
         body,
         out_shape=[jax.ShapeDtypeStruct((n,) + block, LOW) for _, n in chunks],
-        in_specs=[SMEM, VMEM],
+        in_specs=[SMEM, ANY],
         out_specs=[VMEM] * len(chunks),
+        scratch_shapes=[pltpu.VMEM((total,) + block, F32), pltpu.SemaphoreType.DMA],
         compiler_params=pltpu.CompilerParams(vmem_limit_bytes=VMEM_LIMIT),
         name="sort_blocks",
     )(order, weights)
@@ -269,7 +280,8 @@
                     ]
             return carry
 
-        few = rows // 2 if rows % 2 == 0 else rows
+        parts = 1 if first > 0 or rows < 8 else 2
+        few = rows // parts if rows % parts == 0 else rows
         lax.fori_loop(0, rows // few, some, 0)
         for step in range(steps):
 
@@ -323,7 +335,7 @@
     return merged
 
 
-def grad_strips(strips, buffer_size, block):
+def grad_strips(strips, buffer, block):
     def body(*refs):
         out, stage, sem = refs[-3:]
         at = 0
@@ -355,9 +367,10 @@
     return pl.pallas_call(
         body,
         grid=(1,),
-        in_specs=specs,
+        in_specs=specs + [ANY],
         out_specs=ANY,
-        out_shape=jax.ShapeDtypeStruct((buffer_size, block, block), LOW),
+        out_shape=jax.ShapeDtypeStruct(buffer.shape, LOW),
+        input_output_aliases={len(specs): 0},
         scratch_shapes=[pltpu.VMEM((count, block, block), LOW), pltpu.SemaphoreType.DMA],
         compiler_params=pltpu.CompilerParams(vmem_limit_bytes=VMEM_LIMIT),
         cost_estimate=pl.CostEstimate(
@@ -366,62 +379,90 @@
             transcendentals=0,
         ),
         name="grad_strips",
-    )(*values)
+    )(*values, buffer)
 
 
 def feed_forward(pieces, weights, hidden_grad, block):
     share, width = pieces[0].shape
-    rows = share * len(pieces)
+    count = len(pieces)
+    rows = share * count
+    half = rows // 2
     hidden = weights.shape[1] // 2
     steps = hidden // block
+    tile = 2 * block
 
     def body(*refs):
-        gate_w, up_w, grad_ref, hid_ref, out_ref, joined = refs[len(pieces) :]
-
-        @pl.when(pl.program_id(0) == 0)
+        gate_w, up_w, grad_ref, row_w = refs[count : count + 4]
+        hid_ref, out_ref, joined, kept_ref, sent_ref, held = refs[count + 4 :]
+        t = pl.program_id(0)
+
+        @pl.when(t == 0)
         def _():
-            fill(joined, refs[: len(pieces)], None)
-
-        both = jnp.dot(
-            joined[...],
-            jnp.concatenate([gate_w[...], up_w[...]], axis=1),
-            preferred_element_type=F32,
-        )
-        gate, up = both[:, :block], both[:, block:]
-        grad = grad_ref[...]
-        sig = jax.nn.sigmoid(gate)
-        act = gate * sig
-        hid_ref[...] = (act * up).astype(LOW)
-        out_ref[0] = (grad * up * sig * (1.0 + gate * (1.0 - sig))).astype(LOW)
-        out_ref[1] = (grad * act).astype(LOW)
-
-    return pl.pallas_call(
-        body,
-        grid=(steps,),
-        in_specs=[pl.BlockSpec((share, width), lambda j: (0, 0))] * len(pieces)
+            fill(joined, refs[:count], None)
+
+        @pl.when(t < steps)
+        def _():
+            both = dot(joined[...], jnp.concatenate([gate_w[...], up_w[...]], axis=1))
+            gate, up = both[:, :block], both[:, block:]
+            grad = grad_ref[...]
+            sig = jax.nn.sigmoid(gate)
+            act = gate * sig
+            hid_ref[...] = (act * up).astype(LOW)
+            here = pl.ds(pl.multiple_of(t * block, block), block)
+            gate_grad = (grad * up * sig * (1.0 + gate * (1.0 - sig))).astype(LOW)
+            up_grad = (grad * act).astype(LOW)
+            out_ref[0] = gate_grad
+            out_ref[1] = up_grad
+            held[0, :, here] = gate_grad
+            held[1, :, here] = up_grad
+
+        @pl.when(t >= steps)
+        def _():
+            total = dot_turned(held[0], row_w[:, :hidden]) + dot_turned(held[1], row_w[:, hidden:])
+            total = total.astype(LOW)
+            kept_ref[...] = total[:half]
+            sent_ref[...] = total[half:]
+
+    def first(j):
+        return jnp.minimum(j, steps - 1)
+
+    def second(j):
+        return jnp.maximum(j - steps, 0)
+
+    hid, grads, joined, kept, sent = pl.pallas_call(
+        body,
+        grid=(steps + width // tile,),
+        in_specs=[pl.BlockSpec((share, width), lambda j: (0, 0))] * count
         + [
-            pl.BlockSpec((width, block), lambda j: (0, j)),
-            pl.BlockSpec((width, block), lambda j: (0, steps + j)),
-            pl.BlockSpec((rows, block), lambda j: (0, j)),
+            pl.BlockSpec((width, block), lambda j: (0, first(j))),
+            pl.BlockSpec((width, block), lambda j: (0, steps + first(j))),
+            pl.BlockSpec((rows, block), lambda j: (0, first(j))),
+            pl.BlockSpec((tile, 2 * hidden), lambda j: (second(j), 0)),
         ],
         out_specs=[
-            pl.BlockSpec((rows, block), lambda j: (0, j)),
-            pl.BlockSpec((2, rows, block), lambda j: (0, 0, j)),
+            pl.BlockSpec((rows, block), lambda j: (0, first(j))),
+            pl.BlockSpec((2, rows, block), lambda j: (0, 0, first(j))),
             pl.BlockSpec((rows, width), lambda j: (0, 0)),
+            pl.BlockSpec((half, tile), lambda j: (0, second(j))),
+            pl.BlockSpec((half, tile), lambda j: (0, second(j))),
         ],
         out_shape=[
             jax.ShapeDtypeStruct((rows, hidden), LOW),
             jax.ShapeDtypeStruct((2, rows, hidden), LOW),
             jax.ShapeDtypeStruct((rows, width), LOW),
+            jax.ShapeDtypeStruct((half, width), LOW),
+            jax.ShapeDtypeStruct((half, width), LOW),
         ],
+        scratch_shapes=[pltpu.VMEM((2, rows, hidden), LOW)],
         compiler_params=pltpu.CompilerParams(vmem_limit_bytes=VMEM_LIMIT),
         cost_estimate=pl.CostEstimate(
-            flops=4 * rows * width * hidden,
-            bytes_accessed=2 * rows * width + 4 * width * hidden + 10 * rows * hidden,
+            flops=8 * rows * width * hidden,
+            bytes_accessed=2 * rows * width + 8 * width * hidden + 10 * rows * hidden,
             transcendentals=rows * hidden,
         ),
         name="feed_forward",
-    )(*pieces, weights, weights, hidden_grad)
+    )(*pieces, weights, weights, hidden_grad, weights)
+    return hid, grads, joined, sent, kept
 
 
 def project_rows(parts, weights, order, turned, tile):
@@ -493,27 +534,31 @@
     tile = 2 * LANES
     full, rest = divmod(hidden, tile)
 
-    def body(g_ref, w_ref, o_ref):
+    def body(g_ref, w_ref, *refs):
+        o_ref = refs[-1]
         t = pl.program_id(0)
 
         @pl.when(t < full)
         def _():
-            here = pl.ds(pl.multiple_of(t * tile, tile), tile)
-            o_ref[...] = dot_turned(g_ref[...], w_ref[here])
+            o_ref[...] = dot_turned(g_ref[...], w_ref[...])
 
         if rest:
 
             @pl.when(t == full)
             def _():
-                o_ref[:, :rest] = dot_turned(g_ref[...], w_ref[full * tile :])
-
+                o_ref[:, :rest] = dot_turned(g_ref[...], refs[0][...])
+
+    assert rest == 0 or hidden % rest == 0
+    specs = [
+        pl.BlockSpec((rows, depth), lambda j: (0, 0)),
+        pl.BlockSpec((tile, depth), lambda j: (jnp.minimum(j, full - 1), 0)),
+    ]
+    if rest:
+        specs.append(pl.BlockSpec((rest, depth), lambda j: (hidden // rest - 1, 0)))
     return pl.pallas_call(
         body,
         grid=(full + (rest > 0),),
-        in_specs=[
-            pl.BlockSpec((rows, depth), lambda j: (0, 0)),
-            pl.BlockSpec((hidden, depth), lambda j: (0, 0)),
-        ],
+        in_specs=specs,
         out_specs=pl.BlockSpec((rows, tile), lambda j: (0, j)),
         out_shape=jax.ShapeDtypeStruct((rows, hidden), F32),
         compiler_params=pltpu.CompilerParams(vmem_limit_bytes=VMEM_LIMIT),
@@ -523,7 +568,7 @@
             transcendentals=0,
         ),
         name="down_back",
-    )(grads, weights)
+    )(grads, *([weights] * len(specs[1:])))
 
 
 def to_heads(pieces, weights, order):
@@ -531,6 +576,8 @@
     width = weights.shape[0]
 
     rows = share * len(pieces)
+    depth = weights.shape[1]
+    tile = 2 * LANES
 
     def body(order_ref, *refs):
         w_ref, out_ref = refs[-2:]
@@ -540,13 +587,16 @@
 
     return pl.pallas_call(
         body,
-        in_specs=[SMEM] + [VMEM] * (len(pieces) + 1),
-        out_specs=VMEM,
+        grid=(width // tile,),
+        in_specs=[SMEM]
+        + [pl.BlockSpec((share, depth), lambda j: (0, 0))] * len(pieces)
+        + [pl.BlockSpec((tile, depth), lambda j: (j, 0))],
+        out_specs=pl.BlockSpec((rows, tile), lambda j: (0, j)),
         out_shape=jax.ShapeDtypeStruct((rows, width), LOW),
         compiler_params=pltpu.CompilerParams(vmem_limit_bytes=VMEM_LIMIT),
         cost_estimate=pl.CostEstimate(
-            flops=2 * rows * width * weights.shape[1],
-            bytes_accessed=2 * (rows + width) * weights.shape[1],
+            flops=2 * rows * width * depth,
+            bytes_accessed=2 * (rows + width) * depth,
             transcendentals=0,
         ),
         name="to_heads",
@@ -580,15 +630,23 @@
 
     def body(x_ref, w_ref, cos_ref, sin_ref, q_ref, kv_ref):
         t = pl.program_id(0)
-        raw = dot(x_ref[...], w_ref[...])
-
-        @pl.when(t < steps - 1)
-        def _():
-            q_ref[...] = turn(raw, cos_ref[...], sin_ref[...]).astype(LOW) * LOW(HD**-0.5)
-
-        @pl.when(t == steps - 1)
-        def _():
-            kv_ref[...] = turn(raw, *key_tables(cos_ref[...], sin_ref[...])).astype(LOW)
+
+        def one(i, carry):
+            here = pl.ds(pl.multiple_of(i * QUERIES, QUERIES), QUERIES)
+            raw = dot(x_ref[here], w_ref[...])
+
+            @pl.when(t < steps - 1)
+            def _():
+                turned = turn(raw, cos_ref[here], sin_ref[here])
+                q_ref[here] = turned.astype(LOW) * LOW(HD**-0.5)
+
+            @pl.when(t == steps - 1)
+            def _():
+                kv_ref[here] = turn(raw, *key_tables(cos_ref[here], sin_ref[here])).astype(LOW)
+
+            return carry
+
+        lax.fori_loop(0, rows // QUERIES, one, 0)
 
     steps = width // LANES
     whole = pl.BlockSpec((rows, LANES), lambda j: (0, 0))
@@ -767,7 +825,7 @@
 
 def shampoo(sums, places, factor, weights, ema, left, right, left_roots, right_roots, before):
     count, block, _ = sums.shape
-    group = 2 if count % 2 == 0 else 1
+    group = 3 if count % 3 == 0 else 2 if count % 2 == 0 else 1
     steps = count // group
     depth = min(4, steps)
     extra = [] if before is None else list(before)
@@ -854,7 +912,7 @@
     )(places, sums, weights, ema, left, right, left_roots, right_roots, *extra)
 
 
-def rows_call(body, ins, outs, name, step=64, work=10):
+def rows_call(body, ins, outs, name, step=128, work=10):
     rows = max(x.shape[0] for x in ins)
 
     def spec(x):
@@ -881,7 +939,7 @@
 def add_near(kept, got):
     share = kept.shape[0] // 2
     width = kept.shape[1]
-    step = 64
+    step = 128
 
     def body(a_ref, c_ref, b_ref, d_ref, mine_ref, other_ref):
         mine_ref[...] = a_ref[...].astype(F32) + b_ref[...].astype(F32)
@@ -1084,7 +1142,11 @@
             far = after(far, *cover)
         return [mine, far, near, partner(far, 1)]
 
-    sorted_low = sort_blocks(weight_blocks, order, plan.chunks)
+    sorted_low = list(sort_blocks(weight_blocks, order, plan.chunks[:1]))
+    if len(plan.chunks) > 1:
+        sorted_low += sort_blocks(
+            weight_blocks, after(order, *sorted_low), plan.chunks[1:]
+        )
     gathered = [
         lax.all_gather(chunk, "dp", axis=0, tiled=True, axis_index_groups=[plan.ring])
         for chunk in sorted_low
@@ -1134,9 +1196,10 @@
     w_gateup, w_down = matrices[2:]
     hidden_grad = down_back(mlp_grad, w_down)
     second_pieces = spread_share(second_low, hidden_grad)
-    hidden, gateup_grad, second_in = feed_forward(second_pieces, w_gateup, hidden_grad, block)
-
-    second_sent, second_kept = project_rows([gateup_grad], w_gateup, None, True, 256)
+    hidden, gateup_grad, second_in, second_sent, second_kept = feed_forward(
+        second_pieces, w_gateup, hidden_grad, block
+    )
+
     sizes = [dp_count * n for _, n in plan.chunks]
     sums = [None] * len(sizes)
     reduced = [None] * len(sizes)
@@ -1154,6 +1217,20 @@
     if last >= 2:
         cuts = {2: plan.first_late[2], 3: plan.first_late[3] // 2}
         sent = {(last, spot) for *_, spot in plan.strips}
+    def down_grads(sums, hidden, span):
+        table = plan.of_matrix(3, hidden_blocks, row_blocks)
+        return grad_blocks(
+            hidden, [mlp_grad], None, False, table, 2, sums, sizes, block, span, sent
+        )
+
+    def gateup_grads(sums, second_in, span):
+        table = plan.of_matrix(2, row_blocks, 2 * hidden_blocks)
+        return grad_blocks(
+            second_in, [gateup_grad], None, True, table, 2, sums, sizes, block, span, sent
+        )
+
+    sums = down_grads(sums, after(hidden, second_sent), (cuts[3], row_blocks // 2))
+    mine, other = near_sum(second_sent, after(second_kept, *known(sums)))
     if sent:
         strips = {}
         for matrix, r, c, spot in plan.strips:
@@ -1163,7 +1240,7 @@
         sums[last] = grad_strips(
             [
                 (
-                    after(second_in, second_sent) if matrix == 2 else after(hidden, second_sent),
+                    after(second_in, other) if matrix == 2 else hidden,
                     r,
                     gateup_grad if matrix == 2 else mlp_grad,
                     half,
@@ -1171,24 +1248,10 @@
                 )
                 for (matrix, r, half), blocks in strips.items()
             ],
-            sizes[last],
+            sums[last],
             block,
         )
 
-    def down_grads(sums, hidden, span):
-        table = plan.of_matrix(3, hidden_blocks, row_blocks)
-        return grad_blocks(
-            hidden, [mlp_grad], None, False, table, 2, sums, sizes, block, span, sent
-        )
-
-    def gateup_grads(sums, second_in, span):
-        table = plan.of_matrix(2, row_blocks, 2 * hidden_blocks)
-        return grad_blocks(
-            second_in, [gateup_grad], None, True, table, 2, sums, sizes, block, span, sent
-        )
-
-    sums = down_grads(sums, after(hidden, second_sent), (cuts[3], row_blocks // 2))
-    mine, other = near_sum(second_sent, after(second_kept, *known(sums)))
     sums = gateup_grads(sums, after(second_in, other), (cuts[2], hidden_blocks))
     if last >= 2:
         scatter(2)

time: 595 us -> 589 us (0.990)
  Pallas kernels: 325 us -> 317 us
    pallas_call x4 -> x3, Pallas kernels: 41.8 us -> 23.4 us  [project_rows(): pl.pallas_call(body, grid=(width // tile,), in_specs=[SMEM] * n_order + w...]
    pallas_call x4, Pallas kernels: 43.1 us -> 59.4 us  [the longest x1 37.8 us: feed_forward(): pl.pallas_call(body, grid=(steps + width // tile,), in_specs=[pl.BlockSpe...]
    reduce_scatter x3, waiting for transfers between devices: 5.2 us -> 13.7 us  [scatter(): lax.psum_scatter(sums[x], 'dp', scatter_dimension=0, tiled=True, axis_ind...]
    pallas_call x4, Pallas kernels: 26.9 us -> 20.7 us  [rows_call(): pl.pallas_call(body, grid=(rows // step,), in_specs=[spec(x) for x in ins...]
  transfers between devices with their start and end apart: 31 -> 31, of which waited for: 16 -> 17; matrix products, arithmetic and copies ran while one was open for 6% -> 6% of each run, Pallas kernels for 45% -> 45%
where the time goes in v6:
time: 589 us; the launch traced here: 587 us
  Pallas kernels  317 us (54%)
  waiting for transfers between devices  192 us (33%)
  other arithmetic  29.6 us (5%)
  starting transfers between devices  18 us (3%)
  local copies, waits for them, and re-layouts  16.1 us (3%)
  between operations  14.6 us (2%)
    all_gather x3, waiting for transfers between devices, on_device(): lax.all_gather(chunk, 'dp', axis=0, tiled=True, axis_index_groups=[plan.r...  112 us
    pallas_call x6, Pallas kernels, grad_blocks(): pl.pallas_call(body, grid=(steps,), out_shape=[jax.ShapeDtypeStruct((size...  59.8 us
    ppermute x22, waiting for transfers between devices, partner(): return lax.ppermute(values, 'mp', [(i, i ^ bit) for i in range(mp_count)])  58.9 us
    pallas_call x1, Pallas kernels, feed_forward(): pl.pallas_call(body, grid=(steps + width // tile,), in_specs=[pl.BlockSpe...  37.8 us
    pallas_call x1, Pallas kernels, attend_back(): pl.pallas_call(body, grid=(groups,), in_specs=[pl.BlockSpec((1, rows), la...  33.7 us
    pallas_call x3, Pallas kernels, shampoo(): pl.pallas_call(body, out_shape=[jax.ShapeDtypeStruct(weights.shape, F32)]...  31.6 us
    pallas_call x1, Pallas kernels, attend(): pl.pallas_call(body, grid=(groups,), in_specs=[pl.BlockSpec((1, rows), la...  29.4 us
    pallas_call x3, Pallas kernels, project_rows(): pl.pallas_call(body, grid=(width // tile,), in_specs=[SMEM] * n_order + w...  23.4 us
  transfers between devices with their start and end apart: 31, of which 17 were waited for; matrix products, arithmetic and copies ran while one was open for 6% of the time, Pallas kernels for 45%

profile of v6, /device:TPU:0, one launch (start us, length us, event | category | flops | bytes accessed | tf_op | source)
XLA Modules:
  0.0 587.0 jit_solution(5737853855668582936)
XLA Ops:
  8.4 2.9 sort_blocks.2
  11.4 4.7 sort_blocks.3
  19.2 7.3 %first_norm.1.x_ref.refs_0_ = bf16[1024,2048]{1,0:T(8,128)(2,1)} custom-call(bf16[1024,2048]{1,0:T(8,128)(2,1)} %bitcast.48, f32[1,2048]{1,0:T(1,128)} %get-tuple-element.232.gain_ref), custom_call_target="tpu_custom_call" | custom-call | flops 20971520 | bytes 8396800 | tf_op jit(solution)/shard_map/first_norm/pallas_call | solution.py:923
  26.6 1.9 fusion
  28.5 1.9 pad_maximum_fusion.2
  31.5 2.6 multiply_reduce_fusion
  36.5 2.3 pad_maximum_fusion.g_ref.refs_1_.refs_3_
  38.9 28.2 %all-gather.4.cloned.1.call-done.refs_4_ = bf16[144,128,128]{2,1,0:T(8,128)(2,1)} async-done(((bf16[18,128,128]{2,1,0:T(8,128)(2,1)}), bf16[144,128,128]{2,1,0:T(8,128)(2,1)}) %all-gather.4.cloned.1.call-update) | async-done | bytes 4718608 | tf_op jit(solution)/shard_map/all_gather | solution.py:1151
  67.1 5.2 place_blocks.4
  72.3 15.0 %project_heads.1 = (bf16[1024,512]{1,0:T(8,128)(2,1)}, bf16[1024,128]{1,0:T(8,128)(2,1)}) custom-call(bf16[1024,2048]{1,0:T(8,128)(2,1)} %first_norm.1.x_ref.refs_0_, bf16[2048,640]{1,0:T(8,128)(2,1)} %get-tuple-element.109.w_ref.refs_3_, f32[1024,128]{1,0:T(8,128)} %get-tuple-element.240.cos_ref, f32[1024,128]{1,0:T(8,128)} %get-tuple-element.241.sin_ref), custom_call_target="tpu_custom_call" | custom-call | flops 2684354560 | bytes 8126464 | tf_op jit(solution)/shard_map/project_heads/pallas_call | solution.py:653
  87.3 29.4 %attend.1 = (bf16[1024,512]{1,0:T(8,128)(2,1)}, f32[4,2,1024]{2,1,0:T(2,128)}) custom-call(s32[1,1024]{1,0:T(1,128)} %reduce_window_max.29.start_ref, bf16[1024,512]{1,0:T(8,128)(2,1)} %get-tuple-element.112.q_ref, bf16[1024,128]{1,0:T(8,128)(2,1)} %get-tuple-element.113.kv_ref), custom_call_target="tpu_custom_call" | custom-call | flops 16106127360 | bytes 2097152 | tf_op jit(solution)/shard_map/attend/pallas_call | solution.py:720
  116.7 74.1 %all-gather.6.cloned.1.call-done.refs_1_.refs_2_ = bf16[368,128,128]{2,1,0:T(8,128)(2,1)} async-done(((bf16[46,128,128]{2,1,0:T(8,128)(2,1)}), bf16[368,128,128]{2,1,0:T(8,128)(2,1)}) %all-gather.6.cloned.1.call-update) | async-done | bytes 12058640 | tf_op jit(solution)/shard_map/all_gather | solution.py:1151
  190.8 3.2 place_blocks.5.refs_2_.refs_4_
  194.1 5.8 project_rows.3
  199.9 4.4 collective-permute-done.b_ref.d_ref
  205.6 3.5 add_near.4
  210.6 8.7 %place_blocks.6 = (bf16[2048,2816]{1,0:T(8,128)(2,1)}, bf16[1408,2048]{1,0:T(8,128)(2,1)}) custom-call(s32[690]{0:T(1024)} %constant.81.clone.refs_0_, s32[276]{0:T(512)} %constant.82.clone.refs_1_, bf16[368,128,128]{2,1,0:T(8,128)(2,1)} %all-gather.6.cloned.1.call-done.refs_1_.refs_2_, ...), custom_call_target="tpu_custom_call", output_to_operand_aliasing={{0}: (3, {}), {1}: (4, {})} | custom-call | bytes 21102592 | tf_op jit(solution)/shard_map/place_blocks/pallas_call | solution.py:165
  219.3 15.2 %collective-permute-done.1.b_ref = bf16[256,2048]{1,0:T(8,128)(2,1)S(1)} collective-permute-done((bf16[256,2048]{1,0:T(8,128)(2,1)}, bf16[256,2048]{1,0:T(8,128)(2,1)S(1)}, u32[]{:S(2)}, u32[]{:S(2)}) %collective-permute-start.1) | collective-permute-done | bytes 1048608 | tf_op jit(solution)/shard_map/ppermute | solution.py:1110
  235.5 3.8 second_norm.1
  240.8 9.4 %all-gather.8.cloned.1.call-done.refs_2_ = bf16[160,128,128]{2,1,0:T(8,128)(2,1)} async-done(((bf16[20,128,128]{2,1,0:T(8,128)(2,1)}), bf16[160,128,128]{2,1,0:T(8,128)(2,1)}) %all-gather.8.cloned.1.call-update) | async-done | bytes 5242896 | tf_op jit(solution)/shard_map/all_gather | solution.py:1151
  250.1 5.5 place_blocks.7
  255.7 11.9 %down_back.1.refs_6_ = f32[1024,1408]{1,0:T(8,128)} custom-call(bf16[1024,2048]{1,0:T(8,128)(2,1)} %pad_maximum_fusion.g_ref.refs_1_.refs_3_, bf16[1408,2048]{1,0:T(8,128)(2,1)} %get-tuple-element.135.w_ref.refs_0_.refs_1_, bf16[1408,2048]{1,0:T(8,128)(2,1)} %get-tuple-element.135.w_ref.refs_0_.refs_1_), custom_call_target="tpu_custom_call" | custom-call | flops 5905580032 | bytes 15728640 | tf_op jit(solution)/shard_map/down_back/pallas_call | solution.py:558
  267.6 2.6 collective-permute-done.4.refs_3_
  271.3 37.8 %feed_forward.1 = (bf16[1024,1408]{1,0:T(8,128)(2,1)}, bf16[2,1024,1408]{2,1,0:T(8,128)(2,1)}, bf16[1024,2048]{1,0:T(8,128)(2,1)}, bf16[512,2048]{1,0:T(8,128)(2,1)}, bf16[512,2048]{1,0:T(8,128)(2,1)}) custom-call(bf16[256,2048]{1,0:T(8,128)(2,1)} %get-tuple-element.129.refs_0_, bf16[256,2048]{1,0:T(8,128)(2,1)} %copy-done.22, bf16[256,2048]{1,0:T(8,128)(2,1)} %copy-done.23, ...), custom_call_target="tpu_custom_call" | custom-call | flops 23622320128 | bytes 41680896 | tf_op jit(solution)/shard_map/feed_forward/pallas_call | solution.py:432
  309.3 4.9 grad_blocks.6
  315.4 3.5 add_near.5
  318.9 1.5 collective-permute-start.6
  320.4 3.7 grad_strips.1.refs_3_
  324.2 9.4 %grad_blocks.7 = (bf16[368,128,128]{2,1,0:T(8,128)(2,1)}, bf16[160,128,128]{2,1,0:T(8,128)(2,1)}) custom-call(bf16[1024,2048]{1,0:T(8,128)(2,1)} %get-tuple-element.155.refs_0_, bf16[2,1024,1408]{2,1,0:T(8,128)(2,1)} %get-tuple-element.149.refs_1_, bf16[368,128,128]{2,1,0:T(8,128)(2,1)} %get-tuple-element.142.refs_2_, ...), custom_call_target="tpu_custom_call", output_to_operand_aliasing={{0}: (2, {}), {1}: (3, {})} | custom-call | flops 8589934592 | bytes 21495808 | tf_op jit(solution)/shard_map/grad_blocks/pallas_call | solution.py:309
  333.6 11.0 %collective-permute-done.6.b_ref = bf16[256,2048]{1,0:T(8,128)(2,1)S(1)} collective-permute-done((bf16[256,2048]{1,0:T(8,128)(2,1)}, bf16[256,2048]{1,0:T(8,128)(2,1)S(1)}, u32[]{:S(2)}, u32[]{:S(2)}) %collective-permute-start.6) | collective-permute-done | bytes 1048608 | tf_op jit(solution)/shard_map/ppermute | solution.py:1110
  345.6 4.9 norm_back.2
  350.4 1.5 collective-permute-start.7
  352.0 16.6 %grad_blocks.8 = (bf16[144,128,128]{2,1,0:T(8,128)(2,1)}, bf16[368,128,128]{2,1,0:T(8,128)(2,1)}) custom-call(bf16[1024,2048]{1,0:T(8,128)(2,1)} %get-tuple-element.155.refs_0_, bf16[2,1024,1408]{2,1,0:T(8,128)(2,1)} %get-tuple-element.149.refs_1_, bf16[368,128,128]{2,1,0:T(8,128)(2,1)} %get-tuple-element.150.refs_2_), custom_call_target="tpu_custom_call", output_to_operand_aliasing={{1}: (2, {})} | custom-call | flops 15032385536 | bytes 21495808 | tf_op jit(solution)/shard_map/grad_blocks/pallas_call | solution.py:309
  368.6 9.8 %grad_blocks.9 = (bf16[144,128,128]{2,1,0:T(8,128)(2,1)}, bf16[368,128,128]{2,1,0:T(8,128)(2,1)}) custom-call(bf16[1024,1408]{1,0:T(8,128)(2,1)} %get-tuple-element.163.refs_0_.refs_2_, bf16[1024,2048]{1,0:T(8,128)(2,1)} %pad_maximum_fusion.g_ref.refs_1_.refs_3_, ...), custom_call_target="tpu_custom_call", output_to_operand_aliasing={{0}: (2, {}), {1}: (3, {})} | custom-call | flops 8858370048 | bytes 12845056 | tf_op jit(solution)/shard_map/grad_blocks/pallas_call | solution.py:309
  379.1 2.3 collective-permute-done.9.refs_5_.refs_3_
  382.3 6.8 %grad_blocks.10 = (bf16[144,128,128]{2,1,0:T(8,128)(2,1)}, bf16[368,128,128]{2,1,0:T(8,128)(2,1)}) custom-call(s32[4]{0:T(128)} %broadcast_xor_fusion.refs_0_.order_ref, bf16[1024,512]{1,0:T(8,128)(2,1)} %get-tuple-element.114.refs_1_, bf16[256,2048]{1,0:T(8,128)(2,1)} %get-tuple-element.153.refs_2_.refs_0_, ...), custom_call_target="tpu_custom_call", output_to_operand_aliasing={{0}: (6, {}), {1}: (7, {})} | custom-call | flops 4294967296 | bytes 7340032 | tf_op jit(solution)/shard_map/grad_blocks/pallas_call | solution.py:309
  389.3 10.6 %project_rows.4 = (bf16[512,2048]{1,0:T(8,128)(2,1)}, bf16[512,2048]{1,0:T(8,128)(2,1)}) custom-call(bf16[1024,1408]{1,0:T(8,128)(2,1)} %get-tuple-element.163.refs_0_.refs_2_, bf16[1408,2048]{1,0:T(8,128)(2,1)} %get-tuple-element.135.w_ref.refs_0_.refs_1_), custom_call_target="tpu_custom_call" | custom-call | flops 5905580032 | bytes 12845056 | tf_op jit(solution)/shard_map/project_rows/pallas_call | solution.py:513
  400.2 4.0 collective-permute-done.10.b_ref.d_ref
  405.5 3.5 add_near.6
  409.5 6.0 %to_heads.1.g_ref = bf16[1024,512]{1,0:T(8,128)(2,1)} custom-call(s32[4]{0:T(128)} %broadcast_xor_fusion.refs_0_.order_ref, bf16[256,2048]{1,0:T(8,128)(2,1)} %get-tuple-element.153.refs_2_.refs_0_, bf16[256,2048]{1,0:T(8,128)(2,1)} %copy-done.11, bf16[256,2048]{1,0:T(8,128)(2,1)} %copy-done.12, bf16[256,2048]{1,0:T(8,128)(2,1)} %copy-done.13, ...), custom_call_target="tpu_custom_call" | custom-call | flops 2147483648 | bytes 6291456 | tf_op jit(solution)/shard_map/to_heads/pallas_call | solution.py:588
  415.5 33.7 %attend_back.1 = (bf16[1024,512]{1,0:T(8,128)(2,1)}, bf16[1024,128]{1,0:T(8,128)(2,1)}) custom-call(s32[1,1024]{1,0:T(1,128)} %reduce_window_max.29.start_ref, bf16[1024,512]{1,0:T(8,128)(2,1)} %get-tuple-element.112.q_ref, bf16[1024,128]{1,0:T(8,128)(2,1)} %get-tuple-element.113.kv_ref, f32[4,2,1024]{2,1,0:T(2,128)} %get-tuple-element.167.log_ref, ...), custom_call_target="tpu_custom_call" | custom-call | flops 42949672960 | bytes 8388608 | tf_op jit(solution)/shard_map/attend_back/pallas_call | solution.py:795
  449.2 3.1 add_convert_fusion
  452.2 7.0 %project_rows.5 = (bf16[512,2048]{1,0:T(8,128)(2,1)}, bf16[512,2048]{1,0:T(8,128)(2,1)}) custom-call(s32[4]{0:T(128)} %broadcast_xor_fusion.refs_0_.order_ref, bf16[1024,512]{1,0:T(8,128)(2,1)} %get-tuple-element.172.refs_1_, bf16[1024,128]{1,0:T(8,128)(2,1)} %get-tuple-element.173.refs_2_, bf16[2048,640]{1,0:T(8,128)(2,1)} %get-tuple-element.109.w_ref.refs_3_), custom_call_target="tpu_custom_call" | custom-call | flops 2684354560 | bytes 8126464 | tf_op jit(solution)/shard_map/project_rows/pallas_call | solution.py:513
  459.3 4.3 multiply_reduce_fusion.1
  463.7 1.7 collective-permute-start.13
  465.4 2.1 collective-permute-done.13
  469.5 3.4 add_near.7
  472.9 1.6 collective-permute-start.14
  474.5 12.3 %grad_blocks.11 = bf16[144,128,128]{2,1,0:T(8,128)(2,1)} custom-call(bf16[1024,2048]{1,0:T(8,128)(2,1)} %first_norm.1.x_ref.refs_0_, bf16[1024,512]{1,0:T(8,128)(2,1)} %get-tuple-element.172.refs_1_, bf16[1024,128]{1,0:T(8,128)(2,1)} %get-tuple-element.173.refs_2_, bf16[144,128,128]{2,1,0:T(8,128)(2,1)} %get-tuple-element.161.refs_3_), custom_call_target="tpu_custom_call", output_to_operand_aliasing={{}: (3, {})} | custom-call | flops 5368709120 | bytes 8126464 | tf_op jit(solution)/shard_map/grad_blocks/pallas_call | solution.py:309
  486.8 11.0 %collective-permute-done.14.b_ref = bf16[256,2048]{1,0:T(8,128)(2,1)S(1)} collective-permute-done((bf16[256,2048]{1,0:T(8,128)(2,1)}, bf16[256,2048]{1,0:T(8,128)(2,1)S(1)}, u32[]{:S(2)}, u32[]{:S(2)}) %collective-permute-start.14) | collective-permute-done | bytes 1048608 | tf_op jit(solution)/shard_map/ppermute | solution.py:1110
  498.8 4.7 norm_back.3
  503.5 1.6 collective-permute-start.16
  506.8 8.5 %shampoo.3 = (f32[84,128,128]{2,1,0:T(8,128)}, f32[84,128,128]{2,1,0:T(8,128)}, f32[84,128,128]{2,1,0:T(8,128)}, f32[84,128,128]{2,1,0:T(8,128)}, f32[84,128,128]{2,1,0:T(8,128)}) custom-call(s32[20]{0:T(128)} %slice_bitcast_fusion.1.places_ref, bf16[20,128,128]{2,1,0:T(8,128)(2,1)} %reduce-scatter.6.cloned.1.call-done.g_ref, f32[84,128,128]{2,1,0:T(8,128)} %refs_0_.9, ...), custom_call_target="tpu_custom_call" | custom-call | flops 335544320 | bytes 15073280 | tf_op jit(solution)/shard_map/shampoo/pallas_call | solution.py:893
  516.4 15.7 %shampoo.4 = (f32[84,128,128]{2,1,0:T(8,128)}, f32[84,128,128]{2,1,0:T(8,128)}, f32[84,128,128]{2,1,0:T(8,128)}, f32[84,128,128]{2,1,0:T(8,128)}, f32[84,128,128]{2,1,0:T(8,128)}) custom-call(s32[46]{0:T(128)} %slice_bitcast_fusion.2.places_ref, ...), custom_call_target="tpu_custom_call", output_to_operand_aliasing={{0}: (8, {}), {1}: (9, {}), {2}: (10, {}), {3}: (11, {}), {... | custom-call | flops 771751936 | bytes 34668544 | tf_op jit(solution)/shard_map/shampoo/pallas_call | solution.py:893
  532.7 1.8 collective-permute-done.21
  535.8 2.9 collective-permute-done.22
  539.6 3.4 collective-permute-done.23
  543.0 1.8 collective-permute-start.24
  545.4 4.5 collective-permute-done.19
  551.2 2.2 broadcast_select_fusion.11
  553.5 2.3 maximum_bitcast_fusion
  556.1 3.9 maximum_convert_fusion
  560.0 12.6 %reduce-scatter.8.cloned.1.call-done.g_ref = bf16[18,128,128]{2,1,0:T(8,128)(2,1)} async-done(((bf16[144,128,128]{2,1,0:T(8,128)(2,1)}), bf16[18,128,128]{2,1,0:T(8,128)(2,1)}) %reduce-scatter.8.cloned.1.call-update) | async-done | bytes 589840 | tf_op jit(solution)/shard_map/reduce_scatter | solution.py:1208
  572.7 7.5 %shampoo.5 = (f32[84,128,128]{2,1,0:T(8,128)}, f32[84,128,128]{2,1,0:T(8,128)}, f32[84,128,128]{2,1,0:T(8,128)}, f32[84,128,128]{2,1,0:T(8,128)}, f32[84,128,128]{2,1,0:T(8,128)}) custom-call(s32[18]{0:T(128)} %slice_bitcast_fusion.places_ref, ...), custom_call_target="tpu_custom_call", output_to_operand_aliasing={{0}: (8, {}), {1}: (9, {}), {2}: (10, {}), {3}: (11, {}), {... | custom-call | flops 301989888 | bytes 13565952 | tf_op jit(solution)/shard_map/shampoo/pallas_call | solution.py:893
  (133 shorter events, 31.4 us)
Async XLA Ops:
  7.2 59.9 %all-gather.4.cloned.1.call-start = ((), (), s32[]{:S(2)}) async-start(), calls=%async_computation.3 | async-start | bytes 5308416 | tf_op jit(solution)/shard_map/all_gather | solution.py:1151
  11.3 5.7 copy-start.18
  11.4 6.5 %copy-start.17 = (f32[2,2048]{1,0:T(2,128)S(1)}, f32[2,2048]{1,0:T(2,128)}, u32[]{:S(2)}) copy-start(f32[2,2048]{1,0:T(2,128)} %param.26) | copy-start | bytes 49156
  11.4 179.4 %all-gather.6.cloned.1.call-start = ((), (), s32[]{:S(2)}) async-start(), calls=%async_computation.4 | async-start | bytes 13565952 | tf_op jit(solution)/shard_map/all_gather | solution.py:1151
  16.2 233.9 %all-gather.8.cloned.1.call-start = ((), (), s32[]{:S(2)}) async-start(), calls=%async_computation.5 | async-start | bytes 5898240 | tf_op jit(solution)/shard_map/all_gather | solution.py:1151
  17.0 489.9 %reduce-scatter.6.cloned.1.call-start = ((), (), s32[]{:S(2)}) async-start(), calls=%async_computation.7 | async-start | bytes 5898240 | tf_op jit(solution)/shard_map/reduce_scatter | solution.py:1208
  19.2 7.4 %copy-start.20 = (s32[1,1024]{1,0:T(1,128)S(1)}, s32[1,1024]{1,0:T(1,128)}, u32[]{:S(2)}) copy-start(s32[1,1024]{1,0:T(1,128)} %param.24) | copy-start | bytes 12292
  26.5 3.9 copy-start.27
  26.5 4.4 copy-start
  31.5 2.7 copy-start.1
  31.5 4.1 copy-start.6
  36.5 2.4 copy-start.8
  199.9 4.4 collective-permute-start
  204.2 1.3 copy-start.4
  209.1 25.4 %collective-permute-start.1 = (bf16[256,2048]{1,0:T(8,128)(2,1)}, bf16[256,2048]{1,0:T(8,128)(2,1)S(1)}, u32[]{:S(2)}, u32[]{:S(2)}) collective-permute-start(bf16[256,2048]{1,0:T(8,128)(2,1)} %get-tuple-element.121), channel_id=1, source_target_pairs={{0,2},{1,3},{2,0},{3,1},{4,6},{5,7},{6,4},{7,5},{8,10},{9,11},{10,... | collective-permute-start | bytes 3145736 | tf_op jit(solution)/shard_map/ppermute | solution.py:1110
  234.5 1.0 copy-start.14
  239.3 28.3 %collective-permute-start.2 = (bf16[256,2048]{1,0:T(8,128)(2,1)}, bf16[256,2048]{1,0:T(8,128)(2,1)S(1)}, u32[]{:S(2)}, u32[]{:S(2)}) collective-permute-start(bf16[256,2048]{1,0:T(8,128)(2,1)} %get-tuple-element.129.refs_0_), channel_id=1, source_target_pairs={{0,2},{1,3},{2,0},{3,1},{4,6},{5,7},{6,4},{7,5},{8,10},{9,11},{10,... | collective-permute-start | bytes 3145736 | tf_op jit(solution)/shard_map/ppermute | solution.py:1110
  240.7 26.9 %collective-permute-start.3 = (bf16[256,2048]{1,0:T(8,128)(2,1)}, bf16[256,2048]{1,0:T(8,128)(2,1)S(1)}, u32[]{:S(2)}, u32[]{:S(2)}) collective-permute-start(bf16[256,2048]{1,0:T(8,128)(2,1)} %get-tuple-element.129.refs_0_), channel_id=1, source_target_pairs={{0,1},{1,0},{2,3},{3,2},{4,5},{5,4},{6,7},{7,6},{8,9},{9,8},{10,11... | collective-permute-start | bytes 3145736 | tf_op jit(solution)/shard_map/ppermute | solution.py:1110
  267.6 2.7 copy-start.22
  267.6 2.7 collective-permute-start.4
  267.6 2.6 copy-start.23
  270.3 1.0 copy-start.26
  309.1 5.1 collective-permute-start.5
  314.1 1.3 copy-start.3
  318.9 25.7 %collective-permute-start.6 = (bf16[256,2048]{1,0:T(8,128)(2,1)}, bf16[256,2048]{1,0:T(8,128)(2,1)S(1)}, u32[]{:S(2)}, u32[]{:S(2)}) collective-permute-start(bf16[256,2048]{1,0:T(8,128)(2,1)} %get-tuple-element.147), channel_id=1, source_target_pairs={{0,2},{1,3},{2,0},{3,1},{4,6},{5,7},{6,4},{7,5},{8,10},{9,11},{10,... | collective-permute-start | bytes 3145736 | tf_op jit(solution)/shard_map/ppermute | solution.py:1110
  333.6 182.8 %reduce-scatter.4.cloned.1.call-start = ((), (), s32[]{:S(2)}) async-start(), calls=%async_computation.6 | async-start | bytes 13565952 | tf_op jit(solution)/shard_map/reduce_scatter | solution.py:1208
  344.6 1.0 copy-start.24
  350.4 28.0 %collective-permute-start.7 = (bf16[256,2048]{1,0:T(8,128)(2,1)}, bf16[256,2048]{1,0:T(8,128)(2,1)S(1)}, u32[]{:S(2)}, u32[]{:S(2)}) collective-permute-start(bf16[256,2048]{1,0:T(8,128)(2,1)} %get-tuple-element.153.refs_2_.refs_0_), channel_id=1, source_target_pairs={{0,2},{1,3},{2,0},{3,1},{4,6},{5,7},{6,4},{7,5},{8,10},{9,11},{10,... | collective-permute-start | bytes 3145736 | tf_op jit(solution)/shard_map/ppermute | solution.py:1110
  352.0 27.1 %collective-permute-start.8 = (bf16[256,2048]{1,0:T(8,128)(2,1)}, bf16[256,2048]{1,0:T(8,128)(2,1)S(1)}, u32[]{:S(2)}, u32[]{:S(2)}) collective-permute-start(bf16[256,2048]{1,0:T(8,128)(2,1)} %get-tuple-element.153.refs_2_.refs_0_), channel_id=1, source_target_pairs={{0,1},{1,0},{2,3},{3,2},{4,5},{5,4},{6,7},{7,6},{8,9},{9,8},{10,11... | collective-permute-start | bytes 3145736 | tf_op jit(solution)/shard_map/ppermute | solution.py:1110
  378.4 2.9 copy-start.11
  378.4 2.9 collective-permute-start.9
  379.0 2.3 copy-start.12
  381.3 1.0 copy-start.13
  389.2 183.5 %reduce-scatter.8.cloned.1.call-start = ((), (), s32[]{:S(2)}) async-start(), calls=%async_computation.8 | async-start | bytes 5308416 | tf_op jit(solution)/shard_map/reduce_scatter | solution.py:1208
  399.8 4.4 collective-permute-start.10
  404.2 1.3 copy-start.5
  409.0 40.2 %collective-permute-start.11 = (bf16[256,2048]{1,0:T(8,128)(2,1)}, bf16[256,2048]{1,0:T(8,128)(2,1)S(1)}, u32[]{:S(2)}, u32[]{:S(2)}) collective-permute-start(bf16[256,2048]{1,0:T(8,128)(2,1)} %get-tuple-element.168), channel_id=1, source_target_pairs={{0,2},{1,3},{2,0},{3,1},{4,6},{5,7},{6,4},{7,5},{8,10},{9,11},{10,... | collective-permute-start | bytes 3145736 | tf_op jit(solution)/shard_map/ppermute | solution.py:1110
  415.5 33.7 %copy-start.9 = (f32[256,2048]{1,0:T(8,128)S(1)}, f32[256,2048]{1,0:T(8,128)}, u32[]{:S(2)}) copy-start(f32[256,2048]{1,0:T(8,128)} %get-tuple-element.128.x_ref) | copy-start | bytes 6291460
  452.2 7.1 %copy-start.19 = (f32[1024]{0:T(1024)S(1)}, f32[1024]{0:T(1024)}, u32[]{:S(2)}) copy-start(f32[1024]{0:T(1024)} %add_rsqrt_fusion) | copy-start | bytes 12292
  459.2 9.0 %collective-permute-start.12 = (bf16[512,2048]{1,0:T(8,128)(2,1)}, bf16[512,2048]{1,0:T(8,128)(2,1)S(1)}, u32[]{:S(2)}, u32[]{:S(2)}) collective-permute-start(bf16[512,2048]{1,0:T(8,128)(2,1)} %get-tuple-element.175), channel_id=1, source_target_pairs={{0,1},{1,0},{2,3},{3,2},{4,5},{5,4},{6,7},{7,6},{8,9},{9,8},{10,11... | collective-permute-start | bytes 6291464 | tf_op jit(solution)/shard_map/ppermute | solution.py:1110
  459.3 4.4 copy-start.16
  463.7 3.8 collective-permute-start.13
  468.2 1.3 copy-start.2
  472.9 24.9 %collective-permute-start.14 = (bf16[256,2048]{1,0:T(8,128)(2,1)}, bf16[256,2048]{1,0:T(8,128)(2,1)S(1)}, u32[]{:S(2)}, u32[]{:S(2)}) collective-permute-start(bf16[256,2048]{1,0:T(8,128)(2,1)} %get-tuple-element.181), channel_id=1, source_target_pairs={{0,2},{1,3},{2,0},{3,1},{4,6},{5,7},{6,4},{7,5},{8,10},{9,11},{10,... | collective-permute-start | bytes 3145736 | tf_op jit(solution)/shard_map/ppermute | solution.py:1110
  497.8 1.0 copy-start.25
  498.8 4.8 copy-start.7
  498.8 6.3 %copy-start.21 = (s32[1,84]{1,0:T(1,128)S(1)}, s32[1,84]{1,0:T(1,128)}, u32[]{:S(2)}) copy-start(s32[1,84]{1,0:T(1,128)} %get-tuple-element.236) | copy-start | bytes 1012
  503.5 28.5 %collective-permute-start.16 = (bf16[256,2048]{1,0:T(8,128)(2,1)S(1)}, bf16[256,2048]{1,0:T(8,128)(2,1)}, u32[]{:S(2)}, u32[]{:S(2)}) collective-permute-start(bf16[256,2048]{1,0:T(8,128)(2,1)S(1)} %copy-done.7), channel_id=1, source_target_pairs={{0,2},{1,3},{2,0},{3,1},{4,6},{5,7},{6,4},{7,5},{8,10},{9,11},{10,... | collective-permute-start | bytes 3145736 | tf_op jit(solution)/shard_map/ppermute | solution.py:1110
  505.7 44.3 %collective-permute-start.19 = (bf16[256,2048]{1,0:T(8,128)(2,1)}, bf16[256,2048]{1,0:T(8,128)(2,1)S(1)}, u32[]{:S(2)}, u32[]{:S(2)}) collective-permute-start(bf16[256,2048]{1,0:T(8,128)(2,1)} %get-tuple-element.185), channel_id=1, source_target_pairs={{0,2},{1,3},{2,0},{3,1},{4,6},{5,7},{6,4},{7,5},{8,10},{9,11},{10,... | collective-permute-start | bytes 3145736 | tf_op jit(solution)/shard_map/ppermute | solution.py:1110
  506.8 44.4 %collective-permute-start.15 = (bf16[256,2048]{1,0:T(8,128)(2,1)S(1)}, bf16[256,2048]{1,0:T(8,128)(2,1)}, u32[]{:S(2)}, u32[]{:S(2)}) collective-permute-start(bf16[256,2048]{1,0:T(8,128)(2,1)S(1)} %copy-done.7), channel_id=1, source_target_pairs={{0,1},{1,0},{2,3},{3,2},{4,5},{5,4},{6,7},{7,6},{8,9},{9,8},{10,11... | collective-permute-start | bytes 3145736 | tf_op jit(solution)/shard_map/ppermute | solution.py:1110
  516.4 15.8 %copy-start.15 = (f32[2,2048]{1,0:T(2,128)S(1)}, f32[2,2048]{1,0:T(2,128)}, u32[]{:S(2)}) copy-start(f32[2,2048]{1,0:T(2,128)} %fusion.6) | copy-start | bytes 49156
  516.4 29.0 %copy-start.10 = (bf16[256,2048]{1,0:T(8,128)(2,1)S(1)}, bf16[256,2048]{1,0:T(8,128)(2,1)}, u32[]{:S(2)}) copy-start(bf16[256,2048]{1,0:T(8,128)(2,1)} %get-tuple-element.185) | copy-start | bytes 3145732
  532.1 19.1 %collective-permute-start.17 = (bf16[256,2048]{1,0:T(8,128)(2,1)}, bf16[256,2048]{1,0:T(8,128)(2,1)}, u32[]{:S(2)}, u32[]{:S(2)}) collective-permute-start(bf16[256,2048]{1,0:T(8,128)(2,1)} %collective-permute-done.16), channel_id=1, source_target_pairs={{0,1},{1,0},{2,3},{3,2},{4,5},{5,4},{6,7},{7,6},{8,9},{9,8},{10,11... | collective-permute-start | bytes 3145736 | tf_op jit(solution)/shard_map/ppermute | solution.py:1110
  532.2 2.3 collective-permute-start.21
  534.5 4.2 collective-permute-start.22
  538.7 4.3 collective-permute-start.23
  543.0 6.9 %collective-permute-start.24 = (f32[2,2048]{1,0:T(2,128)S(1)}, f32[2,2048]{1,0:T(2,128)S(1)}, u32[]{:S(2)}, u32[]{:S(2)}) collective-permute-start(f32[2,2048]{1,0:T(2,128)S(1)} %add.103), channel_id=1, source_target_pairs={{0,16},{4,20},{8,24},{12,28},{16,0},{20,4},{24,8},{28,12},{1,17},{... | collective-permute-start | bytes 49160 | tf_op jit(solution)/shard_map/ppermute | solution.py:1350
  545.4 10.4 %collective-permute-start.18 = (bf16[256,2048]{1,0:T(8,128)(2,1)S(1)}, bf16[256,2048]{1,0:T(8,128)(2,1)S(1)}, u32[]{:S(2)}, u32[]{:S(2)}) collective-permute-start(bf16[256,2048]{1,0:T(8,128)(2,1)S(1)} %copy-done.10), channel_id=1, source_target_pairs={{0,1},{1,0},{2,3},{3,2},{4,5},{5,4},{6,7},{7,6},{8,9},{9,8},{10,11... | collective-permute-start | bytes 3145736 | tf_op jit(solution)/shard_map/ppermute | solution.py:1110
  550.0 5.8 collective-permute-start.20
Sparse Core Ops, SparseCore 0:
  11.5 55.5 all-gather.3
  69.2 121.5 all-gather.5
  192.4 57.7 all-gather.7
  333.7 57.5 reduce-scatter.5
  393.4 122.9 reduce-scatter.3
  518.5 54.0 reduce-scatter.7

commit v7 on v6

--- a/solution.py
+++ b/solution.py
@@ -86,6 +86,10 @@
         return out
 
 
+def held(values):
+    return pltpu.with_memory_space_constraint(values, pltpu.VMEM)
+
+
 ANY = pl.BlockSpec(memory_space=pl.ANY)
 SMEM = pl.BlockSpec(memory_space=pltpu.SMEM)
 VMEM = pl.BlockSpec(memory_space=pltpu.VMEM)
@@ -432,7 +436,8 @@
     hid, grads, joined, kept, sent = pl.pallas_call(
         body,
         grid=(steps + width // tile,),
-        in_specs=[pl.BlockSpec((share, width), lambda j: (0, 0))] * count
+        in_specs=[pl.BlockSpec((share, width), lambda j: (0, 0))]
+        + [VMEM] * (count - 1)
         + [
             pl.BlockSpec((width, block), lambda j: (0, first(j))),
             pl.BlockSpec((width, block), lambda j: (0, steps + first(j))),
@@ -454,14 +459,14 @@
             jax.ShapeDtypeStruct((half, width), LOW),
         ],
         scratch_shapes=[pltpu.VMEM((2, rows, hidden), LOW)],
-        compiler_params=pltpu.CompilerParams(vmem_limit_bytes=VMEM_LIMIT),
+        compiler_params=pltpu.CompilerParams(vmem_limit_bytes=48 * 1024 * 1024),
         cost_estimate=pl.CostEstimate(
             flops=8 * rows * width * hidden,
             bytes_accessed=2 * rows * width + 8 * width * hidden + 10 * rows * hidden,
             transcendentals=rows * hidden,
         ),
         name="feed_forward",
-    )(*pieces, weights, weights, hidden_grad, weights)
+    )(pieces[0], *[held(x) for x in pieces[1:]], weights, weights, hidden_grad, weights)
     return hid, grads, joined, sent, kept
 
 
@@ -912,7 +917,7 @@
     )(places, sums, weights, ema, left, right, left_roots, right_roots, *extra)
 
 
-def rows_call(body, ins, outs, name, step=128, work=10):
+def rows_call(body, ins, outs, name, step=128, work=10, here=None):
     rows = max(x.shape[0] for x in ins)
 
     def spec(x):
@@ -923,7 +928,7 @@
     return pl.pallas_call(
         body,
         grid=(rows // step,),
-        in_specs=[spec(x) for x in ins],
+        in_specs=[VMEM if i == here else spec(x) for i, x in enumerate(ins)],
         out_specs=[spec(x) for x in outs],
         out_shape=outs,
         compiler_params=pltpu.CompilerParams(vmem_limit_bytes=VMEM_LIMIT),
@@ -941,16 +946,18 @@
     width = kept.shape[1]
     step = 128
 
-    def body(a_ref, c_ref, b_ref, d_ref, mine_ref, other_ref):
-        mine_ref[...] = a_ref[...].astype(F32) + b_ref[...].astype(F32)
-        other_ref[...] = (c_ref[...].astype(F32) + d_ref[...].astype(F32)).astype(LOW)
+    def body(a_ref, c_ref, got_ref, mine_ref, other_ref):
+        at = pl.multiple_of(pl.program_id(0) * step, step)
+        near, far = got_ref[pl.ds(at, step)], got_ref[pl.ds(share + at, step)]
+        mine_ref[...] = a_ref[...].astype(F32) + near.astype(F32)
+        other_ref[...] = (c_ref[...].astype(F32) + far.astype(F32)).astype(LOW)
 
     first = pl.BlockSpec((step, width), lambda j: (j, 0))
     second = pl.BlockSpec((step, width), lambda j: (share // step + j, 0))
     return pl.pallas_call(
         body,
         grid=(share // step,),
-        in_specs=[first, second, first, second],
+        in_specs=[first, second, VMEM],
         out_specs=[first] * 2,
         out_shape=[
             jax.ShapeDtypeStruct((share, width), F32),
@@ -961,21 +968,26 @@
             flops=2 * share * width, bytes_accessed=14 * share * width, transcendentals=0
         ),
         name="add_near",
-    )(kept, kept, got, got)
+    )(kept, kept, held(got))
 
 
 def second_norm(tokens, mine, got, gain):
+    step = 128
+
     def body(x_ref, a_ref, b_ref, gain_ref, middle_ref, low_ref):
-        middle = x_ref[...].astype(F32) + (a_ref[...] + b_ref[...].astype(F32))
+        got = b_ref[pl.ds(pl.multiple_of(pl.program_id(0) * step, step), step)]
+        middle = x_ref[...].astype(F32) + (a_ref[...] + got.astype(F32))
         middle_ref[...] = middle
         scale = lax.rsqrt(jnp.mean(middle * middle, axis=-1, keepdims=True) + 1e-05)
         low_ref[...] = (middle * scale * gain_ref[...]).astype(LOW)
 
     return rows_call(
         body,
-        [tokens, mine, got, gain],
+        [tokens, mine, held(got), gain],
         [jax.ShapeDtypeStruct(tokens.shape, F32), jax.ShapeDtypeStruct(tokens.shape, LOW)],
         "second_norm",
+        step,
+        here=2,
     )
 
 
@@ -994,9 +1006,12 @@
 
 
 def norm_back(values, mine, got, gain, residual):
+    step = 128
+
     def body(x_ref, a_ref, b_ref, gain_ref, r_ref, out_ref, low_ref, sum_ref):
         x = x_ref[...].astype(F32)
-        grad = a_ref[...] + b_ref[...].astype(F32)
+        got = b_ref[pl.ds(pl.multiple_of(pl.program_id(0) * step, step), step)]
+        grad = a_ref[...] + got.astype(F32)
         scale = lax.rsqrt(jnp.mean(x * x, axis=-1, keepdims=True) + 1e-05)
         unit = x * scale
         scaled = grad * gain_ref[...]
@@ -1015,13 +1030,15 @@
     shape = values.shape
     return rows_call(
         body,
-        [values, mine, got, gain, residual],
+        [values, mine, held(got), gain, residual],
         [
             jax.ShapeDtypeStruct(shape, F32),
             jax.ShapeDtypeStruct(shape, LOW),
             jax.ShapeDtypeStruct((1, shape[1]), F32),
         ],
         "norm_back",
+        step,
+        here=2,
         work=1000000,
     )
 

time: 589 us -> 585 us (level)
  no operation moved by 1% of the time
where the time goes in v7:
time: 585 us; the launch traced here: 583 us
  Pallas kernels  313 us (54%)
  waiting for transfers between devices  191 us (33%)
  other arithmetic  29.5 us (5%)
  starting transfers between devices  17.6 us (3%)
  local copies, waits for them, and re-layouts  16.7 us (3%)
  between operations  14.5 us (2%)
    all_gather x3, waiting for transfers between devices, on_device(): lax.all_gather(chunk, 'dp', axis=0, tiled=True, axis_index_groups=[plan.r...  111 us
    pallas_call x6, Pallas kernels, grad_blocks(): pl.pallas_call(body, grid=(steps,), out_shape=[jax.ShapeDtypeStruct((size...  59.8 us
    ppermute x22, waiting for transfers between devices, partner(): return lax.ppermute(values, 'mp', [(i, i ^ bit) for i in range(mp_count)])  59.1 us
    pallas_call x1, Pallas kernels, feed_forward(): pl.pallas_call(body, grid=(steps + width // tile,), in_specs=[pl.BlockSpe...  36.3 us
    pallas_call x1, Pallas kernels, attend_back(): pl.pallas_call(body, grid=(groups,), in_specs=[pl.BlockSpec((1, rows), la...  33.6 us
    pallas_call x3, Pallas kernels, shampoo(): pl.pallas_call(body, out_shape=[jax.ShapeDtypeStruct(weights.shape, F32)]...  31.6 us
    pallas_call x1, Pallas kernels, attend(): pl.pallas_call(body, grid=(groups,), in_specs=[pl.BlockSpec((1, rows), la...  29.4 us
    pallas_call x3, Pallas kernels, project_rows(): pl.pallas_call(body, grid=(width // tile,), in_specs=[SMEM] * n_order + w...  23.4 us
  transfers between devices with their start and end apart: 31, of which 17 were waited for; matrix products, arithmetic and copies ran while one was open for 6% of the time, Pallas kernels for 45%

profile of v7, /device:TPU:0, one launch (start us, length us, event | category | flops | bytes accessed | tf_op | source)
XLA Modules:
  0.0 582.7 jit_solution(8224325869804574703)
XLA Ops:
  8.4 2.9 sort_blocks.2
  11.4 4.8 sort_blocks.3
  19.1 7.3 %first_norm.1.x_ref.refs_0_ = bf16[1024,2048]{1,0:T(8,128)(2,1)} custom-call(bf16[1024,2048]{1,0:T(8,128)(2,1)} %bitcast.48, f32[1,2048]{1,0:T(1,128)} %get-tuple-element.232.gain_ref), custom_call_target="tpu_custom_call" | custom-call | flops 20971520 | bytes 8396800 | tf_op jit(solution)/shard_map/first_norm/pallas_call | solution.py:928
  26.6 1.9 fusion
  28.5 1.9 pad_maximum_fusion.2
  31.5 2.6 multiply_reduce_fusion
  37.5 2.3 pad_maximum_fusion.g_ref.refs_1_.refs_3_
  39.8 27.3 %all-gather.4.cloned.1.call-done.refs_4_ = bf16[144,128,128]{2,1,0:T(8,128)(2,1)} async-done(((bf16[18,128,128]{2,1,0:T(8,128)(2,1)}), bf16[144,128,128]{2,1,0:T(8,128)(2,1)}) %all-gather.4.cloned.1.call-update) | async-done | bytes 4718608 | tf_op jit(solution)/shard_map/all_gather | solution.py:1168
  67.1 5.2 place_blocks.4
  72.3 15.0 %project_heads.1 = (bf16[1024,512]{1,0:T(8,128)(2,1)}, bf16[1024,128]{1,0:T(8,128)(2,1)}) custom-call(bf16[1024,2048]{1,0:T(8,128)(2,1)} %first_norm.1.x_ref.refs_0_, bf16[2048,640]{1,0:T(8,128)(2,1)} %get-tuple-element.109.w_ref.refs_3_, f32[1024,128]{1,0:T(8,128)} %get-tuple-element.240.cos_ref, f32[1024,128]{1,0:T(8,128)} %get-tuple-element.241.sin_ref), custom_call_target="tpu_custom_call" | custom-call | flops 2684354560 | bytes 8126464 | tf_op jit(solution)/shard_map/project_heads/pallas_call | solution.py:658
  87.3 29.4 %attend.1 = (bf16[1024,512]{1,0:T(8,128)(2,1)}, f32[4,2,1024]{2,1,0:T(2,128)}) custom-call(s32[1,1024]{1,0:T(1,128)} %reduce_window_max.29.start_ref, bf16[1024,512]{1,0:T(8,128)(2,1)} %get-tuple-element.112.q_ref, bf16[1024,128]{1,0:T(8,128)(2,1)} %get-tuple-element.113.kv_ref), custom_call_target="tpu_custom_call" | custom-call | flops 16106127360 | bytes 2097152 | tf_op jit(solution)/shard_map/attend/pallas_call | solution.py:725
  116.7 74.1 %all-gather.6.cloned.1.call-done.refs_1_.refs_2_ = bf16[368,128,128]{2,1,0:T(8,128)(2,1)} async-done(((bf16[46,128,128]{2,1,0:T(8,128)(2,1)}), bf16[368,128,128]{2,1,0:T(8,128)(2,1)}) %all-gather.6.cloned.1.call-update) | async-done | bytes 12058640 | tf_op jit(solution)/shard_map/all_gather | solution.py:1168
  190.8 3.2 place_blocks.5.refs_2_.refs_4_
  194.0 5.8 project_rows.3
  199.8 4.4 collective-permute-done.got_ref
  205.5 1.6 copy-done.3
  207.1 3.0 add_near.4
  211.6 8.7 %place_blocks.6 = (bf16[2048,2816]{1,0:T(8,128)(2,1)}, bf16[1408,2048]{1,0:T(8,128)(2,1)}) custom-call(s32[690]{0:T(1024)} %constant.81.clone.refs_0_, s32[276]{0:T(512)} %constant.82.clone.refs_1_, bf16[368,128,128]{2,1,0:T(8,128)(2,1)} %all-gather.6.cloned.1.call-done.refs_1_.refs_2_, ...), custom_call_target="tpu_custom_call", output_to_operand_aliasing={{0}: (3, {}), {1}: (4, {})} | custom-call | bytes 21102592 | tf_op jit(solution)/shard_map/place_blocks/pallas_call | solution.py:169
  220.3 15.2 %collective-permute-done.1.b_ref = bf16[256,2048]{1,0:T(8,128)(2,1)S(1)} collective-permute-done((bf16[256,2048]{1,0:T(8,128)(2,1)}, bf16[256,2048]{1,0:T(8,128)(2,1)S(1)}, u32[]{:S(2)}, u32[]{:S(2)}) %collective-permute-start.1) | collective-permute-done | bytes 1048608 | tf_op jit(solution)/shard_map/ppermute | solution.py:1127
  235.6 3.3 second_norm.1
  240.4 9.8 %all-gather.8.cloned.1.call-done.refs_2_ = bf16[160,128,128]{2,1,0:T(8,128)(2,1)} async-done(((bf16[20,128,128]{2,1,0:T(8,128)(2,1)}), bf16[160,128,128]{2,1,0:T(8,128)(2,1)}) %all-gather.8.cloned.1.call-update) | async-done | bytes 5242896 | tf_op jit(solution)/shard_map/all_gather | solution.py:1168
  250.1 5.5 place_blocks.7
  255.7 12.0 %down_back.1.refs_6_ = f32[1024,1408]{1,0:T(8,128)} custom-call(bf16[1024,2048]{1,0:T(8,128)(2,1)} %pad_maximum_fusion.g_ref.refs_1_.refs_3_, bf16[1408,2048]{1,0:T(8,128)(2,1)} %get-tuple-element.135.w_ref.refs_0_.refs_1_, bf16[1408,2048]{1,0:T(8,128)(2,1)} %get-tuple-element.135.w_ref.refs_0_.refs_1_), custom_call_target="tpu_custom_call" | custom-call | flops 5905580032 | bytes 15728640 | tf_op jit(solution)/shard_map/down_back/pallas_call | solution.py:563
  267.7 2.6 collective-permute-done.4.refs_3_
  270.3 36.3 %feed_forward.1 = (bf16[1024,1408]{1,0:T(8,128)(2,1)}, bf16[2,1024,1408]{2,1,0:T(8,128)(2,1)}, bf16[1024,2048]{1,0:T(8,128)(2,1)}, bf16[512,2048]{1,0:T(8,128)(2,1)}, bf16[512,2048]{1,0:T(8,128)(2,1)}) custom-call(bf16[256,2048]{1,0:T(8,128)(2,1)S(1)} %copy-done.6, bf16[256,2048]{1,0:T(8,128)(2,1)S(1)} %collective-permute-done.2.refs_1_, ...), custom_call_target="tpu_custom_call" | custom-call | flops 23622320128 | bytes 41680896 | tf_op jit(solution)/shard_map/feed_forward/pallas_call | solution.py:436
  306.7 4.9 grad_blocks.6
  311.6 3.0 add_near.5
  316.1 3.7 grad_strips.1.refs_3_
  319.8 9.4 %grad_blocks.7 = (bf16[368,128,128]{2,1,0:T(8,128)(2,1)}, bf16[160,128,128]{2,1,0:T(8,128)(2,1)}) custom-call(bf16[1024,2048]{1,0:T(8,128)(2,1)} %get-tuple-element.155.refs_0_, bf16[2,1024,1408]{2,1,0:T(8,128)(2,1)} %get-tuple-element.149.refs_1_, bf16[368,128,128]{2,1,0:T(8,128)(2,1)} %get-tuple-element.142.refs_2_, ...), custom_call_target="tpu_custom_call", output_to_operand_aliasing={{0}: (2, {}), {1}: (3, {})} | custom-call | flops 8589934592 | bytes 21495808 | tf_op jit(solution)/shard_map/grad_blocks/pallas_call | solution.py:313
  329.3 11.0 %collective-permute-done.6.b_ref = bf16[256,2048]{1,0:T(8,128)(2,1)S(1)} collective-permute-done((bf16[256,2048]{1,0:T(8,128)(2,1)}, bf16[256,2048]{1,0:T(8,128)(2,1)S(1)}, u32[]{:S(2)}, u32[]{:S(2)}) %collective-permute-start.6) | collective-permute-done | bytes 1048608 | tf_op jit(solution)/shard_map/ppermute | solution.py:1127
  340.3 4.7 norm_back.2
  346.5 16.6 %grad_blocks.8 = (bf16[144,128,128]{2,1,0:T(8,128)(2,1)}, bf16[368,128,128]{2,1,0:T(8,128)(2,1)}) custom-call(bf16[1024,2048]{1,0:T(8,128)(2,1)} %get-tuple-element.155.refs_0_, bf16[2,1024,1408]{2,1,0:T(8,128)(2,1)} %get-tuple-element.149.refs_1_, bf16[368,128,128]{2,1,0:T(8,128)(2,1)} %get-tuple-element.150.refs_2_), custom_call_target="tpu_custom_call", output_to_operand_aliasing={{1}: (2, {})} | custom-call | flops 15032385536 | bytes 21495808 | tf_op jit(solution)/shard_map/grad_blocks/pallas_call | solution.py:313
  363.1 9.8 %grad_blocks.9 = (bf16[144,128,128]{2,1,0:T(8,128)(2,1)}, bf16[368,128,128]{2,1,0:T(8,128)(2,1)}) custom-call(bf16[1024,1408]{1,0:T(8,128)(2,1)} %get-tuple-element.163.refs_0_.refs_2_, bf16[1024,2048]{1,0:T(8,128)(2,1)} %pad_maximum_fusion.g_ref.refs_1_.refs_3_, ...), custom_call_target="tpu_custom_call", output_to_operand_aliasing={{0}: (2, {}), {1}: (3, {})} | custom-call | flops 8858370048 | bytes 12845056 | tf_op jit(solution)/shard_map/grad_blocks/pallas_call | solution.py:313
  373.6 2.3 collective-permute-done.9.refs_5_.refs_3_
  376.8 6.8 %grad_blocks.10 = (bf16[144,128,128]{2,1,0:T(8,128)(2,1)}, bf16[368,128,128]{2,1,0:T(8,128)(2,1)}) custom-call(s32[4]{0:T(128)} %broadcast_xor_fusion.refs_0_.order_ref, bf16[1024,512]{1,0:T(8,128)(2,1)} %get-tuple-element.114.refs_1_, bf16[256,2048]{1,0:T(8,128)(2,1)} %get-tuple-element.153.refs_2_.refs_0_, ...), custom_call_target="tpu_custom_call", output_to_operand_aliasing={{0}: (6, {}), {1}: (7, {})} | custom-call | flops 4294967296 | bytes 7340032 | tf_op jit(solution)/shard_map/grad_blocks/pallas_call | solution.py:313
  383.7 10.6 %project_rows.4 = (bf16[512,2048]{1,0:T(8,128)(2,1)}, bf16[512,2048]{1,0:T(8,128)(2,1)}) custom-call(bf16[1024,1408]{1,0:T(8,128)(2,1)} %get-tuple-element.163.refs_0_.refs_2_, bf16[1408,2048]{1,0:T(8,128)(2,1)} %get-tuple-element.135.w_ref.refs_0_.refs_1_), custom_call_target="tpu_custom_call" | custom-call | flops 5905580032 | bytes 12845056 | tf_op jit(solution)/shard_map/project_rows/pallas_call | solution.py:518
  394.7 4.0 collective-permute-done.10.got_ref
  400.0 1.6 copy-done.5
  401.6 3.0 add_near.6
  405.1 6.0 %to_heads.1.g_ref = bf16[1024,512]{1,0:T(8,128)(2,1)} custom-call(s32[4]{0:T(128)} %broadcast_xor_fusion.refs_0_.order_ref, bf16[256,2048]{1,0:T(8,128)(2,1)} %get-tuple-element.153.refs_2_.refs_0_, bf16[256,2048]{1,0:T(8,128)(2,1)} %copy-done.14, bf16[256,2048]{1,0:T(8,128)(2,1)} %copy-done.15, bf16[256,2048]{1,0:T(8,128)(2,1)} %copy-done.16, ...), custom_call_target="tpu_custom_call" | custom-call | flops 2147483648 | bytes 6291456 | tf_op jit(solution)/shard_map/to_heads/pallas_call | solution.py:593
  411.1 33.6 %attend_back.1 = (bf16[1024,512]{1,0:T(8,128)(2,1)}, bf16[1024,128]{1,0:T(8,128)(2,1)}) custom-call(s32[1,1024]{1,0:T(1,128)} %reduce_window_max.29.start_ref, bf16[1024,512]{1,0:T(8,128)(2,1)} %get-tuple-element.112.q_ref, bf16[1024,128]{1,0:T(8,128)(2,1)} %get-tuple-element.113.kv_ref, f32[4,2,1024]{2,1,0:T(2,128)} %get-tuple-element.167.log_ref, ...), custom_call_target="tpu_custom_call" | custom-call | flops 42949672960 | bytes 8388608 | tf_op jit(solution)/shard_map/attend_back/pallas_call | solution.py:800
  444.8 3.1 add_convert_fusion
  447.8 7.0 %project_rows.5 = (bf16[512,2048]{1,0:T(8,128)(2,1)}, bf16[512,2048]{1,0:T(8,128)(2,1)}) custom-call(s32[4]{0:T(128)} %broadcast_xor_fusion.refs_0_.order_ref, bf16[1024,512]{1,0:T(8,128)(2,1)} %get-tuple-element.172.refs_1_, bf16[1024,128]{1,0:T(8,128)(2,1)} %get-tuple-element.173.refs_2_, bf16[2048,640]{1,0:T(8,128)(2,1)} %get-tuple-element.109.w_ref.refs_3_), custom_call_target="tpu_custom_call" | custom-call | flops 2684354560 | bytes 8126464 | tf_op jit(solution)/shard_map/project_rows/pallas_call | solution.py:518
  455.0 4.3 multiply_reduce_fusion.1
  459.3 1.7 collective-permute-start.13
  461.0 2.1 collective-permute-done.13
  465.1 1.6 copy-done.1
  466.7 3.0 add_near.7
  469.7 1.6 collective-permute-start.14
  471.3 12.4 %grad_blocks.11 = bf16[144,128,128]{2,1,0:T(8,128)(2,1)} custom-call(bf16[1024,2048]{1,0:T(8,128)(2,1)} %first_norm.1.x_ref.refs_0_, bf16[1024,512]{1,0:T(8,128)(2,1)} %get-tuple-element.172.refs_1_, bf16[1024,128]{1,0:T(8,128)(2,1)} %get-tuple-element.173.refs_2_, bf16[144,128,128]{2,1,0:T(8,128)(2,1)} %get-tuple-element.161.refs_3_), custom_call_target="tpu_custom_call", output_to_operand_aliasing={{}: (3, {})} | custom-call | flops 5368709120 | bytes 8126464 | tf_op jit(solution)/shard_map/grad_blocks/pallas_call | solution.py:313
  483.7 10.9 %collective-permute-done.14.b_ref = bf16[256,2048]{1,0:T(8,128)(2,1)S(1)} collective-permute-done((bf16[256,2048]{1,0:T(8,128)(2,1)}, bf16[256,2048]{1,0:T(8,128)(2,1)S(1)}, u32[]{:S(2)}, u32[]{:S(2)}) %collective-permute-start.14) | collective-permute-done | bytes 1048608 | tf_op jit(solution)/shard_map/ppermute | solution.py:1127
  494.6 4.6 norm_back.3
  502.5 8.5 %shampoo.3 = (f32[84,128,128]{2,1,0:T(8,128)}, f32[84,128,128]{2,1,0:T(8,128)}, f32[84,128,128]{2,1,0:T(8,128)}, f32[84,128,128]{2,1,0:T(8,128)}, f32[84,128,128]{2,1,0:T(8,128)}) custom-call(s32[20]{0:T(128)} %slice_bitcast_fusion.1.places_ref, bf16[20,128,128]{2,1,0:T(8,128)(2,1)} %reduce-scatter.6.cloned.1.call-done.g_ref, f32[84,128,128]{2,1,0:T(8,128)} %refs_0_.9, ...), custom_call_target="tpu_custom_call" | custom-call | flops 335544320 | bytes 15073280 | tf_op jit(solution)/shard_map/shampoo/pallas_call | solution.py:898
  512.1 15.7 %shampoo.4 = (f32[84,128,128]{2,1,0:T(8,128)}, f32[84,128,128]{2,1,0:T(8,128)}, f32[84,128,128]{2,1,0:T(8,128)}, f32[84,128,128]{2,1,0:T(8,128)}, f32[84,128,128]{2,1,0:T(8,128)}) custom-call(s32[46]{0:T(128)} %slice_bitcast_fusion.2.places_ref, ...), custom_call_target="tpu_custom_call", output_to_operand_aliasing={{0}: (8, {}), {1}: (9, {}), {2}: (10, {}), {3}: (11, {}), {... | custom-call | flops 771751936 | bytes 34668544 | tf_op jit(solution)/shard_map/shampoo/pallas_call | solution.py:898
  528.4 1.8 collective-permute-done.21
  531.4 3.0 collective-permute-done.22
  535.2 3.5 collective-permute-done.23
  538.7 1.8 collective-permute-start.24
  541.1 4.6 collective-permute-done.19
  547.0 2.3 broadcast_select_fusion.11
  549.3 2.3 maximum_bitcast_fusion
  551.9 3.9 maximum_convert_fusion
  555.8 12.5 %reduce-scatter.8.cloned.1.call-done.g_ref = bf16[18,128,128]{2,1,0:T(8,128)(2,1)} async-done(((bf16[144,128,128]{2,1,0:T(8,128)(2,1)}), bf16[18,128,128]{2,1,0:T(8,128)(2,1)}) %reduce-scatter.8.cloned.1.call-update) | async-done | bytes 589840 | tf_op jit(solution)/shard_map/reduce_scatter | solution.py:1225
  568.3 7.5 %shampoo.5 = (f32[84,128,128]{2,1,0:T(8,128)}, f32[84,128,128]{2,1,0:T(8,128)}, f32[84,128,128]{2,1,0:T(8,128)}, f32[84,128,128]{2,1,0:T(8,128)}, f32[84,128,128]{2,1,0:T(8,128)}) custom-call(s32[18]{0:T(128)} %slice_bitcast_fusion.places_ref, ...), custom_call_target="tpu_custom_call", output_to_operand_aliasing={{0}: (8, {}), {1}: (9, {}), {2}: (10, {}), {3}: (11, {}), {... | custom-call | flops 301989888 | bytes 13565952 | tf_op jit(solution)/shard_map/shampoo/pallas_call | solution.py:898
  (127 shorter events, 31.5 us)
Async XLA Ops:
  7.2 59.9 %all-gather.4.cloned.1.call-start = ((), (), s32[]{:S(2)}) async-start(), calls=%async_computation.3 | async-start | bytes 5308416 | tf_op jit(solution)/shard_map/all_gather | solution.py:1168
  11.3 5.7 copy-start.20
  11.4 6.5 %copy-start.19 = (f32[2,2048]{1,0:T(2,128)S(1)}, f32[2,2048]{1,0:T(2,128)}, u32[]{:S(2)}) copy-start(f32[2,2048]{1,0:T(2,128)} %param.26) | copy-start | bytes 49156
  11.4 179.4 %all-gather.6.cloned.1.call-start = ((), (), s32[]{:S(2)}) async-start(), calls=%async_computation.4 | async-start | bytes 13565952 | tf_op jit(solution)/shard_map/all_gather | solution.py:1168
  16.2 233.9 %all-gather.8.cloned.1.call-start = ((), (), s32[]{:S(2)}) async-start(), calls=%async_computation.5 | async-start | bytes 5898240 | tf_op jit(solution)/shard_map/all_gather | solution.py:1168
  17.0 485.5 %reduce-scatter.6.cloned.1.call-start = ((), (), s32[]{:S(2)}) async-start(), calls=%async_computation.7 | async-start | bytes 5898240 | tf_op jit(solution)/shard_map/reduce_scatter | solution.py:1225
  19.1 7.4 %copy-start.22 = (s32[1,1024]{1,0:T(1,128)S(1)}, s32[1,1024]{1,0:T(1,128)}, u32[]{:S(2)}) copy-start(s32[1,1024]{1,0:T(1,128)} %param.24) | copy-start | bytes 12292
  26.5 3.9 copy-start.24
  26.5 4.4 copy-start.7
  31.5 2.7 copy-start.8
  31.5 4.1 copy-start.9
  36.6 1.0 copy-start.11
  199.8 4.4 collective-permute-start
  204.2 1.3 copy-start.2
  205.5 1.6 copy-start.3
  210.1 25.4 %collective-permute-start.1 = (bf16[256,2048]{1,0:T(8,128)(2,1)}, bf16[256,2048]{1,0:T(8,128)(2,1)S(1)}, u32[]{:S(2)}, u32[]{:S(2)}) collective-permute-start(bf16[256,2048]{1,0:T(8,128)(2,1)} %get-tuple-element.121), channel_id=1, source_target_pairs={{0,2},{1,3},{2,0},{3,1},{4,6},{5,7},{6,4},{7,5},{8,10},{9,11},{10,... | collective-permute-start | bytes 3145736 | tf_op jit(solution)/shard_map/ppermute | solution.py:1127
  238.9 28.8 %collective-permute-start.2 = (bf16[256,2048]{1,0:T(8,128)(2,1)}, bf16[256,2048]{1,0:T(8,128)(2,1)S(1)}, u32[]{:S(2)}, u32[]{:S(2)}) collective-permute-start(bf16[256,2048]{1,0:T(8,128)(2,1)} %get-tuple-element.129.refs_0_), channel_id=1, source_target_pairs={{0,2},{1,3},{2,0},{3,1},{4,6},{5,7},{6,4},{7,5},{8,10},{9,11},{10,... | collective-permute-start | bytes 3145736 | tf_op jit(solution)/shard_map/ppermute | solution.py:1127
  240.4 27.3 %collective-permute-start.3 = (bf16[256,2048]{1,0:T(8,128)(2,1)}, bf16[256,2048]{1,0:T(8,128)(2,1)S(1)}, u32[]{:S(2)}, u32[]{:S(2)}) collective-permute-start(bf16[256,2048]{1,0:T(8,128)(2,1)} %get-tuple-element.129.refs_0_), channel_id=1, source_target_pairs={{0,1},{1,0},{2,3},{3,2},{4,5},{5,4},{6,7},{7,6},{8,9},{9,8},{10,11... | collective-permute-start | bytes 3145736 | tf_op jit(solution)/shard_map/ppermute | solution.py:1127
  255.7 14.7 %copy-start.6 = (bf16[256,2048]{1,0:T(8,128)(2,1)S(1)}, bf16[256,2048]{1,0:T(8,128)(2,1)}, u32[]{:S(2)}) copy-start(bf16[256,2048]{1,0:T(8,128)(2,1)} %get-tuple-element.129.refs_0_) | copy-start | bytes 3145732
  267.7 2.7 collective-permute-start.4
  306.6 5.0 collective-permute-start.5
  314.6 25.7 %collective-permute-start.6 = (bf16[256,2048]{1,0:T(8,128)(2,1)}, bf16[256,2048]{1,0:T(8,128)(2,1)S(1)}, u32[]{:S(2)}, u32[]{:S(2)}) collective-permute-start(bf16[256,2048]{1,0:T(8,128)(2,1)} %get-tuple-element.147), channel_id=1, source_target_pairs={{0,2},{1,3},{2,0},{3,1},{4,6},{5,7},{6,4},{7,5},{8,10},{9,11},{10,... | collective-permute-start | bytes 3145736 | tf_op jit(solution)/shard_map/ppermute | solution.py:1127
  329.2 182.9 %reduce-scatter.4.cloned.1.call-start = ((), (), s32[]{:S(2)}) async-start(), calls=%async_computation.6 | async-start | bytes 13565952 | tf_op jit(solution)/shard_map/reduce_scatter | solution.py:1225
  345.0 27.9 %collective-permute-start.7 = (bf16[256,2048]{1,0:T(8,128)(2,1)}, bf16[256,2048]{1,0:T(8,128)(2,1)S(1)}, u32[]{:S(2)}, u32[]{:S(2)}) collective-permute-start(bf16[256,2048]{1,0:T(8,128)(2,1)} %get-tuple-element.153.refs_2_.refs_0_), channel_id=1, source_target_pairs={{0,2},{1,3},{2,0},{3,1},{4,6},{5,7},{6,4},{7,5},{8,10},{9,11},{10,... | collective-permute-start | bytes 3145736 | tf_op jit(solution)/shard_map/ppermute | solution.py:1127
  346.5 27.0 %collective-permute-start.8 = (bf16[256,2048]{1,0:T(8,128)(2,1)}, bf16[256,2048]{1,0:T(8,128)(2,1)S(1)}, u32[]{:S(2)}, u32[]{:S(2)}) collective-permute-start(bf16[256,2048]{1,0:T(8,128)(2,1)} %get-tuple-element.153.refs_2_.refs_0_), channel_id=1, source_target_pairs={{0,1},{1,0},{2,3},{3,2},{4,5},{5,4},{6,7},{7,6},{8,9},{9,8},{10,11... | collective-permute-start | bytes 3145736 | tf_op jit(solution)/shard_map/ppermute | solution.py:1127
  372.9 2.9 copy-start.14
  373.0 2.9 collective-permute-start.9
  373.6 2.3 copy-start.15
  375.8 1.0 copy-start.16
  383.6 184.7 %reduce-scatter.8.cloned.1.call-start = ((), (), s32[]{:S(2)}) async-start(), calls=%async_computation.8 | async-start | bytes 5308416 | tf_op jit(solution)/shard_map/reduce_scatter | solution.py:1225
  394.3 4.4 collective-permute-start.10
  398.7 1.3 copy-start.4
  400.0 1.6 copy-start.5
  404.6 40.2 %collective-permute-start.11 = (bf16[256,2048]{1,0:T(8,128)(2,1)}, bf16[256,2048]{1,0:T(8,128)(2,1)S(1)}, u32[]{:S(2)}, u32[]{:S(2)}) collective-permute-start(bf16[256,2048]{1,0:T(8,128)(2,1)} %get-tuple-element.168), channel_id=1, source_target_pairs={{0,2},{1,3},{2,0},{3,1},{4,6},{5,7},{6,4},{7,5},{8,10},{9,11},{10,... | collective-permute-start | bytes 3145736 | tf_op jit(solution)/shard_map/ppermute | solution.py:1127
  411.1 33.6 %copy-start.12 = (f32[256,2048]{1,0:T(8,128)S(1)}, f32[256,2048]{1,0:T(8,128)}, u32[]{:S(2)}) copy-start(f32[256,2048]{1,0:T(8,128)} %get-tuple-element.128.x_ref) | copy-start | bytes 6291460
  447.8 7.1 %copy-start.21 = (f32[1024]{0:T(1024)S(1)}, f32[1024]{0:T(1024)}, u32[]{:S(2)}) copy-start(f32[1024]{0:T(1024)} %add_rsqrt_fusion) | copy-start | bytes 12292
  454.8 8.9 %collective-permute-start.12 = (bf16[512,2048]{1,0:T(8,128)(2,1)}, bf16[512,2048]{1,0:T(8,128)(2,1)S(1)}, u32[]{:S(2)}, u32[]{:S(2)}) collective-permute-start(bf16[512,2048]{1,0:T(8,128)(2,1)} %get-tuple-element.175), channel_id=1, source_target_pairs={{0,1},{1,0},{2,3},{3,2},{4,5},{5,4},{6,7},{7,6},{8,9},{9,8},{10,11... | collective-permute-start | bytes 6291464 | tf_op jit(solution)/shard_map/ppermute | solution.py:1127
  455.0 4.4 copy-start.18
  459.3 3.8 collective-permute-start.13
  463.8 1.3 copy-start
  465.1 1.6 copy-start.1
  469.7 25.0 %collective-permute-start.14 = (bf16[256,2048]{1,0:T(8,128)(2,1)}, bf16[256,2048]{1,0:T(8,128)(2,1)S(1)}, u32[]{:S(2)}, u32[]{:S(2)}) collective-permute-start(bf16[256,2048]{1,0:T(8,128)(2,1)} %get-tuple-element.181), channel_id=1, source_target_pairs={{0,2},{1,3},{2,0},{3,1},{4,6},{5,7},{6,4},{7,5},{8,10},{9,11},{10,... | collective-permute-start | bytes 3145736 | tf_op jit(solution)/shard_map/ppermute | solution.py:1127
  494.6 4.6 copy-start.10
  494.6 6.1 %copy-start.23 = (s32[1,84]{1,0:T(1,128)S(1)}, s32[1,84]{1,0:T(1,128)}, u32[]{:S(2)}) copy-start(s32[1,84]{1,0:T(1,128)} %get-tuple-element.236) | copy-start | bytes 1012
  499.2 28.5 %collective-permute-start.16 = (bf16[256,2048]{1,0:T(8,128)(2,1)S(1)}, bf16[256,2048]{1,0:T(8,128)(2,1)}, u32[]{:S(2)}, u32[]{:S(2)}) collective-permute-start(bf16[256,2048]{1,0:T(8,128)(2,1)S(1)} %copy-done.10), channel_id=1, source_target_pairs={{0,2},{1,3},{2,0},{3,1},{4,6},{5,7},{6,4},{7,5},{8,10},{9,11},{10,... | collective-permute-start | bytes 3145736 | tf_op jit(solution)/shard_map/ppermute | solution.py:1127
  501.4 44.4 %collective-permute-start.19 = (bf16[256,2048]{1,0:T(8,128)(2,1)}, bf16[256,2048]{1,0:T(8,128)(2,1)S(1)}, u32[]{:S(2)}, u32[]{:S(2)}) collective-permute-start(bf16[256,2048]{1,0:T(8,128)(2,1)} %get-tuple-element.185), channel_id=1, source_target_pairs={{0,2},{1,3},{2,0},{3,1},{4,6},{5,7},{6,4},{7,5},{8,10},{9,11},{10,... | collective-permute-start | bytes 3145736 | tf_op jit(solution)/shard_map/ppermute | solution.py:1127
  502.5 44.5 %collective-permute-start.15 = (bf16[256,2048]{1,0:T(8,128)(2,1)S(1)}, bf16[256,2048]{1,0:T(8,128)(2,1)}, u32[]{:S(2)}, u32[]{:S(2)}) collective-permute-start(bf16[256,2048]{1,0:T(8,128)(2,1)S(1)} %copy-done.10), channel_id=1, source_target_pairs={{0,1},{1,0},{2,3},{3,2},{4,5},{5,4},{6,7},{7,6},{8,9},{9,8},{10,11... | collective-permute-start | bytes 3145736 | tf_op jit(solution)/shard_map/ppermute | solution.py:1127
  512.1 15.8 %copy-start.17 = (f32[2,2048]{1,0:T(2,128)S(1)}, f32[2,2048]{1,0:T(2,128)}, u32[]{:S(2)}) copy-start(f32[2,2048]{1,0:T(2,128)} %fusion.6) | copy-start | bytes 49156
  512.1 29.0 %copy-start.13 = (bf16[256,2048]{1,0:T(8,128)(2,1)S(1)}, bf16[256,2048]{1,0:T(8,128)(2,1)}, u32[]{:S(2)}) copy-start(bf16[256,2048]{1,0:T(8,128)(2,1)} %get-tuple-element.185) | copy-start | bytes 3145732
  527.8 19.2 %collective-permute-start.17 = (bf16[256,2048]{1,0:T(8,128)(2,1)}, bf16[256,2048]{1,0:T(8,128)(2,1)}, u32[]{:S(2)}, u32[]{:S(2)}) collective-permute-start(bf16[256,2048]{1,0:T(8,128)(2,1)} %collective-permute-done.16), channel_id=1, source_target_pairs={{0,1},{1,0},{2,3},{3,2},{4,5},{5,4},{6,7},{7,6},{8,9},{9,8},{10,11... | collective-permute-start | bytes 3145736 | tf_op jit(solution)/shard_map/ppermute | solution.py:1127
  527.9 2.3 collective-permute-start.21
  530.2 4.2 collective-permute-start.22
  534.4 4.3 collective-permute-start.23
  538.7 7.0 %collective-permute-start.24 = (f32[2,2048]{1,0:T(2,128)S(1)}, f32[2,2048]{1,0:T(2,128)S(1)}, u32[]{:S(2)}, u32[]{:S(2)}) collective-permute-start(f32[2,2048]{1,0:T(2,128)S(1)} %add.103), channel_id=1, source_target_pairs={{0,16},{4,20},{8,24},{12,28},{16,0},{20,4},{24,8},{28,12},{1,17},{... | collective-permute-start | bytes 49160 | tf_op jit(solution)/shard_map/ppermute | solution.py:1367
  541.1 10.5 %collective-permute-start.18 = (bf16[256,2048]{1,0:T(8,128)(2,1)S(1)}, bf16[256,2048]{1,0:T(8,128)(2,1)S(1)}, u32[]{:S(2)}, u32[]{:S(2)}) collective-permute-start(bf16[256,2048]{1,0:T(8,128)(2,1)S(1)} %copy-done.13), channel_id=1, source_target_pairs={{0,1},{1,0},{2,3},{3,2},{4,5},{5,4},{6,7},{7,6},{8,9},{9,8},{10,11... | collective-permute-start | bytes 3145736 | tf_op jit(solution)/shard_map/ppermute | solution.py:1127
  545.7 5.8 %collective-permute-start.20 = (bf16[256,2048]{1,0:T(8,128)(2,1)S(1)}, bf16[256,2048]{1,0:T(8,128)(2,1)S(1)}, u32[]{:S(2)}, u32[]{:S(2)}) collective-permute-start(bf16[256,2048]{1,0:T(8,128)(2,1)S(1)} %collective-permute-done.19), channel_id=1, source_target_pairs={{0,1},{1,0},{2,3},{3,2},{4,5},{5,4},{6,7},{7,6},{8,9},{9,8},{10,11... | collective-permute-start | bytes 3145736 | tf_op jit(solution)/shard_map/ppermute | solution.py:1127
Sparse Core Ops, SparseCore 0:
  11.5 55.5 all-gather.3
  69.2 121.5 all-gather.5
  192.4 57.7 all-gather.7
  329.3 57.5 reduce-scatter.5
  389.0 122.9 reduce-scatter.3
  514.2 54.0 reduce-scatter.7

commit v8 on v7

--- a/solution.py
+++ b/solution.py
@@ -832,7 +832,7 @@
     count, block, _ = sums.shape
     group = 3 if count % 3 == 0 else 2 if count % 2 == 0 else 1
     steps = count // group
-    depth = min(4, steps)
+    depth = min(6, steps)
     extra = [] if before is None else list(before)
 
     def mm(a, b, dims):

time: 585 us -> 585 us (level)
  no operation moved by 1% of the time
where the time goes in v8:
time: 585 us; the launch traced here: 583 us
  Pallas kernels  313 us (54%)
  waiting for transfers between devices  191 us (33%)
  other arithmetic  29.5 us (5%)
  starting transfers between devices  17.6 us (3%)
  local copies, waits for them, and re-layouts  16.7 us (3%)
  between operations  14.5 us (2%)
    all_gather x3, waiting for transfers between devices, on_device(): lax.all_gather(chunk, 'dp', axis=0, tiled=True, axis_index_groups=[plan.r...  111 us
    pallas_call x6, Pallas kernels, grad_blocks(): pl.pallas_call(body, grid=(steps,), out_shape=[jax.ShapeDtypeStruct((size...  59.8 us
    ppermute x22, waiting for transfers between devices, partner(): return lax.ppermute(values, 'mp', [(i, i ^ bit) for i in range(mp_count)])  59 us
    pallas_call x1, Pallas kernels, feed_forward(): pl.pallas_call(body, grid=(steps + width // tile,), in_specs=[pl.BlockSpe...  36.3 us
    pallas_call x1, Pallas kernels, attend_back(): pl.pallas_call(body, grid=(groups,), in_specs=[pl.BlockSpec((1, rows), la...  33.6 us
    pallas_call x3, Pallas kernels, shampoo(): pl.pallas_call(body, out_shape=[jax.ShapeDtypeStruct(weights.shape, F32)]...  31.9 us
    pallas_call x1, Pallas kernels, attend(): pl.pallas_call(body, grid=(groups,), in_specs=[pl.BlockSpec((1, rows), la...  29.4 us
    pallas_call x3, Pallas kernels, project_rows(): pl.pallas_call(body, grid=(width // tile,), in_specs=[SMEM] * n_order + w...  23.4 us
  transfers between devices with their start and end apart: 31, of which 17 were waited for; matrix products, arithmetic and copies ran while one was open for 6% of the time, Pallas kernels for 45%

profile of v8, /device:TPU:0, one launch (start us, length us, event | category | flops | bytes accessed | tf_op | source)
XLA Modules:
  0.0 582.8 jit_solution(5237895341858530213)
XLA Ops:
  8.4 2.9 sort_blocks.2
  11.4 4.8 sort_blocks.3
  19.1 7.3 %first_norm.1.x_ref.refs_0_ = bf16[1024,2048]{1,0:T(8,128)(2,1)} custom-call(bf16[1024,2048]{1,0:T(8,128)(2,1)} %bitcast.48, f32[1,2048]{1,0:T(1,128)} %get-tuple-element.232.gain_ref), custom_call_target="tpu_custom_call" | custom-call | flops 20971520 | bytes 8396800 | tf_op jit(solution)/shard_map/first_norm/pallas_call | solution.py:928
  26.6 1.9 fusion
  28.5 1.9 pad_maximum_fusion.2
  31.5 2.6 multiply_reduce_fusion
  37.5 2.3 pad_maximum_fusion.g_ref.refs_1_.refs_3_
  39.8 27.3 %all-gather.4.cloned.1.call-done.refs_4_ = bf16[144,128,128]{2,1,0:T(8,128)(2,1)} async-done(((bf16[18,128,128]{2,1,0:T(8,128)(2,1)}), bf16[144,128,128]{2,1,0:T(8,128)(2,1)}) %all-gather.4.cloned.1.call-update) | async-done | bytes 4718608 | tf_op jit(solution)/shard_map/all_gather | solution.py:1168
  67.1 5.2 place_blocks.4
  72.3 15.0 %project_heads.1 = (bf16[1024,512]{1,0:T(8,128)(2,1)}, bf16[1024,128]{1,0:T(8,128)(2,1)}) custom-call(bf16[1024,2048]{1,0:T(8,128)(2,1)} %first_norm.1.x_ref.refs_0_, bf16[2048,640]{1,0:T(8,128)(2,1)} %get-tuple-element.109.w_ref.refs_3_, f32[1024,128]{1,0:T(8,128)} %get-tuple-element.240.cos_ref, f32[1024,128]{1,0:T(8,128)} %get-tuple-element.241.sin_ref), custom_call_target="tpu_custom_call" | custom-call | flops 2684354560 | bytes 8126464 | tf_op jit(solution)/shard_map/project_heads/pallas_call | solution.py:658
  87.3 29.4 %attend.1 = (bf16[1024,512]{1,0:T(8,128)(2,1)}, f32[4,2,1024]{2,1,0:T(2,128)}) custom-call(s32[1,1024]{1,0:T(1,128)} %reduce_window_max.29.start_ref, bf16[1024,512]{1,0:T(8,128)(2,1)} %get-tuple-element.112.q_ref, bf16[1024,128]{1,0:T(8,128)(2,1)} %get-tuple-element.113.kv_ref), custom_call_target="tpu_custom_call" | custom-call | flops 16106127360 | bytes 2097152 | tf_op jit(solution)/shard_map/attend/pallas_call | solution.py:725
  116.7 74.1 %all-gather.6.cloned.1.call-done.refs_1_.refs_2_ = bf16[368,128,128]{2,1,0:T(8,128)(2,1)} async-done(((bf16[46,128,128]{2,1,0:T(8,128)(2,1)}), bf16[368,128,128]{2,1,0:T(8,128)(2,1)}) %all-gather.6.cloned.1.call-update) | async-done | bytes 12058640 | tf_op jit(solution)/shard_map/all_gather | solution.py:1168
  190.8 3.2 place_blocks.5.refs_2_.refs_4_
  194.0 5.8 project_rows.3
  199.8 4.4 collective-permute-done.got_ref
  205.5 1.6 copy-done.3
  207.1 3.0 add_near.4
  211.6 8.7 %place_blocks.6 = (bf16[2048,2816]{1,0:T(8,128)(2,1)}, bf16[1408,2048]{1,0:T(8,128)(2,1)}) custom-call(s32[690]{0:T(1024)} %constant.81.clone.refs_0_, s32[276]{0:T(512)} %constant.82.clone.refs_1_, bf16[368,128,128]{2,1,0:T(8,128)(2,1)} %all-gather.6.cloned.1.call-done.refs_1_.refs_2_, ...), custom_call_target="tpu_custom_call", output_to_operand_aliasing={{0}: (3, {}), {1}: (4, {})} | custom-call | bytes 21102592 | tf_op jit(solution)/shard_map/place_blocks/pallas_call | solution.py:169
  220.3 15.2 %collective-permute-done.1.b_ref = bf16[256,2048]{1,0:T(8,128)(2,1)S(1)} collective-permute-done((bf16[256,2048]{1,0:T(8,128)(2,1)}, bf16[256,2048]{1,0:T(8,128)(2,1)S(1)}, u32[]{:S(2)}, u32[]{:S(2)}) %collective-permute-start.1) | collective-permute-done | bytes 1048608 | tf_op jit(solution)/shard_map/ppermute | solution.py:1127
  235.6 3.3 second_norm.1
  240.4 9.8 %all-gather.8.cloned.1.call-done.refs_2_ = bf16[160,128,128]{2,1,0:T(8,128)(2,1)} async-done(((bf16[20,128,128]{2,1,0:T(8,128)(2,1)}), bf16[160,128,128]{2,1,0:T(8,128)(2,1)}) %all-gather.8.cloned.1.call-update) | async-done | bytes 5242896 | tf_op jit(solution)/shard_map/all_gather | solution.py:1168
  250.1 5.5 place_blocks.7
  255.7 12.0 %down_back.1.refs_6_ = f32[1024,1408]{1,0:T(8,128)} custom-call(bf16[1024,2048]{1,0:T(8,128)(2,1)} %pad_maximum_fusion.g_ref.refs_1_.refs_3_, bf16[1408,2048]{1,0:T(8,128)(2,1)} %get-tuple-element.135.w_ref.refs_0_.refs_1_, bf16[1408,2048]{1,0:T(8,128)(2,1)} %get-tuple-element.135.w_ref.refs_0_.refs_1_), custom_call_target="tpu_custom_call" | custom-call | flops 5905580032 | bytes 15728640 | tf_op jit(solution)/shard_map/down_back/pallas_call | solution.py:563
  267.7 2.6 collective-permute-done.4.refs_3_
  270.3 36.3 %feed_forward.1 = (bf16[1024,1408]{1,0:T(8,128)(2,1)}, bf16[2,1024,1408]{2,1,0:T(8,128)(2,1)}, bf16[1024,2048]{1,0:T(8,128)(2,1)}, bf16[512,2048]{1,0:T(8,128)(2,1)}, bf16[512,2048]{1,0:T(8,128)(2,1)}) custom-call(bf16[256,2048]{1,0:T(8,128)(2,1)S(1)} %copy-done.6, bf16[256,2048]{1,0:T(8,128)(2,1)S(1)} %collective-permute-done.2.refs_1_, ...), custom_call_target="tpu_custom_call" | custom-call | flops 23622320128 | bytes 41680896 | tf_op jit(solution)/shard_map/feed_forward/pallas_call | solution.py:436
  306.7 4.9 grad_blocks.6
  311.6 3.0 add_near.5
  316.1 3.7 grad_strips.1.refs_3_
  319.8 9.4 %grad_blocks.7 = (bf16[368,128,128]{2,1,0:T(8,128)(2,1)}, bf16[160,128,128]{2,1,0:T(8,128)(2,1)}) custom-call(bf16[1024,2048]{1,0:T(8,128)(2,1)} %get-tuple-element.155.refs_0_, bf16[2,1024,1408]{2,1,0:T(8,128)(2,1)} %get-tuple-element.149.refs_1_, bf16[368,128,128]{2,1,0:T(8,128)(2,1)} %get-tuple-element.142.refs_2_, ...), custom_call_target="tpu_custom_call", output_to_operand_aliasing={{0}: (2, {}), {1}: (3, {})} | custom-call | flops 8589934592 | bytes 21495808 | tf_op jit(solution)/shard_map/grad_blocks/pallas_call | solution.py:313
  329.3 11.0 %collective-permute-done.6.b_ref = bf16[256,2048]{1,0:T(8,128)(2,1)S(1)} collective-permute-done((bf16[256,2048]{1,0:T(8,128)(2,1)}, bf16[256,2048]{1,0:T(8,128)(2,1)S(1)}, u32[]{:S(2)}, u32[]{:S(2)}) %collective-permute-start.6) | collective-permute-done | bytes 1048608 | tf_op jit(solution)/shard_map/ppermute | solution.py:1127
  340.3 4.7 norm_back.2
  346.5 16.6 %grad_blocks.8 = (bf16[144,128,128]{2,1,0:T(8,128)(2,1)}, bf16[368,128,128]{2,1,0:T(8,128)(2,1)}) custom-call(bf16[1024,2048]{1,0:T(8,128)(2,1)} %get-tuple-element.155.refs_0_, bf16[2,1024,1408]{2,1,0:T(8,128)(2,1)} %get-tuple-element.149.refs_1_, bf16[368,128,128]{2,1,0:T(8,128)(2,1)} %get-tuple-element.150.refs_2_), custom_call_target="tpu_custom_call", output_to_operand_aliasing={{1}: (2, {})} | custom-call | flops 15032385536 | bytes 21495808 | tf_op jit(solution)/shard_map/grad_blocks/pallas_call | solution.py:313
  363.1 9.8 %grad_blocks.9 = (bf16[144,128,128]{2,1,0:T(8,128)(2,1)}, bf16[368,128,128]{2,1,0:T(8,128)(2,1)}) custom-call(bf16[1024,1408]{1,0:T(8,128)(2,1)} %get-tuple-element.163.refs_0_.refs_2_, bf16[1024,2048]{1,0:T(8,128)(2,1)} %pad_maximum_fusion.g_ref.refs_1_.refs_3_, ...), custom_call_target="tpu_custom_call", output_to_operand_aliasing={{0}: (2, {}), {1}: (3, {})} | custom-call | flops 8858370048 | bytes 12845056 | tf_op jit(solution)/shard_map/grad_blocks/pallas_call | solution.py:313
  373.6 2.3 collective-permute-done.9.refs_5_.refs_3_
  376.8 6.8 %grad_blocks.10 = (bf16[144,128,128]{2,1,0:T(8,128)(2,1)}, bf16[368,128,128]{2,1,0:T(8,128)(2,1)}) custom-call(s32[4]{0:T(128)} %broadcast_xor_fusion.refs_0_.order_ref, bf16[1024,512]{1,0:T(8,128)(2,1)} %get-tuple-element.114.refs_1_, bf16[256,2048]{1,0:T(8,128)(2,1)} %get-tuple-element.153.refs_2_.refs_0_, ...), custom_call_target="tpu_custom_call", output_to_operand_aliasing={{0}: (6, {}), {1}: (7, {})} | custom-call | flops 4294967296 | bytes 7340032 | tf_op jit(solution)/shard_map/grad_blocks/pallas_call | solution.py:313
  383.7 10.6 %project_rows.4 = (bf16[512,2048]{1,0:T(8,128)(2,1)}, bf16[512,2048]{1,0:T(8,128)(2,1)}) custom-call(bf16[1024,1408]{1,0:T(8,128)(2,1)} %get-tuple-element.163.refs_0_.refs_2_, bf16[1408,2048]{1,0:T(8,128)(2,1)} %get-tuple-element.135.w_ref.refs_0_.refs_1_), custom_call_target="tpu_custom_call" | custom-call | flops 5905580032 | bytes 12845056 | tf_op jit(solution)/shard_map/project_rows/pallas_call | solution.py:518
  394.7 4.0 collective-permute-done.10.got_ref
  400.0 1.6 copy-done.5
  401.6 3.0 add_near.6
  405.1 6.0 %to_heads.1.g_ref = bf16[1024,512]{1,0:T(8,128)(2,1)} custom-call(s32[4]{0:T(128)} %broadcast_xor_fusion.refs_0_.order_ref, bf16[256,2048]{1,0:T(8,128)(2,1)} %get-tuple-element.153.refs_2_.refs_0_, bf16[256,2048]{1,0:T(8,128)(2,1)} %copy-done.14, bf16[256,2048]{1,0:T(8,128)(2,1)} %copy-done.15, bf16[256,2048]{1,0:T(8,128)(2,1)} %copy-done.16, ...), custom_call_target="tpu_custom_call" | custom-call | flops 2147483648 | bytes 6291456 | tf_op jit(solution)/shard_map/to_heads/pallas_call | solution.py:593
  411.1 33.6 %attend_back.1 = (bf16[1024,512]{1,0:T(8,128)(2,1)}, bf16[1024,128]{1,0:T(8,128)(2,1)}) custom-call(s32[1,1024]{1,0:T(1,128)} %reduce_window_max.29.start_ref, bf16[1024,512]{1,0:T(8,128)(2,1)} %get-tuple-element.112.q_ref, bf16[1024,128]{1,0:T(8,128)(2,1)} %get-tuple-element.113.kv_ref, f32[4,2,1024]{2,1,0:T(2,128)} %get-tuple-element.167.log_ref, ...), custom_call_target="tpu_custom_call" | custom-call | flops 42949672960 | bytes 8388608 | tf_op jit(solution)/shard_map/attend_back/pallas_call | solution.py:800
  444.8 3.1 add_convert_fusion
  447.8 7.0 %project_rows.5 = (bf16[512,2048]{1,0:T(8,128)(2,1)}, bf16[512,2048]{1,0:T(8,128)(2,1)}) custom-call(s32[4]{0:T(128)} %broadcast_xor_fusion.refs_0_.order_ref, bf16[1024,512]{1,0:T(8,128)(2,1)} %get-tuple-element.172.refs_1_, bf16[1024,128]{1,0:T(8,128)(2,1)} %get-tuple-element.173.refs_2_, bf16[2048,640]{1,0:T(8,128)(2,1)} %get-tuple-element.109.w_ref.refs_3_), custom_call_target="tpu_custom_call" | custom-call | flops 2684354560 | bytes 8126464 | tf_op jit(solution)/shard_map/project_rows/pallas_call | solution.py:518
  455.0 4.3 multiply_reduce_fusion.1
  459.3 1.7 collective-permute-start.13
  461.0 2.1 collective-permute-done.13
  465.1 1.6 copy-done.1
  466.7 3.0 add_near.7
  469.7 1.6 collective-permute-start.14
  471.3 12.4 %grad_blocks.11 = bf16[144,128,128]{2,1,0:T(8,128)(2,1)} custom-call(bf16[1024,2048]{1,0:T(8,128)(2,1)} %first_norm.1.x_ref.refs_0_, bf16[1024,512]{1,0:T(8,128)(2,1)} %get-tuple-element.172.refs_1_, bf16[1024,128]{1,0:T(8,128)(2,1)} %get-tuple-element.173.refs_2_, bf16[144,128,128]{2,1,0:T(8,128)(2,1)} %get-tuple-element.161.refs_3_), custom_call_target="tpu_custom_call", output_to_operand_aliasing={{}: (3, {})} | custom-call | flops 5368709120 | bytes 8126464 | tf_op jit(solution)/shard_map/grad_blocks/pallas_call | solution.py:313
  483.7 10.9 %collective-permute-done.14.b_ref = bf16[256,2048]{1,0:T(8,128)(2,1)S(1)} collective-permute-done((bf16[256,2048]{1,0:T(8,128)(2,1)}, bf16[256,2048]{1,0:T(8,128)(2,1)S(1)}, u32[]{:S(2)}, u32[]{:S(2)}) %collective-permute-start.14) | collective-permute-done | bytes 1048608 | tf_op jit(solution)/shard_map/ppermute | solution.py:1127
  494.6 4.6 norm_back.3
  502.5 8.5 %shampoo.3 = (f32[84,128,128]{2,1,0:T(8,128)}, f32[84,128,128]{2,1,0:T(8,128)}, f32[84,128,128]{2,1,0:T(8,128)}, f32[84,128,128]{2,1,0:T(8,128)}, f32[84,128,128]{2,1,0:T(8,128)}) custom-call(s32[20]{0:T(128)} %slice_bitcast_fusion.1.places_ref, bf16[20,128,128]{2,1,0:T(8,128)(2,1)} %reduce-scatter.6.cloned.1.call-done.g_ref, f32[84,128,128]{2,1,0:T(8,128)} %refs_0_.9, ...), custom_call_target="tpu_custom_call" | custom-call | flops 335544320 | bytes 15073280 | tf_op jit(solution)/shard_map/shampoo/pallas_call | solution.py:898
  512.1 15.8 %shampoo.4 = (f32[84,128,128]{2,1,0:T(8,128)}, f32[84,128,128]{2,1,0:T(8,128)}, f32[84,128,128]{2,1,0:T(8,128)}, f32[84,128,128]{2,1,0:T(8,128)}, f32[84,128,128]{2,1,0:T(8,128)}) custom-call(s32[46]{0:T(128)} %slice_bitcast_fusion.2.places_ref, ...), custom_call_target="tpu_custom_call", output_to_operand_aliasing={{0}: (8, {}), {1}: (9, {}), {2}: (10, {}), {3}: (11, {}), {... | custom-call | flops 771751936 | bytes 34668544 | tf_op jit(solution)/shard_map/shampoo/pallas_call | solution.py:898
  528.5 1.8 collective-permute-done.21
  531.6 3.0 collective-permute-done.22
  535.3 3.5 collective-permute-done.23
  538.9 1.7 collective-permute-start.24
  541.2 4.5 collective-permute-done.19
  547.0 2.2 broadcast_select_fusion.11
  549.3 2.3 maximum_bitcast_fusion
  551.9 3.9 maximum_convert_fusion
  555.8 12.6 %reduce-scatter.8.cloned.1.call-done.g_ref = bf16[18,128,128]{2,1,0:T(8,128)(2,1)} async-done(((bf16[144,128,128]{2,1,0:T(8,128)(2,1)}), bf16[18,128,128]{2,1,0:T(8,128)(2,1)}) %reduce-scatter.8.cloned.1.call-update) | async-done | bytes 589840 | tf_op jit(solution)/shard_map/reduce_scatter | solution.py:1225
  568.4 7.5 %shampoo.5 = (f32[84,128,128]{2,1,0:T(8,128)}, f32[84,128,128]{2,1,0:T(8,128)}, f32[84,128,128]{2,1,0:T(8,128)}, f32[84,128,128]{2,1,0:T(8,128)}, f32[84,128,128]{2,1,0:T(8,128)}) custom-call(s32[18]{0:T(128)} %slice_bitcast_fusion.places_ref, ...), custom_call_target="tpu_custom_call", output_to_operand_aliasing={{0}: (8, {}), {1}: (9, {}), {2}: (10, {}), {3}: (11, {}), {... | custom-call | flops 301989888 | bytes 13565952 | tf_op jit(solution)/shard_map/shampoo/pallas_call | solution.py:898
  (127 shorter events, 31.5 us)
Async XLA Ops:
  7.2 59.9 %all-gather.4.cloned.1.call-start = ((), (), s32[]{:S(2)}) async-start(), calls=%async_computation.3 | async-start | bytes 5308416 | tf_op jit(solution)/shard_map/all_gather | solution.py:1168
  11.3 5.7 copy-start.20
  11.4 6.5 %copy-start.19 = (f32[2,2048]{1,0:T(2,128)S(1)}, f32[2,2048]{1,0:T(2,128)}, u32[]{:S(2)}) copy-start(f32[2,2048]{1,0:T(2,128)} %param.26) | copy-start | bytes 49156
  11.4 179.4 %all-gather.6.cloned.1.call-start = ((), (), s32[]{:S(2)}) async-start(), calls=%async_computation.4 | async-start | bytes 13565952 | tf_op jit(solution)/shard_map/all_gather | solution.py:1168
  16.2 233.9 %all-gather.8.cloned.1.call-start = ((), (), s32[]{:S(2)}) async-start(), calls=%async_computation.5 | async-start | bytes 5898240 | tf_op jit(solution)/shard_map/all_gather | solution.py:1168
  17.0 485.5 %reduce-scatter.6.cloned.1.call-start = ((), (), s32[]{:S(2)}) async-start(), calls=%async_computation.7 | async-start | bytes 5898240 | tf_op jit(solution)/shard_map/reduce_scatter | solution.py:1225
  19.1 7.4 %copy-start.22 = (s32[1,1024]{1,0:T(1,128)S(1)}, s32[1,1024]{1,0:T(1,128)}, u32[]{:S(2)}) copy-start(s32[1,1024]{1,0:T(1,128)} %param.24) | copy-start | bytes 12292
  26.5 3.9 copy-start.24
  26.5 4.4 copy-start.7
  31.5 2.7 copy-start.8
  31.5 4.1 copy-start.9
  36.6 1.0 copy-start.11
  199.8 4.4 collective-permute-start
  204.2 1.3 copy-start.2
  205.5 1.6 copy-start.3
  210.1 25.4 %collective-permute-start.1 = (bf16[256,2048]{1,0:T(8,128)(2,1)}, bf16[256,2048]{1,0:T(8,128)(2,1)S(1)}, u32[]{:S(2)}, u32[]{:S(2)}) collective-permute-start(bf16[256,2048]{1,0:T(8,128)(2,1)} %get-tuple-element.121), channel_id=1, source_target_pairs={{0,2},{1,3},{2,0},{3,1},{4,6},{5,7},{6,4},{7,5},{8,10},{9,11},{10,... | collective-permute-start | bytes 3145736 | tf_op jit(solution)/shard_map/ppermute | solution.py:1127
  238.9 28.8 %collective-permute-start.2 = (bf16[256,2048]{1,0:T(8,128)(2,1)}, bf16[256,2048]{1,0:T(8,128)(2,1)S(1)}, u32[]{:S(2)}, u32[]{:S(2)}) collective-permute-start(bf16[256,2048]{1,0:T(8,128)(2,1)} %get-tuple-element.129.refs_0_), channel_id=1, source_target_pairs={{0,2},{1,3},{2,0},{3,1},{4,6},{5,7},{6,4},{7,5},{8,10},{9,11},{10,... | collective-permute-start | bytes 3145736 | tf_op jit(solution)/shard_map/ppermute | solution.py:1127
  240.4 27.3 %collective-permute-start.3 = (bf16[256,2048]{1,0:T(8,128)(2,1)}, bf16[256,2048]{1,0:T(8,128)(2,1)S(1)}, u32[]{:S(2)}, u32[]{:S(2)}) collective-permute-start(bf16[256,2048]{1,0:T(8,128)(2,1)} %get-tuple-element.129.refs_0_), channel_id=1, source_target_pairs={{0,1},{1,0},{2,3},{3,2},{4,5},{5,4},{6,7},{7,6},{8,9},{9,8},{10,11... | collective-permute-start | bytes 3145736 | tf_op jit(solution)/shard_map/ppermute | solution.py:1127
  255.7 14.7 %copy-start.6 = (bf16[256,2048]{1,0:T(8,128)(2,1)S(1)}, bf16[256,2048]{1,0:T(8,128)(2,1)}, u32[]{:S(2)}) copy-start(bf16[256,2048]{1,0:T(8,128)(2,1)} %get-tuple-element.129.refs_0_) | copy-start | bytes 3145732
  267.7 2.7 collective-permute-start.4
  306.6 5.0 collective-permute-start.5
  314.6 25.7 %collective-permute-start.6 = (bf16[256,2048]{1,0:T(8,128)(2,1)}, bf16[256,2048]{1,0:T(8,128)(2,1)S(1)}, u32[]{:S(2)}, u32[]{:S(2)}) collective-permute-start(bf16[256,2048]{1,0:T(8,128)(2,1)} %get-tuple-element.147), channel_id=1, source_target_pairs={{0,2},{1,3},{2,0},{3,1},{4,6},{5,7},{6,4},{7,5},{8,10},{9,11},{10,... | collective-permute-start | bytes 3145736 | tf_op jit(solution)/shard_map/ppermute | solution.py:1127
  329.2 182.9 %reduce-scatter.4.cloned.1.call-start = ((), (), s32[]{:S(2)}) async-start(), calls=%async_computation.6 | async-start | bytes 13565952 | tf_op jit(solution)/shard_map/reduce_scatter | solution.py:1225
  345.0 27.9 %collective-permute-start.7 = (bf16[256,2048]{1,0:T(8,128)(2,1)}, bf16[256,2048]{1,0:T(8,128)(2,1)S(1)}, u32[]{:S(2)}, u32[]{:S(2)}) collective-permute-start(bf16[256,2048]{1,0:T(8,128)(2,1)} %get-tuple-element.153.refs_2_.refs_0_), channel_id=1, source_target_pairs={{0,2},{1,3},{2,0},{3,1},{4,6},{5,7},{6,4},{7,5},{8,10},{9,11},{10,... | collective-permute-start | bytes 3145736 | tf_op jit(solution)/shard_map/ppermute | solution.py:1127
  346.5 27.0 %collective-permute-start.8 = (bf16[256,2048]{1,0:T(8,128)(2,1)}, bf16[256,2048]{1,0:T(8,128)(2,1)S(1)}, u32[]{:S(2)}, u32[]{:S(2)}) collective-permute-start(bf16[256,2048]{1,0:T(8,128)(2,1)} %get-tuple-element.153.refs_2_.refs_0_), channel_id=1, source_target_pairs={{0,1},{1,0},{2,3},{3,2},{4,5},{5,4},{6,7},{7,6},{8,9},{9,8},{10,11... | collective-permute-start | bytes 3145736 | tf_op jit(solution)/shard_map/ppermute | solution.py:1127
  372.9 2.9 copy-start.14
  373.0 2.9 collective-permute-start.9
  373.6 2.3 copy-start.15
  375.8 1.0 copy-start.16
  383.6 184.7 %reduce-scatter.8.cloned.1.call-start = ((), (), s32[]{:S(2)}) async-start(), calls=%async_computation.8 | async-start | bytes 5308416 | tf_op jit(solution)/shard_map/reduce_scatter | solution.py:1225
  394.3 4.4 collective-permute-start.10
  398.7 1.3 copy-start.4
  400.0 1.6 copy-start.5
  404.6 40.2 %collective-permute-start.11 = (bf16[256,2048]{1,0:T(8,128)(2,1)}, bf16[256,2048]{1,0:T(8,128)(2,1)S(1)}, u32[]{:S(2)}, u32[]{:S(2)}) collective-permute-start(bf16[256,2048]{1,0:T(8,128)(2,1)} %get-tuple-element.168), channel_id=1, source_target_pairs={{0,2},{1,3},{2,0},{3,1},{4,6},{5,7},{6,4},{7,5},{8,10},{9,11},{10,... | collective-permute-start | bytes 3145736 | tf_op jit(solution)/shard_map/ppermute | solution.py:1127
  411.1 33.6 %copy-start.12 = (f32[256,2048]{1,0:T(8,128)S(1)}, f32[256,2048]{1,0:T(8,128)}, u32[]{:S(2)}) copy-start(f32[256,2048]{1,0:T(8,128)} %get-tuple-element.128.x_ref) | copy-start | bytes 6291460
  447.8 7.1 %copy-start.21 = (f32[1024]{0:T(1024)S(1)}, f32[1024]{0:T(1024)}, u32[]{:S(2)}) copy-start(f32[1024]{0:T(1024)} %add_rsqrt_fusion) | copy-start | bytes 12292
  454.8 8.9 %collective-permute-start.12 = (bf16[512,2048]{1,0:T(8,128)(2,1)}, bf16[512,2048]{1,0:T(8,128)(2,1)S(1)}, u32[]{:S(2)}, u32[]{:S(2)}) collective-permute-start(bf16[512,2048]{1,0:T(8,128)(2,1)} %get-tuple-element.175), channel_id=1, source_target_pairs={{0,1},{1,0},{2,3},{3,2},{4,5},{5,4},{6,7},{7,6},{8,9},{9,8},{10,11... | collective-permute-start | bytes 6291464 | tf_op jit(solution)/shard_map/ppermute | solution.py:1127
  455.0 4.4 copy-start.18
  459.3 3.8 collective-permute-start.13
  463.8 1.3 copy-start
  465.1 1.6 copy-start.1
  469.7 25.0 %collective-permute-start.14 = (bf16[256,2048]{1,0:T(8,128)(2,1)}, bf16[256,2048]{1,0:T(8,128)(2,1)S(1)}, u32[]{:S(2)}, u32[]{:S(2)}) collective-permute-start(bf16[256,2048]{1,0:T(8,128)(2,1)} %get-tuple-element.181), channel_id=1, source_target_pairs={{0,2},{1,3},{2,0},{3,1},{4,6},{5,7},{6,4},{7,5},{8,10},{9,11},{10,... | collective-permute-start | bytes 3145736 | tf_op jit(solution)/shard_map/ppermute | solution.py:1127
  494.6 4.6 copy-start.10
  494.6 6.1 %copy-start.23 = (s32[1,84]{1,0:T(1,128)S(1)}, s32[1,84]{1,0:T(1,128)}, u32[]{:S(2)}) copy-start(s32[1,84]{1,0:T(1,128)} %get-tuple-element.236) | copy-start | bytes 1012
  499.2 28.7 %collective-permute-start.16 = (bf16[256,2048]{1,0:T(8,128)(2,1)S(1)}, bf16[256,2048]{1,0:T(8,128)(2,1)}, u32[]{:S(2)}, u32[]{:S(2)}) collective-permute-start(bf16[256,2048]{1,0:T(8,128)(2,1)S(1)} %copy-done.10), channel_id=1, source_target_pairs={{0,2},{1,3},{2,0},{3,1},{4,6},{5,7},{6,4},{7,5},{8,10},{9,11},{10,... | collective-permute-start | bytes 3145736 | tf_op jit(solution)/shard_map/ppermute | solution.py:1127
  501.4 44.4 %collective-permute-start.19 = (bf16[256,2048]{1,0:T(8,128)(2,1)}, bf16[256,2048]{1,0:T(8,128)(2,1)S(1)}, u32[]{:S(2)}, u32[]{:S(2)}) collective-permute-start(bf16[256,2048]{1,0:T(8,128)(2,1)} %get-tuple-element.185), channel_id=1, source_target_pairs={{0,2},{1,3},{2,0},{3,1},{4,6},{5,7},{6,4},{7,5},{8,10},{9,11},{10,... | collective-permute-start | bytes 3145736 | tf_op jit(solution)/shard_map/ppermute | solution.py:1127
  502.5 44.5 %collective-permute-start.15 = (bf16[256,2048]{1,0:T(8,128)(2,1)S(1)}, bf16[256,2048]{1,0:T(8,128)(2,1)}, u32[]{:S(2)}, u32[]{:S(2)}) collective-permute-start(bf16[256,2048]{1,0:T(8,128)(2,1)S(1)} %copy-done.10), channel_id=1, source_target_pairs={{0,1},{1,0},{2,3},{3,2},{4,5},{5,4},{6,7},{7,6},{8,9},{9,8},{10,11... | collective-permute-start | bytes 3145736 | tf_op jit(solution)/shard_map/ppermute | solution.py:1127
  512.1 15.9 %copy-start.17 = (f32[2,2048]{1,0:T(2,128)S(1)}, f32[2,2048]{1,0:T(2,128)}, u32[]{:S(2)}) copy-start(f32[2,2048]{1,0:T(2,128)} %fusion.6) | copy-start | bytes 49156
  512.1 29.1 %copy-start.13 = (bf16[256,2048]{1,0:T(8,128)(2,1)S(1)}, bf16[256,2048]{1,0:T(8,128)(2,1)}, u32[]{:S(2)}) copy-start(bf16[256,2048]{1,0:T(8,128)(2,1)} %get-tuple-element.185) | copy-start | bytes 3145732
  527.9 19.1 %collective-permute-start.17 = (bf16[256,2048]{1,0:T(8,128)(2,1)}, bf16[256,2048]{1,0:T(8,128)(2,1)}, u32[]{:S(2)}, u32[]{:S(2)}) collective-permute-start(bf16[256,2048]{1,0:T(8,128)(2,1)} %collective-permute-done.16), channel_id=1, source_target_pairs={{0,1},{1,0},{2,3},{3,2},{4,5},{5,4},{6,7},{7,6},{8,9},{9,8},{10,11... | collective-permute-start | bytes 3145736 | tf_op jit(solution)/shard_map/ppermute | solution.py:1127
  528.0 2.3 collective-permute-start.21
  530.3 4.2 collective-permute-start.22
  534.5 4.3 collective-permute-start.23
  538.9 6.9 %collective-permute-start.24 = (f32[2,2048]{1,0:T(2,128)S(1)}, f32[2,2048]{1,0:T(2,128)S(1)}, u32[]{:S(2)}, u32[]{:S(2)}) collective-permute-start(f32[2,2048]{1,0:T(2,128)S(1)} %add.103), channel_id=1, source_target_pairs={{0,16},{4,20},{8,24},{12,28},{16,0},{20,4},{24,8},{28,12},{1,17},{... | collective-permute-start | bytes 49160 | tf_op jit(solution)/shard_map/ppermute | solution.py:1367
  541.2 10.4 %collective-permute-start.18 = (bf16[256,2048]{1,0:T(8,128)(2,1)S(1)}, bf16[256,2048]{1,0:T(8,128)(2,1)S(1)}, u32[]{:S(2)}, u32[]{:S(2)}) collective-permute-start(bf16[256,2048]{1,0:T(8,128)(2,1)S(1)} %copy-done.13), channel_id=1, source_target_pairs={{0,1},{1,0},{2,3},{3,2},{4,5},{5,4},{6,7},{7,6},{8,9},{9,8},{10,11... | collective-permute-start | bytes 3145736 | tf_op jit(solution)/shard_map/ppermute | solution.py:1127
  545.7 5.8 collective-permute-start.20
Sparse Core Ops, SparseCore 0:
  11.5 55.5 all-gather.3
  69.2 121.5 all-gather.5
  192.4 57.7 all-gather.7
  329.3 57.5 reduce-scatter.5
  389.0 123.0 reduce-scatter.3
  514.3 54.0 reduce-scatter.7
